TPU v7x, 32 devices: a whole 2x2x4 slice. The times are simulated.
32 devices in a mesh: dp: 8 (over z, y), seq: 4 (over x, core).
Axes of the slice: x: 2, y: 2, z: 4, core: 2. Of those that a mesh axis runs over, the one named last changes fastest.
Arguments:
- rows_in: bfloat16 [2, 8, 2048, 1120], P(None, 'dp', 'seq'), may hold values from -6 to 6
- out_cotangent: bfloat16 [2, 8, 2048, 1120], P(None, 'dp', 'seq'), may hold values from -6 to 6
- cell_lengths: int32 [2, 8, 11], P(None, 'dp'), may hold values from 0 to 2000, as said below
- cell_starts: int32 [2, 8, 11], P(None, 'dp'), may hold values from 0 to 2048, as said below
- key_mask: int32 [2, 8, 2048], P(None, 'dp'), may hold values from 0 to 1, as said below
- weights_master: float32 [8, 4, 470400], P('dp', 'seq')
- first_moment: float32 [8, 4, 470400], P('dp', 'seq')
- second_moment: float32 [8, 4, 470400], P('dp', 'seq'), as said below
- small_master: float32 [12, 1120], replicated
- small_first: float32 [12, 1120], replicated, may hold values from -192 to 192
- small_second: float32 [12, 1120], replicated, may hold values from 37.02784 to 589.824
- step_count: int32 [1], replicated, may hold values from 1 to 20
Outputs:
- rows_out: bfloat16 [2, 8, 2048, 1120], P(None, 'dp', 'seq')
- input_grad: bfloat16 [2, 8, 2048, 1120], P(None, 'dp', 'seq')
- weight_grads: float32 [8, 4, 470400], P('dp', 'seq')
- weight_moments: float32 [2, 8, 4, 470400], P(None, 'dp', 'seq')
- weights_new: float32 [8, 4, 470400], P('dp', 'seq')
- weights_copy: bfloat16 [8, 4, 470400], P('dp', 'seq')
- lamb_stats: float32 [3, 4], replicated
- small_grads: float32 [12, 1120], replicated
- small_moments: float32 [2, 12, 1120], replicated
- small_new: float32 [12, 1120], replicated
Inputs may be any that keep to these rules, and one draw needn't show every extreme that they name: `cell_lengths`: in each pack the used slots come first and their cells lie end to end from position 0; a used slot holds 200 to 2000 genes, later slots hold 0, and a pack's lengths sum to at most 2048. `cell_starts`: A used slot starts at the sum of the pack's lengths in the slots before it; an empty slot starts at 2048. `key_mask`: 1 exactly at the positions that lie inside a cell of the pack. `second_moment`: positive.
All inputs are finite; a program needn't handle non-finite values.
Results may differ from a plain program's by a relative error of at most 0.01.
The roundings to bfloat16 on the way count: a program that leaves them out, or rounds other values in their place, can miss the bound.
Values may be sent and summed in bfloat16 or wider, within the bound.
No kernel may reach another device: no remote copies, remote signals or barrier semaphores. Data moves between devices by JAX's collectives and lax.ppermute only.
A program may use at most 320 MiB of HBM per device.

v0:
```python
import math

import jax
import jax.numpy as jnp
from jax import lax
from jax.sharding import PartitionSpec as P

HEADS = 20


NORM_EPS = 1e-05
BETA_ONE = 0.9
BETA_TWO = 0.999
ADAM_EPS = 1e-06
DECAY = 0.01
MATRIX_RATE = 0.3
SMALL_RATE = 0.25
MASKED = -1e30


def normalize(row_block, gain, shift):
    center = jnp.mean(row_block, axis=-1, keepdims=True)
    centered = row_block - center
    spread = jnp.mean(centered * centered, axis=-1, keepdims=True)
    return centered * lax.rsqrt(spread + NORM_EPS) * gain + shift


def gelu_tanh(values):
    return jax.nn.gelu(values, approximate=True)


def cell_labels(starts, lengths, length):
    positions = jnp.arange(length, dtype=jnp.int32)
    inside = (positions[:, None] >= starts[None, :]) & (
        positions[:, None] < (starts + lengths)[None, :]
    )
    numbers = jnp.arange(1, starts.shape[0] + 1, dtype=jnp.int32)
    return jnp.max(jnp.where(inside, numbers[None, :], 0), axis=1)


def visible(first_row, labels, key_padding, block_rows):
    row_places = first_row + jnp.arange(block_rows, dtype=jnp.int32)
    col_places = jnp.arange(labels.shape[0], dtype=jnp.int32)
    row_labels = lax.dynamic_slice_in_dim(labels, first_row, block_rows)
    same_cell = (
        (row_labels[:, None] == labels[None, :])
        & (col_places[None, :] < row_places[:, None])
        & (key_padding[None, :] == 1)
    )
    return same_cell | (col_places[None, :] == row_places[:, None])


def attend_forward(queries, key_heads, values, labels, key_padding):
    length, heads_here, head_dim = queries.shape
    block_rows = min(512, length)
    block_count = length // block_rows
    score_scale = head_dim ** (-0.5)

    def one_block(block_args):
        query_block, first_row = block_args
        scores = (
            jnp.einsum("qhd,khd->hqk", query_block, key_heads, preferred_element_type=jnp.float32)
            * score_scale
        )
        allowed = visible(first_row, labels, key_padding, block_rows)
        scores = jnp.where(allowed[None], scores, MASKED)
        row_top = jnp.max(scores, axis=-1, keepdims=True)
        exponent = jnp.exp(scores - row_top)
        row_total = jnp.sum(exponent, axis=-1, keepdims=True)
        probabilities = (exponent / row_total).astype(jnp.bfloat16)
        mixture = jnp.einsum(
            "hqk,khd->qhd", probabilities, values, preferred_element_type=jnp.float32
        )
        return (mixture.astype(jnp.bfloat16), row_top[..., 0] + jnp.log(row_total[..., 0]))

    firsts = jnp.arange(block_count, dtype=jnp.int32) * block_rows
    mixture, log_total = lax.map(
        one_block, (queries.reshape(block_count, block_rows, heads_here, head_dim), firsts)
    )
    return (mixture.reshape(length, heads_here * head_dim), log_total)


def attend_backward(queries, key_heads, values, log_total, grad_heads, labels, key_padding):
    length, heads_here, head_dim = queries.shape
    block_rows = min(512, length)
    block_count = length // block_rows
    score_scale = head_dim ** (-0.5)

    def one_block(carry, block_args):
        grad_keys, grad_values = carry
        query_block, grad_block, total_block, first_row = block_args
        scores = (
            jnp.einsum("qhd,khd->hqk", query_block, key_heads, preferred_element_type=jnp.float32)
            * score_scale
        )
        allowed = visible(first_row, labels, key_padding, block_rows)
        probabilities = jnp.where(
            allowed[None],
            jnp.exp(jnp.where(allowed[None], scores - total_block[..., None], MASKED)),
            0.0,
        )
        grad_probs = jnp.einsum(
            "qhd,khd->hqk", grad_block, values, preferred_element_type=jnp.float32
        )
        row_inner = jnp.sum(probabilities * grad_probs, axis=-1, keepdims=True)
        grad_scores = (probabilities * (grad_probs - row_inner)).astype(jnp.bfloat16)
        grad_values = grad_values + jnp.einsum(
            "hqk,qhd->khd",
            probabilities.astype(jnp.bfloat16),
            grad_block,
            preferred_element_type=jnp.float32,
        )
        grad_keys = (
            grad_keys
            + jnp.einsum(
                "hqk,qhd->khd", grad_scores, query_block, preferred_element_type=jnp.float32
            )
            * score_scale
        )
        grad_query = (
            jnp.einsum("hqk,khd->qhd", grad_scores, key_heads, preferred_element_type=jnp.float32)
            * score_scale
        )
        return ((grad_keys, grad_values), grad_query)

    firsts = jnp.arange(block_count, dtype=jnp.int32) * block_rows
    zeros_heads = jnp.zeros((length, heads_here, head_dim), jnp.float32)
    block_inputs = (
        queries.reshape(block_count, block_rows, heads_here, head_dim),
        grad_heads.reshape(block_count, block_rows, heads_here, head_dim),
        log_total,
        firsts,
    )
    (grad_keys, grad_values), grad_queries = lax.scan(
        one_block, (zeros_heads, zeros_heads), block_inputs
    )
    flat_width = heads_here * head_dim
    return (
        grad_queries.reshape(length, flat_width),
        grad_keys.reshape(length, flat_width),
        grad_values.reshape(length, flat_width),
    )


def per_device(
    rows_in,
    out_cotangent,
    cell_lengths,
    cell_starts,
    key_mask,
    weights_master,
    first_moment,
    second_moment,
    small_master,
    small_first,
    small_second,
    step_count,
):
    model_width = rows_in.shape[3]
    local_rows = rows_in.shape[2]
    length = key_mask.shape[2]
    shard_len = weights_master.shape[2]
    groups = lax.axis_size("seq")
    dp_count = lax.axis_size("dp")
    head_share = model_width // groups
    ff_width = 4 * model_width
    ff_share = ff_width // groups
    heads_here = HEADS // groups
    head_dim = model_width // HEADS
    copies = lax.all_gather(
        weights_master.reshape(1, shard_len).astype(jnp.bfloat16), ("dp", "seq"), axis=0, tiled=True
    )
    per_share = jnp.transpose(copies.reshape(dp_count, groups, shard_len), (1, 0, 2)).reshape(
        groups, dp_count * shard_len
    )
    first_end = 3 * model_width * head_share
    second_end = first_end + head_share * model_width
    third_end = second_end + model_width * ff_share
    w_attn = jnp.transpose(
        per_share[:, :first_end].reshape(groups, model_width, 3, head_share), (1, 2, 0, 3)
    ).reshape(model_width, 3 * model_width)
    w_out = per_share[:, first_end:second_end].reshape(model_width, model_width)
    w_in = jnp.transpose(
        per_share[:, second_end:third_end].reshape(groups, model_width, ff_share), (1, 0, 2)
    ).reshape(model_width, ff_width)
    w_back = per_share[:, third_end:].reshape(ff_width, model_width)
    attn_bias = jnp.concatenate([small_master[4], jnp.zeros_like(small_master[4]), small_master[5]])
    ff_bias = small_master[8:12].reshape(-1)

    def micro_step(carry, micro_batch):
        small_totals, weight_totals = carry
        row_block, cotangent, lengths, starts, padding = micro_batch
        labels = cell_labels(starts[0], lengths[0], length)
        key_padding = padding[0]
        inputs = row_block[0].astype(jnp.float32)
        normed, norm_pull = jax.vjp(normalize, inputs, small_master[0], small_master[1])
        low_one = normed.astype(jnp.bfloat16)
        projected = (
            jnp.dot(low_one, w_attn, preferred_element_type=jnp.float32) + attn_bias
        ).astype(jnp.bfloat16)
        packed = lax.all_to_all(
            projected.reshape(local_rows, 3, groups, head_share),
            "seq",
            split_axis=2,
            concat_axis=0,
            tiled=True,
        ).reshape(length, 3, head_share)
        gathered = lax.all_gather(low_one, "seq", axis=0, tiled=True)
        queries = packed[:, 0].reshape(length, heads_here, head_dim)
        key_heads = packed[:, 1].reshape(length, heads_here, head_dim)
        values = packed[:, 2].reshape(length, heads_here, head_dim)
        mixture, log_total = attend_forward(queries, key_heads, values, labels, key_padding)
        attended = lax.all_to_all(
            mixture.reshape(length, 1, head_share), "seq", split_axis=0, concat_axis=1, tiled=True
        ).reshape(local_rows, model_width)
        branch = jnp.dot(attended, w_out, preferred_element_type=jnp.float32) + small_master[6]
        middle = inputs + branch
        normed_two, second_pull = jax.vjp(normalize, middle, small_master[2], small_master[3])
        low_two = normed_two.astype(jnp.bfloat16)
        inner_sum = jnp.dot(low_two, w_in, preferred_element_type=jnp.float32) + ff_bias
        activated, gelu_pull = jax.vjp(gelu_tanh, inner_sum)
        low_act = activated.astype(jnp.bfloat16)
        mlp_out = jnp.dot(low_act, w_back, preferred_element_type=jnp.float32) + small_master[7]
        result_rows = (middle + mlp_out).astype(jnp.bfloat16)
        grad_y = cotangent[0].astype(jnp.float32)
        grad_e = grad_y.astype(jnp.bfloat16)
        (grad_inner,) = gelu_pull(jnp.dot(grad_e, w_back.T, preferred_element_type=jnp.float32))
        low_inner = grad_inner.astype(jnp.bfloat16)
        act_part, inner_part = (
            lax.all_to_all(
                low_act.reshape(local_rows, groups, ff_share),
                "seq",
                split_axis=1,
                concat_axis=0,
                tiled=True,
            ),
            lax.all_to_all(
                low_inner.reshape(local_rows, groups, ff_share),
                "seq",
                split_axis=1,
                concat_axis=0,
                tiled=True,
            ),
        )
        act_part = act_part.reshape(length, ff_share)
        inner_part = inner_part.reshape(length, ff_share)
        grad_mid_norm, grad_gain_two, grad_shift_two = second_pull(
            jnp.dot(low_inner, w_in.T, preferred_element_type=jnp.float32)
        )
        grad_mid = grad_y + grad_mid_norm
        low_mid = grad_mid.astype(jnp.bfloat16)
        norm_rows, mid_rows, cot_rows = (
            lax.all_gather(low_two, "seq", axis=0, tiled=True),
            lax.all_gather(low_mid, "seq", axis=0, tiled=True),
            lax.all_gather(grad_e, "seq", axis=0, tiled=True),
        )
        share_back = jnp.dot(act_part.T, cot_rows, preferred_element_type=jnp.float32)
        share_in = jnp.dot(norm_rows.T, inner_part, preferred_element_type=jnp.float32)
        share_out = jnp.dot(mixture.T, mid_rows, preferred_element_type=jnp.float32)
        grad_att = jnp.dot(low_mid, w_out.T, preferred_element_type=jnp.float32).astype(
            jnp.bfloat16
        )
        grad_heads = lax.all_to_all(
            grad_att.reshape(local_rows, groups, head_share),
            "seq",
            split_axis=1,
            concat_axis=0,
            tiled=True,
        ).reshape(length, heads_here, head_dim)
        grad_query, grad_key, grad_value = attend_backward(
            queries, key_heads, values, log_total, grad_heads, labels, key_padding
        )
        grad_packed = jnp.stack([grad_query, grad_key, grad_value], axis=1).astype(jnp.bfloat16)
        share_attn = jnp.einsum(
            "rd,rcg->dcg", gathered, grad_packed, preferred_element_type=jnp.float32
        )
        grad_rows = lax.all_to_all(
            grad_packed.reshape(length, 3, 1, head_share),
            "seq",
            split_axis=0,
            concat_axis=2,
            tiled=True,
        ).reshape(local_rows, 3 * model_width)
        grad_bias = jnp.sum(grad_rows.astype(jnp.float32), axis=0)
        grad_low_one = jnp.dot(grad_rows, w_attn.T, preferred_element_type=jnp.float32)
        grad_in_norm, grad_gain_one, grad_shift_one = norm_pull(grad_low_one)
        grad_x = (grad_mid + grad_in_norm).astype(jnp.bfloat16)
        small_rows = jnp.stack(
            [
                grad_gain_one,
                grad_shift_one,
                grad_gain_two,
                grad_shift_two,
                grad_bias[:model_width],
                grad_bias[2 * model_width :],
                jnp.sum(low_mid.astype(jnp.float32), axis=0),
                jnp.sum(grad_e.astype(jnp.float32), axis=0),
            ]
        )
        small_now = jnp.concatenate(
            [small_rows, jnp.sum(low_inner.astype(jnp.float32), axis=0).reshape(4, model_width)]
        )
        matrices = (share_attn, share_out, share_in, share_back)
        summed = tuple((acc_part + new_part for acc_part, new_part in zip(weight_totals, matrices)))
        return ((small_totals + small_now, summed), (result_rows, grad_x))

    start_weights = (
        jnp.zeros((model_width, 3, head_share), jnp.float32),
        jnp.zeros((head_share, model_width), jnp.float32),
        jnp.zeros((model_width, ff_share), jnp.float32),
        jnp.zeros((ff_share, model_width), jnp.float32),
    )
    start_carry = (jnp.zeros((12, model_width), jnp.float32), start_weights)
    (small_totals, weight_totals), (result_all, grad_all) = lax.scan(
        micro_step, start_carry, (rows_in, out_cotangent, cell_lengths, cell_starts, key_mask)
    )
    flat_all = jnp.concatenate([matrix.reshape(-1) for matrix in weight_totals]).reshape(
        dp_count, shard_len
    )
    reduced = lax.psum_scatter(flat_all, "dp", scatter_dimension=0, tiled=True)[0]
    weight = weights_master[0, 0]
    steps_done = step_count[0].astype(jnp.float32)
    fix_one = 1.0 - jnp.exp(steps_done * math.log(BETA_ONE))
    fix_two = 1.0 - jnp.exp(steps_done * math.log(BETA_TWO))
    first_new = BETA_ONE * first_moment[0, 0] + (1.0 - BETA_ONE) * reduced
    second_new = BETA_TWO * second_moment[0, 0] + (1.0 - BETA_TWO) * reduced * reduced
    update = first_new / fix_one / (jnp.sqrt(second_new / fix_two) + ADAM_EPS) + DECAY * weight
    positions = lax.axis_index("dp") * shard_len + jnp.arange(shard_len, dtype=jnp.int32)
    region = (
        (positions >= first_end).astype(jnp.int32)
        + (positions >= second_end).astype(jnp.int32)
        + (positions >= third_end).astype(jnp.int32)
    )
    region_hit = region[None, :] == jnp.arange(4, dtype=jnp.int32)[:, None]
    norm_sums = jnp.stack(
        [
            jnp.sum(jnp.where(region_hit, weight * weight, 0.0), axis=1),
            jnp.sum(jnp.where(region_hit, update * update, 0.0), axis=1),
        ]
    )
    small_grad, norm_sums = lax.psum((small_totals, norm_sums), ("dp", "seq"))
    weight_norms = jnp.sqrt(norm_sums[0])
    update_norms = jnp.sqrt(norm_sums[1])
    ratios = weight_norms / update_norms
    ratio_here = jnp.sum(jnp.where(region_hit, ratios[:, None], 0.0), axis=0)
    new_weight = weight - MATRIX_RATE * ratio_here * update
    small_one = BETA_ONE * small_first + (1.0 - BETA_ONE) * small_grad
    small_two = BETA_TWO * small_second + (1.0 - BETA_TWO) * small_grad * small_grad
    small_updated = small_master - SMALL_RATE * (small_one / fix_one) / (
        jnp.sqrt(small_two / fix_two) + ADAM_EPS
    )
    return (
        result_all[:, None],
        grad_all[:, None],
        reduced[None, None],
        jnp.stack([first_new, second_new])[:, None, None],
        new_weight[None, None],
        new_weight[None, None].astype(jnp.bfloat16),
        jnp.stack([weight_norms, update_norms, ratios]),
        small_grad,
        jnp.stack([small_one, small_two]),
        small_updated,
    )


def solution(mesh):
    in_specs = (
        P(None, "dp", "seq", None),
        P(None, "dp", "seq", None),
        P(None, "dp", None),
        P(None, "dp", None),
        P(None, "dp", None),
        P("dp", "seq", None),
        P("dp", "seq", None),
        P("dp", "seq", None),
        P(),
        P(),
        P(),
        P(),
    )
    out_specs = (
        P(None, "dp", "seq", None),
        P(None, "dp", "seq", None),
        P("dp", "seq", None),
        P(None, "dp", "seq", None),
        P("dp", "seq", None),
        P("dp", "seq", None),
        P(),
        P(),
        P(),
        P(),
    )
    return jax.shard_map(
        per_device, mesh=mesh, in_specs=in_specs, out_specs=out_specs, check_vma=False
    )
```

profile of v0, /device:TPU:0, one launch (start us, length us, event | category | flops | bytes accessed | tf_op | source)
XLA Modules:
  0.0 3342.4 jit_solution(11166793068795374469)
XLA Ops:
  7.2 25.1 multiply_reduce_fusion.4
  34.7 323.7 %all-gather.11.cloned.1.call-done = bf16[32,1,470400]{2,1,0:T(2,128)(2,1)} async-done(((bf16[1,1,470400]{2,1,0:T(2,128)(2,1)}), bf16[32,1,470400]{2,1,0:T(2,128)(2,1)}) %all-gather.11.cloned.1.call-update) | async-done | bytes 30105616 | tf_op jit(solution)/shard_map/all_gather | solution.py:170
  358.4 177.3 %reduce.14 = bf16[32,470400]{1,0:T(8,128)(2,1)} reduce(bf16[32,1,470400]{2,1,0:T(2,128)(2,1)} %all-gather.11.cloned.1.call-done, bf16[]{:T(256)} %constant.231), dimensions={1}, to_apply=%all-gather.1.reduce_sub_computation | reduce | bytes 60211200 | tf_op jit(solution)/shard_map/all_gather | solution.py:170
  535.7 31.3 reshape.657
  577.5 18.9 fusion.123
  605.0 24.9 reshape.718
  639.0 20.0 reshape.663
  659.0 15.3 copy.182
  674.3 14.3 copy.184
  688.5 26.8 reshape.659
  715.4 20.7 copy.181
  736.0 12.0 copy.183
  748.1 24.8 reshape.714
  772.8 20.1 reshape.661
  793.0 1873.8 %while.83 = (s32[]{:T(128)}, f32[12,1120]{1,0:T(8,128)}, f32[1120,3,280]{0,2,1:T(8,128)}, f32[280,1120]{1,0:T(8,128)}, f32[1120,1120]{1,0:T(8,128)}, /*index=5*/...) while((s32[]{:T(128)}, f32[12,1120]{1,0:T(8,128)}, ...), condition=%wide.region_25.26_spmd.clone, body=%wide.region_0.25_spmd.clone.sunk | while | flops 50677227520 | bytes 1060744064 | solution.py:314
  815.9 62.3 %all-to-all-done = bf16[512,3,4,280]{0,3,1,2:T(8,128)(2,1)S(1)} async-done(((bf16[512,3,4,280]{0,3,1,2:T(8,128)(2,1)}), bf16[512,3,4,280]{0,3,1,2:T(8,128)(2,1)S(1)}, u32[]{:S(2)}, u32[]{:S(2)}) %all-to-all-start) | async-done | bytes 3440672 | tf_op jit(solution)/shard_map/while/body/eval_jaxpr/all_to_all | solution.py:201
  894.7 144.3 %while.84 = (s32[]{:T(128)}, bf16[4,512,5,56]{1,3,2,0:T(8,128)(2,1)S(1)}, f32[4,5,512]{2,1,0:T(8,128)}, s32[4]{0:T(128)S(1)}, s32[2048]{0:T(1024)S(1)}, /*index=...) while((s32[]{:T(128)}, ...), condition=%wide.region_7.7_spmd, body=%wide.region_4.6_spmd.sunk | while | flops 1243754496 | bytes 153993440 | solution.py:77
  1054.9 16.9 all-to-all-done.1
  1090.8 16.1 multiply_convert_fusion.4
  1106.9 16.2 convert_reduce_fusion.12
  1123.1 11.1 multiply_reduce_fusion.10
  1172.6 70.3 %all-to-all-done.5 = bf16[512,4,1120]{0,2,1:T(8,128)(2,1)} async-done(((bf16[512,4,1120]{0,2,1:T(8,128)(2,1)}), bf16[512,4,1120]{0,2,1:T(8,128)(2,1)}, u32[]{:S(2)}, u32[]{:S(2)}) %all-to-all-start.5) | async-done | bytes 4587552 | tf_op jit(solution)/shard_map/while/body/eval_jaxpr/all_to_all | solution.py:230
  1247.9 282.2 %while.85 = (s32[]{:T(128)}, f32[2048,5,56]{0,2,1:T(8,128)}, f32[2048,5,56]{0,2,1:T(8,128)}, bf16[4,512,5,56]{1,3,2,0:T(8,128)(2,1)}, bf16[4,512,5,56]{1,3,2,0:T...) while((s32[]{:T(128)}, f32[2048,5,56]{0,2,1:T(8,128)}, ...), condition=%wide.region_14.14_spmd.clone, body=%wide.region_12.13_spmd.clone.sunk | while | flops 3039686656 | bytes 259805424 | solution.py:134
  1276.8 16.2 multiply_reduce_fusion.11
  1293.0 14.9 multiply_convert_fusion.5
  1346.7 16.2 multiply_reduce_fusion.11
  1362.9 14.9 multiply_convert_fusion.5
  1417.5 16.2 multiply_reduce_fusion.11
  1433.7 14.9 multiply_convert_fusion.5
  1488.3 16.2 multiply_reduce_fusion.11
  1504.5 14.9 multiply_convert_fusion.5
  1556.3 14.0 fusion.243
  1585.6 62.1 %all-to-all-done.3 = bf16[2048,3,1,280]{3,1,2,0:T(4,128)(2,1)} async-done(((bf16[2048,3,1,280]{3,1,2,0:T(4,128)(2,1)}), bf16[2048,3,1,280]{3,1,2,0:T(4,128)(2,1)}, u32[]{:S(2)}, u32[]{:S(2)}) %all-to-all-start.3) | async-done | bytes 3440672 | tf_op jit(solution)/shard_map/while/body/eval_jaxpr/all_to_all | solution.py:277
  1694.7 12.8 convolution_add_fusion.10
  1746.3 62.5 %all-to-all-done = bf16[512,3,4,280]{0,3,1,2:T(8,128)(2,1)S(1)} async-done(((bf16[512,3,4,280]{0,3,1,2:T(8,128)(2,1)}), bf16[512,3,4,280]{0,3,1,2:T(8,128)(2,1)S(1)}, u32[]{:S(2)}, u32[]{:S(2)}) %all-to-all-start) | async-done | bytes 3440672 | tf_op jit(solution)/shard_map/while/body/eval_jaxpr/all_to_all | solution.py:201
  1825.3 144.3 %while.84 = (s32[]{:T(128)}, bf16[4,512,5,56]{1,3,2,0:T(8,128)(2,1)S(1)}, f32[4,5,512]{2,1,0:T(8,128)}, s32[4]{0:T(128)S(1)}, s32[2048]{0:T(1024)S(1)}, /*index=...) while((s32[]{:T(128)}, ...), condition=%wide.region_7.7_spmd, body=%wide.region_4.6_spmd.sunk | while | flops 1243754496 | bytes 153993440 | solution.py:77
  1985.5 17.8 all-to-all-done.1
  2022.3 16.1 multiply_convert_fusion.4
  2038.4 16.2 convert_reduce_fusion.12
  2054.6 11.1 multiply_reduce_fusion.10
  2104.2 70.3 %all-to-all-done.5 = bf16[512,4,1120]{0,2,1:T(8,128)(2,1)} async-done(((bf16[512,4,1120]{0,2,1:T(8,128)(2,1)}), bf16[512,4,1120]{0,2,1:T(8,128)(2,1)}, u32[]{:S(2)}, u32[]{:S(2)}) %all-to-all-start.5) | async-done | bytes 4587552 | tf_op jit(solution)/shard_map/while/body/eval_jaxpr/all_to_all | solution.py:230
  2179.4 282.2 %while.85 = (s32[]{:T(128)}, f32[2048,5,56]{0,2,1:T(8,128)}, f32[2048,5,56]{0,2,1:T(8,128)}, bf16[4,512,5,56]{1,3,2,0:T(8,128)(2,1)}, bf16[4,512,5,56]{1,3,2,0:T...) while((s32[]{:T(128)}, f32[2048,5,56]{0,2,1:T(8,128)}, ...), condition=%wide.region_14.14_spmd.clone, body=%wide.region_12.13_spmd.clone.sunk | while | flops 3039686656 | bytes 259805424 | solution.py:134
  2208.3 16.2 multiply_reduce_fusion.11
  2224.5 14.9 multiply_convert_fusion.5
  2278.3 16.2 multiply_reduce_fusion.11
  2294.5 14.9 multiply_convert_fusion.5
  2349.1 16.2 multiply_reduce_fusion.11
  2365.3 14.9 multiply_convert_fusion.5
  2419.9 16.2 multiply_reduce_fusion.11
  2436.1 14.9 multiply_convert_fusion.5
  2487.9 14.0 fusion.243
  2517.1 62.1 %all-to-all-done.3 = bf16[2048,3,1,280]{3,1,2,0:T(4,128)(2,1)} async-done(((bf16[2048,3,1,280]{3,1,2,0:T(4,128)(2,1)}), bf16[2048,3,1,280]{3,1,2,0:T(4,128)(2,1)}, u32[]{:S(2)}, u32[]{:S(2)}) %all-to-all-start.3) | async-done | bytes 3440672 | tf_op jit(solution)/shard_map/while/body/eval_jaxpr/all_to_all | solution.py:277
  2617.3 11.0 fusion.242
  2628.3 14.2 convolution_add_fusion.10
  2642.6 11.6 convolution_add_fusion.9
  2700.0 18.8 pad_maximum_fusion.1
  2718.9 14.8 reshape.669
  2735.2 22.7 fusion.108
  2758.5 436.1 %all-reduce.4.cloned.1.call-done = f32[8,470400]{1,0:T(8,128)} async-done(((f32[8,470400]{1,0:T(8,128)}), f32[8,470400]{1,0:T(8,128)}) %all-reduce.4.cloned.1.call-update) | async-done | bytes 15052816
  3194.6 29.0 bitcast_add_fusion
  3235.1 18.4 select_reduce_fusion.3
  3253.4 40.2 %all-reduce.1 = (f32[2,4]{1,0:T(2,128)S(1)}, f32[12,1120]{1,0:T(8,128)S(1)}) all-reduce(f32[2,4]{1,0:T(2,128)S(1)} %pad_maximum_fusion.4, f32[12,1120]{1,0:T(8,128)S(1)} %copy-done.35), channel_id=1, replica_groups=mesh['dp'=8,'seq'=4] {'dp','seq'}, use_global_device_ids=true, to_apply=%region_29.30 | all-reduce | flops 13448 | bytes 107584 | tf_op jit(solution)/shard_map/psum | solution.py:341
  3293.7 19.7 select_reduce_fusion.1
  3316.7 18.7 fusion.118
  (631 shorter events, 1075.2 us)
Async XLA Ops:
  7.2 351.2 %all-gather.11.cloned.1.call-start = ((), (), s32[]{:S(2)}) async-start(), calls=%async_computation.6 | async-start | bytes 62092800 | tf_op jit(solution)/shard_map/all_gather | solution.py:170
  772.8 20.2 copy-start.9
  797.1 10.7 copy-start.17
  809.9 68.4 %all-to-all-start = ((bf16[512,3,4,280]{0,3,1,2:T(8,128)(2,1)}), bf16[512,3,4,280]{0,3,1,2:T(8,128)(2,1)S(1)}, u32[]{:S(2)}, u32[]{:S(2)}) async-start(bf16[512,3,4,280]{0,3,1,2:T(8,128)(2,1)} %copy.211), calls=%async_computation | async-start | bytes 6881280 | tf_op jit(solution)/shard_map/while/body/eval_jaxpr/all_to_all | solution.py:201
  813.6 871.2 %all-gather.13.cloned.1.call-start = ((), (), s32[]{:S(2)}) async-start(), calls=%async_computation.8 | async-start | bytes 5734400 | tf_op jit(solution)/shard_map/while/body/eval_jaxpr/all_gather | solution.py:208
  907.1 7.1 copy-start
  943.1 7.1 copy-start
  979.1 7.1 copy-start
  1015.1 7.1 copy-start
  1048.5 23.3 all-to-all-start.1
  1052.9 641.8 %all-gather.19.cloned.1.call-start = ((), (), s32[]{:S(2)}) async-start(), calls=%async_computation.11 | async-start | bytes 5734400 | tf_op jit(solution)/shard_map/while/body/eval_jaxpr/all_gather | solution.py:255
  1089.6 44.7 %copy-start.5 = (f32[512,1120]{0,1:T(8,128)}, f32[512,1120]{0,1:T(8,128)S(1)}, u32[]{:S(2)}) copy-start(f32[512,1120]{0,1:T(8,128)S(1)} %get-tuple-element.1335) | copy-start | bytes 6881284 | tf_op jit(solution)/shard_map/while
  1090.8 16.1 copy-start.19
  1090.8 16.1 copy-start.7
  1123.1 11.1 copy-start.16
  1141.0 19.9 all-to-all-start.2
  1160.9 82.0 %all-to-all-start.5 = ((bf16[512,4,1120]{0,2,1:T(8,128)(2,1)}), bf16[512,4,1120]{0,2,1:T(8,128)(2,1)}, u32[]{:S(2)}, u32[]{:S(2)}) async-start(bf16[512,4,1120]{0,2,1:T(8,128)(2,1)} %bitcast.375), calls=%async_computation.5 | async-start | bytes 9175040 | tf_op jit(solution)/shard_map/while/body/eval_jaxpr/all_to_all | solution.py:230
  1165.9 541.6 %all-gather.17.cloned.1.call-start = ((), (), s32[]{:S(2)}) async-start(), calls=%async_computation.10 | async-start | bytes 5734400 | tf_op jit(solution)/shard_map/while/body/eval_jaxpr/all_gather | solution.py:253
  1242.9 304.1 %all-to-all-start.4 = ((bf16[512,4,1120]{0,2,1:T(8,128)(2,1)}), bf16[512,4,1120]{0,2,1:T(8,128)(2,1)}, u32[]{:S(2)}, u32[]{:S(2)}) async-start(bf16[512,4,1120]{0,2,1:T(8,128)(2,1)} %bitcast.374), calls=%async_computation.4 | async-start | bytes 9175040 | tf_op jit(solution)/shard_map/while/body/eval_jaxpr/all_to_all | solution.py:237
  1260.5 7.0 copy-start.1
  1329.8 7.0 copy-start.1
  1547.0 7.4 copy-start.45
  1547.0 100.7 %all-to-all-start.3 = ((bf16[2048,3,1,280]{3,1,2,0:T(4,128)(2,1)}), bf16[2048,3,1,280]{3,1,2,0:T(4,128)(2,1)}, u32[]{:S(2)}, u32[]{:S(2)}) async-start(bf16[2048,3,1,280]{3,1,2,0:T(4,128)(2,1)} %copy.219), calls=%async_computation.3 | async-start | bytes 12582912 | tf_op jit(solution)/shard_map/while/body/eval_jaxpr/all_to_all | solution.py:277
  1552.5 165.9 %all-gather.15.cloned.1.call-start = ((), (), s32[]{:S(2)}) async-start(), calls=%async_computation.9 | async-start | bytes 5734400 | tf_op jit(solution)/shard_map/while/body/eval_jaxpr/all_gather | solution.py:254
  1556.3 14.0 copy-start.14
  1664.6 8.2 copy-start.49
  1664.6 9.5 copy-start.43
  1672.7 8.2 copy-start.4
  1672.7 8.2 copy-start.8
  1672.7 8.2 copy-start.47
  1707.5 10.9 copy-start.22
  1727.7 10.7 copy-start.17
  1740.5 68.4 %all-to-all-start = ((bf16[512,3,4,280]{0,3,1,2:T(8,128)(2,1)}), bf16[512,3,4,280]{0,3,1,2:T(8,128)(2,1)S(1)}, u32[]{:S(2)}, u32[]{:S(2)}) async-start(bf16[512,3,4,280]{0,3,1,2:T(8,128)(2,1)} %copy.211), calls=%async_computation | async-start | bytes 6881280 | tf_op jit(solution)/shard_map/while/body/eval_jaxpr/all_to_all | solution.py:201
  1744.2 873.1 %all-gather.13.cloned.1.call-start = ((), (), s32[]{:S(2)}) async-start(), calls=%async_computation.8 | async-start | bytes 5734400 | tf_op jit(solution)/shard_map/while/body/eval_jaxpr/all_gather | solution.py:208
  1837.7 7.1 copy-start
  1873.7 7.1 copy-start
  1909.7 7.1 copy-start
  1945.7 7.1 copy-start
  1979.1 24.2 all-to-all-start.1
  1983.5 644.8 %all-gather.19.cloned.1.call-start = ((), (), s32[]{:S(2)}) async-start(), calls=%async_computation.11 | async-start | bytes 5734400 | tf_op jit(solution)/shard_map/while/body/eval_jaxpr/all_gather | solution.py:255
  2021.1 44.7 %copy-start.5 = (f32[512,1120]{0,1:T(8,128)}, f32[512,1120]{0,1:T(8,128)S(1)}, u32[]{:S(2)}) copy-start(f32[512,1120]{0,1:T(8,128)S(1)} %get-tuple-element.1335) | copy-start | bytes 6881284 | tf_op jit(solution)/shard_map/while
  2022.3 16.1 copy-start.19
  2022.3 16.1 copy-start.7
  2054.6 11.1 copy-start.16
  2072.6 19.9 all-to-all-start.2
  2092.4 82.0 %all-to-all-start.5 = ((bf16[512,4,1120]{0,2,1:T(8,128)(2,1)}), bf16[512,4,1120]{0,2,1:T(8,128)(2,1)}, u32[]{:S(2)}, u32[]{:S(2)}) async-start(bf16[512,4,1120]{0,2,1:T(8,128)(2,1)} %bitcast.375), calls=%async_computation.5 | async-start | bytes 9175040 | tf_op jit(solution)/shard_map/while/body/eval_jaxpr/all_to_all | solution.py:230
  2097.4 545.1 %all-gather.17.cloned.1.call-start = ((), (), s32[]{:S(2)}) async-start(), calls=%async_computation.10 | async-start | bytes 5734400 | tf_op jit(solution)/shard_map/while/body/eval_jaxpr/all_gather | solution.py:253
  2174.5 304.1 %all-to-all-start.4 = ((bf16[512,4,1120]{0,2,1:T(8,128)(2,1)}), bf16[512,4,1120]{0,2,1:T(8,128)(2,1)}, u32[]{:S(2)}, u32[]{:S(2)}) async-start(bf16[512,4,1120]{0,2,1:T(8,128)(2,1)} %bitcast.374), calls=%async_computation.4 | async-start | bytes 9175040 | tf_op jit(solution)/shard_map/while/body/eval_jaxpr/all_to_all | solution.py:237
  2478.5 7.4 copy-start.45
  2478.6 100.7 %all-to-all-start.3 = ((bf16[2048,3,1,280]{3,1,2,0:T(4,128)(2,1)}), bf16[2048,3,1,280]{3,1,2,0:T(4,128)(2,1)}, u32[]{:S(2)}, u32[]{:S(2)}) async-start(bf16[2048,3,1,280]{3,1,2,0:T(4,128)(2,1)} %copy.219), calls=%async_computation.3 | async-start | bytes 12582912 | tf_op jit(solution)/shard_map/while/body/eval_jaxpr/all_to_all | solution.py:277
  2484.0 170.2 %all-gather.15.cloned.1.call-start = ((), (), s32[]{:S(2)}) async-start(), calls=%async_computation.9 | async-start | bytes 5734400 | tf_op jit(solution)/shard_map/while/body/eval_jaxpr/all_gather | solution.py:254
  2487.9 14.0 copy-start.14
  2596.1 8.2 copy-start.49
  2596.2 9.5 copy-start.43
  2604.3 9.1 copy-start.4
  2604.3 9.1 copy-start.8
  2604.3 9.1 copy-start.47
  2642.6 11.6 copy-start.22
  2666.8 527.8 %all-reduce.4.cloned.1.call-start = ((), (), s32[]{:S(2)}) async-start(), calls=%async_computation.7 | async-start | bytes 30105600
  3235.1 18.4 copy-start.35
  3293.7 20.0 copy-start.57
  3293.7 20.0 copy-start.55
  3293.7 20.0 copy-start.56
  3293.7 23.0 copy-start.32
  (78 other events, 261.6 us)
Sparse Core Ops, SparseCore 0:
  32.4 325.8 all-gather.10
  816.0 60.9 all-gather.12
  1055.3 39.2 all-gather.18
  1172.7 59.9 all-gather.16
  1556.4 60.0 all-gather.14
  1746.3 60.0 all-gather.12
  1985.9 39.2 all-gather.18
  2104.3 59.9 all-gather.16
  2488.0 60.0 all-gather.14
  2733.8 460.7 all-reduce.3
where the time goes:
time: 3360 us; the launch traced here: 3340 us
  waiting for transfers between devices  1200 us (36%)
  matrix products  699 us (21%)
  local copies, waits for them, and re-layouts  659 us (20%)
  other arithmetic  629 us (19%)
  starting transfers between devices  56 us (2%)
  loops' own time  40.3 us (1%)
  blocking collectives  40.2 us (1%)
    unnamed x3, waiting for transfers between devices  436 us
    all_gather x1, waiting for transfers between devices, per_device(): lax.all_gather(weights_master.reshape(1, shard_len).astype(jnp.bfloat16),...  324 us
    all_gather x1, other arithmetic, per_device(): lax.all_gather(weights_master.reshape(1, shard_len).astype(jnp.bfloat16),...  177 us
    while x222, local copies, waits for them, and re-layouts  147 us
    all_to_all x2, waiting for transfers between devices, micro_step(): lax.all_to_all(low_act.reshape(local_rows, groups, ff_share), 'seq', spli...  141 us
    dot_general x8, matrix products, one_block(): jnp.einsum('qhd,khd->hqk', grad_block, values, preferred_element_type=jnp...  130 us
    all_to_all x2, waiting for transfers between devices, micro_step(): lax.all_to_all(projected.reshape(local_rows, 3, groups, head_share), 'seq...  125 us
    all_to_all x2, waiting for transfers between devices, micro_step(): lax.all_to_all(grad_packed.reshape(length, 3, 1, head_share), 'seq', spli...  124 us
  transfers between devices with their start and end apart: 22, of which 12 were waited for; matrix products, arithmetic and copies ran while one was open for 36% of the time, Pallas kernels for 0%

commit v1 on v0

v1 whole, which is shorter than its diff:
```python
import functools
import math

import jax
import jax.numpy as jnp
from jax import lax
from jax.experimental import pallas as pl
from jax.experimental.pallas import tpu as pltpu
from jax.sharding import PartitionSpec as P

HEADS = 20


NORM_EPS = 1e-05
BETA_ONE = 0.9
BETA_TWO = 0.999
ADAM_EPS = 1e-06
DECAY = 0.01
MATRIX_RATE = 0.3
SMALL_RATE = 0.25
MASKED = -1e30
LOG2_E = 1.4426950408889634
QUERY_BLOCK = 512
KEY_BLOCK = 512

F32 = jnp.float32
BF16 = jnp.bfloat16


def dot_rows(left, right):
    return lax.dot_general(left, right, (((1,), (0,)), ((), ())), preferred_element_type=F32)


def dot_transposed(left, right):
    return lax.dot_general(left, right, (((1,), (1,)), ((), ())), preferred_element_type=F32)


def dot_columns(left, right):
    return lax.dot_general(left, right, (((0,), (0,)), ((), ())), preferred_element_type=F32)


def norm_stats(rows):
    center = jnp.mean(rows, axis=-1, keepdims=True)
    centered = rows - center
    spread = jnp.mean(centered * centered, axis=-1, keepdims=True)
    scale = lax.rsqrt(spread + NORM_EPS)
    return centered * scale, scale


def norm_backward(upstream, hat, scale, gain):
    weighted = upstream * gain
    return (
        weighted
        - jnp.mean(weighted, axis=-1, keepdims=True)
        - hat * jnp.mean(weighted * hat, axis=-1, keepdims=True)
    ) * scale


def gelu_parts(values):
    inner = math.sqrt(2.0 / math.pi)
    squares = values * values
    bent = jnp.tanh(inner * (values + 0.044715 * values * squares))
    half = 0.5 * (1.0 + bent)
    slope = half + 0.5 * values * (1.0 - bent * bent) * inner * (1.0 + 3.0 * 0.044715 * squares)
    return values * half, slope


def attention_forward_body(
    heads, width, bq, bk, low_ref, start_ref, qkv_ref, out_ref, outt_ref, lse_ref, qs, ks, vt, acc
):
    length = qkv_ref.shape[0]
    flat = heads * width
    factor = width**-0.5 * LOG2_E
    for h in range(heads):
        qs[h] = qkv_ref[:, h * width : (h + 1) * width]
        ks[h] = qkv_ref[:, flat + h * width : flat + (h + 1) * width]

    def turn_values(kb, carry):
        rows = pl.ds(pl.multiple_of(kb * bk, bk), bk)
        turned = qkv_ref[rows, 2 * flat : 3 * flat].astype(F32).T
        for h in range(heads):
            vt[h, kb] = turned[h * width : (h + 1) * width].astype(BF16)
        return carry

    lax.fori_loop(0, length // bk, turn_values, 0)

    def query_step(qb, carry):
        q0 = pl.multiple_of(qb * bq, bq)
        start = start_ref[qb]
        query_place = q0 + lax.broadcasted_iota(jnp.int32, (1, bq), 1)
        acc[...] = jnp.zeros_like(acc)

        def key_step(kb, tops_totals):
            tops, totals = tops_totals
            k0 = pl.multiple_of(kb * bk, bk)
            key_place = k0 + lax.broadcasted_iota(jnp.int32, (bk, bq), 0)
            allowed = (key_place <= query_place) & (key_place >= start)
            new_tops, new_totals = [], []
            for h in range(heads):
                scores = dot_transposed(ks[h, pl.ds(k0, bk)], qs[h, pl.ds(q0, bq)]) * factor
                scores = jnp.where(allowed, scores, MASKED)
                top = jnp.maximum(tops[h], jnp.max(scores, axis=0, keepdims=True))
                fade = jnp.exp2(tops[h] - top)
                weights = jnp.exp2(scores - top)
                own = slice(h * width, (h + 1) * width)
                acc[own] = acc[own] * fade + dot_rows(vt[h, kb], weights.astype(BF16))
                new_tops.append(top)
                new_totals.append(totals[h] * fade + jnp.sum(weights, axis=0, keepdims=True))
            return tuple(new_tops), tuple(new_totals)

        first = (
            tuple(jnp.full((1, bq), -1e29, F32) for _ in range(heads)),
            tuple(jnp.zeros((1, bq), F32) for _ in range(heads)),
        )
        tops, totals = lax.fori_loop(low_ref[qb], (q0 + bq + bk - 1) // bk, key_step, first)
        for h in range(heads):
            own = slice(h * width, (h + 1) * width)
            acc[own] = acc[own] * (1.0 / totals[h])
            lse_ref[qb, h : h + 1, :] = tops[h] + jnp.log2(totals[h])
        mixed = acc[...]
        outt_ref[qb] = mixed
        out_ref[pl.ds(q0, bq), :] = mixed.T.astype(BF16)
        return carry

    lax.fori_loop(0, length // bq, query_step, 0)


def attention_backward_body(
    heads,
    width,
    bq,
    bk,
    low_ref,
    start_ref,
    qkv_ref,
    dout_ref,
    outt_ref,
    lse_ref,
    grad_ref,
    qs,
    ks,
    vs,
    ds,
    kt,
    dk,
    dv,
    dqt,
):
    length = qkv_ref.shape[0]
    flat = heads * width
    score_scale = width**-0.5
    factor = score_scale * LOG2_E
    for h in range(heads):
        own = slice(h * width, (h + 1) * width)
        qs[h] = qkv_ref[:, own]
        ks[h] = qkv_ref[:, flat + h * width : flat + (h + 1) * width]
        vs[h] = qkv_ref[:, 2 * flat + h * width : 2 * flat + (h + 1) * width]
        ds[h] = dout_ref[:, own]
    dk[...] = jnp.zeros_like(dk)
    dv[...] = jnp.zeros_like(dv)

    def turn_keys(kb, carry):
        rows = pl.ds(pl.multiple_of(kb * bk, bk), bk)
        turned = qkv_ref[rows, flat : 2 * flat].astype(F32).T
        for h in range(heads):
            kt[h, kb] = turned[h * width : (h + 1) * width].astype(BF16)
        return carry

    lax.fori_loop(0, length // bk, turn_keys, 0)

    def query_step(qb, carry):
        q0 = pl.multiple_of(qb * bq, bq)
        queries = pl.ds(q0, bq)
        start = start_ref[qb]
        query_place = q0 + lax.broadcasted_iota(jnp.int32, (1, bq), 1)
        products = dout_ref[queries, :].astype(F32).T * outt_ref[qb]
        inners = [
            jnp.sum(products[h * width : (h + 1) * width], axis=0, keepdims=True)
            for h in range(heads)
        ]
        dqt[...] = jnp.zeros_like(dqt)

        def key_step(kb, inner_carry):
            k0 = pl.multiple_of(kb * bk, bk)
            keys = pl.ds(k0, bk)
            key_place = k0 + lax.broadcasted_iota(jnp.int32, (bk, bq), 0)
            allowed = (key_place <= query_place) & (key_place >= start)
            for h in range(heads):
                scores = dot_transposed(ks[h, keys], qs[h, queries]) * factor
                weights = jnp.exp2(
                    jnp.where(allowed, scores - lse_ref[qb, h : h + 1, :], MASKED)
                )
                dweights = dot_transposed(vs[h, keys], ds[h, queries])
                dscores = (weights * (dweights - inners[h])).astype(BF16)
                dv[h, keys] += dot_rows(weights.astype(BF16), ds[h, queries])
                dk[h, keys] += dot_rows(dscores, qs[h, queries])
                dqt[h * width : (h + 1) * width] += dot_rows(kt[h, kb], dscores)
            return inner_carry

        lax.fori_loop(low_ref[qb], (q0 + bq + bk - 1) // bk, key_step, 0)
        grad_ref[queries, 0:flat] = (dqt[...] * score_scale).T.astype(BF16)
        return carry

    lax.fori_loop(0, length // bq, query_step, 0)

    def write_keys(kb, carry):
        rows = pl.ds(pl.multiple_of(kb * bk, bk), bk)
        grad_ref[rows, flat : 2 * flat] = jnp.concatenate(
            [dk[h, rows] * score_scale for h in range(heads)], axis=1
        ).astype(BF16)
        grad_ref[rows, 2 * flat : 3 * flat] = jnp.concatenate(
            [dv[h, rows] for h in range(heads)], axis=1
        ).astype(BF16)
        return carry

    lax.fori_loop(0, length // bk, write_keys, 0)


def whole_block(shape):
    return pl.BlockSpec(shape, lambda step, *refs: (0,) * len(shape))


def attention_forward(low_blocks, starts, qkv, heads):
    length, triple = qkv.shape
    flat = triple // 3
    width = flat // heads
    bq, bk = min(QUERY_BLOCK, length), min(KEY_BLOCK, length)
    blocks = length // bq
    grid_spec = pltpu.PrefetchScalarGridSpec(
        num_scalar_prefetch=1,
        grid=(1,),
        in_specs=[whole_block((blocks, 1, bq)), whole_block((length, triple))],
        out_specs=[
            whole_block((length, flat)),
            whole_block((blocks, flat, bq)),
            whole_block((blocks, 8, bq)),
        ],
        scratch_shapes=[
            pltpu.VMEM((heads, length, width), BF16),
            pltpu.VMEM((heads, length, width), BF16),
            pltpu.VMEM((heads, length // bk, width, bk), BF16),
            pltpu.VMEM((flat, bq), F32),
        ],
    )
    return pl.pallas_call(
        functools.partial(attention_forward_body, heads, width, bq, bk),
        out_shape=[
            jax.ShapeDtypeStruct((length, flat), BF16),
            jax.ShapeDtypeStruct((blocks, flat, bq), F32),
            jax.ShapeDtypeStruct((blocks, 8, bq), F32),
        ],
        grid_spec=grid_spec,
        compiler_params=pltpu.CompilerParams(vmem_limit_bytes=48 << 20),
        cost_estimate=pl.CostEstimate(
            flops=10 * length * length * flat,
            bytes_accessed=12 * length * flat,
            transcendentals=heads * length * length,
        ),
        name="attention_forward",
    )(low_blocks, starts, qkv)


def attention_backward(low_blocks, starts, qkv, grad_out, out_turned, log_total, heads):
    length, triple = qkv.shape
    flat = triple // 3
    width = flat // heads
    bq, bk = min(QUERY_BLOCK, length), min(KEY_BLOCK, length)
    blocks = length // bq
    per_head = pltpu.VMEM((heads, length, width), BF16)
    sums = pltpu.VMEM((heads, length, width), F32)
    grid_spec = pltpu.PrefetchScalarGridSpec(
        num_scalar_prefetch=1,
        grid=(1,),
        in_specs=[
            whole_block((blocks, 1, bq)),
            whole_block((length, triple)),
            whole_block((length, flat)),
            whole_block((blocks, flat, bq)),
            whole_block((blocks, 8, bq)),
        ],
        out_specs=whole_block((length, triple)),
        scratch_shapes=[
            per_head,
            per_head,
            per_head,
            per_head,
            pltpu.VMEM((heads, length // bk, width, bk), BF16),
            sums,
            sums,
            pltpu.VMEM((flat, bq), F32),
        ],
    )
    return pl.pallas_call(
        functools.partial(attention_backward_body, heads, width, bq, bk),
        out_shape=jax.ShapeDtypeStruct((length, triple), BF16),
        grid_spec=grid_spec,
        compiler_params=pltpu.CompilerParams(vmem_limit_bytes=60 << 20),
        cost_estimate=pl.CostEstimate(
            flops=14 * length * length * flat,
            bytes_accessed=20 * length * flat,
            transcendentals=heads * length * length,
        ),
        name="attention_backward",
    )(low_blocks, starts, qkv, grad_out, out_turned, log_total)


def swap(value, axis_name, distance):
    count = lax.axis_size(axis_name)
    return lax.ppermute(value, axis_name, [(i, i ^ distance) for i in range(count)])


def lower_pairs(pairs, y_count):
    return [
        (source * y_count + y, target * y_count + y)
        for source, target in pairs
        for y in range(y_count)
    ]


def spread_plane(block, plane, z_here, y_here, x_here):
    far = lax.ppermute(block, "dp", lower_pairs([(plane, plane ^ 2)], 2))
    held = jnp.where(z_here == plane, block, far)
    near = lax.ppermute(
        held, "dp", lower_pairs([(plane, plane ^ 1), (plane ^ 2, plane ^ 3)], 2)
    )
    held = jnp.where((z_here == plane) | (z_here == plane ^ 2), held, near)
    if plane < 2:
        across = swap(held, "dp", 1)
        pair = jnp.where(y_here == 0, jnp.stack([held, across]), jnp.stack([across, held]))
        other = swap(pair, "seq", 2)
        return jnp.where(x_here == 0, jnp.stack([pair, other]), jnp.stack([other, pair]))
    across = swap(held, "seq", 2)
    pair = jnp.where(
        x_here == 0, jnp.stack([held, across], 0), jnp.stack([across, held], 0)
    )
    other = swap(pair, "dp", 1)
    return jnp.where(y_here == 0, jnp.stack([pair, other], 1), jnp.stack([other, pair], 1))


def pick(stacked, index, axis=0):
    return lax.dynamic_index_in_dim(stacked, index, axis, keepdims=False)


def gather_plane(blocks, plane, z_here, y_here, x_here):
    def over_x(value, axis):
        sent = swap(pick(value, 1 - x_here, axis).astype(BF16), "seq", 2)
        return pick(value, x_here, axis) + sent.astype(F32)

    def over_y(value, axis):
        sent = swap(pick(value, 1 - y_here, axis).astype(BF16), "dp", 1)
        return pick(value, y_here, axis) + sent.astype(F32)

    if plane < 2:
        held = over_y(over_x(blocks, 0), 0)
    else:
        held = over_x(over_y(blocks, 1), 0)
    near = lax.ppermute(
        held.astype(BF16), "dp", lower_pairs([(plane ^ 1, plane), (plane ^ 3, plane ^ 2)], 2)
    )
    held = held + near.astype(F32)
    far = lax.ppermute(held.astype(BF16), "dp", lower_pairs([(plane ^ 2, plane)], 2))
    return held + far.astype(F32)


def per_device(
    rows_in,
    out_cotangent,
    cell_lengths,
    cell_starts,
    key_mask,
    weights_master,
    first_moment,
    second_moment,
    small_master,
    small_first,
    small_second,
    step_count,
):
    model_width = rows_in.shape[3]
    local_rows = rows_in.shape[2]
    length = key_mask.shape[2]
    shard_len = weights_master.shape[2]
    groups = lax.axis_size("seq")
    dp_count = lax.axis_size("dp")
    head_share = model_width // groups
    heads_here = HEADS // groups
    triple = 3 * head_share
    first_end = model_width * triple
    second_end = first_end + head_share * model_width
    third_end = second_end + model_width * model_width
    seq_here = lax.axis_index("seq")
    dp_here = lax.axis_index("dp")
    chip = seq_here // 2
    core = seq_here % 2
    z_here = dp_here // 2
    y_here = dp_here % 2
    planar = dp_count == 8 and shard_len * 2 == first_end

    def exchange_micro(array):
        own = pick(array[:, 0], chip)
        received = swap(pick(array[:, 0], 1 - chip), "seq", 2)
        return jnp.where(chip == 0, jnp.stack([own, received]), jnp.stack([received, own]))

    row_pair = exchange_micro(rows_in)
    cot_pair = exchange_micro(out_cotangent)

    weight = weights_master[0, 0]
    low_weight = weight.astype(BF16)
    if planar:
        tall = low_weight.reshape(shard_len // triple, triple)
        wide = low_weight.reshape(shard_len // model_width, model_width)
        attn_all = spread_plane(tall, 0, z_here, y_here, x_here=chip)
        w_attn = attn_all.reshape(2, model_width, triple)
        rest = [spread_plane(wide, plane, z_here, y_here, x_here=chip) for plane in (1, 2, 3)]
        rest = jnp.concatenate(
            [part.reshape(2, 2 * wide.shape[0], model_width) for part in rest], axis=1
        )
        w_out = rest[:, :head_share]
        w_in = rest[:, head_share : head_share + model_width]
        w_back = rest[:, head_share + model_width :]
    else:
        copies = lax.all_gather(low_weight.reshape(1, shard_len), ("dp", "seq"), axis=0, tiled=True)
        copies = copies.reshape(dp_count, 2, 2, shard_len)
        per_share = jnp.transpose(pick(copies, core, 2), (1, 0, 2)).reshape(2, dp_count * shard_len)
        w_attn = per_share[:, :first_end].reshape(2, model_width, triple)
        w_out = per_share[:, first_end:second_end].reshape(2, head_share, model_width)
        w_in = per_share[:, second_end:third_end].reshape(2, model_width, model_width)
        w_back = per_share[:, third_end:].reshape(2, model_width, model_width)

    def share_columns(vector, part):
        return lax.dynamic_slice_in_dim(vector, (core + 2 * part) * head_share, head_share)

    attn_biases = [
        jnp.concatenate(
            [
                share_columns(small_master[4], part),
                jnp.zeros((head_share,), F32),
                share_columns(small_master[5], part),
            ]
        )
        for part in range(2)
    ]
    ff_biases = [pick(small_master, 8 + core + 2 * part) for part in range(2)]

    starts = pick(cell_starts[:, 0], chip)
    lengths = pick(cell_lengths[:, 0], chip)
    places = jnp.arange(length, dtype=jnp.int32)
    inside = (places[:, None] >= starts[None, :]) & (places[:, None] < (starts + lengths)[None, :])
    first_key = jnp.max(jnp.where(inside, starts[None, :], -1), axis=1)
    first_key = jnp.where(first_key < 0, places, first_key)
    bq, bk = min(QUERY_BLOCK, length), min(KEY_BLOCK, length)
    low_blocks = first_key.reshape(-1, bq)[:, 0] // bk
    block_starts = first_key.reshape(-1, 1, bq)

    def both_cores(mine):
        theirs = swap(mine, "seq", 1)
        whole = jnp.where(
            core == 0,
            jnp.stack([mine, theirs], axis=1),
            jnp.stack([theirs, mine], axis=1),
        )
        return whole.reshape(length, mine.shape[-1])

    def own_rows(whole, index):
        return pick(whole.reshape(2, 2, local_rows, whole.shape[-1]), index, 1).reshape(
            2 * local_rows, whole.shape[-1]
        )

    def across_cores(multiply):
        received = swap(multiply(1 - core), "seq", 1)
        return multiply(core) + received

    inputs = row_pair.astype(F32).reshape(2 * local_rows, model_width)
    hat_one, scale_one = norm_stats(inputs)
    low_one = (hat_one * small_master[0] + small_master[1]).astype(BF16)
    rows_one = both_cores(low_one.reshape(2, local_rows, model_width))
    grad_y = cot_pair.astype(F32).reshape(2 * local_rows, model_width)
    rows_e = both_cores(cot_pair)

    qkv = [
        (dot_rows(rows_one, w_attn[part]) + attn_biases[part]).astype(BF16) for part in range(2)
    ]
    attended = [
        attention_forward(low_blocks, block_starts, qkv[part], heads_here) for part in range(2)
    ]
    mixture = jnp.concatenate([attended[0][0], attended[1][0]], axis=1)
    w_out_both = w_out.reshape(2 * head_share, model_width)
    branch = across_cores(lambda who: dot_rows(own_rows(mixture, who), w_out_both))
    middle = inputs + (branch + small_master[6])
    hat_two, scale_two = norm_stats(middle)
    low_two = (hat_two * small_master[2] + small_master[3]).astype(BF16)
    rows_two = both_cores(low_two.reshape(2, local_rows, model_width))

    activated, inner = [], []
    for part in range(2):
        hidden = dot_rows(rows_two, w_in[part]) + ff_biases[part]
        value, slope = gelu_parts(hidden)
        activated.append(value.astype(BF16))
        inner.append((dot_transposed(rows_e, w_back[part]) * slope).astype(BF16))
    mlp_out = across_cores(
        lambda who: dot_rows(own_rows(activated[0], who), w_back[0])
        + dot_rows(own_rows(activated[1], who), w_back[1])
    )
    grad_low_two = across_cores(
        lambda who: dot_transposed(own_rows(inner[0], who), w_in[0])
        + dot_transposed(own_rows(inner[1], who), w_in[1])
    )
    result_rows = (middle + (mlp_out + small_master[7])).astype(BF16)
    grad_mid = grad_y + norm_backward(grad_low_two, hat_two, scale_two, small_master[2])
    low_mid = grad_mid.astype(BF16)
    rows_mid = both_cores(low_mid.reshape(2, local_rows, model_width))

    share_back = [dot_columns(activated[part], rows_e) for part in range(2)]
    share_in = [dot_columns(rows_two, inner[part]) for part in range(2)]
    share_out = [dot_columns(attended[part][0], rows_mid) for part in range(2)]
    grad_packed = []
    for part in range(2):
        grad_att = dot_transposed(rows_mid, w_out[part]).astype(BF16)
        grad_packed.append(
            attention_backward(
                low_blocks,
                block_starts,
                qkv[part],
                grad_att,
                attended[part][1],
                attended[part][2],
                heads_here,
            )
        )
    share_attn = [dot_columns(rows_one, grad_packed[part]) for part in range(2)]
    grad_low_one = across_cores(
        lambda who: dot_transposed(own_rows(grad_packed[0], who), w_attn[0])
        + dot_transposed(own_rows(grad_packed[1], who), w_attn[1])
    )
    grad_x = (
        grad_mid + norm_backward(grad_low_one, hat_one, scale_one, small_master[0])
    ).astype(BF16)

    def return_micro(rows):
        blocks = rows.reshape(2, local_rows, model_width)
        own = pick(blocks, chip)
        received = swap(pick(blocks, 1 - chip), "seq", 2)
        ordered = jnp.where(chip == 0, jnp.stack([own, received]), jnp.stack([received, own]))
        return ordered[:, None]

    result_all = return_micro(result_rows)
    grad_all = return_micro(grad_x)

    def at_shares(columns):
        row = jnp.zeros((model_width,), F32)
        for part in range(2):
            row = lax.dynamic_update_slice(row, columns[part], ((core + 2 * part) * head_share,))
        return row

    bias_sums = [jnp.sum(grad_packed[part].astype(F32), axis=0) for part in range(2)]
    inner_rows = jnp.zeros((4, model_width), F32)
    for part in range(2):
        inner_rows = lax.dynamic_update_slice(
            inner_rows, jnp.sum(inner[part].astype(F32), axis=0)[None], (core + 2 * part, 0)
        )
    small_now = jnp.concatenate(
        [
            jnp.stack(
                [
                    jnp.sum(grad_low_one * hat_one, axis=0),
                    jnp.sum(grad_low_one, axis=0),
                    jnp.sum(grad_low_two * hat_two, axis=0),
                    jnp.sum(grad_low_two, axis=0),
                    at_shares([sums[:head_share] for sums in bias_sums]),
                    at_shares([sums[2 * head_share :] for sums in bias_sums]),
                    jnp.sum(low_mid.astype(F32), axis=0),
                    jnp.sum(grad_y, axis=0),
                ]
            ),
            inner_rows,
        ]
    )

    if planar:
        tall_rows, wide_rows = tall.shape[0], wide.shape[0]
        attn_sum = gather_plane(
            jnp.stack(share_attn).reshape(2, 2, tall_rows, triple), 0, z_here, y_here, chip
        )
        joined = jnp.stack(
            [
                jnp.concatenate([share_out[part], share_in[part], share_back[part]], axis=0)
                for part in range(2)
            ]
        ).reshape(2, 3, 2, wide_rows, model_width)
        sums = [
            gather_plane(joined[:, plane - 1], plane, z_here, y_here, chip)
            for plane in (1, 2, 3)
        ]
        wide_sum = jnp.where(z_here == 1, sums[0], jnp.where(z_here == 2, sums[1], sums[2]))
        reduced = jnp.where(z_here == 0, attn_sum.reshape(shard_len), wide_sum.reshape(shard_len))
    else:
        flat_all = jnp.stack(
            [
                jnp.concatenate(
                    [
                        matrix[part].reshape(-1)
                        for matrix in (share_attn, share_out, share_in, share_back)
                    ]
                )
                for part in range(2)
            ]
        )
        flat_here = pick(flat_all, chip) + swap(pick(flat_all, 1 - chip), "seq", 2)
        reduced = lax.psum_scatter(
            flat_here.reshape(dp_count, shard_len), "dp", scatter_dimension=0, tiled=True
        )[0]

    steps_done = step_count[0].astype(F32)
    fix_one = 1.0 - jnp.exp(steps_done * math.log(BETA_ONE))
    fix_two = 1.0 - jnp.exp(steps_done * math.log(BETA_TWO))
    first_new = BETA_ONE * first_moment[0, 0] + (1.0 - BETA_ONE) * reduced
    second_new = BETA_TWO * second_moment[0, 0] + (1.0 - BETA_TWO) * reduced * reduced
    update = first_new / fix_one / (jnp.sqrt(second_new / fix_two) + ADAM_EPS) + DECAY * weight
    positions = dp_here * shard_len + jnp.arange(shard_len, dtype=jnp.int32)
    region = (
        (positions >= first_end).astype(jnp.int32)
        + (positions >= second_end).astype(jnp.int32)
        + (positions >= third_end).astype(jnp.int32)
    )
    region_hit = region[None, :] == jnp.arange(4, dtype=jnp.int32)[:, None]
    norm_sums = jnp.stack(
        [
            jnp.sum(jnp.where(region_hit, weight * weight, 0.0), axis=1),
            jnp.sum(jnp.where(region_hit, update * update, 0.0), axis=1),
        ]
    )
    small_grad, norm_sums = lax.psum((small_now, norm_sums), ("dp", "seq"))
    weight_norms = jnp.sqrt(norm_sums[0])
    update_norms = jnp.sqrt(norm_sums[1])
    ratios = weight_norms / update_norms
    ratio_here = jnp.sum(jnp.where(region_hit, ratios[:, None], 0.0), axis=0)
    new_weight = weight - MATRIX_RATE * ratio_here * update
    small_one = BETA_ONE * small_first + (1.0 - BETA_ONE) * small_grad
    small_two = BETA_TWO * small_second + (1.0 - BETA_TWO) * small_grad * small_grad
    small_updated = small_master - SMALL_RATE * (small_one / fix_one) / (
        jnp.sqrt(small_two / fix_two) + ADAM_EPS
    )
    return (
        result_all,
        grad_all,
        reduced[None, None],
        jnp.stack([first_new, second_new])[:, None, None],
        new_weight[None, None],
        new_weight[None, None].astype(BF16),
        jnp.stack([weight_norms, update_norms, ratios]),
        small_grad,
        jnp.stack([small_one, small_two]),
        small_updated,
    )


def solution(mesh):
    in_specs = (
        P(None, "dp", "seq", None),
        P(None, "dp", "seq", None),
        P(None, "dp", None),
        P(None, "dp", None),
        P(None, "dp", None),
        P("dp", "seq", None),
        P("dp", "seq", None),
        P("dp", "seq", None),
        P(),
        P(),
        P(),
        P(),
    )
    out_specs = (
        P(None, "dp", "seq", None),
        P(None, "dp", "seq", None),
        P("dp", "seq", None),
        P(None, "dp", "seq", None),
        P("dp", "seq", None),
        P("dp", "seq", None),
        P(),
        P(),
        P(),
        P(),
    )
    return jax.shard_map(
        per_device, mesh=mesh, in_specs=in_specs, out_specs=out_specs, check_vma=False
    )
```

time: 3360 us -> 1540 us (0.46)
  waiting for transfers between devices: 1200 us -> 252 us
  matrix products: 699 us -> 218 us
  other arithmetic: 629 us -> 261 us
  Pallas kernels: 0 us -> 183 us
  local copies, waits for them, and re-layouts: 659 us -> 499 us
  loops' own time: 40.3 us -> 0 us
    dot_general x80 -> x30, matrix products: 699 us -> 218 us  [the longest x10 78.3 us: dot_rows(): lax.dot_general(left, right, (((1,), (0,)), ((), ())), preferred_element_...]
    all_to_all x12 -> x0, waiting for transfers between devices: 442 us -> none  [the longest x2 141 us: micro_step(): lax.all_to_all(low_act.reshape(local_rows, groups, ff_share), 'seq', spli...]
    unnamed x3 -> x0, waiting for transfers between devices: 436 us -> none
    all_gather x9 -> x0, waiting for transfers between devices: 324 us -> none  [the longest x1 324 us: per_device(): lax.all_gather(weights_master.reshape(1, shard_len).astype(jnp.bfloat16),...]
    ppermute x0 -> x44, waiting for transfers between devices: none -> 252 us  [the longest x28 209 us: swap(): lax.ppermute(value, axis_name, [(i, i ^ distance) for i in range(count)])]
    pallas_call x0 -> x4, Pallas kernels: none -> 183 us  [the longest x2 112 us: attention_backward(): pl.pallas_call(functools.partial(attention_backward_body, heads, width, b...]
    all_gather x1 -> x0, other arithmetic: 177 us -> none  [per_device(): lax.all_gather(weights_master.reshape(1, shard_len).astype(jnp.bfloat16),...]
    while x225 -> x0, local copies, waits for them, and re-layouts: 156 us -> none
  transfers between devices with their start and end apart: 22 -> 44, of which waited for: 12 -> 21; matrix products, arithmetic and copies ran while one was open for 36% -> 48% of each run, Pallas kernels for 0% -> 5%
where the time goes in v1:
time: 1540 us; the launch traced here: 1520 us
  local copies, waits for them, and re-layouts  499 us (32%)
  other arithmetic  261 us (17%)
  waiting for transfers between devices  252 us (16%)
  matrix products  218 us (14%)
  Pallas kernels  183 us (12%)
  starting transfers between devices  56.2 us (4%)
  blocking collectives  48.4 us (3%)
    ppermute x28, waiting for transfers between devices, swap(): lax.ppermute(value, axis_name, [(i, i ^ distance) for i in range(count)])  209 us
    unnamed x320, local copies, waits for them, and re-layouts  117 us
    pallas_call x2, Pallas kernels, attention_backward(): pl.pallas_call(functools.partial(attention_backward_body, heads, width, b...  112 us
    another operation x4, local copies, waits for them, and re-layouts, per_device(): jnp.stack([jnp.concatenate([share_out[part], share_in[part], share_back[p...  83.6 us
    dot_general x10, matrix products, dot_rows(): lax.dot_general(left, right, (((1,), (0,)), ((), ())), preferred_element_...  78.3 us
    dot_general x12, matrix products, dot_transposed(): lax.dot_general(left, right, (((1,), (1,)), ((), ())), preferred_element_...  77.3 us
    pallas_call x2, Pallas kernels, attention_forward(): pl.pallas_call(functools.partial(attention_forward_body, heads, width, bq...  70.6 us
    dynamic_slice x11, local copies, waits for them, and re-layouts, pick(): return lax.dynamic_index_in_dim(stacked, index, axis, keepdims=False)  67.8 us
  transfers between devices with their start and end apart: 44, of which 21 were waited for; matrix products, arithmetic and copies ran while one was open for 48% of the time, Pallas kernels for 5%

profile of v1, /device:TPU:0, one launch (start us, length us, event | category | flops | bytes accessed | tf_op | source)
XLA Modules:
  0.0 1520.9 jit_solution(10865944605367845584)
XLA Ops:
  0.7 20.7 %convert_reduce_fusion.7 = bf16[470400]{0:T(1024)(128)(2,1)S(1)} fusion(f32[1,1,470400]{2,1,0:T(1,128)} %param.16), kind=kLoop, calls=%fused_computation.167 | loop fusion | flops 470400 | bytes 2822400 | tf_op jit(solution)/shard_map/convert_element_type | solution.py:408
  30.9 7.9 collective-permute-start.2
  44.4 21.7 %multiply_reduce_fusion.7 = (f32[470400]{0:T(1024)}, f32[470400]{0:T(1024)}) fusion(f32[1,1,470400]{2,1,0:T(1,128)S(1)} %copy-done.29), kind=kLoop, calls=%fused_computation.166 | loop fusion | flops 940800 | bytes 5644800 | tf_op jit(solution)/shard_map/mul | solution.py:628
  72.3 22.6 %fusion.61 = (f32[470400]{0:T(1024)}, f32[470400]{0:T(1024)}) fusion(f32[1,1,470400]{2,1,0:T(1,128)} %param.17, f32[1,1,470400]{2,1,0:T(1,128)S(1)} %copy-done.26), kind=kLoop, calls=%fused_computation.206 | loop fusion | flops 940800 | bytes 7526400 | tf_op jit(solution)/shard_map/mul | solution.py:616
  115.6 12.6 collective-permute-done.7
  129.9 14.9 collective-permute-done.3
  157.7 13.2 collective-permute-done.4
  198.2 18.1 %collective-permute-done.9 = bf16[2,420,1120]{2,0,1:T(2,128)(2,1)} collective-permute-done((bf16[2,420,1120]{2,0,1:T(2,128)(2,1)}, bf16[2,420,1120]{2,0,1:T(2,128)(2,1)}, u32[]{:S(2)}, u32[]{:S(2)}) %collective-permute-start.9) | collective-permute-done | bytes 1881632 | tf_op jit(solution)/shard_map/ppermute | solution.py:309
  223.2 31.9 %collective-permute-done.5 = bf16[2,560,840]{2,1,0:T(8,128)(2,1)} collective-permute-done((bf16[2,560,840]{2,1,0:T(8,128)(2,1)}, bf16[2,560,840]{2,1,0:T(8,128)(2,1)}, u32[]{:S(2)}, u32[]{:S(2)}) %collective-permute-start.5) | collective-permute-done | bytes 1881632 | tf_op jit(solution)/shard_map/ppermute | solution.py:309
  266.1 7.0 add_convert_fusion.qkv_ref
  273.1 34.9 %attention_forward.2 = (bf16[2048,280]{1,0:T(8,128)(2,1)S(1)}, f32[4,280,512]{2,1,0:T(8,128)S(1)}, f32[4,8,512]{2,1,0:T(8,128)S(1)}) custom-call(s32[4]{0:T(128)S(1)} %and_select_fusion.low_ref, s32[4,1,512]{2,1,0:T(1,128)S(1)} %compare_select_fusion.start_ref, bf16[2048,840]{1,0:T(8,128)(2,1)} %add_convert_fusion.1.qkv_ref), custom_call_target="tpu_custom_call" | custom-call | flops 11744051200 | bytes 6881280 | tf_op jit(solution)/shard_map/attention_forward/pallas_call | solution.py:245
  310.1 35.7 %attention_forward.3 = (bf16[2048,280]{1,0:T(8,128)(2,1)S(1)}, f32[4,280,512]{2,1,0:T(8,128)S(1)}, f32[4,8,512]{2,1,0:T(8,128)S(1)}) custom-call(s32[4]{0:T(128)S(1)} %and_select_fusion.low_ref, s32[4,1,512]{2,1,0:T(1,128)S(1)} %compare_select_fusion.start_ref, bf16[2048,840]{1,0:T(8,128)(2,1)} %add_convert_fusion.qkv_ref), custom_call_target="tpu_custom_call" | custom-call | flops 11744051200 | bytes 6881280 | tf_op jit(solution)/shard_map/attention_forward/pallas_call | solution.py:245
  367.9 12.8 collective-permute-done.14
  384.1 17.0 %collective-permute-done.18 = bf16[420,1120]{1,0:T(8,128)(2,1)S(1)} collective-permute-done((bf16[420,1120]{1,0:T(8,128)(2,1)S(1)}, bf16[420,1120]{1,0:T(8,128)(2,1)S(1)}, u32[]{:S(2)}, u32[]{:S(2)}) %collective-permute-start.18) | collective-permute-done | bytes 940832 | tf_op jit(solution)/shard_map/ppermute | solution.py:309
  413.4 7.1 copy.266
  438.4 30.7 %collective-permute-done.19 = bf16[2,420,1120]{2,0,1:T(2,128)(2,1)} collective-permute-done((bf16[2,420,1120]{2,0,1:T(2,128)(2,1)}, bf16[2,420,1120]{2,0,1:T(2,128)(2,1)}, u32[]{:S(2)}, u32[]{:S(2)}) %collective-permute-start.19) | collective-permute-done | bytes 1881632 | tf_op jit(solution)/shard_map/ppermute | solution.py:309
  520.5 12.9 multiply_convert_fusion.1
  533.4 12.1 convert_reduce_fusion.1
  545.5 11.4 reshape.1081
  557.0 12.4 constant_dynamic-slice_fusion.9
  569.4 11.1 copy.309
  580.5 12.9 multiply_convert_fusion
  593.5 12.1 convert_reduce_fusion
  605.6 11.4 reshape.1083
  617.0 12.7 constant_dynamic-slice_fusion.8
  629.7 11.0 copy.312
  640.7 11.1 copy.311
  662.4 11.4 reshape.1074
  673.8 12.3 constant_dynamic-slice_fusion.17
  686.1 11.4 reshape.1076
  697.6 12.3 constant_dynamic-slice_fusion.15
  709.9 11.0 copy.306
  720.9 11.2 copy.305
  745.4 8.1 fusion.96
  753.6 8.8 fusion.94
  767.1 11.1 copy.310
  778.2 11.0 copy.303
  789.2 11.1 copy.304
  800.6 7.9 fusion.33
  808.5 10.0 fusion.95
  818.7 8.3 multiply_reduce_fusion
  835.6 7.8 add_convert_fusion.3
  849.8 7.6 constant_dynamic-slice_fusion.12
  859.2 12.3 fusion.92
  878.7 7.5 collective-permute-done.21
  918.1 55.9 %attention_backward.3 = bf16[2048,840]{1,0:T(8,128)(2,1)} custom-call(s32[4]{0:T(128)} %copy-done.7, s32[4,1,512]{2,1,0:T(1,128)} %copy-done.6, bf16[2048,840]{1,0:T(8,128)(2,1)} %add_convert_fusion.qkv_ref, bf16[2048,280]{1,0:T(8,128)(2,1)} %copy.276.dout_ref, f32[4,280,512]{2,1,0:T(8,128)} %copy-done.9, f32[4,8,512]{2,1,0:T(8,128)} %copy-done.11), custom_call_target="tpu_custom_call" | custom-call | flops 16441671680 | bytes 11468800 | tf_op jit(solution)/shard_map/attention_backward/pallas_call | solution.py:293
  978.5 56.1 %attention_backward.2 = bf16[2048,840]{1,0:T(8,128)(2,1)} custom-call(s32[4]{0:T(128)} %copy-done.7, s32[4,1,512]{2,1,0:T(1,128)} %copy-done.6, bf16[2048,840]{1,0:T(8,128)(2,1)} %add_convert_fusion.1.qkv_ref, bf16[2048,280]{1,0:T(8,128)(2,1)} %copy.275.dout_ref, f32[4,280,512]{2,1,0:T(8,128)} %copy-done.8, f32[4,8,512]{2,1,0:T(8,128)} %copy-done.10), custom_call_target="tpu_custom_call" | custom-call | flops 16441671680 | bytes 11468800 | tf_op jit(solution)/shard_map/attention_backward/pallas_call | solution.py:293
  1049.3 13.9 concatenate.135
  1063.3 21.0 %reshape.1107 = f32[1,3,2,420,1120]{3,2,1,4,0:T(2,128)} reshape(f32[2520,1120]{0,1:T(8,128)} %concatenate.135) | data formatting | bytes 22579200 | tf_op jit(solution)/shard_map/stack | solution.py:584
  1084.2 20.8 %copy.302 = f32[1,3,2,420,1120]{4,3,2,1,0:T(8,128)} copy(f32[1,3,2,420,1120]{3,2,1,4,0:T(2,128)} %reshape.1107) | data formatting | bytes 22579200 | tf_op jit(solution)/shard_map/stack | solution.py:584
  1105.1 14.0 concatenate.134
  1119.1 21.0 %reshape.1106 = f32[1,3,2,420,1120]{3,2,1,4,0:T(2,128)} reshape(f32[2520,1120]{0,1:T(8,128)} %concatenate.134) | data formatting | bytes 22579200 | tf_op jit(solution)/shard_map/stack | solution.py:584
  1140.1 20.8 %copy.301 = f32[1,3,2,420,1120]{4,3,2,1,0:T(8,128)} copy(f32[1,3,2,420,1120]{3,2,1,4,0:T(2,128)} %reshape.1106) | data formatting | bytes 22579200 | tf_op jit(solution)/shard_map/stack | solution.py:584
  1182.7 8.5 fusion.25
  1199.6 7.0 fusion.89
  1206.5 9.7 collective-permute-done.32
  1226.7 34.8 %collective-permute-done.40 = bf16[2,420,1120]{2,0,1:T(2,128)(2,1)} collective-permute-done((bf16[2,420,1120]{2,0,1:T(2,128)(2,1)}, bf16[2,420,1120]{2,0,1:T(2,128)(2,1)}, u32[]{:S(2)}, u32[]{:S(2)}) %collective-permute-start.40) | collective-permute-done | bytes 1881632 | tf_op jit(solution)/shard_map/ppermute | solution.py:309
  1271.9 10.4 collective-permute-done.33
  1285.7 14.9 collective-permute-done.41
  1316.6 10.5 collective-permute-done.42
  1393.6 18.2 %select_reduce_fusion.2 = (f32[4]{0:T(128)S(1)}, f32[4]{0:T(128)S(1)}) fusion(f32[470400]{0:T(1024)S(1)} %copy-done.54, s32[470400]{0:T(1024)S(1)} %copy-done.25, f32[470400]{0:T(1024)S(1)} %add_multiply_fusion.2), kind=kLoop, calls=%fused_computation.28 | loop fusion | flops 9407992 | bytes 5644832 | tf_op jit(solution)/shard_map/reduce_sum | solution.py:628
  1416.4 48.4 %all-reduce = (f32[2,4]{1,0:T(2,128)S(1)}, f32[12,1120]{1,0:T(8,128)S(1)}) all-reduce(f32[2,4]{1,0:T(2,128)S(1)} %pad_maximum_fusion.7, f32[12,1120]{1,0:T(8,128)S(1)} %concatenate.136), channel_id=1, replica_groups=mesh['dp'=8,'seq'=4] {'dp','seq'}, use_global_device_ids=true, to_apply=%region_11.12 | all-reduce | flops 13448 | bytes 107584 | tf_op jit(solution)/shard_map/psum | solution.py:632
  1464.9 20.3 %select_reduce_fusion = f32[470400]{0:T(1024)S(1)} fusion(f32[4]{0:T(128)S(1)} %bitcast.413, s32[470400]{0:T(1024)} %convert_add_fusion.5), kind=kLoop, calls=%fused_computation.26 | loop fusion | flops 5174400 | bytes 3763216 | tf_op jit(solution)/shard_map/reduce_sum | solution.py:636
  1493.8 14.4 fusion.80
  (584 shorter events, 475.1 us)
Async XLA Ops:
  0.6 38.1 %copy-start = (bf16[2,1,512,1120]{2,3,1,0:T(8,128)(2,1)S(1)}, bf16[2,1,512,1120]{2,3,1,0:T(8,128)(2,1)}, u32[]{:S(2)}) copy-start(bf16[2,1,512,1120]{2,3,1,0:T(8,128)(2,1)} %param.12) | copy-start | bytes 6881284
  23.6 72.3 %collective-permute-start.12 = (bf16[420,1120]{1,0:T(8,128)(2,1)}, bf16[420,1120]{1,0:T(8,128)(2,1)}, u32[]{:S(2)}, u32[]{:S(2)}) collective-permute-start(bf16[420,1120]{1,0:T(8,128)(2,1)} %convert_element_type.266), channel_id=1, source_target_pairs={{16,0},{20,4},{17,1},{21,5},{18,2},{22,6},{19,3},{23,7}} | collective-permute-start | bytes 2822408 | tf_op jit(solution)/shard_map/ppermute | solution.py:321
  24.8 71.1 %collective-permute-start.16 = (bf16[420,1120]{1,0:T(8,128)(2,1)}, bf16[420,1120]{1,0:T(8,128)(2,1)}, u32[]{:S(2)}, u32[]{:S(2)}) collective-permute-start(bf16[420,1120]{1,0:T(8,128)(2,1)} %convert_element_type.266), channel_id=1, source_target_pairs={{24,8},{28,12},{25,9},{29,13},{26,10},{30,14},{27,11},{31,15}} | collective-permute-start | bytes 2822408 | tf_op jit(solution)/shard_map/ppermute | solution.py:321
  26.5 69.5 %collective-permute-start.6 = (bf16[420,1120]{1,0:T(8,128)(2,1)}, bf16[420,1120]{1,0:T(8,128)(2,1)}, u32[]{:S(2)}, u32[]{:S(2)}) collective-permute-start(bf16[420,1120]{1,0:T(8,128)(2,1)} %convert_element_type.266), channel_id=1, source_target_pairs={{8,24},{12,28},{9,25},{13,29},{10,26},{14,30},{11,27},{15,31}} | collective-permute-start | bytes 2822408 | tf_op jit(solution)/shard_map/ppermute | solution.py:321
  30.9 74.8 %collective-permute-start.2 = (bf16[560,840]{1,0:T(8,128)(2,1)}, bf16[560,840]{1,0:T(8,128)(2,1)}, u32[]{:S(2)}, u32[]{:S(2)}) collective-permute-start(bf16[560,840]{1,0:T(8,128)(2,1)} %convert_element_type.263), channel_id=1, source_target_pairs={{0,16},{4,20},{1,17},{5,21},{2,18},{6,22},{3,19},{7,23}} | collective-permute-start | bytes 2822408 | tf_op jit(solution)/shard_map/ppermute | solution.py:321
  39.8 72.2 %collective-permute-start = (bf16[512,1120]{0,1:T(8,128)(2,1)}, bf16[512,1120]{0,1:T(8,128)(2,1)S(1)}, u32[]{:S(2)}, u32[]{:S(2)}) collective-permute-start(bf16[512,1120]{0,1:T(8,128)(2,1)} %dynamic-slice_bitcast_fusion.1), channel_id=1, source_target_pairs={{0,2},{1,3},{2,0},{3,1},{4,6},{5,7},{6,4},{7,5},{8,10},{9,11},{10,... | collective-permute-start | bytes 3440648 | tf_op jit(solution)/shard_map/ppermute | solution.py:309
  66.3 241.7 %copy-start.6 = (s32[4,1,512]{2,1,0:T(1,128)}, s32[4,1,512]{2,1,0:T(1,128)S(1)}, u32[]{:S(2)}) copy-start(s32[4,1,512]{2,1,0:T(1,128)S(1)} %compare_select_fusion.start_ref) | copy-start | bytes 24580
  72.2 74.5 %copy-start.85 = (f32[1120]{0:T(1024)}, f32[1120]{0:T(1024)S(1)}, u32[]{:S(2)}) copy-start(f32[1120]{0:T(1024)S(1)} %get-tuple-element.101) | copy-start | bytes 13444
  72.2 405.5 %copy-start.91 = (f32[1120]{0:T(1024)}, f32[1120]{0:T(1024)S(1)}, u32[]{:S(2)}) copy-start(f32[1120]{0:T(1024)S(1)} %get-tuple-element.98) | copy-start | bytes 13444
  94.9 213.2 %copy-start.7 = (s32[4]{0:T(128)}, s32[4]{0:T(128)S(1)}, u32[]{:S(2)}) copy-start(s32[4]{0:T(128)S(1)} %and_select_fusion.low_ref) | copy-start | bytes 52
  95.9 78.4 %collective-permute-start.22 = (bf16[512,1120]{0,1:T(8,128)(2,1)}, bf16[512,1120]{0,1:T(8,128)(2,1)S(1)}, u32[]{:S(2)}, u32[]{:S(2)}) collective-permute-start(bf16[512,1120]{0,1:T(8,128)(2,1)} %get-tuple-element.142), channel_id=1, source_target_pairs={{0,2},{1,3},{2,0},{3,1},{4,6},{5,7},{6,4},{7,5},{8,10},{9,11},{10,... | collective-permute-start | bytes 3440648 | tf_op jit(solution)/shard_map/ppermute | solution.py:309
  99.7 255.1 %collective-permute-start.13 = (bf16[420,1120]{1,0:T(8,128)(2,1)}, bf16[420,1120]{1,0:T(8,128)(2,1)}, u32[]{:S(2)}, u32[]{:S(2)}) collective-permute-start(bf16[420,1120]{1,0:T(8,128)(2,1)} %get-tuple-element.147), channel_id=1, source_target_pairs={{16,24},{20,28},{0,8},{4,12},{17,25},{21,29},{1,9},{5,13},{18,26},... | collective-permute-start | bytes 2822408 | tf_op jit(solution)/shard_map/ppermute | solution.py:323
  104.4 23.8 %collective-permute-start.7 = (bf16[420,1120]{1,0:T(8,128)(2,1)S(1)}, bf16[420,1120]{1,0:T(8,128)(2,1)S(1)}, u32[]{:S(2)}, u32[]{:S(2)}) collective-permute-start(bf16[420,1120]{1,0:T(8,128)(2,1)S(1)} %get-tuple-element.148), channel_id=1, source_target_pairs={{8,0},{12,4},{24,16},{28,20},{9,1},{13,5},{25,17},{29,21},{10,2},{... | collective-permute-start | bytes 2822408 | tf_op jit(solution)/shard_map/ppermute | solution.py:323
  105.9 39.0 %collective-permute-start.3 = (bf16[560,840]{1,0:T(8,128)(2,1)S(1)}, bf16[560,840]{1,0:T(8,128)(2,1)S(1)}, u32[]{:S(2)}, u32[]{:S(2)}) collective-permute-start(bf16[560,840]{1,0:T(8,128)(2,1)S(1)} %broadcast_select_fusion.2), channel_id=1, source_target_pairs={{0,8},{4,12},{16,24},{20,28},{1,9},{5,13},{17,25},{21,29},{2,10},{... | collective-permute-start | bytes 2822408 | tf_op jit(solution)/shard_map/ppermute | solution.py:323
  115.6 70.9 %collective-permute-start.1 = (bf16[2,512,1120]{1,2,0:T(8,128)(2,1)}, bf16[2,512,1120]{1,2,0:T(8,128)(2,1)}, u32[]{:S(2)}, u32[]{:S(2)}) collective-permute-start(bf16[2,512,1120]{1,2,0:T(8,128)(2,1)} %fusion.9), channel_id=1, source_target_pairs={{0,1},{1,0},{2,3},{3,2},{4,5},{5,4},{6,7},{7,6},{8,9},{9,8},{10,11... | collective-permute-start | bytes 6881288 | tf_op jit(solution)/shard_map/ppermute | solution.py:309
  128.4 24.6 %collective-permute-start.8 = (bf16[420,1120]{1,0:T(8,128)(2,1)S(1)}, bf16[420,1120]{1,0:T(8,128)(2,1)S(1)}, u32[]{:S(2)}, u32[]{:S(2)}) collective-permute-start(bf16[420,1120]{1,0:T(8,128)(2,1)S(1)} %broadcast_select_fusion.9), channel_id=1, source_target_pairs={{0,4},{4,0},{8,12},{12,8},{16,20},{20,16},{24,28},{28,24},{1,5},{5... | collective-permute-start | bytes 2822408 | tf_op jit(solution)/shard_map/ppermute | solution.py:309
  145.1 25.9 %collective-permute-start.4 = (bf16[560,840]{1,0:T(8,128)(2,1)S(1)}, bf16[560,840]{1,0:T(8,128)(2,1)S(1)}, u32[]{:S(2)}, u32[]{:S(2)}) collective-permute-start(bf16[560,840]{1,0:T(8,128)(2,1)S(1)} %broadcast_select_fusion.3), channel_id=1, source_target_pairs={{0,4},{4,0},{8,12},{12,8},{16,20},{20,16},{24,28},{28,24},{1,5},{5... | collective-permute-start | bytes 2822408 | tf_op jit(solution)/shard_map/ppermute | solution.py:309
  153.0 203.3 %collective-permute-start.17 = (bf16[420,1120]{1,0:T(8,128)(2,1)}, bf16[420,1120]{1,0:T(8,128)(2,1)}, u32[]{:S(2)}, u32[]{:S(2)}) collective-permute-start(bf16[420,1120]{1,0:T(8,128)(2,1)} %get-tuple-element.146), channel_id=1, source_target_pairs={{24,16},{28,20},{8,0},{12,4},{25,17},{29,21},{9,1},{13,5},{26,18},... | collective-permute-start | bytes 2822408 | tf_op jit(solution)/shard_map/ppermute | solution.py:323
  171.0 45.4 %collective-permute-start.9 = (bf16[2,420,1120]{2,0,1:T(2,128)(2,1)}, bf16[2,420,1120]{2,0,1:T(2,128)(2,1)}, u32[]{:S(2)}, u32[]{:S(2)}) collective-permute-start(bf16[2,420,1120]{2,0,1:T(2,128)(2,1)} %copy.248), channel_id=1, source_target_pairs={{0,2},{1,3},{2,0},{3,1},{4,6},{5,7},{6,4},{7,5},{8,10},{9,11},{10,... | collective-permute-start | bytes 5644808 | tf_op jit(solution)/shard_map/ppermute | solution.py:309
  174.3 80.8 %collective-permute-start.5 = (bf16[2,560,840]{2,1,0:T(8,128)(2,1)}, bf16[2,560,840]{2,1,0:T(8,128)(2,1)}, u32[]{:S(2)}, u32[]{:S(2)}) collective-permute-start(bf16[2,560,840]{2,1,0:T(8,128)(2,1)} %maximum_select_fusion.14), channel_id=1, source_target_pairs={{0,2},{1,3},{2,0},{3,1},{4,6},{5,7},{6,4},{7,5},{8,10},{9,11},{10,... | collective-permute-start | bytes 5644808 | tf_op jit(solution)/shard_map/ppermute | solution.py:309
  186.5 221.8 %collective-permute-start.23 = (bf16[2,512,1120]{1,2,0:T(8,128)(2,1)}, bf16[2,512,1120]{1,2,0:T(8,128)(2,1)}, u32[]{:S(2)}, u32[]{:S(2)}) collective-permute-start(bf16[2,512,1120]{1,2,0:T(8,128)(2,1)} %copy-done.42), channel_id=1, source_target_pairs={{0,1},{1,0},{2,3},{3,2},{4,5},{5,4},{6,7},{7,6},{8,9},{9,8},{10,11... | collective-permute-start | bytes 6881288 | tf_op jit(solution)/shard_map/ppermute | solution.py:309
  219.4 35.6 %copy-start.49 = (bf16[1,2,560,840]{3,2,1,0:T(8,128)(2,1)S(1)}, bf16[1,2,560,840]{3,2,1,0:T(8,128)(2,1)}, u32[]{:S(2)}) copy-start(bf16[1,2,560,840]{3,2,1,0:T(8,128)(2,1)} %maximum_select_fusion.13) | copy-start | bytes 5644804
  310.1 37.5 %copy-start.2 = (bf16[2048,280]{1,0:T(8,128)(2,1)}, bf16[2048,280]{1,0:T(8,128)(2,1)S(1)}, u32[]{:S(2)}) copy-start(bf16[2048,280]{1,0:T(8,128)(2,1)S(1)} %get-tuple-element.16) | copy-start | bytes 3440644
  310.1 35.7 %copy-start.52 = (bf16[1,840,1120]{2,1,0:T(8,128)(2,1)S(1)}, bf16[1,840,1120]{2,1,0:T(8,128)(2,1)}, u32[]{:S(2)}) copy-start(bf16[1,840,1120]{2,1,0:T(8,128)(2,1)} %select_n.527) | copy-start | bytes 5644804
  310.1 35.8 %copy-start.53 = (bf16[1,840,1120]{2,1,0:T(8,128)(2,1)S(1)}, bf16[1,840,1120]{2,1,0:T(8,128)(2,1)}, u32[]{:S(2)}) copy-start(bf16[1,840,1120]{2,1,0:T(8,128)(2,1)} %stack.343) | copy-start | bytes 5644804
  354.8 116.1 %collective-permute-start.10 = (f32[1024,1120]{0,1:T(8,128)}, f32[1024,1120]{0,1:T(8,128)}, u32[]{:S(2)}, u32[]{:S(2)}) collective-permute-start(f32[1024,1120]{0,1:T(8,128)} %fusion.86), channel_id=1, source_target_pairs={{0,1},{1,0},{2,3},{3,2},{4,5},{5,4},{6,7},{7,6},{8,9},{9,8},{10,11... | collective-permute-start | bytes 13762568 | tf_op jit(solution)/shard_map/ppermute | solution.py:309
  356.2 24.5 %collective-permute-start.14 = (bf16[420,1120]{1,0:T(8,128)(2,1)S(1)}, bf16[420,1120]{1,0:T(8,128)(2,1)S(1)}, u32[]{:S(2)}, u32[]{:S(2)}) collective-permute-start(bf16[420,1120]{1,0:T(8,128)(2,1)S(1)} %broadcast_select_fusion.6), channel_id=1, source_target_pairs={{0,2},{1,3},{2,0},{3,1},{4,6},{5,7},{6,4},{7,5},{8,10},{9,11},{10,... | collective-permute-start | bytes 2822408 | tf_op jit(solution)/shard_map/ppermute | solution.py:309
  357.6 43.5 %collective-permute-start.18 = (bf16[420,1120]{1,0:T(8,128)(2,1)S(1)}, bf16[420,1120]{1,0:T(8,128)(2,1)S(1)}, u32[]{:S(2)}, u32[]{:S(2)}) collective-permute-start(bf16[420,1120]{1,0:T(8,128)(2,1)S(1)} %broadcast_select_fusion.8), channel_id=1, source_target_pairs={{0,2},{1,3},{2,0},{3,1},{4,6},{5,7},{6,4},{7,5},{8,10},{9,11},{10,... | collective-permute-start | bytes 2822408 | tf_op jit(solution)/shard_map/ppermute | solution.py:309
  384.1 45.4 %collective-permute-start.15 = (bf16[2,420,1120]{2,0,1:T(2,128)(2,1)}, bf16[2,420,1120]{2,0,1:T(2,128)(2,1)}, u32[]{:S(2)}, u32[]{:S(2)}) collective-permute-start(bf16[2,420,1120]{2,0,1:T(2,128)(2,1)} %copy.254), channel_id=1, source_target_pairs={{0,4},{4,0},{8,12},{12,8},{16,20},{20,16},{24,28},{28,24},{1,5},{5... | collective-permute-start | bytes 5644808 | tf_op jit(solution)/shard_map/ppermute | solution.py:309
  404.6 64.6 %collective-permute-start.19 = (bf16[2,420,1120]{2,0,1:T(2,128)(2,1)}, bf16[2,420,1120]{2,0,1:T(2,128)(2,1)}, u32[]{:S(2)}, u32[]{:S(2)}) collective-permute-start(bf16[2,420,1120]{2,0,1:T(2,128)(2,1)} %copy.257), channel_id=1, source_target_pairs={{0,4},{4,0},{8,12},{12,8},{16,20},{20,16},{24,28},{28,24},{1,5},{5... | collective-permute-start | bytes 5644808 | tf_op jit(solution)/shard_map/ppermute | solution.py:309
  438.4 32.5 %copy-start.61 = (bf16[2,280,1120]{2,1,0:T(8,128)(2,1)S(1)}, bf16[2,280,1120]{2,1,0:T(8,128)(2,1)}, u32[]{:S(2)}) copy-start(bf16[2,280,1120]{2,1,0:T(8,128)(2,1)} %copy-done.60) | copy-start | bytes 3763204
  480.8 28.3 %collective-permute-start.11 = (bf16[2,512,1120]{1,2,0:T(8,128)(2,1)}, bf16[2,512,1120]{1,2,0:T(8,128)(2,1)}, u32[]{:S(2)}, u32[]{:S(2)}) collective-permute-start(bf16[2,512,1120]{1,2,0:T(8,128)(2,1)} %bitcast.286), channel_id=1, source_target_pairs={{0,1},{1,0},{2,3},{3,2},{4,5},{5,4},{6,7},{7,6},{8,9},{9,8},{10,11... | collective-permute-start | bytes 6881288 | tf_op jit(solution)/shard_map/ppermute | solution.py:309
  662.4 156.2 %collective-permute-start.24 = (f32[1024,1120]{0,1:T(8,128)}, f32[1024,1120]{0,1:T(8,128)}, u32[]{:S(2)}, u32[]{:S(2)}) collective-permute-start(f32[1024,1120]{0,1:T(8,128)} %convolution_add_fusion.3), channel_id=1, source_target_pairs={{0,1},{1,0},{2,3},{3,2},{4,5},{5,4},{6,7},{7,6},{8,9},{9,8},{10,11... | collective-permute-start | bytes 13762568 | tf_op jit(solution)/shard_map/ppermute | solution.py:309
  744.9 89.9 %collective-permute-start.20 = (f32[1024,1120]{0,1:T(8,128)}, f32[1024,1120]{0,1:T(8,128)}, u32[]{:S(2)}, u32[]{:S(2)}) collective-permute-start(f32[1024,1120]{0,1:T(8,128)} %convolution_add_fusion.4), channel_id=1, source_target_pairs={{0,1},{1,0},{2,3},{3,2},{4,5},{5,4},{6,7},{7,6},{8,9},{9,8},{10,11... | collective-permute-start | bytes 13762568 | tf_op jit(solution)/shard_map/ppermute | solution.py:309
  834.7 53.2 %collective-permute-start.25 = (bf16[2,512,1120]{1,2,0:T(8,128)(2,1)}, bf16[2,512,1120]{1,2,0:T(8,128)(2,1)}, u32[]{:S(2)}, u32[]{:S(2)}) collective-permute-start(bf16[2,512,1120]{1,2,0:T(8,128)(2,1)} %bitcast.285), channel_id=1, source_target_pairs={{0,1},{1,0},{2,3},{3,2},{4,5},{5,4},{6,7},{7,6},{8,9},{9,8},{10,11... | collective-permute-start | bytes 6881288 | tf_op jit(solution)/shard_map/ppermute | solution.py:309
  858.7 27.4 %collective-permute-start.21 = (bf16[512,1120]{0,1:T(8,128)(2,1)}, bf16[512,1120]{0,1:T(8,128)(2,1)S(1)}, u32[]{:S(2)}, u32[]{:S(2)}) collective-permute-start(bf16[512,1120]{0,1:T(8,128)(2,1)} %bitcast.291), channel_id=1, source_target_pairs={{0,2},{1,3},{2,0},{3,1},{4,6},{5,7},{6,4},{7,5},{8,10},{9,11},{10,... | collective-permute-start | bytes 3440648 | tf_op jit(solution)/shard_map/ppermute | solution.py:309
  1049.3 284.0 %collective-permute-start.26 = (f32[1024,1120]{0,1:T(8,128)}, f32[1024,1120]{0,1:T(8,128)}, u32[]{:S(2)}, u32[]{:S(2)}) collective-permute-start(f32[1024,1120]{0,1:T(8,128)} %convolution_add_fusion.2), channel_id=1, source_target_pairs={{0,1},{1,0},{2,3},{3,2},{4,5},{5,4},{6,7},{7,6},{8,9},{9,8},{10,11... | collective-permute-start | bytes 13762568 | tf_op jit(solution)/shard_map/ppermute | solution.py:309
  1170.9 45.3 %collective-permute-start.32 = (bf16[2,420,1120]{2,0,1:T(2,128)(2,1)}, bf16[2,420,1120]{2,0,1:T(2,128)(2,1)}, u32[]{:S(2)}, u32[]{:S(2)}) collective-permute-start(bf16[2,420,1120]{2,0,1:T(2,128)(2,1)} %copy.286), channel_id=1, source_target_pairs={{0,2},{1,3},{2,0},{3,1},{4,6},{5,7},{6,4},{7,5},{8,10},{9,11},{10,... | collective-permute-start | bytes 5644808 | tf_op jit(solution)/shard_map/ppermute | solution.py:309
  1174.8 45.7 %collective-permute-start.36 = (bf16[2,420,1120]{2,0,1:T(2,128)(2,1)}, bf16[2,420,1120]{2,0,1:T(2,128)(2,1)}, u32[]{:S(2)}, u32[]{:S(2)}) collective-permute-start(bf16[2,420,1120]{2,0,1:T(2,128)(2,1)} %copy.288), channel_id=1, source_target_pairs={{0,4},{4,0},{8,12},{12,8},{16,20},{20,16},{24,28},{28,24},{1,5},{5... | collective-permute-start | bytes 5644808 | tf_op jit(solution)/shard_map/ppermute | solution.py:309
  1194.3 67.2 %collective-permute-start.40 = (bf16[2,420,1120]{2,0,1:T(2,128)(2,1)}, bf16[2,420,1120]{2,0,1:T(2,128)(2,1)}, u32[]{:S(2)}, u32[]{:S(2)}) collective-permute-start(bf16[2,420,1120]{2,0,1:T(2,128)(2,1)} %copy.290), channel_id=1, source_target_pairs={{0,4},{4,0},{8,12},{12,8},{16,20},{20,16},{24,28},{28,24},{1,5},{5... | collective-permute-start | bytes 5644808 | tf_op jit(solution)/shard_map/ppermute | solution.py:309
  1197.3 70.9 %collective-permute-start.28 = (bf16[2,560,840]{2,1,0:T(8,128)(2,1)}, bf16[2,560,840]{2,1,0:T(8,128)(2,1)}, u32[]{:S(2)}, u32[]{:S(2)}) collective-permute-start(bf16[2,560,840]{2,1,0:T(8,128)(2,1)} %fusion.31), channel_id=1, source_target_pairs={{0,2},{1,3},{2,0},{3,1},{4,6},{5,7},{6,4},{7,5},{8,10},{9,11},{10,... | collective-permute-start | bytes 5644808 | tf_op jit(solution)/shard_map/ppermute | solution.py:309
  1199.5 62.0 %slice-start.9 = ((s8[11722752]{0:T(1024)(128)(4,1)}), s8[4194304]{0:T(1024)(128)(4,1)S(1)}, s32[]{:S(2)}) async-start(s8[11722752]{0:T(1024)(128)(4,1)} %bitcast.301), calls=%async_computation.9 | async-start | bytes 8388608
  1199.6 62.0 %slice-start.10 = ((s8[11722752]{0:T(1024)(128)(4,1)}), s8[4194304]{0:T(1024)(128)(4,1)S(1)}, s32[]{:S(2)}) async-start(s8[11722752]{0:T(1024)(128)(4,1)} %bitcast.301), calls=%async_computation.10 | async-start | bytes 8388608
  1216.2 45.3 %slice-start.3 = ((s8[11722752]{0:T(1024)(128)(4,1)}), s8[4194304]{0:T(1024)(128)(4,1)S(1)}, s32[]{:S(2)}) async-start(s8[11722752]{0:T(1024)(128)(4,1)} %bitcast.297), calls=%async_computation.3 | async-start | bytes 8388608
  1216.2 45.3 %slice-start.4 = ((s8[11722752]{0:T(1024)(128)(4,1)}), s8[4194304]{0:T(1024)(128)(4,1)S(1)}, s32[]{:S(2)}) async-start(s8[11722752]{0:T(1024)(128)(4,1)} %bitcast.297), calls=%async_computation.4 | async-start | bytes 8388608
  1219.4 86.8 %copy-start.16 = (f32[2,420,1120]{2,1,0:T(8,128)}, f32[2,420,1120]{2,1,0:T(8,128)S(1)}, u32[]{:S(2)}) copy-start(f32[2,420,1120]{2,1,0:T(8,128)S(1)} %bitcast_add_fusion.1) | copy-start | bytes 11289604
  1219.4 42.1 %slice-start.11 = ((s8[11722752]{0:T(1024)(128)(4,1)}), s8[3334144]{0:T(1024)(128)(4,1)S(1)}, s32[]{:S(2)}) async-start(s8[11722752]{0:T(1024)(128)(4,1)} %bitcast.301), calls=%async_computation.11 | async-start | bytes 6668288
  1220.5 41.1 %slice-start.5 = ((s8[11722752]{0:T(1024)(128)(4,1)}), s8[3334144]{0:T(1024)(128)(4,1)S(1)}, s32[]{:S(2)}) async-start(s8[11722752]{0:T(1024)(128)(4,1)} %bitcast.297), calls=%async_computation.5 | async-start | bytes 6668288
  1220.5 61.9 %collective-permute-start.33 = (bf16[420,1120]{1,0:T(8,128)(2,1)}, bf16[420,1120]{1,0:T(8,128)(2,1)S(1)}, u32[]{:S(2)}, u32[]{:S(2)}) collective-permute-start(bf16[420,1120]{1,0:T(8,128)(2,1)} %fusion.53), channel_id=1, source_target_pairs={{0,4},{4,0},{8,12},{12,8},{16,20},{20,16},{24,28},{28,24},{1,5},{5... | collective-permute-start | bytes 2822408 | tf_op jit(solution)/shard_map/ppermute | solution.py:309
  1225.3 85.1 %copy-start.17 = (f32[2,420,1120]{2,1,0:T(8,128)}, f32[2,420,1120]{2,1,0:T(8,128)S(1)}, u32[]{:S(2)}) copy-start(f32[2,420,1120]{2,1,0:T(8,128)S(1)} %bitcast_add_fusion) | copy-start | bytes 11289604
  1226.4 57.8 %collective-permute-start.37 = (bf16[420,1120]{1,0:T(8,128)(2,1)}, bf16[420,1120]{1,0:T(8,128)(2,1)S(1)}, u32[]{:S(2)}, u32[]{:S(2)}) collective-permute-start(bf16[420,1120]{1,0:T(8,128)(2,1)} %fusion.54), channel_id=1, source_target_pairs={{0,2},{1,3},{2,0},{3,1},{4,6},{5,7},{6,4},{7,5},{8,10},{9,11},{10,... | collective-permute-start | bytes 2822408 | tf_op jit(solution)/shard_map/ppermute | solution.py:309
  1267.0 33.6 %collective-permute-start.41 = (bf16[420,1120]{1,0:T(8,128)(2,1)S(1)}, bf16[420,1120]{1,0:T(8,128)(2,1)S(1)}, u32[]{:S(2)}, u32[]{:S(2)}) collective-permute-start(bf16[420,1120]{1,0:T(8,128)(2,1)S(1)} %fusion.55), channel_id=1, source_target_pairs={{0,2},{1,3},{2,0},{3,1},{4,6},{5,7},{6,4},{7,5},{8,10},{9,11},{10,... | collective-permute-start | bytes 2822408 | tf_op jit(solution)/shard_map/ppermute | solution.py:309
  1271.7 59.0 %copy-start.15 = (f32[2,560,840]{2,1,0:T(8,128)}, f32[2,560,840]{2,1,0:T(8,128)S(1)}, u32[]{:S(2)}) copy-start(f32[2,560,840]{2,1,0:T(8,128)S(1)} %fusion.14) | copy-start | bytes 11289604
  1271.9 31.6 %collective-permute-start.29 = (bf16[560,840]{1,0:T(8,128)(2,1)S(1)}, bf16[560,840]{1,0:T(8,128)(2,1)S(1)}, u32[]{:S(2)}, u32[]{:S(2)}) collective-permute-start(bf16[560,840]{1,0:T(8,128)(2,1)S(1)} %fusion.52), channel_id=1, source_target_pairs={{0,4},{4,0},{8,12},{12,8},{16,20},{20,16},{24,28},{28,24},{1,5},{5... | collective-permute-start | bytes 2822408 | tf_op jit(solution)/shard_map/ppermute | solution.py:309
  1282.6 23.6 %collective-permute-start.34 = (bf16[420,1120]{1,0:T(8,128)(2,1)S(1)}, bf16[420,1120]{1,0:T(8,128)(2,1)S(1)}, u32[]{:S(2)}, u32[]{:S(2)}) collective-permute-start(bf16[420,1120]{1,0:T(8,128)(2,1)S(1)} %fusion.57), channel_id=1, source_target_pairs={{0,8},{4,12},{16,24},{20,28},{1,9},{5,13},{17,25},{21,29},{2,10},{... | collective-permute-start | bytes 2822408 | tf_op jit(solution)/shard_map/ppermute | solution.py:357
  1284.4 26.0 %collective-permute-start.38 = (bf16[420,1120]{1,0:T(8,128)(2,1)S(1)}, bf16[420,1120]{1,0:T(8,128)(2,1)S(1)}, u32[]{:S(2)}, u32[]{:S(2)}) collective-permute-start(bf16[420,1120]{1,0:T(8,128)(2,1)S(1)} %fusion.58), channel_id=1, source_target_pairs={{24,16},{28,20},{8,0},{12,4},{25,17},{29,21},{9,1},{13,5},{26,18},... | collective-permute-start | bytes 2822408 | tf_op jit(solution)/shard_map/ppermute | solution.py:357
  1300.8 26.3 %collective-permute-start.42 = (bf16[420,1120]{1,0:T(8,128)(2,1)S(1)}, bf16[420,1120]{1,0:T(8,128)(2,1)S(1)}, u32[]{:S(2)}, u32[]{:S(2)}) collective-permute-start(bf16[420,1120]{1,0:T(8,128)(2,1)S(1)} %fusion.59), channel_id=1, source_target_pairs={{16,24},{20,28},{0,8},{4,12},{17,25},{21,29},{1,9},{5,13},{18,26},... | collective-permute-start | bytes 2822408 | tf_op jit(solution)/shard_map/ppermute | solution.py:357
  1303.7 27.0 %collective-permute-start.30 = (bf16[560,840]{1,0:T(8,128)(2,1)S(1)}, bf16[560,840]{1,0:T(8,128)(2,1)S(1)}, u32[]{:S(2)}, u32[]{:S(2)}) collective-permute-start(bf16[560,840]{1,0:T(8,128)(2,1)S(1)} %fusion.56), channel_id=1, source_target_pairs={{8,0},{12,4},{24,16},{28,20},{9,1},{13,5},{25,17},{29,21},{10,2},{... | collective-permute-start | bytes 2822408 | tf_op jit(solution)/shard_map/ppermute | solution.py:357
  1307.5 50.1 %collective-permute-start.35 = (bf16[420,1120]{1,0:T(8,128)(2,1)}, bf16[420,1120]{1,0:T(8,128)(2,1)}, u32[]{:S(2)}, u32[]{:S(2)}) collective-permute-start(bf16[420,1120]{1,0:T(8,128)(2,1)} %fusion.49), channel_id=1, source_target_pairs={{24,8},{28,12},{25,9},{29,13},{26,10},{30,14},{27,11},{31,15}} | collective-permute-start | bytes 2822408 | tf_op jit(solution)/shard_map/ppermute | solution.py:361
  1311.8 45.8 %collective-permute-start.39 = (bf16[420,1120]{1,0:T(8,128)(2,1)}, bf16[420,1120]{1,0:T(8,128)(2,1)}, u32[]{:S(2)}, u32[]{:S(2)}) collective-permute-start(bf16[420,1120]{1,0:T(8,128)(2,1)} %fusion.50), channel_id=1, source_target_pairs={{0,16},{4,20},{1,17},{5,21},{2,18},{6,22},{3,19},{7,23}} | collective-permute-start | bytes 2822408 | tf_op jit(solution)/shard_map/ppermute | solution.py:361
  1328.4 29.2 %collective-permute-start.43 = (bf16[420,1120]{1,0:T(8,128)(2,1)}, bf16[420,1120]{1,0:T(8,128)(2,1)}, u32[]{:S(2)}, u32[]{:S(2)}) collective-permute-start(bf16[420,1120]{1,0:T(8,128)(2,1)} %fusion.51), channel_id=1, source_target_pairs={{8,24},{12,28},{9,25},{13,29},{10,26},{14,30},{11,27},{15,31}} | collective-permute-start | bytes 2822408 | tf_op jit(solution)/shard_map/ppermute | solution.py:361
  1332.0 41.0 %collective-permute-start.31 = (bf16[560,840]{1,0:T(8,128)(2,1)}, bf16[560,840]{1,0:T(8,128)(2,1)}, u32[]{:S(2)}, u32[]{:S(2)}) collective-permute-start(bf16[560,840]{1,0:T(8,128)(2,1)} %fusion.48), channel_id=1, source_target_pairs={{16,0},{20,4},{17,1},{21,5},{18,2},{22,6},{19,3},{23,7}} | collective-permute-start | bytes 2822408 | tf_op jit(solution)/shard_map/ppermute | solution.py:361
  1355.4 161.9 %collective-permute-start.27 = (bf16[512,1120]{0,1:T(8,128)(2,1)}, bf16[512,1120]{0,1:T(8,128)(2,1)}, u32[]{:S(2)}, u32[]{:S(2)}) collective-permute-start(bf16[512,1120]{0,1:T(8,128)(2,1)} %bitcast.289), channel_id=1, source_target_pairs={{0,2},{1,3},{2,0},{3,1},{4,6},{5,7},{6,4},{7,5},{8,10},{9,11},{10,... | collective-permute-start | bytes 3440648 | tf_op jit(solution)/shard_map/ppermute | solution.py:309
  1464.8 46.9 %copy-start.97 = (f32[12,1120]{1,0:T(8,128)}, f32[12,1120]{1,0:T(8,128)S(1)}, u32[]{:S(2)}) copy-start(f32[12,1120]{1,0:T(8,128)S(1)} %get-tuple-element.107) | copy-start | bytes 161284
  (132 other events, 1135.9 us)

commit v2 on v1

v2 whole, which is shorter than its diff:
```python
import functools
import math

import jax
import jax.numpy as jnp
from jax import lax
from jax.experimental import pallas as pl
from jax.experimental.pallas import tpu as pltpu
from jax.sharding import PartitionSpec as P

HEADS = 20


NORM_EPS = 1e-05
BETA_ONE = 0.9
BETA_TWO = 0.999
ADAM_EPS = 1e-06
DECAY = 0.01
MATRIX_RATE = 0.3
SMALL_RATE = 0.25
MASKED = -1e30
LOG2_E = 1.4426950408889634
FF_ROWS = 256

F32 = jnp.float32
BF16 = jnp.bfloat16


def dot_rows(left, right):
    return lax.dot_general(left, right, (((1,), (0,)), ((), ())), preferred_element_type=F32)


def dot_transposed(left, right):
    return lax.dot_general(left, right, (((1,), (1,)), ((), ())), preferred_element_type=F32)


def dot_columns(left, right):
    return lax.dot_general(left, right, (((0,), (0,)), ((), ())), preferred_element_type=F32)


def norm_stats(rows):
    center = jnp.mean(rows, axis=-1, keepdims=True)
    centered = rows - center
    spread = jnp.mean(centered * centered, axis=-1, keepdims=True)
    scale = lax.rsqrt(spread + NORM_EPS)
    return centered * scale, scale


def norm_backward(upstream, hat, scale, gain):
    weighted = upstream * gain
    return (
        weighted
        - jnp.mean(weighted, axis=-1, keepdims=True)
        - hat * jnp.mean(weighted * hat, axis=-1, keepdims=True)
    ) * scale


def gelu_parts(values):
    inner = math.sqrt(2.0 / math.pi)
    squares = values * values
    bent = jnp.tanh(inner * (values + 0.044715 * values * squares))
    half = 0.5 * (1.0 + bent)
    slope = half + 0.5 * values * (1.0 - bent * bent) * inner * (1.0 + 3.0 * 0.044715 * squares)
    return values * half, slope


def block_place(core, block):
    return jnp.where(block % 2 == core, 0, 2) + block // 2


def block_rows(core, block, rows):
    return pl.ds(pl.multiple_of(block_place(core, block) * rows, rows), rows)


def attention_forward_body(
    heads, width, bq, low_ref, core_ref, start_ref, qkv_ref, out_ref, outt_ref, lse_ref, qs, ks, vt, acc
):
    length = qkv_ref.shape[0]
    flat = heads * width
    factor = width**-0.5 * LOG2_E
    core = core_ref[0]

    def unpack(block, carry):
        here = block_rows(core, block, bq)
        there = pl.ds(pl.multiple_of(block * bq, bq), bq)
        for h in range(heads):
            qs[h, there] = qkv_ref[here, h * width : (h + 1) * width]
            ks[h, there] = qkv_ref[here, flat + h * width : flat + (h + 1) * width]
        turned = qkv_ref[here, 2 * flat : 3 * flat].astype(F32).T
        for h in range(heads):
            vt[h, block] = turned[h * width : (h + 1) * width].astype(BF16)
        return carry

    lax.fori_loop(0, length // bq, unpack, 0)

    def query_step(qb, carry):
        q0 = pl.multiple_of(qb * bq, bq)
        start = start_ref[qb]
        query_place = q0 + lax.broadcasted_iota(jnp.int32, (1, bq), 1)
        acc[...] = jnp.zeros_like(acc)

        def key_step(kb, tops_totals):
            tops, totals = tops_totals
            k0 = pl.multiple_of(kb * bq, bq)
            key_place = k0 + lax.broadcasted_iota(jnp.int32, (bq, bq), 0)
            allowed = (key_place <= query_place) & (key_place >= start)
            new_tops, new_totals = [], []
            for h in range(heads):
                scores = dot_transposed(ks[h, pl.ds(k0, bq)], qs[h, pl.ds(q0, bq)]) * factor
                scores = jnp.where(allowed, scores, MASKED)
                top = jnp.maximum(tops[h], jnp.max(scores, axis=0, keepdims=True))
                fade = jnp.exp2(tops[h] - top)
                weights = jnp.exp2(scores - top)
                own = slice(h * width, (h + 1) * width)
                acc[own] = acc[own] * fade + dot_rows(vt[h, kb], weights.astype(BF16))
                new_tops.append(top)
                new_totals.append(totals[h] * fade + jnp.sum(weights, axis=0, keepdims=True))
            return tuple(new_tops), tuple(new_totals)

        first = (
            tuple(jnp.full((1, bq), -1e29, F32) for _ in range(heads)),
            tuple(jnp.zeros((1, bq), F32) for _ in range(heads)),
        )
        tops, totals = lax.fori_loop(low_ref[qb], qb + 1, key_step, first)
        for h in range(heads):
            own = slice(h * width, (h + 1) * width)
            acc[own] = acc[own] * (1.0 / totals[h])
            lse_ref[qb, h : h + 1, :] = tops[h] + jnp.log2(totals[h])
        mixed = acc[...]
        outt_ref[qb] = mixed
        out_ref[block_rows(core, qb, bq), :] = mixed.T.astype(BF16)
        return carry

    lax.fori_loop(0, length // bq, query_step, 0)


def attention_backward_body(
    heads,
    width,
    bq,
    low_ref,
    core_ref,
    start_ref,
    qkv_ref,
    dout_ref,
    outt_ref,
    lse_ref,
    grad_ref,
    qs,
    ks,
    vs,
    ds,
    kt,
    dk,
    dv,
    dqt,
):
    length = qkv_ref.shape[0]
    flat = heads * width
    score_scale = width**-0.5
    factor = score_scale * LOG2_E
    core = core_ref[0]

    def unpack(block, carry):
        here = block_rows(core, block, bq)
        there = pl.ds(pl.multiple_of(block * bq, bq), bq)
        for h in range(heads):
            qs[h, there] = qkv_ref[here, h * width : (h + 1) * width]
            ks[h, there] = qkv_ref[here, flat + h * width : flat + (h + 1) * width]
            vs[h, there] = qkv_ref[here, 2 * flat + h * width : 2 * flat + (h + 1) * width]
            ds[h, there] = dout_ref[here, h * width : (h + 1) * width]
        turned = qkv_ref[here, flat : 2 * flat].astype(F32).T
        for h in range(heads):
            kt[h, block] = turned[h * width : (h + 1) * width].astype(BF16)
        return carry

    lax.fori_loop(0, length // bq, unpack, 0)
    dk[...] = jnp.zeros_like(dk)
    dv[...] = jnp.zeros_like(dv)

    def query_step(qb, carry):
        q0 = pl.multiple_of(qb * bq, bq)
        queries = pl.ds(q0, bq)
        here = block_rows(core, qb, bq)
        start = start_ref[qb]
        query_place = q0 + lax.broadcasted_iota(jnp.int32, (1, bq), 1)
        products = dout_ref[here, :].astype(F32).T * outt_ref[qb]
        inners = [
            jnp.sum(products[h * width : (h + 1) * width], axis=0, keepdims=True)
            for h in range(heads)
        ]
        dqt[...] = jnp.zeros_like(dqt)

        def key_step(kb, inner_carry):
            k0 = pl.multiple_of(kb * bq, bq)
            keys = pl.ds(k0, bq)
            key_place = k0 + lax.broadcasted_iota(jnp.int32, (bq, bq), 0)
            allowed = (key_place <= query_place) & (key_place >= start)
            for h in range(heads):
                scores = dot_transposed(ks[h, keys], qs[h, queries]) * factor
                weights = jnp.exp2(
                    jnp.where(allowed, scores - lse_ref[qb, h : h + 1, :], MASKED)
                )
                dweights = dot_transposed(vs[h, keys], ds[h, queries])
                dscores = (weights * (dweights - inners[h])).astype(BF16)
                dv[h, keys] += dot_rows(weights.astype(BF16), ds[h, queries])
                dk[h, keys] += dot_rows(dscores, qs[h, queries])
                dqt[h * width : (h + 1) * width] += dot_rows(kt[h, kb], dscores)
            return inner_carry

        lax.fori_loop(low_ref[qb], qb + 1, key_step, 0)
        grad_ref[here, 0:flat] = (dqt[...] * score_scale).T.astype(BF16)
        return carry

    lax.fori_loop(0, length // bq, query_step, 0)

    def write_keys(kb, carry):
        here = block_rows(core, kb, bq)
        rows = pl.ds(pl.multiple_of(kb * bq, bq), bq)
        grad_ref[here, flat : 2 * flat] = jnp.concatenate(
            [dk[h, rows] * score_scale for h in range(heads)], axis=1
        ).astype(BF16)
        grad_ref[here, 2 * flat : 3 * flat] = jnp.concatenate(
            [dv[h, rows] for h in range(heads)], axis=1
        ).astype(BF16)
        rest = grad_ref.shape[1] - 3 * flat
        if rest:
            grad_ref[here, 3 * flat :] = jnp.zeros((bq, rest), BF16)
        return carry

    lax.fori_loop(0, length // bq, write_keys, 0)


def whole_block(shape):
    return pl.BlockSpec(shape, lambda step, *refs: (0,) * len(shape))


def attention_forward(low_blocks, core, starts, qkv, heads):
    length, triple = qkv.shape
    flat = triple // 3
    width = flat // heads
    blocks, _, bq = starts.shape
    grid_spec = pltpu.PrefetchScalarGridSpec(
        num_scalar_prefetch=2,
        grid=(1,),
        in_specs=[whole_block((blocks, 1, bq)), whole_block((length, triple))],
        out_specs=[
            whole_block((length, flat)),
            whole_block((blocks, flat, bq)),
            whole_block((blocks, 8, bq)),
        ],
        scratch_shapes=[
            pltpu.VMEM((heads, length, width), BF16),
            pltpu.VMEM((heads, length, width), BF16),
            pltpu.VMEM((heads, blocks, width, bq), BF16),
            pltpu.VMEM((flat, bq), F32),
        ],
    )
    return pl.pallas_call(
        functools.partial(attention_forward_body, heads, width, bq),
        out_shape=[
            jax.ShapeDtypeStruct((length, flat), BF16),
            jax.ShapeDtypeStruct((blocks, flat, bq), F32),
            jax.ShapeDtypeStruct((blocks, 8, bq), F32),
        ],
        grid_spec=grid_spec,
        compiler_params=pltpu.CompilerParams(vmem_limit_bytes=48 << 20),
        cost_estimate=pl.CostEstimate(
            flops=10 * length * length * flat,
            bytes_accessed=12 * length * flat,
            transcendentals=heads * length * length,
        ),
        name="attention_forward",
    )(low_blocks, core, starts, qkv)


def attention_backward(low_blocks, core, starts, qkv, grad_out, out_turned, log_total, heads):
    length, triple = qkv.shape
    flat = triple // 3
    width = flat // heads
    blocks, _, bq = starts.shape
    per_head = pltpu.VMEM((heads, length, width), BF16)
    sums = pltpu.VMEM((heads, length, width), F32)
    grid_spec = pltpu.PrefetchScalarGridSpec(
        num_scalar_prefetch=2,
        grid=(1,),
        in_specs=[
            whole_block((blocks, 1, bq)),
            whole_block((length, triple)),
            whole_block((length, flat)),
            whole_block((blocks, flat, bq)),
            whole_block((blocks, 8, bq)),
        ],
        out_specs=whole_block((length, lanes(triple))),
        scratch_shapes=[
            per_head,
            per_head,
            per_head,
            per_head,
            pltpu.VMEM((heads, blocks, width, bq), BF16),
            sums,
            sums,
            pltpu.VMEM((flat, bq), F32),
        ],
    )
    return pl.pallas_call(
        functools.partial(attention_backward_body, heads, width, bq),
        out_shape=jax.ShapeDtypeStruct((length, lanes(triple)), BF16),
        grid_spec=grid_spec,
        compiler_params=pltpu.CompilerParams(vmem_limit_bytes=60 << 20),
        cost_estimate=pl.CostEstimate(
            flops=14 * length * length * flat,
            bytes_accessed=20 * length * flat,
            transcendentals=heads * length * length,
        ),
        name="attention_backward",
    )(low_blocks, core, starts, qkv, grad_out, out_turned, log_total)


def lanes(width):
    return -(-width // 128) * 128


def put(ref, value):
    width = value.shape[1]
    ref[:, :width] = value
    if width < ref.shape[1]:
        ref[:, width:] = jnp.zeros((value.shape[0], ref.shape[1] - width), ref.dtype)


def vmem(count):
    return pltpu.CompilerParams(vmem_limit_bytes=count << 20)


def fixed(shape):
    return pl.BlockSpec(shape, lambda *step: (0,) * len(shape), pipeline_mode=pl.Buffered(1))


def hbm():
    return pl.BlockSpec(memory_space=pl.ANY)


def round_weights_body(bound_ref, weight_ref, low_ref, sums_ref):
    values = weight_ref[...]
    low_ref[...] = values[0, 0].astype(BF16)
    place = lax.broadcasted_iota(jnp.int32, values.shape, 2)
    squares = values * values
    lower = jnp.sum(jnp.where(place < bound_ref[0], squares, 0.0))
    sums_ref[0] = lower
    sums_ref[1] = jnp.sum(squares) - lower


def round_weights(bound, weight):
    smem = pl.BlockSpec(memory_space=pltpu.SMEM)
    whole = pl.BlockSpec(memory_space=pltpu.VMEM)
    return pl.pallas_call(
        round_weights_body,
        in_specs=[smem, whole],
        out_specs=[whole, smem],
        out_shape=[
            jax.ShapeDtypeStruct(weight.shape[2:], BF16),
            jax.ShapeDtypeStruct((2,), F32),
        ],
        compiler_params=vmem(32),
        name="round_weights",
    )(bound, weight)


def moments_body(
    ints_ref, floats_ref, lead_ref, rest_ref, first_ref, second_ref, weight_ref,
    grad_ref, moments_ref, update_ref, sums_ref,
):
    step = pl.program_id(0)
    grad = jnp.where(ints_ref[1] == 1, lead_ref[...], rest_ref[...])
    grad_ref[...] = grad
    first = BETA_ONE * first_ref[...] + (1.0 - BETA_ONE) * grad
    second = BETA_TWO * second_ref[...] + (1.0 - BETA_TWO) * grad * grad
    moments_ref[0] = first
    moments_ref[1] = second
    update = (first / floats_ref[0]) / (jnp.sqrt(second / floats_ref[1]) + ADAM_EPS)
    update = update + DECAY * weight_ref[...]
    update_ref[...] = update
    count = grad.shape[2]
    place = step * count + lax.broadcasted_iota(jnp.int32, grad.shape, 2)
    squares = update * update
    lower = jnp.sum(jnp.where(place < ints_ref[0], squares, 0.0))
    upper = jnp.sum(squares) - lower

    @pl.when(step == 0)
    def clear():
        sums_ref[0] = 0.0
        sums_ref[1] = 0.0

    sums_ref[0] += lower
    sums_ref[1] += upper


def flat_steps(count):
    return 7 if count % (7 * 128) == 0 else 1


def new_moments(ints, floats, lead, rest, first, second, weight):
    count = weight.shape[2]
    steps = flat_steps(count)
    smem = pl.BlockSpec(memory_space=pltpu.SMEM)
    flat = pl.BlockSpec((1, 1, count // steps), lambda i: (0, 0, i))
    pair = pl.BlockSpec((2, 1, 1, count // steps), lambda i: (0, 0, 0, i))
    return pl.pallas_call(
        moments_body,
        grid=(steps,),
        in_specs=[smem, smem] + [flat] * 5,
        out_specs=[flat, pair, flat, smem],
        out_shape=[
            jax.ShapeDtypeStruct(weight.shape, F32),
            jax.ShapeDtypeStruct((2,) + weight.shape, F32),
            jax.ShapeDtypeStruct(weight.shape, F32),
            jax.ShapeDtypeStruct((2,), F32),
        ],
        compiler_params=vmem(48),
        name="new_moments",
    )(ints, floats, lead, rest, first, second, weight)


def new_weights_body(ints_ref, ratio_ref, weight_ref, update_ref, new_ref, copy_ref):
    count = weight_ref.shape[2]
    place = pl.program_id(0) * count + lax.broadcasted_iota(jnp.int32, weight_ref.shape, 2)
    rate = jnp.where(place < ints_ref[0], ratio_ref[0], ratio_ref[1])
    new = weight_ref[...] - MATRIX_RATE * rate * update_ref[...]
    new_ref[...] = new
    copy_ref[...] = new.astype(BF16)


def new_weights(ints, ratios, weight, update):
    count = weight.shape[2]
    steps = flat_steps(count)
    smem = pl.BlockSpec(memory_space=pltpu.SMEM)
    flat = pl.BlockSpec((1, 1, count // steps), lambda i: (0, 0, i))
    return pl.pallas_call(
        new_weights_body,
        grid=(steps,),
        in_specs=[smem, smem, flat, flat],
        out_specs=[flat, flat],
        out_shape=[
            jax.ShapeDtypeStruct(weight.shape, F32),
            jax.ShapeDtypeStruct(weight.shape, BF16),
        ],
        compiler_params=vmem(32),
        name="new_weights",
    )(ints, ratios, weight, update)


def unpack_body(cut, out_rows, in_rows, place_ref, *refs):
    blocks, (w_out, w_in, w_back, held, sems) = refs[:8], refs[8:]
    here = place_ref[0]
    copies = [
        pltpu.make_async_copy(block, held.at[index ^ here], sems.at[index])
        for index, block in enumerate(blocks)
    ]
    for copy in copies:
        copy.start()
    for copy in copies:
        copy.wait()
    begin = 2 * cut
    for target, rows in ((w_out, out_rows), (w_in, in_rows), (w_back, in_rows)):
        done = 0
        while done < rows:
            block, offset = divmod(begin + done, cut)
            count = min(cut - offset, rows - done)
            target[done : done + count] = held[block, offset : offset + count]
            done += count
        begin += rows


def unpack_share(place, blocks, out_rows, in_rows):
    cut, columns = blocks[0].shape
    shapes = [(out_rows, columns), (in_rows, columns), (in_rows, columns)]
    return pl.pallas_call(
        functools.partial(unpack_body, cut, out_rows, in_rows),
        grid_spec=pltpu.PrefetchScalarGridSpec(
            num_scalar_prefetch=1,
            grid=(1,),
            in_specs=[hbm()] * 8,
            out_specs=[whole_block(shape) for shape in shapes],
            scratch_shapes=[
                pltpu.VMEM((8, cut, columns), BF16),
                pltpu.SemaphoreType.DMA((8,)),
            ],
        ),
        out_shape=[jax.ShapeDtypeStruct(shape, BF16) for shape in shapes],
        compiler_params=vmem(48),
        cost_estimate=pl.CostEstimate(flops=0, bytes_accessed=20 << 20, transcendentals=0),
        name="unpack_share",
    )(place, *blocks)


def rows_of(step, steps, own_ref, other_ref, width):
    return jnp.where(step < steps, own_ref[:, :width], other_ref[:, :width])


def both_specs(block, width, steps):
    own = pl.BlockSpec((block, width), lambda i, *refs: (jnp.minimum(i, steps - 1), 0))
    other = pl.BlockSpec((block, width), lambda i, *refs: (jnp.maximum(i - steps, 0), 0))
    return own, other


def project_body(
    steps, place_ref, own_ref, other_ref, a0, a1, b0, b1, bias_ref,
    out_a, out_b, rows_ref, w_a, w_b, sems,
):
    step = pl.program_id(0)

    @pl.when(step == 0)
    def load():
        cut = a0.shape[0]
        here = place_ref[0]
        first = pl.ds(pl.multiple_of(here * cut, cut), cut)
        second = pl.ds(pl.multiple_of((1 - here) * cut, cut), cut)
        copies = [
            pltpu.make_async_copy(a0, w_a.at[first], sems.at[0]),
            pltpu.make_async_copy(a1, w_a.at[second], sems.at[1]),
            pltpu.make_async_copy(b0, w_b.at[first], sems.at[2]),
            pltpu.make_async_copy(b1, w_b.at[second], sems.at[3]),
        ]
        for copy in copies:
            copy.start()
        for copy in copies:
            copy.wait()

    rows = rows_of(step, steps, own_ref, other_ref, rows_ref.shape[1])
    rows_ref[...] = rows
    out_a[...] = (dot_rows(rows, w_a[...]) + bias_ref[0:1]).astype(BF16)
    out_b[...] = (dot_rows(rows, w_b[...]) + bias_ref[1:2]).astype(BF16)


def project(place, own, other, halves, biases):
    count, sent_width = own.shape
    cut, triple = halves[0].shape
    model_width = 2 * cut
    block = min(512, count)
    steps = count // block
    row_out = lambda width: pl.BlockSpec((block, width), lambda i, *refs: (i, 0))
    matrix = jax.ShapeDtypeStruct((2 * cut, triple), BF16)
    return pl.pallas_call(
        functools.partial(project_body, steps),
        grid_spec=pltpu.PrefetchScalarGridSpec(
            num_scalar_prefetch=1,
            grid=(2 * steps,),
            in_specs=[*both_specs(block, sent_width, steps)]
            + [hbm()] * 4
            + [fixed((2, triple))],
            out_specs=[row_out(triple), row_out(triple), row_out(model_width)]
            + [pl.BlockSpec(matrix.shape, lambda i, *refs: (0, 0))] * 2,
            scratch_shapes=[pltpu.SemaphoreType.DMA((4,))],
        ),
        out_shape=[jax.ShapeDtypeStruct((2 * count, triple), BF16)] * 2
        + [jax.ShapeDtypeStruct((2 * count, model_width), BF16), matrix, matrix],
        compiler_params=vmem(48),
        cost_estimate=pl.CostEstimate(
            flops=8 * count * model_width * triple, bytes_accessed=24 << 20, transcendentals=0
        ),
        name="project",
    )(place, own, other, *halves, biases)


def out_grads_body(steps, own_ref, other_ref, w_a, w_b, out_a, out_b, rows_ref):
    rows = rows_of(pl.program_id(0), steps, own_ref, other_ref, rows_ref.shape[1])
    rows_ref[...] = rows
    out_a[...] = dot_transposed(rows, w_a[...]).astype(BF16)
    out_b[...] = dot_transposed(rows, w_b[...]).astype(BF16)


def out_grads(own, other, w_out):
    count, sent_width = own.shape
    width, model_width = w_out[0].shape
    block = min(512, count)
    steps = count // block
    row_out = lambda columns: pl.BlockSpec((block, columns), lambda i: (i, 0))
    return pl.pallas_call(
        functools.partial(out_grads_body, steps),
        grid=(2 * steps,),
        in_specs=[*both_specs(block, sent_width, steps)] + [fixed(w_out[0].shape)] * 2,
        out_specs=[row_out(width), row_out(width), row_out(model_width)],
        out_shape=[jax.ShapeDtypeStruct((2 * count, width), BF16)] * 2
        + [jax.ShapeDtypeStruct((2 * count, model_width), BF16)],
        compiler_params=vmem(48),
        cost_estimate=pl.CostEstimate(
            flops=8 * count * model_width * width, bytes_accessed=14 << 20, transcendentals=0
        ),
        name="out_grads",
    )(own, other, *w_out)


def split_product_body(steps, turned, left_a, left_b, w_a, w_b, sent_ref, kept_ref):
    multiply = dot_transposed if turned else dot_rows
    inner = w_a.shape[1] if turned else w_a.shape[0]
    product = multiply(left_a[:, :inner], w_a[...]) + multiply(left_b[:, :inner], w_b[...])
    step = pl.program_id(0)

    @pl.when(step < steps)
    def other_rows():
        put(sent_ref, product)

    @pl.when(step >= steps)
    def own_rows():
        kept_ref[...] = product


def split_product(lefts, weights, turned, model_width):
    count, width = lefts[0].shape
    block = min(512, count // 2)
    steps = count // 2 // block
    left = pl.BlockSpec((block, width), lambda i: ((i + steps) % (2 * steps), 0))
    parts = [
        jax.ShapeDtypeStruct((count // 2, lanes(model_width)), F32),
        jax.ShapeDtypeStruct((count // 2, model_width), F32),
    ]
    return pl.pallas_call(
        functools.partial(split_product_body, steps, turned),
        grid=(2 * steps,),
        in_specs=[left, left] + [fixed(weights[0].shape)] * 2,
        out_specs=[
            pl.BlockSpec((block, lanes(model_width)), lambda i: (jnp.minimum(i, steps - 1), 0)),
            pl.BlockSpec((block, model_width), lambda i: (jnp.maximum(i - steps, 0), 0)),
        ],
        out_shape=parts,
        compiler_params=vmem(48),
        cost_estimate=pl.CostEstimate(
            flops=4 * count * model_width * width, bytes_accessed=20 << 20, transcendentals=0
        ),
        name="split_product",
    )(*lefts, *weights)


def middle_body(rows_ref, kept_ref, got_ref, small_ref, middle_ref, low_ref):
    middle = rows_ref[...].astype(F32) + (
        kept_ref[...] + got_ref[:, : kept_ref.shape[1]] + small_ref[6:7]
    )
    middle_ref[...] = middle
    hat, _ = norm_stats(middle)
    put(low_ref, (hat * small_ref[2:3] + small_ref[3:4]).astype(BF16))


def middle_norm(rows, kept, got, small):
    count, width = rows.shape
    block = min(256, count)
    part = pl.BlockSpec((block, width), lambda i: (i, 0))
    sent = pl.BlockSpec((block, lanes(width)), lambda i: (i, 0))
    return pl.pallas_call(
        middle_body,
        grid=(count // block,),
        in_specs=[part, part, sent, fixed(small.shape)],
        out_specs=[part, sent],
        out_shape=[
            jax.ShapeDtypeStruct((count, width), F32),
            jax.ShapeDtypeStruct((count, lanes(width)), BF16),
        ],
        compiler_params=vmem(32),
        name="middle_norm",
    )(rows, kept, got, small)


def norm_back_body(wide_out, rows_ref, kept_ref, got_ref, base_ref, gain_ref, *outs):
    (full_ref, low_ref, sums_ref) = outs if wide_out else (None, *outs)
    rows = rows_ref[...].astype(F32)
    hat, scale = norm_stats(rows)
    width = rows.shape[1]
    upstream = kept_ref[:, :width] + got_ref[:, :width]
    base = base_ref[:, :width].astype(F32)
    grad = base + norm_backward(upstream, hat, scale, gain_ref[...])
    low = grad.astype(BF16)
    if wide_out:
        full_ref[...] = grad
    put(low_ref, low)

    @pl.when(pl.program_id(0) == 0)
    def clear():
        sums_ref[...] = jnp.zeros_like(sums_ref)

    for index, term in enumerate((upstream * hat, upstream, low.astype(F32), base)):
        sums_ref[index : index + 1] += jnp.sum(term, axis=0, keepdims=True)


def norm_back(rows, kept, got, base, gain, wide_out):
    count, width = rows.shape
    block = min(256, count)
    part = pl.BlockSpec((block, width), lambda i: (i, 0))
    sent = pl.BlockSpec((block, lanes(width)), lambda i: (i, 0))
    full = [jax.ShapeDtypeStruct((count, width), F32)] if wide_out else []
    return pl.pallas_call(
        functools.partial(norm_back_body, wide_out),
        grid=(count // block,),
        in_specs=[part, pl.BlockSpec((block, kept.shape[1]), lambda i: (i, 0)), sent]
        + [pl.BlockSpec((block, base.shape[1]), lambda i: (i, 0)), fixed((1, width))],
        out_specs=[part] * len(full) + [sent, pl.BlockSpec((8, width), lambda i: (0, 0))],
        out_shape=full
        + [
            jax.ShapeDtypeStruct((count, lanes(width)), BF16),
            jax.ShapeDtypeStruct((8, width), F32),
        ],
        compiler_params=vmem(40),
        name="norm_back",
    )(rows, kept, got, base, gain)


def feed_forward_body(
    skipped,
    rows_ref,
    cot_ref,
    w_in_mine,
    w_in_theirs,
    w_back_mine,
    w_back_theirs,
    bias_ref,
    *refs,
):
    (
        act_mine, act_theirs, inner_mine, inner_theirs, rows_out, cot_out, out_ref, up_ref, sums_ref
    ) = refs[skipped:]
    model_width = rows_out.shape[1]
    rows, cot = rows_ref[:, :model_width], cot_ref[:, :model_width]
    rows_out[...] = rows
    cot_out[...] = cot

    @pl.when(pl.program_id(0) == 0)
    def clear():
        sums_ref[...] = jnp.zeros_like(sums_ref)

    out, up = None, None
    shares = (
        (w_in_mine, w_back_mine, act_mine, inner_mine),
        (w_in_theirs, w_back_theirs, act_theirs, inner_theirs),
    )
    for part, (w_in, w_back, act_ref, inner_ref) in enumerate(shares):
        hidden = dot_rows(rows, w_in[...]) + bias_ref[part : part + 1]
        value, slope = gelu_parts(hidden)
        act = value.astype(BF16)
        act_ref[...] = act
        inner = (dot_transposed(cot, w_back[...]) * slope).astype(BF16)
        inner_ref[...] = inner
        sums_ref[part : part + 1] += jnp.sum(inner.astype(F32), axis=0, keepdims=True)
        one_out = dot_rows(act, w_back[...])
        one_up = dot_transposed(inner, w_in[...])
        out = one_out if out is None else out + one_out
        up = one_up if up is None else up + one_up
    put(out_ref, out)
    put(up_ref, up)


def feed_forward(rows, cot, half, weights, biases, filled):
    count, sent_width = rows.shape
    model_width, ff_share = weights[0].shape
    block = min(FF_ROWS, count)
    steps = count // block
    row_spec = pl.BlockSpec((block, sent_width), lambda i: (i, 0))
    joined = lambda width: pl.BlockSpec((block, width), lambda i: (half * steps + i, 0))
    act_shape = jax.ShapeDtypeStruct((2 * count, ff_share), BF16)
    row_shape = jax.ShapeDtypeStruct((2 * count, model_width), BF16)
    part_shape = jax.ShapeDtypeStruct((count, sent_width), F32)
    filled = () if filled is None else tuple(filled)
    return pl.pallas_call(
        functools.partial(feed_forward_body, len(filled)),
        out_shape=[act_shape] * 4
        + [row_shape] * 2
        + [part_shape] * 2
        + [jax.ShapeDtypeStruct((8, ff_share), F32)],
        grid=(steps,),
        in_specs=[row_spec, row_spec]
        + [fixed(matrix.shape) for matrix in weights]
        + [fixed((2, ff_share))]
        + [hbm()] * len(filled),
        out_specs=[joined(ff_share)] * 4
        + [joined(model_width)] * 2
        + [row_spec] * 2
        + [pl.BlockSpec((8, ff_share), lambda i: (0, 0))],
        input_output_aliases={7 + i: i for i in range(len(filled))},
        compiler_params=vmem(58),
        cost_estimate=pl.CostEstimate(
            flops=16 * count * model_width * ff_share,
            bytes_accessed=8 * model_width * ff_share + 16 * count * model_width,
            transcendentals=2 * count * ff_share,
        ),
        name="feed_forward",
    )(rows, cot, *weights, biases, *filled)


def permute(value, axis_name, pairs):
    return lax.ppermute(value, axis_name, pairs)


def swap(value, axis_name, distance):
    count = lax.axis_size(axis_name)
    return permute(value, axis_name, [(i, i ^ distance) for i in range(count)])


def tie(*values):
    return lax.optimization_barrier(values)


def lower_pairs(pairs, y_count):
    return [
        (source * y_count + y, target * y_count + y)
        for source, target in pairs
        for y in range(y_count)
    ]


def spread_lead(block, z_here):
    far = permute(block, "dp", lower_pairs([(0, 2)], 2))
    held = jnp.where(z_here == 0, block, far)
    near = permute(held, "dp", lower_pairs([(0, 1), (2, 3)], 2))
    return jnp.where(z_here % 2 == 0, held, near)


def move_rest(block, distance, plane_distance):
    over_dp, over_seq = distance
    pairs = []
    for d in range(8):
        if (d // 2) ^ plane_distance != 0:
            pairs += [(d * 4 + q, (d ^ over_dp) * 4 + (q ^ over_seq)) for q in range(4)]
    return permute(block, ("dp", "seq"), pairs)


def pick(stacked, index, axis=0):
    return lax.dynamic_index_in_dim(stacked, index, axis, keepdims=False)


def halve_plane(lower, upper, y_here):
    return (
        jnp.where(y_here == 0, lower, upper),
        jnp.where(y_here == 0, upper, lower).astype(BF16),
    )


def nearer_planes(held, plane):
    near = permute(
        held.astype(BF16), "dp", lower_pairs([(plane ^ 1, plane), (plane ^ 3, plane ^ 2)], 2)
    )
    return held + near.astype(F32)


def farther_planes(held, plane):
    far = permute(held.astype(BF16), "dp", lower_pairs([(plane ^ 2, plane)], 2))
    return held + far.astype(F32)


def sum_everywhere(value):
    for axis_name in ("seq", "dp"):
        distance = 1
        while distance < lax.axis_size(axis_name):
            value = value + swap(value, axis_name, distance)
            distance *= 2
    return value


def per_device(
    rows_in,
    out_cotangent,
    cell_lengths,
    cell_starts,
    key_mask,
    weights_master,
    first_moment,
    second_moment,
    small_master,
    small_first,
    small_second,
    step_count,
):
    model_width = rows_in.shape[3]
    local_rows = rows_in.shape[2]
    length = key_mask.shape[2]
    shard_len = weights_master.shape[2]
    groups = lax.axis_size("seq")
    dp_count = lax.axis_size("dp")
    head_share = model_width // groups
    heads_here = HEADS // groups
    triple = 3 * head_share
    first_end = model_width * triple
    second_end = first_end + head_share * model_width
    third_end = second_end + model_width * model_width
    seq_here = lax.axis_index("seq")
    dp_here = lax.axis_index("dp")
    chip = seq_here // 2
    core = seq_here % 2
    z_here = dp_here // 2
    y_here = dp_here % 2
    planar = dp_count == 8 and shard_len * 2 == first_end
    shares = (core + 2 * chip, core + 2 * (1 - chip))

    def exchange_micro(array):
        own = pick(array[:, 0], chip)
        received = swap(widen(pick(array[:, 0], 1 - chip)), "seq", 2)[:, :model_width]
        first = jnp.where(chip == 0, own, received)
        second = jnp.where(chip == 0, received, own)
        return jnp.concatenate([first, second], axis=0)

    def widen(rows):
        return jnp.pad(rows, ((0, 0), (0, lanes(model_width) - model_width)))

    own_in = exchange_micro(rows_in)

    ends = jnp.array([first_end, second_end, third_end, dp_count * shard_len], jnp.int32)
    begin = dp_here * shard_len
    lower_matrix = jnp.sum((begin >= ends).astype(jnp.int32))
    upper_matrix = jnp.sum((begin + shard_len - 1 >= ends).astype(jnp.int32))
    bound = jnp.minimum(pick(ends, lower_matrix) - begin, shard_len).reshape(1)
    matrices = jnp.arange(4, dtype=jnp.int32)

    def matrix_sums(pair):
        return jnp.where(matrices == lower_matrix, pair[0], 0.0) + jnp.where(
            matrices == upper_matrix, pair[1], 0.0
        )

    weight = weights_master
    low_weight, weight_sums = round_weights(bound, weight)
    y_index = y_here.reshape(1).astype(jnp.int32)
    if planar:
        tall = low_weight.reshape(shard_len // triple, triple)
        wide = low_weight.reshape(shard_len // model_width, model_width)
        cut, tall_rows = wide.shape[0], tall.shape[0]
        lead = spread_lead(tall, z_here)
        lead, wide = tie(lead, wide)
        lead_across = swap(lead, "dp", 1)
        halves = (lead, lead_across, swap(lead, "seq", 2), swap(lead_across, "seq", 2))
        dp_index = dp_here.reshape(1).astype(jnp.int32)
        far = move_rest(wide, (4, 0), 0)
        near = move_rest(wide, (2, 0), 0)
    else:
        copies = lax.all_gather(low_weight.reshape(1, shard_len), ("dp", "seq"), axis=0, tiled=True)
        copies = copies.reshape(dp_count, groups, shard_len)
        per_share = [pick(copies, share, 1).reshape(dp_count * shard_len) for share in shares]
        halves = []
        for flat in per_share:
            matrix = flat[:first_end].reshape(model_width, triple)
            first = jnp.where(y_here == 0, matrix[: model_width // 2], matrix[model_width // 2 :])
            second = jnp.where(y_here == 0, matrix[model_width // 2 :], matrix[: model_width // 2])
            halves += [first, second]
        w_out = [flat[first_end:second_end].reshape(head_share, model_width) for flat in per_share]
        w_in = [flat[second_end:third_end].reshape(model_width, model_width) for flat in per_share]
        w_back = [flat[third_end:].reshape(model_width, model_width) for flat in per_share]

    def share_columns(vector, share):
        return lax.dynamic_slice_in_dim(vector, share * head_share, head_share)

    attn_biases = [
        jnp.concatenate(
            [
                share_columns(small_master[4], share),
                jnp.zeros((head_share,), F32),
                share_columns(small_master[5], share),
            ]
        )
        for share in shares
    ]
    ff_biases = jnp.stack([pick(small_master, 8 + share) for share in shares])

    starts = pick(cell_starts[:, 0], chip)
    lengths = pick(cell_lengths[:, 0], chip)
    places = jnp.arange(length, dtype=jnp.int32)
    inside = (places[:, None] >= starts[None, :]) & (places[:, None] < (starts + lengths)[None, :])
    first_key = jnp.max(jnp.where(inside, starts[None, :], -1), axis=1)
    first_key = jnp.where(first_key < 0, places, first_key)
    low_blocks = first_key.reshape(-1, local_rows)[:, 0] // local_rows
    block_starts = first_key.reshape(-1, 1, local_rows)
    core_index = core.reshape(1).astype(jnp.int32)

    inputs = own_in.astype(F32)
    hat_one, _ = norm_stats(inputs)
    low_one = widen((hat_one * small_master[0] + small_master[1]).astype(BF16))
    other_one = swap(low_one, "seq", 1)

    *qkv, rows_one, w_attn_mine, w_attn_theirs = project(
        y_index, low_one, other_one, halves, jnp.stack(attn_biases)
    )

    def attend(part):
        return attention_forward(low_blocks, core_index, block_starts, qkv[part], heads_here)

    if planar:
        near, far, qkv[0] = tie(near, far, qkv[0])
        planes = (wide, near, far, move_rest(far, (2, 0), 2))
        across = [move_rest(block, (1, 0), plane) for plane, block in enumerate(planes[:3])]
        over = [move_rest(block, (0, 2), plane) for plane, block in enumerate(planes[:3])]
    attended = [attend(0)]
    if planar:
        qkv[1], planes, across, over, own_e_in, _ = tie(
            qkv[1], planes, across, over, out_cotangent, attended[0][2]
        )
        across.append(move_rest(planes[3], (1, 0), 3))
        over.append(move_rest(planes[3], (0, 2), 3))
        both = [
            move_rest(over[plane], (1, 0), plane)
            if plane % 2 == 0
            else move_rest(across[plane], (0, 2), plane)
            for plane in range(4)
        ]
    else:
        own_e_in = out_cotangent
    own_e = widen(exchange_micro(own_e_in))
    other_e = swap(own_e, "seq", 1)
    attended.append(attend(1))
    if planar:
        dp_index, _ = tie(dp_index, attended[1][2])
        rest_mine = [block for pair in zip(planes, across) for block in pair]
        rest_theirs = [block for pair in zip(over, both) for block in pair]
        matrices_mine = unpack_share(dp_index, rest_mine, head_share, model_width)
        matrices_theirs = unpack_share(dp_index, rest_theirs, head_share, model_width)
        w_out, w_in, w_back = (list(pair) for pair in zip(matrices_mine, matrices_theirs))
    sent, kept = split_product([attended[0][0], attended[1][0]], w_out, False, model_width)
    middle, low_two = middle_norm(own_in, kept, swap(sent, "seq", 1), small_master)
    other_two = swap(low_two, "seq", 1)

    weights = (w_in[0], w_in[1], w_back[0], w_back[1])
    *filled, out_sent, up_sent, sums_sent = feed_forward(
        other_two, other_e, 1, weights, ff_biases, None
    )
    out_received = swap(out_sent, "seq", 1)
    up_received = swap(up_sent, "seq", 1)
    *filled, out_kept, up_kept, sums_kept = feed_forward(
        low_two, own_e, 0, weights, ff_biases, filled
    )
    activated, inner, (rows_two, rows_e) = filled[:2], filled[2:4], filled[4:]
    inner_sums = sums_sent + sums_kept

    link = BF16 if planar else F32
    back_sent = dot_columns(activated[1], rows_e).astype(link)
    in_sent = dot_columns(rows_two, inner[1]).astype(link)
    back_sent, in_sent, up_kept = tie(*(back_sent, in_sent, up_kept))
    back_received = swap(back_sent, "seq", 2)
    in_received = swap(in_sent, "seq", 2)

    grad_mid, low_mid, sums_two = norm_back(
        middle, up_kept, up_received, own_e, small_master[2:3], True
    )
    grad_att_mine, grad_att_theirs, rows_mid = out_grads(low_mid, swap(low_mid, "seq", 1), w_out)
    out_sent_theirs = dot_columns(attended[1][0], rows_mid).astype(link)
    out_sent_theirs, grad_att_theirs = tie(*(out_sent_theirs, grad_att_theirs))
    outer_received = swap(out_sent_theirs, "seq", 2)

    def attend_back(part, grad_att):
        return attention_backward(
            low_blocks,
            core_index,
            block_starts,
            qkv[part],
            grad_att,
            attended[part][1],
            attended[part][2],
            heads_here,
        )

    packed_theirs = attend_back(1, grad_att_theirs)
    attn_sent = dot_columns(rows_one, packed_theirs).astype(link)
    attn_sent, packed_theirs, rows_two, rows_e, rows_mid = tie(
        attn_sent, packed_theirs, rows_two, rows_e, rows_mid
    )
    attn_received = swap(attn_sent, "seq", 2)
    share_back = dot_columns(activated[0], rows_e)
    share_in = dot_columns(rows_two, inner[0])
    share_out = dot_columns(attended[0][0], rows_mid)
    share_back, share_in, share_out, back_received, in_received, outer_received = tie(
        share_back, share_in, share_out, back_received, in_received, outer_received
    )
    share_back = share_back + back_received.astype(F32)
    share_in = share_in + in_received.astype(F32)
    share_out = share_out + outer_received.astype(F32)
    if planar:
        rest = cut - head_share
        seams = [rest, rest + cut, rest + 2 * cut]
        taken = cut - (model_width - seams[2])
        pieces = [
            jnp.concatenate([share_out, share_in[: seams[0]]], axis=0),
            share_in[seams[0] : seams[1]],
            share_in[seams[1] : seams[2]],
            jnp.concatenate([share_in[seams[2] :], share_back[:taken]], axis=0),
            share_back[taken : taken + cut],
            share_back[taken + cut :],
        ]
        split = [halve_plane(pieces[2 * i], pieces[2 * i + 1], y_here) for i in range(3)]
        kept_rest, sent_rest = [pair[0] for pair in split], [pair[1] for pair in split]
        kept_rest, sent_rest, grad_att_mine = tie(kept_rest, sent_rest, grad_att_mine)
        got_rest = [swap(block, "dp", 1) for block in sent_rest]

    packed_mine = attend_back(0, grad_att_mine)
    share_attn = dot_columns(rows_one, packed_mine) + attn_received.astype(F32)
    if planar:
        kept_lead, sent_lead = halve_plane(share_attn[:tall_rows], share_attn[tall_rows:], y_here)
        kept_lead, sent_lead, kept_rest, packed_mine, out_received = tie(
            kept_lead, sent_lead, kept_rest, packed_mine, out_received
        )
        got_lead = swap(sent_lead, "dp", 1)
        sums_rest = [
            nearer_planes(kept + got.astype(F32), plane)
            for plane, kept, got in zip((1, 2, 3), kept_rest, got_rest)
        ]
    result_rows = widen(
        (middle + ((out_kept + out_received)[:, :model_width] + small_master[7])).astype(BF16)
    )
    packed = [packed_mine, packed_theirs]
    sent, kept = split_product(packed, [w_attn_mine, w_attn_theirs], True, model_width)
    grad_x, sums_one = norm_back(
        own_in, kept, swap(sent, "seq", 1), grad_mid, small_master[0:1], False
    )

    def return_micro(rows):
        lower, upper = rows[:local_rows], rows[local_rows:]
        own = jnp.where(chip == 0, lower, upper)[:, :model_width]
        received = swap(jnp.where(chip == 0, upper, lower), "seq", 2)[:, :model_width]
        first = jnp.where(chip == 0, own, received)
        second = jnp.where(chip == 0, received, own)
        return jnp.stack([first, second])[:, None]

    result_all = return_micro(result_rows)
    grad_all = return_micro(grad_x)

    def at_shares(columns):
        row = jnp.zeros((model_width,), F32)
        for share, column in zip(shares, columns):
            row = lax.dynamic_update_slice(row, column, (share * head_share,))
        return row

    bias_sums = [jnp.sum(packed[part].astype(F32), axis=0) for part in range(2)]
    inner_rows = jnp.zeros((4, model_width), F32)
    for part in range(2):
        inner_rows = lax.dynamic_update_slice(
            inner_rows, inner_sums[part : part + 1], (shares[part], 0)
        )
    small_now = jnp.concatenate(
        [
            sums_one[:2],
            sums_two[:2],
            at_shares([sums[:head_share] for sums in bias_sums])[None],
            at_shares([sums[2 * head_share : triple] for sums in bias_sums])[None],
            sums_two[2:4],
            inner_rows,
            jnp.pad(matrix_sums(weight_sums), (0, model_width - 4))[None],
        ]
    )

    if planar:
        sum_lead = nearer_planes(kept_lead + got_lead.astype(F32), 0)
        sums_rest = [farther_planes(held, plane) for plane, held in zip((1, 2, 3), sums_rest)]
        wide_sum = jnp.where(
            z_here == 1, sums_rest[0], jnp.where(z_here == 2, sums_rest[1], sums_rest[2])
        )
        lead_grad = farther_planes(sum_lead, 0)[:, :triple].reshape(1, 1, shard_len)
        rest_grad = wide_sum.reshape(1, 1, shard_len)
        leads = z_here == 0
    else:
        flat_here = jnp.concatenate(
            [matrix.reshape(-1) for matrix in (share_attn[:, :triple], share_out, share_in, share_back)]
        )
        lead_grad = lax.psum_scatter(
            flat_here.reshape(dp_count, shard_len), "dp", scatter_dimension=0, tiled=True
        ).reshape(1, 1, shard_len)
        rest_grad = lead_grad
        leads = z_here >= 0

    steps_done = step_count[0].astype(F32)
    fix_one = 1.0 - jnp.exp(steps_done * math.log(BETA_ONE))
    fix_two = 1.0 - jnp.exp(steps_done * math.log(BETA_TWO))
    ints = jnp.concatenate([bound, leads.astype(jnp.int32).reshape(1)])
    reduced, moments, update, update_sums = new_moments(
        ints,
        jnp.stack([fix_one, fix_two]),
        lead_grad,
        rest_grad,
        first_moment,
        second_moment,
        weight,
    )
    small_sum = sum_everywhere(small_now)
    small_grad = small_sum[:12]
    weight_norms = jnp.sqrt(small_sum[12, :4])
    update_norms = jnp.sqrt(sum_everywhere(matrix_sums(update_sums)[None])[0])
    ratios = weight_norms / update_norms
    new_weight, weight_copy = new_weights(
        ints, jnp.stack([pick(ratios, lower_matrix), pick(ratios, upper_matrix)]), weight, update
    )
    small_one = BETA_ONE * small_first + (1.0 - BETA_ONE) * small_grad
    small_two = BETA_TWO * small_second + (1.0 - BETA_TWO) * small_grad * small_grad
    small_updated = small_master - SMALL_RATE * (small_one / fix_one) / (
        jnp.sqrt(small_two / fix_two) + ADAM_EPS
    )
    return (
        result_all,
        grad_all,
        reduced,
        moments,
        new_weight,
        weight_copy,
        jnp.stack([weight_norms, update_norms, ratios]),
        small_grad,
        jnp.stack([small_one, small_two]),
        small_updated,
    )


def solution(mesh):
    in_specs = (
        P(None, "dp", "seq", None),
        P(None, "dp", "seq", None),
        P(None, "dp", None),
        P(None, "dp", None),
        P(None, "dp", None),
        P("dp", "seq", None),
        P("dp", "seq", None),
        P("dp", "seq", None),
        P(),
        P(),
        P(),
        P(),
    )
    out_specs = (
        P(None, "dp", "seq", None),
        P(None, "dp", "seq", None),
        P("dp", "seq", None),
        P(None, "dp", "seq", None),
        P("dp", "seq", None),
        P("dp", "seq", None),
        P(),
        P(),
        P(),
        P(),
    )
    return jax.shard_map(
        per_device, mesh=mesh, in_specs=in_specs, out_specs=out_specs, check_vma=False
    )
```

time: 1540 us -> 903 us (0.59)
  local copies, waits for them, and re-layouts: 499 us -> 72.3 us
  other arithmetic: 261 us -> 86 us
  Pallas kernels: 183 us -> 354 us
  matrix products: 218 us -> 64 us
  blocking collectives: 48.4 us -> 0 us
  waiting for transfers between devices: 252 us -> 223 us
  starting transfers between devices: 56.2 us -> 79.7 us
    pallas_call x0 -> x14, Pallas kernels: none -> 173 us  [the longest x2 69.6 us: feed_forward(): pl.pallas_call(functools.partial(feed_forward_body, len(filled)), out_sha...]
    dot_general x22 -> x0, matrix products: 156 us -> none  [the longest x10 78.3 us: dot_rows(): lax.dot_general(left, right, (((1,), (0,)), ((), ())), preferred_element_...]
    another operation x22 -> x3, local copies, waits for them, and re-layouts: 99.9 us -> 0.01 us  [the longest x2 0.01 us: per_device(): jnp.stack(attn_biases)]
    unnamed x320 -> x163, local copies, waits for them, and re-layouts: 117 us -> 34.9 us
    reshape x14 -> x4, local copies, waits for them, and re-layouts: 85.4 us -> 14.7 us  [the longest x1 6.03 us: per_device(): lead_grad = farther_planes(sum_lead, 0)[:, :triple].reshape(1, 1, shard_len)]
    dynamic_slice x11 -> x8, local copies, waits for them, and re-layouts: 67.8 us -> 14 us  [pick(): return lax.dynamic_index_in_dim(stacked, index, axis, keepdims=False)]
    mul x4 -> x0, other arithmetic: 49 us -> none  [the longest x1 22.6 us: per_device(): first_new = BETA_ONE * first_moment[0, 0] + (1.0 - BETA_ONE) * reduced]
    reduce_sum x6 -> x3, other arithmetic: 51.4 us -> 2.51 us  [the longest x1 1.38 us: per_device(): upper_matrix = jnp.sum((begin + shard_len - 1 >= ends).astype(jnp.int32))]
  transfers between devices with their start and end apart: 44 -> 58, of which waited for: 21 -> 22; matrix products, arithmetic and copies ran while one was open for 48% -> 21% of each run, Pallas kernels for 5% -> 32%
where the time goes in v2:
time: 903 us; the launch traced here: 887 us
  Pallas kernels  354 us (39%)
  waiting for transfers between devices  223 us (25%)
  other arithmetic  86 us (10%)
  starting transfers between devices  79.7 us (9%)
  local copies, waits for them, and re-layouts  72.3 us (8%)
  matrix products  64 us (7%)
    ppermute x58, waiting for transfers between devices, permute(): return lax.ppermute(value, axis_name, pairs)  223 us
    pallas_call x2, Pallas kernels, attention_backward(): pl.pallas_call(functools.partial(attention_backward_body, heads, width, b...  112 us
    ppermute x58, starting transfers between devices, permute(): return lax.ppermute(value, axis_name, pairs)  79.7 us
    pallas_call x2, Pallas kernels, feed_forward(): pl.pallas_call(functools.partial(feed_forward_body, len(filled)), out_sha...  69.6 us
    pallas_call x2, Pallas kernels, attention_forward(): pl.pallas_call(functools.partial(attention_forward_body, heads, width, bq...  69.5 us
    dot_general x8, matrix products, dot_columns(): lax.dot_general(left, right, (((0,), (0,)), ((), ())), preferred_element_...  64 us
    unnamed x163, local copies, waits for them, and re-layouts  34.9 us
    pallas_call x2, Pallas kernels, split_product(): pl.pallas_call(functools.partial(split_product_body, steps, turned), grid...  24.7 us
  transfers between devices with their start and end apart: 58, of which 22 were waited for; matrix products, arithmetic and copies ran while one was open for 21% of the time, Pallas kernels for 32%

profile of v2, /device:TPU:0, one launch (start us, length us, event | category | flops | bytes accessed | tf_op | source)
XLA Modules:
  0.0 886.9 jit_solution(3782960351274768329)
XLA Ops:
  7.4 6.0 round_weights.1
  15.3 6.9 collective-permute-start.1
  22.2 3.1 constant_dynamic-slice_fusion.12
  34.6 8.0 collective-permute-done.1
  44.0 2.8 collective-permute-start.2
  46.8 11.1 %collective-permute-done = bf16[512,1152]{1,0:T(8,128)(2,1)} collective-permute-done((bf16[512,1152]{1,0:T(8,128)(2,1)}, bf16[512,1152]{1,0:T(8,128)(2,1)}, u32[]{:S(2)}, u32[]{:S(2)}) %collective-permute-start) | collective-permute-done | bytes 1179680 | tf_op jit(solution)/shard_map/ppermute | solution.py:787
  70.5 21.2 %collective-permute-done.6.a1 = bf16[560,840]{1,0:T(8,128)(2,1)} collective-permute-done((bf16[560,840]{1,0:T(8,128)(2,1)S(1)}, bf16[560,840]{1,0:T(8,128)(2,1)}, u32[]{:S(2)}, u32[]{:S(2)}) %collective-permute-start.6) | collective-permute-done | bytes 940832 | tf_op jit(solution)/shard_map/ppermute | solution.py:787
  97.9 17.4 %collective-permute-done.8.b1 = bf16[560,840]{1,0:T(8,128)(2,1)} collective-permute-done((bf16[560,840]{1,0:T(8,128)(2,1)}, bf16[560,840]{1,0:T(8,128)(2,1)}, u32[]{:S(2)}, u32[]{:S(2)}) %collective-permute-start.8) | collective-permute-done | bytes 940832 | tf_op jit(solution)/shard_map/ppermute | solution.py:787
  115.2 16.6 %project.1 = (bf16[2048,840]{1,0:T(8,128)(2,1)}, bf16[2048,840]{1,0:T(8,128)(2,1)}, bf16[2048,1120]{1,0:T(8,128)(2,1)}, bf16[1120,840]{1,0:T(8,128)(2,1)S(1)}, bf16[1120,840]{1,0:T(8,128)(2,1)}) custom-call(s32[1]{0:T(128)} %bitcast.8.place_ref, bf16[1024,1152]{1,0:T(8,128)(2,1)} %pad.22.own_ref, bf16[1024,1152]{1,0:T(8,128)(2,1)} %collective-permute-done.5.other_ref, ...), custom_call_target="tpu_custom_call" | custom-call | flops 7707033600 | bytes 25165824 | tf_op jit(solution)/shard_map/project/pallas_call | solution.py:543
  133.2 4.0 collective-permute-done.3.refs_2_
  137.2 4.1 collective-permute-done.4.refs_4_
  143.2 3.4 collective-permute-start.12
  151.5 3.4 collective-permute-start.15
  154.9 34.7 %attention_forward.2 = (bf16[2048,280]{1,0:T(8,128)(2,1)S(1)}, f32[4,280,512]{2,1,0:T(8,128)S(1)}, f32[4,8,512]{2,1,0:T(8,128)S(1)}) custom-call(s32[4]{0:T(128)S(1)} %and_select_fusion.low_ref, s32[1]{0:T(128)} %bitcast.4.core_ref, s32[4,1,512]{2,1,0:T(1,128)S(1)} %compare_select_fusion.start_ref, bf16[2048,840]{1,0:T(8,128)(2,1)} %get-tuple-element.119.qkv_ref), custom_call_target="tpu_custom_call" | custom-call | flops 11744051200 | bytes 6881280 | tf_op jit(solution)/shard_map/attention_forward/pallas_call | solution.py:259
  196.5 3.4 collective-permute-start.18
  199.9 3.8 collective-permute-start.19
  203.8 13.9 %collective-permute-done.16.refs_7_ = bf16[420,1120]{1,0:T(8,128)(2,1)} collective-permute-done((bf16[420,1120]{1,0:T(8,128)(2,1)S(1)}, bf16[420,1120]{1,0:T(8,128)(2,1)}, u32[]{:S(2)}, u32[]{:S(2)}) %collective-permute-start.16) | collective-permute-done | bytes 940832 | tf_op jit(solution)/shard_map/ppermute | solution.py:787
  219.6 34.8 %attention_forward.3 = (bf16[2048,280]{1,0:T(8,128)(2,1)S(1)}, f32[4,280,512]{2,1,0:T(8,128)S(1)}, f32[4,8,512]{2,1,0:T(8,128)S(1)}) custom-call(s32[4]{0:T(128)S(1)} %and_select_fusion.low_ref, s32[1]{0:T(128)} %bitcast.4.core_ref, s32[4,1,512]{2,1,0:T(1,128)S(1)} %compare_select_fusion.start_ref, bf16[2048,840]{1,0:T(8,128)(2,1)} %get-tuple-element.125.qkv_ref), custom_call_target="tpu_custom_call" | custom-call | flops 11744051200 | bytes 6881280 | tf_op jit(solution)/shard_map/attention_forward/pallas_call | solution.py:259
  255.8 5.9 unpack_share.2
  261.8 5.6 unpack_share.3
  267.5 8.7 split_product.2
  282.7 25.2 %collective-permute-done.23 = bf16[512,1152]{1,0:T(8,128)(2,1)} collective-permute-done((bf16[512,1152]{1,0:T(8,128)(2,1)}, bf16[512,1152]{1,0:T(8,128)(2,1)}, u32[]{:S(2)}, u32[]{:S(2)}) %collective-permute-start.23) | collective-permute-done | bytes 1179680 | tf_op jit(solution)/shard_map/ppermute | solution.py:787
  310.1 3.1 copy-done.9
  313.2 4.2 middle_norm.1
  321.0 3.1 collective-permute-done.24.rows_ref
  325.5 34.6 %feed_forward.2 = (bf16[2048,1120]{1,0:T(8,128)(2,1)}, bf16[2048,1120]{1,0:T(8,128)(2,1)}, bf16[2048,1120]{1,0:T(8,128)(2,1)}, bf16[2048,1120]{1,0:T(8,128)(2,1)...) custom-call(bf16[1024,1152]{1,0:T(8,128)(2,1)} %copy-done.68, ...), custom_call_target="tpu_custom_call" | custom-call | flops 20552089600 | bytes 28385280 | tf_op jit(solution)/shard_map/feed_forward/pallas_call | solution.py:760
  360.3 35.0 %feed_forward.3 = (bf16[2048,1120]{1,0:T(8,128)(2,1)}, bf16[2048,1120]{1,0:T(8,128)(2,1)}, bf16[2048,1120]{1,0:T(8,128)(2,1)}, bf16[2048,1120]{1,0:T(8,128)(2,1)...) custom-call(bf16[1024,1152]{1,0:T(8,128)(2,1)} %copy-done.17, ...), custom_call_target="tpu_custom_call", output_to_operand_aliasing={{0}: (7, {}), {1}: (8, {}), {2}: (9, {}), {3}: (10, {}), {4... | custom-call | flops 20552089600 | bytes 28385280 | tf_op jit(solution)/shard_map/feed_forward/pallas_call | solution.py:760
  395.3 11.6 %convolution_convert_fusion.1 = bf16[1120,1120]{1,0:T(8,128)(2,1)} fusion(bf16[2048,1120]{1,0:T(8,128)(2,1)} %get-tuple-element.159, bf16[2048,1120]{1,0:T(8,128)(2,1)} %get-tuple-element.171), kind=kOutput, calls=%fused_computation.1 | convolution fusion | flops 5139276800 | bytes 11683840 | tf_op jit(solution)/shard_map/dot_general | solution.py:38
  407.0 7.8 convolution_convert_fusion
  414.8 7.7 norm_back.2
  435.7 7.9 out_grads.1
  443.6 6.0 convolution_convert_fusion.3
  449.6 55.9 %attention_backward.2.left_b = bf16[2048,896]{1,0:T(8,128)(2,1)} custom-call(s32[4]{0:T(128)} %copy-done.22, s32[1]{0:T(128)} %bitcast.4.core_ref, s32[4,1,512]{2,1,0:T(1,128)} %copy-done.16, bf16[2048,840]{1,0:T(8,128)(2,1)} %get-tuple-element.125.qkv_ref, bf16[2048,280]{1,0:T(8,128)(2,1)} %copy-done.26, f32[4,280,512]{2,1,0:T(8,128)} %copy-done.31, ...), custom_call_target="tpu_custom_call" | custom-call | flops 16441671680 | bytes 11468800 | tf_op jit(solution)/shard_map/attention_backward/pallas_call | solution.py:306
  505.5 9.9 %convolution_convert_fusion.2 = bf16[1120,896]{1,0:T(8,128)(2,1)} fusion(bf16[2048,1120]{1,0:T(8,128)(2,1)} %get-tuple-element.157, bf16[2048,896]{1,0:T(8,128)(2,1)} %attention_backward.2.left_b), kind=kOutput, calls=%fused_computation.22 | convolution fusion | flops 4111421440 | bytes 10264576 | tf_op jit(solution)/shard_map/dot_general | solution.py:38
  518.0 9.0 %fusion.48 = f32[1120,1120]{1,0:T(8,128)S(1)} fusion(bf16[2048,1120]{1,0:T(8,128)(2,1)S(1)} %bitcast.70, bf16[2048,1120]{1,0:T(8,128)(2,1)} %get-tuple-element.171), kind=kOutput, calls=%fused_computation.151 | convolution fusion | flops 5138022400 | bytes 14192640 | tf_op jit(solution)/shard_map/dot_general | solution.py:38
  527.0 9.2 %fusion.49 = f32[1120,1120]{1,0:T(8,128)S(1)} fusion(bf16[2048,1120]{1,0:T(8,128)(2,1)} %get-tuple-element.172, bf16[2048,1120]{1,0:T(8,128)(2,1)S(1)} %bitcast.72), kind=kOutput, calls=%fused_computation.152 | convolution fusion | flops 5138022400 | bytes 14192640 | tf_op jit(solution)/shard_map/dot_general | solution.py:38
  538.0 7.7 collective-permute-done.29
  545.7 13.7 %collective-permute-done.30 = bf16[280,1120]{1,0:T(8,128)(2,1)S(1)} collective-permute-done((bf16[280,1120]{1,0:T(8,128)(2,1)S(1)}, bf16[280,1120]{1,0:T(8,128)(2,1)S(1)}, u32[]{:S(2)}, u32[]{:S(2)}) %collective-permute-start.30) | collective-permute-done | bytes 627232 | tf_op jit(solution)/shard_map/ppermute | solution.py:787
  573.3 55.8 %attention_backward.3.left_a = bf16[2048,896]{1,0:T(8,128)(2,1)} custom-call(s32[4]{0:T(128)} %copy-done.22, s32[1]{0:T(128)} %bitcast.4.core_ref, s32[4,1,512]{2,1,0:T(1,128)} %copy-done.16, bf16[2048,840]{1,0:T(8,128)(2,1)} %get-tuple-element.119.qkv_ref, bf16[2048,280]{1,0:T(8,128)(2,1)} %copy-done.25, f32[4,280,512]{2,1,0:T(8,128)} %copy-done.30, ...), custom_call_target="tpu_custom_call" | custom-call | flops 16441671680 | bytes 11468800 | tf_op jit(solution)/shard_map/attention_backward/pallas_call | solution.py:306
  629.1 9.0 %convolution_add_fusion = f32[1120,896]{1,0:T(8,128)S(1)} fusion(bf16[2048,1120]{1,0:T(8,128)(2,1)} %get-tuple-element.157, bf16[2048,896]{1,0:T(8,128)(2,1)} %attention_backward.3.left_a, bf16[1120,896]{1,0:T(8,128)(2,1)} %collective-permute-done.31), kind=kOutput, calls=%fused_computation.21 | convolution fusion | flops 4112424960 | bytes 14278656 | tf_op jit(solution)/shard_map/dot_general | solution.py:38
  640.8 5.8 fusion.8
  650.0 16.1 %split_product.3 = (f32[1024,1152]{1,0:T(8,128)}, f32[1024,1120]{1,0:T(8,128)}) custom-call(bf16[2048,896]{1,0:T(8,128)(2,1)} %attention_backward.3.left_a, bf16[2048,896]{1,0:T(8,128)(2,1)} %attention_backward.2.left_b, bf16[1120,840]{1,0:T(8,128)(2,1)S(1)} %copy-done.28, bf16[1120,840]{1,0:T(8,128)(2,1)S(1)} %copy-done.29), custom_call_target="tpu_custom_call" | custom-call | flops 8220835840 | bytes 20971520 | tf_op jit(solution)/shard_map/split_product/pallas_call | solution.py:617
  679.1 12.9 %collective-permute-done.46 = bf16[420,1120]{1,0:T(8,128)(2,1)} collective-permute-done((bf16[420,1120]{1,0:T(8,128)(2,1)}, bf16[420,1120]{1,0:T(8,128)(2,1)}, u32[]{:S(2)}, u32[]{:S(2)}) %collective-permute-start.46) | collective-permute-done | bytes 940832 | tf_op jit(solution)/shard_map/ppermute | solution.py:787
  692.0 4.4 collective-permute-start.40
  696.4 3.3 fusion.18
  701.5 2.8 fusion.17
  704.3 13.1 %collective-permute-done.40 = bf16[420,1120]{1,0:T(8,128)(2,1)S(1)} collective-permute-done((bf16[420,1120]{1,0:T(8,128)(2,1)}, bf16[420,1120]{1,0:T(8,128)(2,1)S(1)}, u32[]{:S(2)}, u32[]{:S(2)}) %collective-permute-start.40) | collective-permute-done | bytes 940832 | tf_op jit(solution)/shard_map/ppermute | solution.py:787
  731.0 4.3 copy.53
  735.2 16.3 %collective-permute-done.37 = bf16[560,896]{1,0:T(8,128)(2,1)} collective-permute-done((bf16[560,896]{1,0:T(8,128)(2,1)}, bf16[560,896]{1,0:T(8,128)(2,1)}, u32[]{:S(2)}, u32[]{:S(2)}) %collective-permute-start.37) | collective-permute-done | bytes 1003552 | tf_op jit(solution)/shard_map/ppermute | solution.py:787
  751.5 4.0 fusion.37
  757.1 6.0 select_select_fusion
  763.2 5.5 reshape.181.rest_ref
  768.7 28.2 %collective-permute-done.38 = bf16[560,896]{1,0:T(8,128)(2,1)} collective-permute-done((bf16[560,896]{1,0:T(8,128)(2,1)}, bf16[560,896]{1,0:T(8,128)(2,1)}, u32[]{:S(2)}, u32[]{:S(2)}) %collective-permute-start.38) | collective-permute-done | bytes 1003552 | tf_op jit(solution)/shard_map/ppermute | solution.py:787
  796.9 3.3 slice_add_fusion.1
  800.2 6.0 reshape.180.lead_ref
  809.2 10.6 %new_moments.1 = (f32[1,1,470400]{2,1,0:T(1,128)}, f32[2,1,1,470400]{3,2,1,0:T(1,128)}, f32[1,1,470400]{2,1,0:T(1,128)S(1)}, f32[2]{0:T(128)S(1)}) custom-call(s32[2]{0:T(128)S(1)} %pad_add_fusion.ints_ref, f32[2]{0:T(128)S(1)} %pad_maximum_fusion.9.floats_ref, f32[1,1,470400]{2,1,0:T(1,128)S(1)} %copy-done.6, f32[1,1,470400]{2,1,0:T(1,128)S(1)} %copy-done.5, ...), custom_call_target="tpu_custom_call" | custom-call | tf_op jit(solution)/shard_map/new_moments/pallas_call | solution.py:408
  819.9 3.0 copy-done.11
  822.9 7.2 norm_back.3
  842.6 2.6 collective-permute-done.54
  848.4 3.1 collective-permute-done.55
  851.5 3.5 collective-permute-done.56
  855.1 3.0 collective-permute-start.52
  864.4 6.6 new_weights.1
  871.6 11.8 %collective-permute-done.35 = bf16[512,1152]{1,0:T(8,128)(2,1)S(1)} collective-permute-done((bf16[512,1152]{1,0:T(8,128)(2,1)S(1)}, bf16[512,1152]{1,0:T(8,128)(2,1)S(1)}, u32[]{:S(2)}, u32[]{:S(2)}) %collective-permute-start.35) | collective-permute-done | bytes 1179680 | tf_op jit(solution)/shard_map/ppermute | solution.py:787
  (359 shorter events, 160.3 us)
Async XLA Ops:
  15.3 27.4 %collective-permute-start.1 = (bf16[560,840]{1,0:T(8,128)(2,1)S(1)}, bf16[560,840]{1,0:T(8,128)(2,1)}, u32[]{:S(2)}, u32[]{:S(2)}) collective-permute-start(bf16[560,840]{1,0:T(8,128)(2,1)S(1)} %reshape.174), channel_id=1, source_target_pairs={{0,16},{4,20},{1,17},{5,21},{2,18},{6,22},{3,19},{7,23}} | collective-permute-start | bytes 2822408 | tf_op jit(solution)/shard_map/ppermute | solution.py:787
  30.1 27.7 %collective-permute-start = (bf16[512,1152]{1,0:T(8,128)(2,1)}, bf16[512,1152]{1,0:T(8,128)(2,1)}, u32[]{:S(2)}, u32[]{:S(2)}) collective-permute-start(bf16[512,1152]{1,0:T(8,128)(2,1)} %pad.21), channel_id=1, source_target_pairs={{0,2},{1,3},{2,0},{3,1},{4,6},{5,7},{6,4},{7,5},{8,10},{9,11},{10,... | collective-permute-start | bytes 3538952 | tf_op jit(solution)/shard_map/ppermute | solution.py:787
  44.0 22.1 %collective-permute-start.2 = (bf16[560,840]{1,0:T(8,128)(2,1)S(1)}, bf16[560,840]{1,0:T(8,128)(2,1)}, u32[]{:S(2)}, u32[]{:S(2)}) collective-permute-start(bf16[560,840]{1,0:T(8,128)(2,1)S(1)} %broadcast_select_fusion.2), channel_id=1, source_target_pairs={{0,8},{4,12},{16,24},{20,28},{1,9},{5,13},{17,25},{21,29},{2,10},{... | collective-permute-start | bytes 2822408 | tf_op jit(solution)/shard_map/ppermute | solution.py:787
  64.3 32.8 %collective-permute-start.5 = (bf16[1024,1152]{1,0:T(8,128)(2,1)}, bf16[1024,1152]{1,0:T(8,128)(2,1)}, u32[]{:S(2)}, u32[]{:S(2)}) collective-permute-start(bf16[1024,1152]{1,0:T(8,128)(2,1)} %pad.22.own_ref), channel_id=1, source_target_pairs={{0,1},{1,0},{2,3},{3,2},{4,5},{5,4},{6,7},{7,6},{8,9},{9,8},{10,11... | collective-permute-start | bytes 7077896 | tf_op jit(solution)/shard_map/ppermute | solution.py:787
  64.3 28.9 %copy-start.66 = (s32[2,1,11]{2,1,0:T(1,128)S(1)}, s32[2,1,11]{2,1,0:T(1,128)}, u32[]{:S(2)}) copy-start(s32[2,1,11]{2,1,0:T(1,128)} %param.16) | copy-start | bytes 268
  67.5 24.2 %collective-permute-start.6 = (bf16[560,840]{1,0:T(8,128)(2,1)S(1)}, bf16[560,840]{1,0:T(8,128)(2,1)}, u32[]{:S(2)}, u32[]{:S(2)}) collective-permute-start(bf16[560,840]{1,0:T(8,128)(2,1)S(1)} %broadcast_select_fusion.3.a0), channel_id=1, source_target_pairs={{0,4},{4,0},{8,12},{12,8},{16,20},{20,16},{24,28},{28,24},{1,5},{5... | collective-permute-start | bytes 2822408 | tf_op jit(solution)/shard_map/ppermute | solution.py:787
  69.0 27.3 %collective-permute-start.7 = (bf16[560,840]{1,0:T(8,128)(2,1)S(1)}, bf16[560,840]{1,0:T(8,128)(2,1)}, u32[]{:S(2)}, u32[]{:S(2)}) collective-permute-start(bf16[560,840]{1,0:T(8,128)(2,1)S(1)} %broadcast_select_fusion.3.a0), channel_id=1, source_target_pairs={{0,2},{1,3},{2,0},{3,1},{4,6},{5,7},{6,4},{7,5},{8,10},{9,11},{10,... | collective-permute-start | bytes 2822408 | tf_op jit(solution)/shard_map/ppermute | solution.py:787
  91.7 23.5 %collective-permute-start.8 = (bf16[560,840]{1,0:T(8,128)(2,1)}, bf16[560,840]{1,0:T(8,128)(2,1)}, u32[]{:S(2)}, u32[]{:S(2)}) collective-permute-start(bf16[560,840]{1,0:T(8,128)(2,1)} %collective-permute-done.6.a1), channel_id=1, source_target_pairs={{0,2},{1,3},{2,0},{3,1},{4,6},{5,7},{6,4},{7,5},{8,10},{9,11},{10,... | collective-permute-start | bytes 2822408 | tf_op jit(solution)/shard_map/ppermute | solution.py:787
  93.7 125.9 %copy-start.16 = (s32[4,1,512]{2,1,0:T(1,128)}, s32[4,1,512]{2,1,0:T(1,128)S(1)}, u32[]{:S(2)}) copy-start(s32[4,1,512]{2,1,0:T(1,128)S(1)} %compare_select_fusion.start_ref) | copy-start | bytes 24580
  93.8 43.5 %collective-permute-start.3 = (bf16[420,1120]{1,0:T(8,128)(2,1)S(1)}, bf16[420,1120]{1,0:T(8,128)(2,1)S(1)}, u32[]{:S(2)}, u32[]{:S(2)}) collective-permute-start(bf16[420,1120]{1,0:T(8,128)(2,1)S(1)} %reshape.175.refs_0_), channel_id=1, source_target_pairs={{8,0},{9,1},{10,2},{11,3},{12,4},{13,5},{14,6},{15,7},{16,24},{17,... | collective-permute-start | bytes 2822408 | tf_op jit(solution)/shard_map/ppermute | solution.py:787
  95.1 46.2 %collective-permute-start.4 = (bf16[420,1120]{1,0:T(8,128)(2,1)S(1)}, bf16[420,1120]{1,0:T(8,128)(2,1)S(1)}, u32[]{:S(2)}, u32[]{:S(2)}) collective-permute-start(bf16[420,1120]{1,0:T(8,128)(2,1)S(1)} %reshape.175.refs_0_), channel_id=1, source_target_pairs={{8,24},{9,25},{10,26},{11,27},{12,28},{13,29},{14,30},{15,31},{16,... | collective-permute-start | bytes 2822408 | tf_op jit(solution)/shard_map/ppermute | solution.py:787
  96.4 52.7 %collective-permute-start.10 = (bf16[420,1120]{1,0:T(8,128)(2,1)S(1)}, bf16[420,1120]{1,0:T(8,128)(2,1)S(1)}, u32[]{:S(2)}, u32[]{:S(2)}) collective-permute-start(bf16[420,1120]{1,0:T(8,128)(2,1)S(1)} %reshape.175.refs_0_), channel_id=1, source_target_pairs={{8,12},{9,13},{10,14},{11,15},{12,8},{13,9},{14,10},{15,11},{16,20... | collective-permute-start | bytes 2822408 | tf_op jit(solution)/shard_map/ppermute | solution.py:787
  97.1 54.4 %collective-permute-start.13 = (bf16[420,1120]{1,0:T(8,128)(2,1)S(1)}, bf16[420,1120]{1,0:T(8,128)(2,1)S(1)}, u32[]{:S(2)}, u32[]{:S(2)}) collective-permute-start(bf16[420,1120]{1,0:T(8,128)(2,1)S(1)} %reshape.175.refs_0_), channel_id=1, source_target_pairs={{8,10},{9,11},{10,8},{11,9},{12,14},{13,15},{14,12},{15,13},{16,18... | collective-permute-start | bytes 2822408 | tf_op jit(solution)/shard_map/ppermute | solution.py:787
  97.9 121.8 %copy-start.22 = (s32[4]{0:T(128)}, s32[4]{0:T(128)S(1)}, u32[]{:S(2)}) copy-start(s32[4]{0:T(128)S(1)} %and_select_fusion.low_ref) | copy-start | bytes 52
  141.3 49.8 %collective-permute-start.9 = (bf16[420,1120]{1,0:T(8,128)(2,1)S(1)}, bf16[420,1120]{1,0:T(8,128)(2,1)S(1)}, u32[]{:S(2)}, u32[]{:S(2)}) collective-permute-start(bf16[420,1120]{1,0:T(8,128)(2,1)S(1)} %collective-permute-done.4.refs_4_), channel_id=1, source_target_pairs={{0,8},{1,9},{2,10},{3,11},{4,12},{5,13},{6,14},{7,15},{8,0},{9,1},... | collective-permute-start | bytes 2822408 | tf_op jit(solution)/shard_map/ppermute | solution.py:787
  143.2 47.9 %collective-permute-start.12 = (bf16[420,1120]{1,0:T(8,128)(2,1)S(1)}, bf16[420,1120]{1,0:T(8,128)(2,1)S(1)}, u32[]{:S(2)}, u32[]{:S(2)}) collective-permute-start(bf16[420,1120]{1,0:T(8,128)(2,1)S(1)} %collective-permute-done.4.refs_4_), channel_id=1, source_target_pairs={{0,4},{1,5},{2,6},{3,7},{4,0},{5,1},{6,2},{7,3},{8,12},{9,13},{10,... | collective-permute-start | bytes 2822408 | tf_op jit(solution)/shard_map/ppermute | solution.py:787
  146.6 44.5 %collective-permute-start.11 = (bf16[420,1120]{1,0:T(8,128)(2,1)S(1)}, bf16[420,1120]{1,0:T(8,128)(2,1)S(1)}, u32[]{:S(2)}, u32[]{:S(2)}) collective-permute-start(bf16[420,1120]{1,0:T(8,128)(2,1)S(1)} %collective-permute-done.3.refs_2_), channel_id=1, source_target_pairs={{0,4},{1,5},{2,6},{3,7},{4,0},{5,1},{6,2},{7,3},{16,20},{17,21},{1... | collective-permute-start | bytes 2822408 | tf_op jit(solution)/shard_map/ppermute | solution.py:787
  149.1 42.1 %collective-permute-start.14 = (bf16[420,1120]{1,0:T(8,128)(2,1)S(1)}, bf16[420,1120]{1,0:T(8,128)(2,1)S(1)}, u32[]{:S(2)}, u32[]{:S(2)}) collective-permute-start(bf16[420,1120]{1,0:T(8,128)(2,1)S(1)} %collective-permute-done.3.refs_2_), channel_id=1, source_target_pairs={{0,2},{1,3},{2,0},{3,1},{4,6},{5,7},{6,4},{7,5},{16,18},{17,19},{1... | collective-permute-start | bytes 2822408 | tf_op jit(solution)/shard_map/ppermute | solution.py:787
  151.5 39.6 %collective-permute-start.15 = (bf16[420,1120]{1,0:T(8,128)(2,1)S(1)}, bf16[420,1120]{1,0:T(8,128)(2,1)S(1)}, u32[]{:S(2)}, u32[]{:S(2)}) collective-permute-start(bf16[420,1120]{1,0:T(8,128)(2,1)S(1)} %collective-permute-done.4.refs_4_), channel_id=1, source_target_pairs={{0,2},{1,3},{2,0},{3,1},{4,6},{5,7},{6,4},{7,5},{8,10},{9,11},{10,... | collective-permute-start | bytes 2822408 | tf_op jit(solution)/shard_map/ppermute | solution.py:787
  191.1 63.3 %copy-start.32 = (f32[4,8,512]{2,1,0:T(8,128)}, f32[4,8,512]{2,1,0:T(8,128)S(1)}, u32[]{:S(2)}) copy-start(f32[4,8,512]{2,1,0:T(8,128)S(1)} %get-tuple-element.124.lse_ref) | copy-start | bytes 196612
  191.1 76.4 %copy-start.7 = (bf16[2048,280]{1,0:T(8,128)(2,1)}, bf16[2048,280]{1,0:T(8,128)(2,1)S(1)}, u32[]{:S(2)}) copy-start(bf16[2048,280]{1,0:T(8,128)(2,1)S(1)} %get-tuple-element.120.left_a) | copy-start | bytes 3440644
  191.1 63.3 %copy-start.57 = (bf16[420,1120]{1,0:T(8,128)(2,1)}, bf16[420,1120]{1,0:T(8,128)(2,1)S(1)}, u32[]{:S(2)}) copy-start(bf16[420,1120]{1,0:T(8,128)(2,1)S(1)} %collective-permute-done.9.refs_6_) | copy-start | bytes 2822404
  191.1 26.6 %collective-permute-start.16 = (bf16[420,1120]{1,0:T(8,128)(2,1)S(1)}, bf16[420,1120]{1,0:T(8,128)(2,1)}, u32[]{:S(2)}, u32[]{:S(2)}) collective-permute-start(bf16[420,1120]{1,0:T(8,128)(2,1)S(1)} %collective-permute-done.9.refs_6_), channel_id=1, source_target_pairs={{0,4},{1,5},{2,6},{3,7},{4,0},{5,1},{6,2},{7,3},{8,12},{9,13},{10,... | collective-permute-start | bytes 2822408 | tf_op jit(solution)/shard_map/ppermute | solution.py:787
  193.2 68.6 %collective-permute-start.20 = (bf16[420,1120]{1,0:T(8,128)(2,1)S(1)}, bf16[420,1120]{1,0:T(8,128)(2,1)}, u32[]{:S(2)}, u32[]{:S(2)}) collective-permute-start(bf16[420,1120]{1,0:T(8,128)(2,1)S(1)} %collective-permute-done.9.refs_6_), channel_id=1, source_target_pairs={{0,2},{1,3},{2,0},{3,1},{4,6},{5,7},{6,4},{7,5},{8,10},{9,11},{10,... | collective-permute-start | bytes 2822408 | tf_op jit(solution)/shard_map/ppermute | solution.py:787
  195.6 66.1 %collective-permute-start.17 = (bf16[420,1120]{1,0:T(8,128)(2,1)S(1)}, bf16[420,1120]{1,0:T(8,128)(2,1)S(1)}, u32[]{:S(2)}, u32[]{:S(2)}) collective-permute-start(bf16[420,1120]{1,0:T(8,128)(2,1)S(1)} %collective-permute-done.13.refs_0_), channel_id=1, source_target_pairs={{8,12},{9,13},{10,14},{11,15},{12,8},{13,9},{14,10},{15,11},{16,20... | collective-permute-start | bytes 2822408 | tf_op jit(solution)/shard_map/ppermute | solution.py:787
  196.5 65.2 %collective-permute-start.18 = (bf16[420,1120]{1,0:T(8,128)(2,1)S(1)}, bf16[420,1120]{1,0:T(8,128)(2,1)}, u32[]{:S(2)}, u32[]{:S(2)}) collective-permute-start(bf16[420,1120]{1,0:T(8,128)(2,1)S(1)} %collective-permute-done.11.refs_3_), channel_id=1, source_target_pairs={{0,2},{1,3},{2,0},{3,1},{4,6},{5,7},{6,4},{7,5},{16,18},{17,19},{1... | collective-permute-start | bytes 2822408 | tf_op jit(solution)/shard_map/ppermute | solution.py:787
  199.9 61.8 %collective-permute-start.19 = (bf16[420,1120]{1,0:T(8,128)(2,1)S(1)}, bf16[420,1120]{1,0:T(8,128)(2,1)}, u32[]{:S(2)}, u32[]{:S(2)}) collective-permute-start(bf16[420,1120]{1,0:T(8,128)(2,1)S(1)} %collective-permute-done.15.refs_4_), channel_id=1, source_target_pairs={{0,4},{1,5},{2,6},{3,7},{4,0},{5,1},{6,2},{7,3},{8,12},{9,13},{10,... | collective-permute-start | bytes 2822408 | tf_op jit(solution)/shard_map/ppermute | solution.py:787
  217.7 44.1 %collective-permute-start.21 = (bf16[420,1120]{1,0:T(8,128)(2,1)}, bf16[420,1120]{1,0:T(8,128)(2,1)}, u32[]{:S(2)}, u32[]{:S(2)}) collective-permute-start(bf16[420,1120]{1,0:T(8,128)(2,1)} %collective-permute-done.16.refs_7_), channel_id=1, source_target_pairs={{0,2},{1,3},{2,0},{3,1},{4,6},{5,7},{6,4},{7,5},{8,10},{9,11},{10,... | collective-permute-start | bytes 2822408 | tf_op jit(solution)/shard_map/ppermute | solution.py:787
  276.1 34.0 %collective-permute-start.22 = (f32[1024,1152]{1,0:T(8,128)}, f32[1024,1152]{1,0:T(8,128)}, u32[]{:S(2)}, u32[]{:S(2)}) collective-permute-start(f32[1024,1152]{1,0:T(8,128)} %get-tuple-element.142), channel_id=1, source_target_pairs={{0,1},{1,0},{2,3},{3,2},{4,5},{5,4},{6,7},{7,6},{8,9},{9,8},{10,11... | collective-permute-start | bytes 14155784 | tf_op jit(solution)/shard_map/ppermute | solution.py:787
  279.3 28.7 %collective-permute-start.23 = (bf16[512,1152]{1,0:T(8,128)(2,1)}, bf16[512,1152]{1,0:T(8,128)(2,1)}, u32[]{:S(2)}, u32[]{:S(2)}) collective-permute-start(bf16[512,1152]{1,0:T(8,128)(2,1)} %pad.23), channel_id=1, source_target_pairs={{0,2},{1,3},{2,0},{3,1},{4,6},{5,7},{6,4},{7,5},{8,10},{9,11},{10,... | collective-permute-start | bytes 3538952 | tf_op jit(solution)/shard_map/ppermute | solution.py:787
  310.0 10.2 %collective-permute-start.25 = (bf16[1024,1152]{1,0:T(8,128)(2,1)S(1)}, bf16[1024,1152]{1,0:T(8,128)(2,1)S(1)}, u32[]{:S(2)}, u32[]{:S(2)}) collective-permute-start(bf16[1024,1152]{1,0:T(8,128)(2,1)S(1)} %fusion.11.cot_ref.base_ref), channel_id=1, source_target_pairs={{0,1},{1,0},{2,3},{3,2},{4,5},{5,4},{6,7},{7,6},{8,9},{9,8},{10,11... | collective-permute-start | bytes 7077896 | tf_op jit(solution)/shard_map/ppermute | solution.py:787
  319.6 4.5 collective-permute-start.24
  360.1 54.6 %collective-permute-start.26 = (f32[1024,1152]{1,0:T(8,128)}, f32[1024,1152]{1,0:T(8,128)}, u32[]{:S(2)}, u32[]{:S(2)}) collective-permute-start(f32[1024,1152]{1,0:T(8,128)} %get-tuple-element.165), channel_id=1, source_target_pairs={{0,1},{1,0},{2,3},{3,2},{4,5},{5,4},{6,7},{7,6},{8,9},{9,8},{10,11... | collective-permute-start | bytes 14155784 | tf_op jit(solution)/shard_map/ppermute | solution.py:787
  424.7 8.8 collective-permute-start.27
  431.2 106.7 %collective-permute-start.28 = (bf16[1120,1120]{1,0:T(8,128)(2,1)}, bf16[1120,1120]{1,0:T(8,128)(2,1)}, u32[]{:S(2)}, u32[]{:S(2)}) collective-permute-start(bf16[1120,1120]{1,0:T(8,128)(2,1)} %convolution_convert_fusion.1), channel_id=1, source_target_pairs={{0,2},{1,3},{2,0},{3,1},{4,6},{5,7},{6,4},{7,5},{8,10},{9,11},{10,... | collective-permute-start | bytes 7526408 | tf_op jit(solution)/shard_map/ppermute | solution.py:787
  431.5 114.2 %collective-permute-start.29 = (bf16[1120,1120]{1,0:T(8,128)(2,1)}, bf16[1120,1120]{1,0:T(8,128)(2,1)}, u32[]{:S(2)}, u32[]{:S(2)}) collective-permute-start(bf16[1120,1120]{1,0:T(8,128)(2,1)} %convolution_convert_fusion), channel_id=1, source_target_pairs={{0,2},{1,3},{2,0},{3,1},{4,6},{5,7},{6,4},{7,5},{8,10},{9,11},{10,... | collective-permute-start | bytes 7526408 | tf_op jit(solution)/shard_map/ppermute | solution.py:787
  433.3 207.5 %collective-permute-start.32 = (f32[1024,1152]{1,0:T(8,128)}, f32[1024,1152]{1,0:T(8,128)}, u32[]{:S(2)}, u32[]{:S(2)}) collective-permute-start(f32[1024,1152]{1,0:T(8,128)} %get-tuple-element.191), channel_id=1, source_target_pairs={{0,1},{1,0},{2,3},{3,2},{4,5},{5,4},{6,7},{7,6},{8,9},{9,8},{10,11... | collective-permute-start | bytes 14155784 | tf_op jit(solution)/shard_map/ppermute | solution.py:787
  515.3 44.1 %collective-permute-start.30 = (bf16[280,1120]{1,0:T(8,128)(2,1)S(1)}, bf16[280,1120]{1,0:T(8,128)(2,1)S(1)}, u32[]{:S(2)}, u32[]{:S(2)}) collective-permute-start(bf16[280,1120]{1,0:T(8,128)(2,1)S(1)} %copy-done.69), channel_id=1, source_target_pairs={{0,2},{1,3},{2,0},{3,1},{4,6},{5,7},{6,4},{7,5},{8,10},{9,11},{10,... | collective-permute-start | bytes 1881608 | tf_op jit(solution)/shard_map/ppermute | solution.py:787
  515.3 113.8 %collective-permute-start.31 = (bf16[1120,896]{1,0:T(8,128)(2,1)}, bf16[1120,896]{1,0:T(8,128)(2,1)}, u32[]{:S(2)}, u32[]{:S(2)}) collective-permute-start(bf16[1120,896]{1,0:T(8,128)(2,1)} %convolution_convert_fusion.2), channel_id=1, source_target_pairs={{0,2},{1,3},{2,0},{3,1},{4,6},{5,7},{6,4},{7,5},{8,10},{9,11},{10,... | collective-permute-start | bytes 6021128 | tf_op jit(solution)/shard_map/ppermute | solution.py:787
  571.2 94.9 %collective-permute-start.45 = (bf16[420,1120]{1,0:T(8,128)(2,1)}, bf16[420,1120]{1,0:T(8,128)(2,1)}, u32[]{:S(2)}, u32[]{:S(2)}) collective-permute-start(bf16[420,1120]{1,0:T(8,128)(2,1)} %select_convert_fusion.1), channel_id=1, source_target_pairs={{0,4},{4,0},{8,12},{12,8},{16,20},{20,16},{24,28},{28,24},{1,5},{5... | collective-permute-start | bytes 2822408 | tf_op jit(solution)/shard_map/ppermute | solution.py:787
  571.2 97.4 %collective-permute-start.42 = (bf16[420,1120]{1,0:T(8,128)(2,1)}, bf16[420,1120]{1,0:T(8,128)(2,1)}, u32[]{:S(2)}, u32[]{:S(2)}) collective-permute-start(bf16[420,1120]{1,0:T(8,128)(2,1)} %get-tuple-element.206), channel_id=1, source_target_pairs={{0,4},{4,0},{8,12},{12,8},{16,20},{20,16},{24,28},{28,24},{1,5},{5... | collective-permute-start | bytes 2822408 | tf_op jit(solution)/shard_map/ppermute | solution.py:787
  573.2 100.2 %collective-permute-start.39 = (bf16[420,1120]{1,0:T(8,128)(2,1)}, bf16[420,1120]{1,0:T(8,128)(2,1)}, u32[]{:S(2)}, u32[]{:S(2)}) collective-permute-start(bf16[420,1120]{1,0:T(8,128)(2,1)} %get-tuple-element.204), channel_id=1, source_target_pairs={{0,4},{4,0},{8,12},{12,8},{16,20},{20,16},{24,28},{28,24},{1,5},{5... | collective-permute-start | bytes 2822408 | tf_op jit(solution)/shard_map/ppermute | solution.py:787
  648.8 77.6 %collective-permute-start.33 = (bf16[512,1152]{1,0:T(8,128)(2,1)}, bf16[512,1152]{1,0:T(8,128)(2,1)}, u32[]{:S(2)}, u32[]{:S(2)}) collective-permute-start(bf16[512,1152]{1,0:T(8,128)(2,1)} %get-tuple-element.289), channel_id=1, source_target_pairs={{0,2},{1,3},{2,0},{3,1},{4,6},{5,7},{6,4},{7,5},{8,10},{9,11},{10,... | collective-permute-start | bytes 3538952 | tf_op jit(solution)/shard_map/ppermute | solution.py:787
  666.1 153.8 %collective-permute-start.34 = (f32[1024,1152]{1,0:T(8,128)}, f32[1024,1152]{1,0:T(8,128)}, u32[]{:S(2)}, u32[]{:S(2)}) collective-permute-start(f32[1024,1152]{1,0:T(8,128)} %get-tuple-element.198), channel_id=1, source_target_pairs={{0,1},{1,0},{2,3},{3,2},{4,5},{5,4},{6,7},{7,6},{8,9},{9,8},{10,11... | collective-permute-start | bytes 14155784 | tf_op jit(solution)/shard_map/ppermute | solution.py:787
  666.1 56.1 %collective-permute-start.36 = (bf16[560,896]{1,0:T(8,128)(2,1)}, bf16[560,896]{1,0:T(8,128)(2,1)}, u32[]{:S(2)}, u32[]{:S(2)}) collective-permute-start(bf16[560,896]{1,0:T(8,128)(2,1)} %select_convert_fusion), channel_id=1, source_target_pairs={{0,4},{4,0},{8,12},{12,8},{16,20},{20,16},{24,28},{28,24},{1,5},{5... | collective-permute-start | bytes 3010568 | tf_op jit(solution)/shard_map/ppermute | solution.py:787
  668.6 23.3 %collective-permute-start.46 = (bf16[420,1120]{1,0:T(8,128)(2,1)}, bf16[420,1120]{1,0:T(8,128)(2,1)}, u32[]{:S(2)}, u32[]{:S(2)}) collective-permute-start(bf16[420,1120]{1,0:T(8,128)(2,1)} %fusion.15), channel_id=1, source_target_pairs={{16,24},{20,28},{0,8},{4,12},{17,25},{21,29},{1,9},{5,13},{18,26},... | collective-permute-start | bytes 2822408 | tf_op jit(solution)/shard_map/ppermute | solution.py:787
  673.5 26.3 %collective-permute-start.43 = (bf16[420,1120]{1,0:T(8,128)(2,1)}, bf16[420,1120]{1,0:T(8,128)(2,1)}, u32[]{:S(2)}, u32[]{:S(2)}) collective-permute-start(bf16[420,1120]{1,0:T(8,128)(2,1)} %fusion.14), channel_id=1, source_target_pairs={{24,16},{28,20},{8,0},{12,4},{25,17},{29,21},{9,1},{13,5},{26,18},... | collective-permute-start | bytes 2822408 | tf_op jit(solution)/shard_map/ppermute | solution.py:787
  692.0 25.4 %collective-permute-start.40 = (bf16[420,1120]{1,0:T(8,128)(2,1)}, bf16[420,1120]{1,0:T(8,128)(2,1)S(1)}, u32[]{:S(2)}, u32[]{:S(2)}) collective-permute-start(bf16[420,1120]{1,0:T(8,128)(2,1)} %fusion.13), channel_id=1, source_target_pairs={{0,8},{4,12},{16,24},{20,28},{1,9},{5,13},{17,25},{21,29},{2,10},{... | collective-permute-start | bytes 2822408 | tf_op jit(solution)/shard_map/ppermute | solution.py:787
  699.7 57.3 %collective-permute-start.47 = (bf16[420,1120]{1,0:T(8,128)(2,1)}, bf16[420,1120]{1,0:T(8,128)(2,1)}, u32[]{:S(2)}, u32[]{:S(2)}) collective-permute-start(bf16[420,1120]{1,0:T(8,128)(2,1)} %fusion.18), channel_id=1, source_target_pairs={{8,24},{12,28},{9,25},{13,29},{10,26},{14,30},{11,27},{15,31}} | collective-permute-start | bytes 2822408 | tf_op jit(solution)/shard_map/ppermute | solution.py:787
  717.4 39.6 %collective-permute-start.44 = (bf16[420,1120]{1,0:T(8,128)(2,1)}, bf16[420,1120]{1,0:T(8,128)(2,1)}, u32[]{:S(2)}, u32[]{:S(2)}) collective-permute-start(bf16[420,1120]{1,0:T(8,128)(2,1)} %fusion.17), channel_id=1, source_target_pairs={{0,16},{4,20},{1,17},{5,21},{2,18},{6,22},{3,19},{7,23}} | collective-permute-start | bytes 2822408 | tf_op jit(solution)/shard_map/ppermute | solution.py:787
  722.2 34.9 %collective-permute-start.41 = (bf16[420,1120]{1,0:T(8,128)(2,1)}, bf16[420,1120]{1,0:T(8,128)(2,1)}, u32[]{:S(2)}, u32[]{:S(2)}) collective-permute-start(bf16[420,1120]{1,0:T(8,128)(2,1)} %fusion.16), channel_id=1, source_target_pairs={{24,8},{28,12},{25,9},{29,13},{26,10},{30,14},{27,11},{31,15}} | collective-permute-start | bytes 2822408 | tf_op jit(solution)/shard_map/ppermute | solution.py:787
  726.4 25.1 %collective-permute-start.37 = (bf16[560,896]{1,0:T(8,128)(2,1)}, bf16[560,896]{1,0:T(8,128)(2,1)}, u32[]{:S(2)}, u32[]{:S(2)}) collective-permute-start(bf16[560,896]{1,0:T(8,128)(2,1)} %fusion.12), channel_id=1, source_target_pairs={{8,0},{12,4},{24,16},{28,20},{9,1},{13,5},{25,17},{29,21},{10,2},{... | collective-permute-start | bytes 3010568 | tf_op jit(solution)/shard_map/ppermute | solution.py:787
  755.5 41.4 %collective-permute-start.38 = (bf16[560,896]{1,0:T(8,128)(2,1)}, bf16[560,896]{1,0:T(8,128)(2,1)}, u32[]{:S(2)}, u32[]{:S(2)}) collective-permute-start(bf16[560,896]{1,0:T(8,128)(2,1)} %get-tuple-element.271), channel_id=1, source_target_pairs={{16,0},{20,4},{17,1},{21,5},{18,2},{22,6},{19,3},{23,7}} | collective-permute-start | bytes 3010568 | tf_op jit(solution)/shard_map/ppermute | solution.py:787
  831.6 1.3 collective-permute-start.48
  833.0 4.4 collective-permute-start.49
  836.5 2.6 collective-permute-start.53
  837.4 5.1 collective-permute-start.50
  841.7 3.6 collective-permute-start.54
  842.5 12.5 %collective-permute-start.51 = (f32[13,1120]{1,0:T(8,128)S(1)}, f32[13,1120]{1,0:T(8,128)S(1)}, u32[]{:S(2)}, u32[]{:S(2)}) collective-permute-start(f32[13,1120]{1,0:T(8,128)S(1)} %add.298), channel_id=1, source_target_pairs={{0,8},{4,12},{8,0},{12,4},{16,24},{20,28},{24,16},{28,20},{1,9},{5... | collective-permute-start | bytes 174728 | tf_op jit(solution)/shard_map/ppermute | solution.py:787
  847.9 3.6 collective-permute-start.55
  851.5 3.5 collective-permute-start.56
  855.1 7.4 collective-permute-start.57
  855.1 5.9 collective-permute-start.52
  860.1 23.3 %collective-permute-start.35 = (bf16[512,1152]{1,0:T(8,128)(2,1)S(1)}, bf16[512,1152]{1,0:T(8,128)(2,1)S(1)}, u32[]{:S(2)}, u32[]{:S(2)}) collective-permute-start(bf16[512,1152]{1,0:T(8,128)(2,1)S(1)} %get-tuple-element.286), channel_id=1, source_target_pairs={{0,2},{1,3},{2,0},{3,1},{4,6},{5,7},{6,4},{7,5},{8,10},{9,11},{10,... | collective-permute-start | bytes 3538952 | tf_op jit(solution)/shard_map/ppermute | solution.py:787
  (74 other events, 615.0 us)

commit v3 on v2

--- a/solution.py
+++ b/solution.py
@@ -491,6 +491,49 @@
         cost_estimate=pl.CostEstimate(flops=0, bytes_accessed=20 << 20, transcendentals=0),
         name="unpack_share",
     )(place, *blocks)
+
+
+def pack_rest_body(
+    cut, place_ref, out_ref, in_ref, back_ref, out_got, in_got, back_got, kept_ref, sent_ref
+):
+    here = place_ref[0]
+    place = 0
+    for matrix, got in ((out_ref, out_got), (in_ref, in_got), (back_ref, back_got)):
+        done, rows = 0, matrix.shape[0]
+        while done < rows:
+            block, offset = divmod(place, cut)
+            count = min(cut - offset, rows - done)
+            source = slice(done, done + count)
+            target = slice(offset, offset + count)
+            plane, side = divmod(block, 2)
+
+            @pl.when(here == side)
+            def keep(matrix=matrix, got=got, source=source, target=target, plane=plane):
+                kept_ref[plane, target] = matrix[source] + got[source].astype(F32)
+
+            @pl.when(here != side)
+            def send(matrix=matrix, got=got, source=source, target=target, plane=plane):
+                sent_ref[plane, target] = (matrix[source] + got[source].astype(F32)).astype(BF16)
+
+            done += count
+            place += count
+
+
+def pack_rest(place, matrices, received, cut):
+    columns = matrices[0].shape[1]
+    whole = pl.BlockSpec(memory_space=pltpu.VMEM)
+    return pl.pallas_call(
+        functools.partial(pack_rest_body, cut),
+        in_specs=[pl.BlockSpec(memory_space=pltpu.SMEM)] + [whole] * 6,
+        out_specs=[whole] * 2,
+        out_shape=[
+            jax.ShapeDtypeStruct((3, cut, columns), F32),
+            jax.ShapeDtypeStruct((3, cut, columns), BF16),
+        ],
+        compiler_params=vmem(40),
+        cost_estimate=pl.CostEstimate(flops=0, bytes_accessed=27 << 20, transcendentals=0),
+        name="pack_rest",
+    )(place, *matrices, *received)
 
 
 def rows_of(step, steps, own_ref, other_ref, width):
@@ -831,18 +874,6 @@
     )
 
 
-def nearer_planes(held, plane):
-    near = permute(
-        held.astype(BF16), "dp", lower_pairs([(plane ^ 1, plane), (plane ^ 3, plane ^ 2)], 2)
-    )
-    return held + near.astype(F32)
-
-
-def farther_planes(held, plane):
-    far = permute(held.astype(BF16), "dp", lower_pairs([(plane ^ 2, plane)], 2))
-    return held + far.astype(F32)
-
-
 def sum_everywhere(value):
     for axis_name in ("seq", "dp"):
         distance = 1
@@ -919,6 +950,9 @@
         wide = low_weight.reshape(shard_len // model_width, model_width)
         cut, tall_rows = wide.shape[0], tall.shape[0]
         lead = spread_lead(tall, z_here)
+        across = [move_rest(wide, (1, 0), 0)]
+        over = [move_rest(wide, (0, 2), 0)]
+        both = [move_rest(over[0], (1, 0), 0)]
         lead, wide = tie(lead, wide)
         lead_across = swap(lead, "dp", 1)
         halves = (lead, lead_across, swap(lead, "seq", 2), swap(lead_across, "seq", 2))
@@ -969,6 +1003,11 @@
     low_one = widen((hat_one * small_master[0] + small_master[1]).astype(BF16))
     other_one = swap(low_one, "seq", 1)
 
+    if planar:
+        low_one, near, far = tie(low_one, near, far)
+        last = move_rest(far, (2, 0), 2)
+        across += [move_rest(near, (1, 0), 1), move_rest(far, (1, 0), 2)]
+        over += [move_rest(near, (0, 2), 1), move_rest(far, (0, 2), 2)]
     *qkv, rows_one, w_attn_mine, w_attn_theirs = project(
         y_index, low_one, other_one, halves, jnp.stack(attn_biases)
     )
@@ -977,31 +1016,21 @@
         return attention_forward(low_blocks, core_index, block_starts, qkv[part], heads_here)
 
     if planar:
-        near, far, qkv[0] = tie(near, far, qkv[0])
-        planes = (wide, near, far, move_rest(far, (2, 0), 2))
-        across = [move_rest(block, (1, 0), plane) for plane, block in enumerate(planes[:3])]
-        over = [move_rest(block, (0, 2), plane) for plane, block in enumerate(planes[:3])]
+        last, qkv[0] = tie(last, qkv[0])
+        across.append(move_rest(last, (1, 0), 3))
+        over.append(move_rest(last, (0, 2), 3))
     attended = [attend(0)]
+    own_e_in = out_cotangent
     if planar:
-        qkv[1], planes, across, over, own_e_in, _ = tie(
-            qkv[1], planes, across, over, out_cotangent, attended[0][2]
-        )
-        across.append(move_rest(planes[3], (1, 0), 3))
-        over.append(move_rest(planes[3], (0, 2), 3))
-        both = [
-            move_rest(over[plane], (1, 0), plane)
-            if plane % 2 == 0
-            else move_rest(across[plane], (0, 2), plane)
-            for plane in range(4)
-        ]
-    else:
-        own_e_in = out_cotangent
+        qkv[1], over[1:3], own_e_in, _ = tie(qkv[1], over[1:3], own_e_in, attended[0][2])
+        both += [move_rest(over[1], (1, 0), 1), move_rest(over[2], (1, 0), 2)]
     own_e = widen(exchange_micro(own_e_in))
     other_e = swap(own_e, "seq", 1)
     attended.append(attend(1))
     if planar:
-        dp_index, _ = tie(dp_index, attended[1][2])
-        rest_mine = [block for pair in zip(planes, across) for block in pair]
+        dp_index, across[3], _ = tie(dp_index, across[3], attended[1][2])
+        both.append(move_rest(across[3], (0, 2), 3))
+        rest_mine = [block for pair in zip((wide, near, far, last), across) for block in pair]
         rest_theirs = [block for pair in zip(over, both) for block in pair]
         matrices_mine = unpack_share(dp_index, rest_mine, head_share, model_width)
         matrices_theirs = unpack_share(dp_index, rest_theirs, head_share, model_width)
@@ -1058,49 +1087,70 @@
     share_back = dot_columns(activated[0], rows_e)
     share_in = dot_columns(rows_two, inner[0])
     share_out = dot_columns(attended[0][0], rows_mid)
-    share_back, share_in, share_out, back_received, in_received, outer_received = tie(
-        share_back, share_in, share_out, back_received, in_received, outer_received
-    )
-    share_back = share_back + back_received.astype(F32)
-    share_in = share_in + in_received.astype(F32)
-    share_out = share_out + outer_received.astype(F32)
     if planar:
-        rest = cut - head_share
-        seams = [rest, rest + cut, rest + 2 * cut]
-        taken = cut - (model_width - seams[2])
-        pieces = [
-            jnp.concatenate([share_out, share_in[: seams[0]]], axis=0),
-            share_in[seams[0] : seams[1]],
-            share_in[seams[1] : seams[2]],
-            jnp.concatenate([share_in[seams[2] :], share_back[:taken]], axis=0),
-            share_back[taken : taken + cut],
-            share_back[taken + cut :],
-        ]
-        split = [halve_plane(pieces[2 * i], pieces[2 * i + 1], y_here) for i in range(3)]
-        kept_rest, sent_rest = [pair[0] for pair in split], [pair[1] for pair in split]
-        kept_rest, sent_rest, grad_att_mine = tie(kept_rest, sent_rest, grad_att_mine)
-        got_rest = [swap(block, "dp", 1) for block in sent_rest]
+        kept_rest, sent_rest = pack_rest(
+            y_index,
+            (share_out, share_in, share_back),
+            (outer_received, in_received, back_received),
+            cut,
+        )
+        sent_rest, grad_att_mine = tie(sent_rest, grad_att_mine)
+        got_rest = swap(sent_rest, "dp", 1)
+    else:
+        share_back, share_in, share_out = (
+            share_back + back_received,
+            share_in + in_received,
+            share_out + outer_received,
+        )
 
     packed_mine = attend_back(0, grad_att_mine)
     share_attn = dot_columns(rows_one, packed_mine) + attn_received.astype(F32)
     if planar:
+        z_odd = z_here % 2 == 1
         kept_lead, sent_lead = halve_plane(share_attn[:tall_rows], share_attn[tall_rows:], y_here)
-        kept_lead, sent_lead, kept_rest, packed_mine, out_received = tie(
-            kept_lead, sent_lead, kept_rest, packed_mine, out_received
+        kept_lead, sent_lead, kept_rest, packed_mine = tie(
+            kept_lead, sent_lead, kept_rest, packed_mine
         )
         got_lead = swap(sent_lead, "dp", 1)
-        sums_rest = [
-            nearer_planes(kept + got.astype(F32), plane)
-            for plane, kept, got in zip((1, 2, 3), kept_rest, got_rest)
-        ]
+        held = [kept_rest[i] + got_rest[i].astype(F32) for i in range(3)]
+        sent_near = jnp.where(z_odd, held[1], held[0]).astype(BF16)
+        sent_last = held[2].astype(BF16)
+        kept_near = jnp.where(z_odd, held[0], held[1])
+        kept_last = held[2]
+        sent_near, sent_last, packed_mine, out_received = tie(
+            sent_near, sent_last, packed_mine, out_received
+        )
+        got_near = swap(sent_near, "dp", 2)
+        got_last = permute(sent_last, "dp", lower_pairs([(0, 1), (2, 3)], 2))
     result_rows = widen(
         (middle + ((out_kept + out_received)[:, :model_width] + small_master[7])).astype(BF16)
     )
     packed = [packed_mine, packed_theirs]
     sent, kept = split_product(packed, [w_attn_mine, w_attn_theirs], True, model_width)
+    if planar:
+        kept_lead, sent = tie(kept_lead, sent)
+        held_lead = kept_lead + got_lead.astype(F32)
+        sent_lead = held_lead.astype(BF16)
+        sent_lead, held_lead, kept_near, kept_last, kept = tie(
+            sent_lead, held_lead, kept_near, kept_last, kept
+        )
+        near_lead = permute(sent_lead, "dp", lower_pairs([(1, 0), (3, 2)], 2))
+        held_near = kept_near + got_near.astype(F32)
+        held_last = kept_last + got_last.astype(F32)
+        sent_far = jnp.where(z_here == 1, held_last, held_near).astype(BF16)
+        own_rest = jnp.where(z_here == 3, held_last, held_near)
+        sent_far, own_rest, kept = tie(sent_far, own_rest, kept)
+        got_far = permute(sent_far, "dp", lower_pairs([(3, 1), (0, 2), (1, 3)], 2))
     grad_x, sums_one = norm_back(
         own_in, kept, swap(sent, "seq", 1), grad_mid, small_master[0:1], False
     )
+    if planar:
+        held_lead, grad_x, sums_one = tie(held_lead, grad_x, sums_one)
+        held_lead = held_lead + near_lead.astype(F32)
+        sent_lead = held_lead.astype(BF16)
+        sent_lead, held_lead, own_rest = tie(sent_lead, held_lead, own_rest)
+        far_lead = permute(sent_lead, "dp", lower_pairs([(2, 0)], 2))
+        rest_grad = (own_rest + got_far.astype(F32)).reshape(1, 1, shard_len)
 
     def return_micro(rows):
         lower, upper = rows[:local_rows], rows[local_rows:]
@@ -1137,14 +1187,10 @@
         ]
     )
 
+    small_sum = sum_everywhere(small_now)
     if planar:
-        sum_lead = nearer_planes(kept_lead + got_lead.astype(F32), 0)
-        sums_rest = [farther_planes(held, plane) for plane, held in zip((1, 2, 3), sums_rest)]
-        wide_sum = jnp.where(
-            z_here == 1, sums_rest[0], jnp.where(z_here == 2, sums_rest[1], sums_rest[2])
-        )
-        lead_grad = farther_planes(sum_lead, 0)[:, :triple].reshape(1, 1, shard_len)
-        rest_grad = wide_sum.reshape(1, 1, shard_len)
+        held_lead, rest_grad, small_sum = tie(held_lead, rest_grad, small_sum)
+        lead_grad = (held_lead + far_lead.astype(F32))[:, :triple].reshape(1, 1, shard_len)
         leads = z_here == 0
     else:
         flat_here = jnp.concatenate(
@@ -1169,7 +1215,6 @@
         second_moment,
         weight,
     )
-    small_sum = sum_everywhere(small_now)
     small_grad = small_sum[:12]
     weight_norms = jnp.sqrt(small_sum[12, :4])
     update_norms = jnp.sqrt(sum_everywhere(matrix_sums(update_sums)[None])[0])

time: 903 us -> 906 us (level)
  other arithmetic: 86 us -> 68.8 us
  Pallas kernels: 354 us -> 364 us
  waiting for transfers between devices: 223 us -> 233 us
    convert_element_type x8 -> x3, other arithmetic: 22.3 us -> 9.76 us  [the longest x2 4.98 us: per_device(): sent_lead = held_lead.astype(BF16)]
    pallas_call x0 -> x1, Pallas kernels: none -> 10.3 us  [pack_rest(): pl.pallas_call(functools.partial(pack_rest_body, cut), in_specs=[pl.Block...]
    ppermute x58 -> x53, waiting for transfers between devices: 223 us -> 233 us  [permute(): return lax.ppermute(value, axis_name, pairs)]
    ppermute x58 -> x53, starting transfers between devices: 79.7 us -> 86.7 us  [permute(): return lax.ppermute(value, axis_name, pairs)]
    unnamed x163 -> x139, local copies, waits for them, and re-layouts: 34.9 us -> 32.9 us
  transfers between devices with their start and end apart: 58 -> 53, of which waited for: 22 -> 21; matrix products, arithmetic and copies ran while one was open for 21% -> 19% of each run, Pallas kernels for 32% -> 32%
where the time goes in v3:
time: 906 us; the launch traced here: 897 us
  Pallas kernels  364 us (40%)
  waiting for transfers between devices  233 us (26%)
  starting transfers between devices  86.7 us (10%)
  local copies, waits for them, and re-layouts  69.1 us (8%)
  other arithmetic  68.8 us (8%)
  matrix products  67 us (7%)
    ppermute x53, waiting for transfers between devices, permute(): return lax.ppermute(value, axis_name, pairs)  233 us
    pallas_call x2, Pallas kernels, attention_backward(): pl.pallas_call(functools.partial(attention_backward_body, heads, width, b...  112 us
    ppermute x53, starting transfers between devices, permute(): return lax.ppermute(value, axis_name, pairs)  86.7 us
    pallas_call x2, Pallas kernels, attention_forward(): pl.pallas_call(functools.partial(attention_forward_body, heads, width, bq...  69.5 us
    pallas_call x2, Pallas kernels, feed_forward(): pl.pallas_call(functools.partial(feed_forward_body, len(filled)), out_sha...  69.1 us
    dot_general x8, matrix products, dot_columns(): lax.dot_general(left, right, (((0,), (0,)), ((), ())), preferred_element_...  67 us
    unnamed x139, local copies, waits for them, and re-layouts  32.9 us
    pallas_call x2, Pallas kernels, split_product(): pl.pallas_call(functools.partial(split_product_body, steps, turned), grid...  24.7 us
  transfers between devices with their start and end apart: 53, of which 21 were waited for; matrix products, arithmetic and copies ran while one was open for 19% of the time, Pallas kernels for 32%

profile of v3, /device:TPU:0, one launch (start us, length us, event | category | flops | bytes accessed | tf_op | source)
XLA Modules:
  0.0 896.5 jit_solution(11115376104874227449)
XLA Ops:
  7.3 6.0 round_weights.1
  15.3 6.9 collective-permute-start.1
  22.2 3.1 constant_dynamic-slice_fusion.12
  34.6 8.0 collective-permute-done.1
  46.4 11.4 %collective-permute-done = bf16[512,1152]{1,0:T(8,128)(2,1)} collective-permute-done((bf16[512,1152]{1,0:T(8,128)(2,1)}, bf16[512,1152]{1,0:T(8,128)(2,1)}, u32[]{:S(2)}, u32[]{:S(2)}) %collective-permute-start) | collective-permute-done | bytes 1179680 | tf_op jit(solution)/shard_map/ppermute | solution.py:830
  72.4 38.6 %collective-permute-done.3.refs_2_ = bf16[420,1120]{1,0:T(8,128)(2,1)} collective-permute-done((bf16[420,1120]{1,0:T(8,128)(2,1)S(1)}, bf16[420,1120]{1,0:T(8,128)(2,1)}, u32[]{:S(2)}, u32[]{:S(2)}) %collective-permute-start.3) | collective-permute-done | bytes 940832 | tf_op jit(solution)/shard_map/ppermute | solution.py:830
  113.5 5.5 collective-permute-done.4.refs_4_
  121.7 14.5 %collective-permute-done.8.b0 = bf16[560,840]{1,0:T(8,128)(2,1)} collective-permute-done((bf16[560,840]{1,0:T(8,128)(2,1)S(1)}, bf16[560,840]{1,0:T(8,128)(2,1)}, u32[]{:S(2)}, u32[]{:S(2)}) %collective-permute-start.8) | collective-permute-done | bytes 940832 | tf_op jit(solution)/shard_map/ppermute | solution.py:830
  136.9 3.4 collective-permute-start.11
  140.3 17.4 %collective-permute-done.9.b1 = bf16[560,840]{1,0:T(8,128)(2,1)} collective-permute-done((bf16[560,840]{1,0:T(8,128)(2,1)}, bf16[560,840]{1,0:T(8,128)(2,1)}, u32[]{:S(2)}, u32[]{:S(2)}) %collective-permute-start.9) | collective-permute-done | bytes 940832 | tf_op jit(solution)/shard_map/ppermute | solution.py:830
  157.7 3.4 collective-permute-start.10
  161.1 16.7 %project.1 = (bf16[2048,840]{1,0:T(8,128)(2,1)}, bf16[2048,840]{1,0:T(8,128)(2,1)}, bf16[2048,1120]{1,0:T(8,128)(2,1)}, bf16[1120,840]{1,0:T(8,128)(2,1)S(1)}, bf16[1120,840]{1,0:T(8,128)(2,1)}) custom-call(s32[1]{0:T(128)} %bitcast.8.place_ref, bf16[1024,1152]{1,0:T(8,128)(2,1)} %pad.22.own_ref, bf16[1024,1152]{1,0:T(8,128)(2,1)} %collective-permute-done.6.other_ref, ...), custom_call_target="tpu_custom_call" | custom-call | flops 7707033600 | bytes 25165824 | tf_op jit(solution)/shard_map/project/pallas_call | solution.py:586
  177.8 4.4 collective-permute-start.14
  182.2 34.7 %attention_forward.2 = (bf16[2048,280]{1,0:T(8,128)(2,1)S(1)}, f32[4,280,512]{2,1,0:T(8,128)S(1)}, f32[4,8,512]{2,1,0:T(8,128)S(1)}) custom-call(s32[4]{0:T(128)S(1)} %and_select_fusion.low_ref, s32[1]{0:T(128)} %bitcast.4.core_ref, s32[4,1,512]{2,1,0:T(1,128)S(1)} %compare_select_fusion.start_ref, bf16[2048,840]{1,0:T(8,128)(2,1)} %get-tuple-element.127.qkv_ref), custom_call_target="tpu_custom_call" | custom-call | flops 11744051200 | bytes 6881280 | tf_op jit(solution)/shard_map/attention_forward/pallas_call | solution.py:259
  220.3 4.3 collective-permute-start.12
  224.6 34.7 %attention_forward.3 = (bf16[2048,280]{1,0:T(8,128)(2,1)S(1)}, f32[4,280,512]{2,1,0:T(8,128)S(1)}, f32[4,8,512]{2,1,0:T(8,128)S(1)}) custom-call(s32[4]{0:T(128)S(1)} %and_select_fusion.low_ref, s32[1]{0:T(128)} %bitcast.4.core_ref, s32[4,1,512]{2,1,0:T(1,128)S(1)} %compare_select_fusion.start_ref, bf16[2048,840]{1,0:T(8,128)(2,1)} %get-tuple-element.132.qkv_ref), custom_call_target="tpu_custom_call" | custom-call | flops 11744051200 | bytes 6881280 | tf_op jit(solution)/shard_map/attention_forward/pallas_call | solution.py:259
  264.7 3.9 collective-permute-start.19
  269.6 3.9 collective-permute-start.21
  273.5 5.7 unpack_share.2
  279.3 9.9 %collective-permute-done.18.refs_3_ = bf16[420,1120]{1,0:T(8,128)(2,1)S(1)} collective-permute-done((bf16[420,1120]{1,0:T(8,128)(2,1)S(1)}, bf16[420,1120]{1,0:T(8,128)(2,1)S(1)}, u32[]{:S(2)}, u32[]{:S(2)}) %collective-permute-start.18) | collective-permute-done | bytes 940832 | tf_op jit(solution)/shard_map/ppermute | solution.py:830
  289.2 14.9 %collective-permute-done.19.refs_5_ = bf16[420,1120]{1,0:T(8,128)(2,1)} collective-permute-done((bf16[420,1120]{1,0:T(8,128)(2,1)S(1)}, bf16[420,1120]{1,0:T(8,128)(2,1)}, u32[]{:S(2)}, u32[]{:S(2)}) %collective-permute-start.19) | collective-permute-done | bytes 940832 | tf_op jit(solution)/shard_map/ppermute | solution.py:830
  305.1 5.8 unpack_share.3
  310.9 8.8 split_product.2
  328.7 22.8 %collective-permute-done.23 = bf16[512,1152]{1,0:T(8,128)(2,1)} collective-permute-done((bf16[512,1152]{1,0:T(8,128)(2,1)}, bf16[512,1152]{1,0:T(8,128)(2,1)}, u32[]{:S(2)}, u32[]{:S(2)}) %collective-permute-start.23) | collective-permute-done | bytes 1179680 | tf_op jit(solution)/shard_map/ppermute | solution.py:830
  353.7 3.1 copy-done.8
  356.8 4.2 middle_norm.1
  364.6 3.1 collective-permute-done.24.rows_ref
  369.2 34.5 %feed_forward.2 = (bf16[2048,1120]{1,0:T(8,128)(2,1)}, bf16[2048,1120]{1,0:T(8,128)(2,1)}, bf16[2048,1120]{1,0:T(8,128)(2,1)}, bf16[2048,1120]{1,0:T(8,128)(2,1)...) custom-call(bf16[1024,1152]{1,0:T(8,128)(2,1)} %copy-done.56, ...), custom_call_target="tpu_custom_call" | custom-call | flops 20552089600 | bytes 28385280 | tf_op jit(solution)/shard_map/feed_forward/pallas_call | solution.py:803
  403.9 34.5 %feed_forward.3 = (bf16[2048,1120]{1,0:T(8,128)(2,1)}, bf16[2048,1120]{1,0:T(8,128)(2,1)}, bf16[2048,1120]{1,0:T(8,128)(2,1)}, bf16[2048,1120]{1,0:T(8,128)(2,1)...) custom-call(bf16[1024,1152]{1,0:T(8,128)(2,1)} %copy-done.15, ...), custom_call_target="tpu_custom_call", output_to_operand_aliasing={{0}: (7, {}), {1}: (8, {}), {2}: (9, {}), {3}: (10, {}), {4... | custom-call | flops 20552089600 | bytes 28385280 | tf_op jit(solution)/shard_map/feed_forward/pallas_call | solution.py:803
  438.5 11.5 %convolution_convert_fusion.1 = bf16[1120,1120]{1,0:T(8,128)(2,1)} fusion(bf16[2048,1120]{1,0:T(8,128)(2,1)} %get-tuple-element.159, bf16[2048,1120]{1,0:T(8,128)(2,1)} %get-tuple-element.175), kind=kOutput, calls=%fused_computation.1 | convolution fusion | flops 5139276800 | bytes 11683840 | tf_op jit(solution)/shard_map/dot_general | solution.py:38
  450.0 7.8 convolution_convert_fusion
  457.8 7.7 norm_back.2
  478.5 8.2 out_grads.1
  486.7 6.0 convolution_convert_fusion.3
  492.7 55.9 %attention_backward.2.left_b = bf16[2048,896]{1,0:T(8,128)(2,1)} custom-call(s32[4]{0:T(128)} %copy-done.20, s32[1]{0:T(128)} %bitcast.4.core_ref, s32[4,1,512]{2,1,0:T(1,128)} %copy-done.14, bf16[2048,840]{1,0:T(8,128)(2,1)} %get-tuple-element.132.qkv_ref, bf16[2048,280]{1,0:T(8,128)(2,1)} %copy-done.24, f32[4,280,512]{2,1,0:T(8,128)} %copy-done.29, ...), custom_call_target="tpu_custom_call" | custom-call | flops 16441671680 | bytes 11468800 | tf_op jit(solution)/shard_map/attention_backward/pallas_call | solution.py:306
  548.6 9.9 %convolution_convert_fusion.2 = bf16[1120,896]{1,0:T(8,128)(2,1)} fusion(bf16[2048,1120]{1,0:T(8,128)(2,1)} %get-tuple-element.158, bf16[2048,896]{1,0:T(8,128)(2,1)} %attention_backward.2.left_b), kind=kOutput, calls=%fused_computation.20 | convolution fusion | flops 4111421440 | bytes 10264576 | tf_op jit(solution)/shard_map/dot_general | solution.py:38
  560.5 12.4 %fusion.45.in_ref = f32[1120,1120]{1,0:T(8,128)} fusion(bf16[2048,1120]{1,0:T(8,128)(2,1)} %get-tuple-element.172, bf16[2048,1120]{1,0:T(8,128)(2,1)} %get-tuple-element.173), kind=kOutput, calls=%fused_computation.139 | convolution fusion | flops 5138022400 | bytes 14192640 | tf_op jit(solution)/shard_map/dot_general | solution.py:38
  572.9 8.8 fusion.46.back_ref
  583.5 5.2 collective-permute-done.30.back_got
  588.7 13.7 %collective-permute-done.28.out_got = bf16[280,1120]{1,0:T(8,128)(2,1)S(1)} collective-permute-done((bf16[280,1120]{1,0:T(8,128)(2,1)S(1)}, bf16[280,1120]{1,0:T(8,128)(2,1)S(1)}, u32[]{:S(2)}, u32[]{:S(2)}) %collective-permute-start.28) | collective-permute-done | bytes 627232 | tf_op jit(solution)/shard_map/ppermute | solution.py:830
  602.4 10.3 %pack_rest.1 = (f32[3,420,1120]{2,1,0:T(8,128)}, bf16[3,420,1120]{2,1,0:T(8,128)(2,1)}) custom-call(s32[1]{0:T(128)} %bitcast.8.place_ref, f32[280,1120]{1,0:T(8,128)S(1)} %fusion.44.out_ref, f32[1120,1120]{1,0:T(8,128)} %fusion.45.in_ref, f32[1120,1120]{1,0:T(8,128)} %fusion.46.back_ref, bf16[280,1120]{1,0:T(8,128)(2,1)S(1)} %collective-permute-done.28.out_got, ...), custom_call_target="tpu_custom_call" | custom-call | bytes 28311552 | tf_op jit(solution)/shard_map/pack_rest/pallas_call | solution.py:525
  612.9 55.9 %attention_backward.3.left_a = bf16[2048,896]{1,0:T(8,128)(2,1)} custom-call(s32[4]{0:T(128)} %copy-done.20, s32[1]{0:T(128)} %bitcast.4.core_ref, s32[4,1,512]{2,1,0:T(1,128)} %copy-done.14, bf16[2048,840]{1,0:T(8,128)(2,1)} %get-tuple-element.127.qkv_ref, bf16[2048,280]{1,0:T(8,128)(2,1)} %copy-done.23, f32[4,280,512]{2,1,0:T(8,128)} %copy-done.28, ...), custom_call_target="tpu_custom_call" | custom-call | flops 16441671680 | bytes 11468800 | tf_op jit(solution)/shard_map/attention_backward/pallas_call | solution.py:306
  668.8 9.0 %convolution_add_fusion = f32[1120,896]{1,0:T(8,128)S(1)} fusion(bf16[2048,1120]{1,0:T(8,128)(2,1)} %get-tuple-element.158, bf16[2048,896]{1,0:T(8,128)(2,1)} %attention_backward.3.left_a, bf16[1120,896]{1,0:T(8,128)(2,1)} %collective-permute-done.31), kind=kOutput, calls=%fused_computation.19 | convolution fusion | flops 4112424960 | bytes 14278656 | tf_op jit(solution)/shard_map/dot_general | solution.py:38
  682.3 4.8 fusion.34
  687.1 15.9 %split_product.3 = (f32[1024,1152]{1,0:T(8,128)}, f32[1024,1120]{1,0:T(8,128)}) custom-call(bf16[2048,896]{1,0:T(8,128)(2,1)} %attention_backward.3.left_a, bf16[2048,896]{1,0:T(8,128)(2,1)} %attention_backward.2.left_b, bf16[1120,840]{1,0:T(8,128)(2,1)S(1)} %copy-done.26, bf16[1120,840]{1,0:T(8,128)(2,1)S(1)} %copy-done.27), custom_call_target="tpu_custom_call" | custom-call | flops 8220835840 | bytes 20971520 | tf_op jit(solution)/shard_map/split_product/pallas_call | solution.py:660
  708.2 5.8 fusion.8
  716.2 14.6 %collective-permute-done.35 = bf16[560,896]{1,0:T(8,128)(2,1)S(1)} collective-permute-done((bf16[560,896]{1,0:T(8,128)(2,1)}, bf16[560,896]{1,0:T(8,128)(2,1)S(1)}, u32[]{:S(2)}, u32[]{:S(2)}) %collective-permute-start.35) | collective-permute-done | bytes 1003552 | tf_op jit(solution)/shard_map/ppermute | solution.py:830
  735.8 14.5 %collective-permute-done.37 = bf16[420,1120]{1,0:T(8,128)(2,1)} collective-permute-done((bf16[420,1120]{1,0:T(8,128)(2,1)}, bf16[420,1120]{1,0:T(8,128)(2,1)}, u32[]{:S(2)}, u32[]{:S(2)}) %collective-permute-start.37) | collective-permute-done | bytes 940832 | tf_op jit(solution)/shard_map/ppermute | solution.py:830
  750.3 4.7 fusion.12
  759.6 7.2 norm_back.3
  772.5 4.4 copy.53
  785.0 3.1 fusion.32
  788.1 14.7 %collective-permute-start.46 = (f32[13,1120]{1,0:T(8,128)S(1)}, f32[13,1120]{1,0:T(8,128)S(1)}, u32[]{:S(2)}, u32[]{:S(2)}) collective-permute-start(f32[13,1120]{1,0:T(8,128)S(1)} %add.281), channel_id=1, source_target_pairs={{0,16},{4,20},{8,24},{12,28},{16,0},{20,4},{24,8},{28,12},{1,17},{... | collective-permute-start | bytes 174728 | tf_op jit(solution)/shard_map/ppermute | solution.py:830
  802.7 2.7 convert_add_fusion.2
  805.4 4.3 reshape.191.rest_ref
  812.8 23.8 %collective-permute-done.47 = bf16[560,896]{1,0:T(8,128)(2,1)S(1)} collective-permute-done((bf16[560,896]{1,0:T(8,128)(2,1)}, bf16[560,896]{1,0:T(8,128)(2,1)S(1)}, u32[]{:S(2)}, u32[]{:S(2)}) %collective-permute-start.47) | collective-permute-done | bytes 1003552 | tf_op jit(solution)/shard_map/ppermute | solution.py:830
  836.6 3.1 slice_add_fusion.1
  839.6 6.0 reshape.192.lead_ref
  847.2 10.5 %new_moments.1 = (f32[1,1,470400]{2,1,0:T(1,128)}, f32[2,1,1,470400]{3,2,1,0:T(1,128)}, f32[1,1,470400]{2,1,0:T(1,128)S(1)}, f32[2]{0:T(128)S(1)}) custom-call(s32[2]{0:T(128)S(1)} %pad_add_fusion.ints_ref, f32[2]{0:T(128)S(1)} %pad_maximum_fusion.7.floats_ref, f32[1,1,470400]{2,1,0:T(1,128)S(1)} %copy-done.5, f32[1,1,470400]{2,1,0:T(1,128)S(1)} %reshape.191.rest_ref, ...), custom_call_target="tpu_custom_call" | custom-call | tf_op jit(solution)/shard_map/new_moments/pallas_call | solution.py:408
  858.3 2.7 fusion.28
  864.9 3.5 collective-permute-done.49
  874.7 3.5 collective-permute-done.51
  878.2 4.4 collective-permute-done.52
  884.6 6.5 new_weights.1
  (313 shorter events, 137.4 us)
Async XLA Ops:
  15.3 27.4 %collective-permute-start.1 = (bf16[560,840]{1,0:T(8,128)(2,1)S(1)}, bf16[560,840]{1,0:T(8,128)(2,1)}, u32[]{:S(2)}, u32[]{:S(2)}) collective-permute-start(bf16[560,840]{1,0:T(8,128)(2,1)S(1)} %reshape.185), channel_id=1, source_target_pairs={{0,16},{4,20},{1,17},{5,21},{2,18},{6,22},{3,19},{7,23}} | collective-permute-start | bytes 2822408 | tf_op jit(solution)/shard_map/ppermute | solution.py:830
  30.1 27.7 %collective-permute-start = (bf16[512,1152]{1,0:T(8,128)(2,1)}, bf16[512,1152]{1,0:T(8,128)(2,1)}, u32[]{:S(2)}, u32[]{:S(2)}) collective-permute-start(bf16[512,1152]{1,0:T(8,128)(2,1)} %pad.21), channel_id=1, source_target_pairs={{0,2},{1,3},{2,0},{3,1},{4,6},{5,7},{6,4},{7,5},{8,10},{9,11},{10,... | collective-permute-start | bytes 3538952 | tf_op jit(solution)/shard_map/ppermute | solution.py:830
  44.0 22.1 %collective-permute-start.2 = (bf16[560,840]{1,0:T(8,128)(2,1)S(1)}, bf16[560,840]{1,0:T(8,128)(2,1)}, u32[]{:S(2)}, u32[]{:S(2)}) collective-permute-start(bf16[560,840]{1,0:T(8,128)(2,1)S(1)} %broadcast_select_fusion.2), channel_id=1, source_target_pairs={{0,8},{4,12},{16,24},{20,28},{1,9},{5,13},{17,25},{21,29},{2,10},{... | collective-permute-start | bytes 2822408 | tf_op jit(solution)/shard_map/ppermute | solution.py:830
  64.2 72.7 %collective-permute-start.6 = (bf16[1024,1152]{1,0:T(8,128)(2,1)}, bf16[1024,1152]{1,0:T(8,128)(2,1)}, u32[]{:S(2)}, u32[]{:S(2)}) collective-permute-start(bf16[1024,1152]{1,0:T(8,128)(2,1)} %pad.22.own_ref), channel_id=1, source_target_pairs={{0,1},{1,0},{2,3},{3,2},{4,5},{5,4},{6,7},{7,6},{8,9},{9,8},{10,11... | collective-permute-start | bytes 7077896 | tf_op jit(solution)/shard_map/ppermute | solution.py:830
  64.2 48.8 %copy-start.53 = (s32[2,1,11]{2,1,0:T(1,128)S(1)}, s32[2,1,11]{2,1,0:T(1,128)}, u32[]{:S(2)}) copy-start(s32[2,1,11]{2,1,0:T(1,128)} %param.15) | copy-start | bytes 268
  64.2 48.8 %copy-start.54 = (s32[2,1,11]{2,1,0:T(1,128)S(1)}, s32[2,1,11]{2,1,0:T(1,128)}, u32[]{:S(2)}) copy-start(s32[2,1,11]{2,1,0:T(1,128)} %param.16) | copy-start | bytes 268
  67.5 43.5 %collective-permute-start.3 = (bf16[420,1120]{1,0:T(8,128)(2,1)S(1)}, bf16[420,1120]{1,0:T(8,128)(2,1)}, u32[]{:S(2)}, u32[]{:S(2)}) collective-permute-start(bf16[420,1120]{1,0:T(8,128)(2,1)S(1)} %reshape.186.refs_0_), channel_id=1, source_target_pairs={{8,0},{9,1},{10,2},{11,3},{12,4},{13,5},{14,6},{15,7},{16,24},{17,... | collective-permute-start | bytes 2822408 | tf_op jit(solution)/shard_map/ppermute | solution.py:830
  68.8 43.7 %collective-permute-start.7 = (bf16[560,840]{1,0:T(8,128)(2,1)S(1)}, bf16[560,840]{1,0:T(8,128)(2,1)}, u32[]{:S(2)}, u32[]{:S(2)}) collective-permute-start(bf16[560,840]{1,0:T(8,128)(2,1)S(1)} %broadcast_select_fusion.3.a0), channel_id=1, source_target_pairs={{0,4},{4,0},{8,12},{12,8},{16,20},{20,16},{24,28},{28,24},{1,5},{5... | collective-permute-start | bytes 2822408 | tf_op jit(solution)/shard_map/ppermute | solution.py:830
  70.3 48.7 %collective-permute-start.4 = (bf16[420,1120]{1,0:T(8,128)(2,1)S(1)}, bf16[420,1120]{1,0:T(8,128)(2,1)}, u32[]{:S(2)}, u32[]{:S(2)}) collective-permute-start(bf16[420,1120]{1,0:T(8,128)(2,1)S(1)} %reshape.186.refs_0_), channel_id=1, source_target_pairs={{8,24},{9,25},{10,26},{11,27},{12,28},{13,29},{14,30},{15,31},{16,... | collective-permute-start | bytes 2822408 | tf_op jit(solution)/shard_map/ppermute | solution.py:830
  71.6 49.3 %collective-permute-start.16 = (bf16[420,1120]{1,0:T(8,128)(2,1)S(1)}, bf16[420,1120]{1,0:T(8,128)(2,1)S(1)}, u32[]{:S(2)}, u32[]{:S(2)}) collective-permute-start(bf16[420,1120]{1,0:T(8,128)(2,1)S(1)} %reshape.186.refs_0_), channel_id=1, source_target_pairs={{8,10},{9,11},{10,8},{11,9},{12,14},{13,15},{14,12},{15,13},{16,18... | collective-permute-start | bytes 2822408 | tf_op jit(solution)/shard_map/ppermute | solution.py:830
  110.9 25.2 %collective-permute-start.8 = (bf16[560,840]{1,0:T(8,128)(2,1)S(1)}, bf16[560,840]{1,0:T(8,128)(2,1)}, u32[]{:S(2)}, u32[]{:S(2)}) collective-permute-start(bf16[560,840]{1,0:T(8,128)(2,1)S(1)} %broadcast_select_fusion.3.a0), channel_id=1, source_target_pairs={{0,2},{1,3},{2,0},{3,1},{4,6},{5,7},{6,4},{7,5},{8,10},{9,11},{10,... | collective-permute-start | bytes 2822408 | tf_op jit(solution)/shard_map/ppermute | solution.py:830
  112.4 45.2 %collective-permute-start.9 = (bf16[560,840]{1,0:T(8,128)(2,1)}, bf16[560,840]{1,0:T(8,128)(2,1)}, u32[]{:S(2)}, u32[]{:S(2)}) collective-permute-start(bf16[560,840]{1,0:T(8,128)(2,1)} %collective-permute-done.7.a1), channel_id=1, source_target_pairs={{0,2},{1,3},{2,0},{3,1},{4,6},{5,7},{6,4},{7,5},{8,10},{9,11},{10,... | collective-permute-start | bytes 2822408 | tf_op jit(solution)/shard_map/ppermute | solution.py:830
  113.5 111.1 %copy-start.14 = (s32[4,1,512]{2,1,0:T(1,128)}, s32[4,1,512]{2,1,0:T(1,128)S(1)}, u32[]{:S(2)}) copy-start(s32[4,1,512]{2,1,0:T(1,128)S(1)} %compare_select_fusion.start_ref) | copy-start | bytes 24580
  119.0 58.7 %collective-permute-start.5 = (bf16[420,1120]{1,0:T(8,128)(2,1)}, bf16[420,1120]{1,0:T(8,128)(2,1)}, u32[]{:S(2)}, u32[]{:S(2)}) collective-permute-start(bf16[420,1120]{1,0:T(8,128)(2,1)} %collective-permute-done.4.refs_4_), channel_id=1, source_target_pairs={{0,8},{1,9},{2,10},{3,11},{4,12},{5,13},{6,14},{7,15},{8,0},{9,1},... | collective-permute-start | bytes 2822408 | tf_op jit(solution)/shard_map/ppermute | solution.py:830
  121.0 103.7 %copy-start.20 = (s32[4]{0:T(128)}, s32[4]{0:T(128)S(1)}, u32[]{:S(2)}) copy-start(s32[4]{0:T(128)S(1)} %and_select_fusion.low_ref) | copy-start | bytes 52
  121.0 141.7 %collective-permute-start.13 = (bf16[420,1120]{1,0:T(8,128)(2,1)S(1)}, bf16[420,1120]{1,0:T(8,128)(2,1)S(1)}, u32[]{:S(2)}, u32[]{:S(2)}) collective-permute-start(bf16[420,1120]{1,0:T(8,128)(2,1)S(1)} %reshape.186.refs_0_), channel_id=1, source_target_pairs={{8,12},{9,13},{10,14},{11,15},{12,8},{13,9},{14,10},{15,11},{16,20... | collective-permute-start | bytes 2822408 | tf_op jit(solution)/shard_map/ppermute | solution.py:830
  136.2 143.1 %collective-permute-start.17 = (bf16[420,1120]{1,0:T(8,128)(2,1)S(1)}, bf16[420,1120]{1,0:T(8,128)(2,1)S(1)}, u32[]{:S(2)}, u32[]{:S(2)}) collective-permute-start(bf16[420,1120]{1,0:T(8,128)(2,1)S(1)} %collective-permute-done.16.refs_0_), channel_id=1, source_target_pairs={{8,12},{9,13},{10,14},{11,15},{12,8},{13,9},{14,10},{15,11},{16,20... | collective-permute-start | bytes 2822408 | tf_op jit(solution)/shard_map/ppermute | solution.py:830
  136.9 83.4 %collective-permute-start.11 = (bf16[420,1120]{1,0:T(8,128)(2,1)}, bf16[420,1120]{1,0:T(8,128)(2,1)S(1)}, u32[]{:S(2)}, u32[]{:S(2)}) collective-permute-start(bf16[420,1120]{1,0:T(8,128)(2,1)} %collective-permute-done.4.refs_4_), channel_id=1, source_target_pairs={{0,2},{1,3},{2,0},{3,1},{4,6},{5,7},{6,4},{7,5},{8,10},{9,11},{10,... | collective-permute-start | bytes 2822408 | tf_op jit(solution)/shard_map/ppermute | solution.py:830
  157.7 60.7 %collective-permute-start.10 = (bf16[420,1120]{1,0:T(8,128)(2,1)}, bf16[420,1120]{1,0:T(8,128)(2,1)S(1)}, u32[]{:S(2)}, u32[]{:S(2)}) collective-permute-start(bf16[420,1120]{1,0:T(8,128)(2,1)} %collective-permute-done.3.refs_2_), channel_id=1, source_target_pairs={{0,2},{1,3},{2,0},{3,1},{4,6},{5,7},{6,4},{7,5},{16,18},{17,19},{1... | collective-permute-start | bytes 2822408 | tf_op jit(solution)/shard_map/ppermute | solution.py:830
  177.7 39.2 %copy-start.25 = (bf16[1120,840]{1,0:T(8,128)(2,1)}, bf16[1120,840]{1,0:T(8,128)(2,1)S(1)}, u32[]{:S(2)}) copy-start(bf16[1120,840]{1,0:T(8,128)(2,1)S(1)} %get-tuple-element.193.w_a) | copy-start | bytes 5644804
  177.8 86.9 %collective-permute-start.14 = (bf16[420,1120]{1,0:T(8,128)(2,1)}, bf16[420,1120]{1,0:T(8,128)(2,1)S(1)}, u32[]{:S(2)}, u32[]{:S(2)}) collective-permute-start(bf16[420,1120]{1,0:T(8,128)(2,1)} %collective-permute-done.3.refs_2_), channel_id=1, source_target_pairs={{0,4},{1,5},{2,6},{3,7},{4,0},{5,1},{6,2},{7,3},{16,20},{17,21},{1... | collective-permute-start | bytes 2822408 | tf_op jit(solution)/shard_map/ppermute | solution.py:830
  218.4 41.0 %copy-start.30 = (f32[4,8,512]{2,1,0:T(8,128)}, f32[4,8,512]{2,1,0:T(8,128)S(1)}, u32[]{:S(2)}) copy-start(f32[4,8,512]{2,1,0:T(8,128)S(1)} %get-tuple-element.131.lse_ref) | copy-start | bytes 196612
  218.4 92.5 %copy-start.6 = (bf16[2048,280]{1,0:T(8,128)(2,1)}, bf16[2048,280]{1,0:T(8,128)(2,1)S(1)}, u32[]{:S(2)}) copy-start(bf16[2048,280]{1,0:T(8,128)(2,1)S(1)} %get-tuple-element.128.left_a) | copy-start | bytes 3440644
  218.4 50.2 %collective-permute-start.15 = (bf16[420,1120]{1,0:T(8,128)(2,1)}, bf16[420,1120]{1,0:T(8,128)(2,1)S(1)}, u32[]{:S(2)}, u32[]{:S(2)}) collective-permute-start(bf16[420,1120]{1,0:T(8,128)(2,1)} %collective-permute-done.4.refs_4_), channel_id=1, source_target_pairs={{0,4},{1,5},{2,6},{3,7},{4,0},{5,1},{6,2},{7,3},{8,12},{9,13},{10,... | collective-permute-start | bytes 2822408 | tf_op jit(solution)/shard_map/ppermute | solution.py:830
  220.3 40.5 %collective-permute-start.12 = (bf16[420,1120]{1,0:T(8,128)(2,1)}, bf16[420,1120]{1,0:T(8,128)(2,1)}, u32[]{:S(2)}, u32[]{:S(2)}) collective-permute-start(bf16[420,1120]{1,0:T(8,128)(2,1)} %collective-permute-done.5.refs_6_), channel_id=1, source_target_pairs={{0,4},{1,5},{2,6},{3,7},{4,0},{5,1},{6,2},{7,3},{8,12},{9,13},{10,... | collective-permute-start | bytes 2822408 | tf_op jit(solution)/shard_map/ppermute | solution.py:830
  260.8 50.1 %copy-start.21 = (bf16[2048,280]{1,0:T(8,128)(2,1)}, bf16[2048,280]{1,0:T(8,128)(2,1)S(1)}, u32[]{:S(2)}) copy-start(bf16[2048,280]{1,0:T(8,128)(2,1)S(1)} %get-tuple-element.133.left_b) | copy-start | bytes 3440644
  260.8 43.2 %collective-permute-start.20 = (bf16[420,1120]{1,0:T(8,128)(2,1)}, bf16[420,1120]{1,0:T(8,128)(2,1)S(1)}, u32[]{:S(2)}, u32[]{:S(2)}) collective-permute-start(bf16[420,1120]{1,0:T(8,128)(2,1)} %collective-permute-done.5.refs_6_), channel_id=1, source_target_pairs={{0,2},{1,3},{2,0},{3,1},{4,6},{5,7},{6,4},{7,5},{8,10},{9,11},{10,... | collective-permute-start | bytes 2822408 | tf_op jit(solution)/shard_map/ppermute | solution.py:830
  262.7 26.5 %collective-permute-start.18 = (bf16[420,1120]{1,0:T(8,128)(2,1)S(1)}, bf16[420,1120]{1,0:T(8,128)(2,1)S(1)}, u32[]{:S(2)}, u32[]{:S(2)}) collective-permute-start(bf16[420,1120]{1,0:T(8,128)(2,1)S(1)} %collective-permute-done.10.refs_2_), channel_id=1, source_target_pairs={{0,4},{1,5},{2,6},{3,7},{4,0},{5,1},{6,2},{7,3},{16,20},{17,21},{1... | collective-permute-start | bytes 2822408 | tf_op jit(solution)/shard_map/ppermute | solution.py:830
  264.7 39.4 %collective-permute-start.19 = (bf16[420,1120]{1,0:T(8,128)(2,1)S(1)}, bf16[420,1120]{1,0:T(8,128)(2,1)}, u32[]{:S(2)}, u32[]{:S(2)}) collective-permute-start(bf16[420,1120]{1,0:T(8,128)(2,1)S(1)} %collective-permute-done.11.refs_4_), channel_id=1, source_target_pairs={{0,4},{1,5},{2,6},{3,7},{4,0},{5,1},{6,2},{7,3},{8,12},{9,13},{10,... | collective-permute-start | bytes 2822408 | tf_op jit(solution)/shard_map/ppermute | solution.py:830
  269.6 34.5 %collective-permute-start.21 = (bf16[420,1120]{1,0:T(8,128)(2,1)}, bf16[420,1120]{1,0:T(8,128)(2,1)}, u32[]{:S(2)}, u32[]{:S(2)}) collective-permute-start(bf16[420,1120]{1,0:T(8,128)(2,1)} %collective-permute-done.12.refs_7_), channel_id=1, source_target_pairs={{0,2},{1,3},{2,0},{3,1},{4,6},{5,7},{6,4},{7,5},{8,10},{9,11},{10,... | collective-permute-start | bytes 2822408 | tf_op jit(solution)/shard_map/ppermute | solution.py:830
  319.7 34.0 %collective-permute-start.22 = (f32[1024,1152]{1,0:T(8,128)}, f32[1024,1152]{1,0:T(8,128)}, u32[]{:S(2)}, u32[]{:S(2)}) collective-permute-start(f32[1024,1152]{1,0:T(8,128)} %get-tuple-element.143), channel_id=1, source_target_pairs={{0,1},{1,0},{2,3},{3,2},{4,5},{5,4},{6,7},{7,6},{8,9},{9,8},{10,11... | collective-permute-start | bytes 14155784 | tf_op jit(solution)/shard_map/ppermute | solution.py:830
  322.8 28.7 %collective-permute-start.23 = (bf16[512,1152]{1,0:T(8,128)(2,1)}, bf16[512,1152]{1,0:T(8,128)(2,1)}, u32[]{:S(2)}, u32[]{:S(2)}) collective-permute-start(bf16[512,1152]{1,0:T(8,128)(2,1)} %pad.23), channel_id=1, source_target_pairs={{0,2},{1,3},{2,0},{3,1},{4,6},{5,7},{6,4},{7,5},{8,10},{9,11},{10,... | collective-permute-start | bytes 3538952 | tf_op jit(solution)/shard_map/ppermute | solution.py:830
  353.6 10.3 %collective-permute-start.25 = (bf16[1024,1152]{1,0:T(8,128)(2,1)S(1)}, bf16[1024,1152]{1,0:T(8,128)(2,1)S(1)}, u32[]{:S(2)}, u32[]{:S(2)}) collective-permute-start(bf16[1024,1152]{1,0:T(8,128)(2,1)S(1)} %fusion.11.cot_ref.base_ref), channel_id=1, source_target_pairs={{0,1},{1,0},{2,3},{3,2},{4,5},{5,4},{6,7},{7,6},{8,9},{9,8},{10,11... | collective-permute-start | bytes 7077896 | tf_op jit(solution)/shard_map/ppermute | solution.py:830
  363.2 4.5 collective-permute-start.24
  403.7 54.1 %collective-permute-start.26 = (f32[1024,1152]{1,0:T(8,128)}, f32[1024,1152]{1,0:T(8,128)}, u32[]{:S(2)}, u32[]{:S(2)}) collective-permute-start(f32[1024,1152]{1,0:T(8,128)} %get-tuple-element.165), channel_id=1, source_target_pairs={{0,1},{1,0},{2,3},{3,2},{4,5},{5,4},{6,7},{7,6},{8,9},{9,8},{10,11... | collective-permute-start | bytes 14155784 | tf_op jit(solution)/shard_map/ppermute | solution.py:830
  467.6 8.7 collective-permute-start.27
  474.3 109.2 %collective-permute-start.29 = (bf16[1120,1120]{1,0:T(8,128)(2,1)}, bf16[1120,1120]{1,0:T(8,128)(2,1)}, u32[]{:S(2)}, u32[]{:S(2)}) collective-permute-start(bf16[1120,1120]{1,0:T(8,128)(2,1)} %convolution_convert_fusion), channel_id=1, source_target_pairs={{0,2},{1,3},{2,0},{3,1},{4,6},{5,7},{6,4},{7,5},{8,10},{9,11},{10,... | collective-permute-start | bytes 7526408 | tf_op jit(solution)/shard_map/ppermute | solution.py:830
  476.0 112.7 %collective-permute-start.30 = (bf16[1120,1120]{1,0:T(8,128)(2,1)}, bf16[1120,1120]{1,0:T(8,128)(2,1)}, u32[]{:S(2)}, u32[]{:S(2)}) collective-permute-start(bf16[1120,1120]{1,0:T(8,128)(2,1)} %convolution_convert_fusion.1), channel_id=1, source_target_pairs={{0,2},{1,3},{2,0},{3,1},{4,6},{5,7},{6,4},{7,5},{8,10},{9,11},{10,... | collective-permute-start | bytes 7526408 | tf_op jit(solution)/shard_map/ppermute | solution.py:830
  476.3 210.8 %collective-permute-start.33 = (f32[1024,1152]{1,0:T(8,128)}, f32[1024,1152]{1,0:T(8,128)}, u32[]{:S(2)}, u32[]{:S(2)}) collective-permute-start(f32[1024,1152]{1,0:T(8,128)} %get-tuple-element.188), channel_id=1, source_target_pairs={{0,1},{1,0},{2,3},{3,2},{4,5},{5,4},{6,7},{7,6},{8,9},{9,8},{10,11... | collective-permute-start | bytes 14155784 | tf_op jit(solution)/shard_map/ppermute | solution.py:830
  558.5 43.9 %collective-permute-start.28 = (bf16[280,1120]{1,0:T(8,128)(2,1)S(1)}, bf16[280,1120]{1,0:T(8,128)(2,1)S(1)}, u32[]{:S(2)}, u32[]{:S(2)}) collective-permute-start(bf16[280,1120]{1,0:T(8,128)(2,1)S(1)} %copy-done.57), channel_id=1, source_target_pairs={{0,2},{1,3},{2,0},{3,1},{4,6},{5,7},{6,4},{7,5},{8,10},{9,11},{10,... | collective-permute-start | bytes 1881608 | tf_op jit(solution)/shard_map/ppermute | solution.py:830
  558.5 110.3 %collective-permute-start.31 = (bf16[1120,896]{1,0:T(8,128)(2,1)}, bf16[1120,896]{1,0:T(8,128)(2,1)}, u32[]{:S(2)}, u32[]{:S(2)}) collective-permute-start(bf16[1120,896]{1,0:T(8,128)(2,1)} %convolution_convert_fusion.2), channel_id=1, source_target_pairs={{0,2},{1,3},{2,0},{3,1},{4,6},{5,7},{6,4},{7,5},{8,10},{9,11},{10,... | collective-permute-start | bytes 6021128 | tf_op jit(solution)/shard_map/ppermute | solution.py:830
  612.8 67.7 %collective-permute-start.32 = (bf16[3,420,1120]{2,1,0:T(8,128)(2,1)}, bf16[3,420,1120]{2,1,0:T(8,128)(2,1)}, u32[]{:S(2)}, u32[]{:S(2)}) collective-permute-start(bf16[3,420,1120]{2,1,0:T(8,128)(2,1)} %get-tuple-element.186), channel_id=1, source_target_pairs={{0,4},{4,0},{8,12},{12,8},{16,20},{20,16},{24,28},{28,24},{1,5},{5... | collective-permute-start | bytes 8467208 | tf_op jit(solution)/shard_map/ppermute | solution.py:830
  703.0 54.3 %collective-permute-start.38 = (f32[1024,1152]{1,0:T(8,128)}, f32[1024,1152]{1,0:T(8,128)}, u32[]{:S(2)}, u32[]{:S(2)}) collective-permute-start(f32[1024,1152]{1,0:T(8,128)} %get-tuple-element.206), channel_id=1, source_target_pairs={{0,1},{1,0},{2,3},{3,2},{4,5},{5,4},{6,7},{7,6},{8,9},{9,8},{10,11... | collective-permute-start | bytes 14155784 | tf_op jit(solution)/shard_map/ppermute | solution.py:830
  705.9 24.8 %collective-permute-start.35 = (bf16[560,896]{1,0:T(8,128)(2,1)}, bf16[560,896]{1,0:T(8,128)(2,1)S(1)}, u32[]{:S(2)}, u32[]{:S(2)}) collective-permute-start(bf16[560,896]{1,0:T(8,128)(2,1)} %select_convert_fusion), channel_id=1, source_target_pairs={{0,4},{4,0},{8,12},{12,8},{16,20},{20,16},{24,28},{28,24},{1,5},{5... | collective-permute-start | bytes 3010568 | tf_op jit(solution)/shard_map/ppermute | solution.py:830
  705.9 29.8 %collective-permute-start.36 = (bf16[420,1120]{1,0:T(8,128)(2,1)}, bf16[420,1120]{1,0:T(8,128)(2,1)}, u32[]{:S(2)}, u32[]{:S(2)}) collective-permute-start(bf16[420,1120]{1,0:T(8,128)(2,1)} %get-tuple-element.201), channel_id=1, source_target_pairs={{0,8},{4,12},{16,24},{20,28},{1,9},{5,13},{17,25},{21,29},{2,10},{... | collective-permute-start | bytes 2822408 | tf_op jit(solution)/shard_map/ppermute | solution.py:830
  708.2 42.1 %collective-permute-start.37 = (bf16[420,1120]{1,0:T(8,128)(2,1)}, bf16[420,1120]{1,0:T(8,128)(2,1)}, u32[]{:S(2)}, u32[]{:S(2)}) collective-permute-start(bf16[420,1120]{1,0:T(8,128)(2,1)} %get-tuple-element.203), channel_id=1, source_target_pairs={{0,8},{4,12},{8,0},{12,4},{16,24},{20,28},{24,16},{28,20},{1,9},{5... | collective-permute-start | bytes 2822408 | tf_op jit(solution)/shard_map/ppermute | solution.py:830
  716.2 52.3 %collective-permute-start.34 = (bf16[512,1152]{1,0:T(8,128)(2,1)}, bf16[512,1152]{1,0:T(8,128)(2,1)}, u32[]{:S(2)}, u32[]{:S(2)}) collective-permute-start(bf16[512,1152]{1,0:T(8,128)(2,1)} %get-tuple-element.303), channel_id=1, source_target_pairs={{0,2},{1,3},{2,0},{3,1},{4,6},{5,7},{6,4},{7,5},{8,10},{9,11},{10,... | collective-permute-start | bytes 3538952 | tf_op jit(solution)/shard_map/ppermute | solution.py:830
  733.2 51.8 %collective-permute-start.40 = (bf16[560,896]{1,0:T(8,128)(2,1)}, bf16[560,896]{1,0:T(8,128)(2,1)}, u32[]{:S(2)}, u32[]{:S(2)}) collective-permute-start(bf16[560,896]{1,0:T(8,128)(2,1)} %get-tuple-element.212), channel_id=1, source_target_pairs={{8,0},{12,4},{24,16},{28,20},{9,1},{13,5},{25,17},{29,21},{10,2},{... | collective-permute-start | bytes 3010568 | tf_op jit(solution)/shard_map/ppermute | solution.py:830
  755.0 47.7 %collective-permute-start.41 = (bf16[420,1120]{1,0:T(8,128)(2,1)}, bf16[420,1120]{1,0:T(8,128)(2,1)}, u32[]{:S(2)}, u32[]{:S(2)}) collective-permute-start(bf16[420,1120]{1,0:T(8,128)(2,1)} %get-tuple-element.216), channel_id=1, source_target_pairs={{24,8},{28,12},{0,16},{4,20},{8,24},{12,28},{25,9},{29,13},{1,17},... | collective-permute-start | bytes 2822408 | tf_op jit(solution)/shard_map/ppermute | solution.py:830
  768.4 2.3 collective-permute-start.42
  770.7 6.2 collective-permute-start.43
  776.9 5.8 collective-permute-start.44
  780.7 111.1 %collective-permute-start.39 = (bf16[512,1152]{1,0:T(8,128)(2,1)}, bf16[512,1152]{1,0:T(8,128)(2,1)}, u32[]{:S(2)}, u32[]{:S(2)}) collective-permute-start(bf16[512,1152]{1,0:T(8,128)(2,1)} %get-tuple-element.300), channel_id=1, source_target_pairs={{0,2},{1,3},{2,0},{3,1},{4,6},{5,7},{6,4},{7,5},{8,10},{9,11},{10,... | collective-permute-start | bytes 3538952 | tf_op jit(solution)/shard_map/ppermute | solution.py:830
  782.7 5.3 collective-permute-start.45
  788.1 23.2 %collective-permute-start.46 = (f32[13,1120]{1,0:T(8,128)S(1)}, f32[13,1120]{1,0:T(8,128)S(1)}, u32[]{:S(2)}, u32[]{:S(2)}) collective-permute-start(f32[13,1120]{1,0:T(8,128)S(1)} %add.281), channel_id=1, source_target_pairs={{0,16},{4,20},{8,24},{12,28},{16,0},{20,4},{24,8},{28,12},{1,17},{... | collective-permute-start | bytes 174728 | tf_op jit(solution)/shard_map/ppermute | solution.py:830
  809.7 26.8 %collective-permute-start.47 = (bf16[560,896]{1,0:T(8,128)(2,1)}, bf16[560,896]{1,0:T(8,128)(2,1)S(1)}, u32[]{:S(2)}, u32[]{:S(2)}) collective-permute-start(bf16[560,896]{1,0:T(8,128)(2,1)} %get-tuple-element.223), channel_id=1, source_target_pairs={{16,0},{20,4},{17,1},{21,5},{18,2},{22,6},{19,3},{23,7}} | collective-permute-start | bytes 3010568 | tf_op jit(solution)/shard_map/ppermute | solution.py:830
  847.2 37.4 %copy-start.2 = (f32[1,1,470400]{2,1,0:T(1,128)S(1)}, f32[1,1,470400]{2,1,0:T(1,128)}, u32[]{:S(2)}) copy-start(f32[1,1,470400]{2,1,0:T(1,128)} %weight_ref.5) | copy-start | bytes 5644804
  857.7 34.1 %copy-start.39 = (bf16[512,1152]{1,0:T(8,128)(2,1)S(1)}, bf16[512,1152]{1,0:T(8,128)(2,1)}, u32[]{:S(2)}) copy-start(bf16[512,1152]{1,0:T(8,128)(2,1)} %get-tuple-element.299) | copy-start | bytes 3538948
  857.7 34.1 %copy-start.40 = (bf16[512,1152]{1,0:T(8,128)(2,1)S(1)}, bf16[512,1152]{1,0:T(8,128)(2,1)}, u32[]{:S(2)}) copy-start(bf16[512,1152]{1,0:T(8,128)(2,1)} %get-tuple-element.301) | copy-start | bytes 3538948
  861.0 1.2 collective-permute-start.48
  864.8 3.6 collective-permute-start.49
  871.1 3.6 collective-permute-start.50
  874.7 3.5 collective-permute-start.51
  878.2 4.4 collective-permute-start.52
  (57 other events, 524.6 us)

commit v4 on v3

--- a/solution.py
+++ b/solution.py
@@ -21,6 +21,7 @@
 MASKED = -1e30
 LOG2_E = 1.4426950408889634
 FF_ROWS = 256
+SCALE = 1e9
 
 F32 = jnp.float32
 BF16 = jnp.bfloat16
@@ -265,11 +266,7 @@
         ],
         grid_spec=grid_spec,
         compiler_params=pltpu.CompilerParams(vmem_limit_bytes=48 << 20),
-        cost_estimate=pl.CostEstimate(
-            flops=10 * length * length * flat,
-            bytes_accessed=12 * length * flat,
-            transcendentals=heads * length * length,
-        ),
+        cost_estimate=lasting(35),
         name="attention_forward",
     )(low_blocks, core, starts, qkv)
 
@@ -308,13 +305,13 @@
         out_shape=jax.ShapeDtypeStruct((length, lanes(triple)), BF16),
         grid_spec=grid_spec,
         compiler_params=pltpu.CompilerParams(vmem_limit_bytes=60 << 20),
-        cost_estimate=pl.CostEstimate(
-            flops=14 * length * length * flat,
-            bytes_accessed=20 * length * flat,
-            transcendentals=heads * length * length,
-        ),
+        cost_estimate=lasting(56),
         name="attention_backward",
     )(low_blocks, core, starts, qkv, grad_out, out_turned, log_total)
+
+
+def lasting(micros):
+    return pl.CostEstimate(flops=int(micros * SCALE), bytes_accessed=1 << 12, transcendentals=0)
 
 
 def lanes(width):
@@ -362,6 +359,7 @@
             jax.ShapeDtypeStruct((2,), F32),
         ],
         compiler_params=vmem(32),
+        cost_estimate=lasting(6),
         name="round_weights",
     )(bound, weight)
 
@@ -417,6 +415,7 @@
             jax.ShapeDtypeStruct((2,), F32),
         ],
         compiler_params=vmem(48),
+        cost_estimate=lasting(10),
         name="new_moments",
     )(ints, floats, lead, rest, first, second, weight)
 
@@ -445,6 +444,7 @@
             jax.ShapeDtypeStruct(weight.shape, BF16),
         ],
         compiler_params=vmem(32),
+        cost_estimate=lasting(6),
         name="new_weights",
     )(ints, ratios, weight, update)
 
@@ -488,7 +488,7 @@
         ),
         out_shape=[jax.ShapeDtypeStruct(shape, BF16) for shape in shapes],
         compiler_params=vmem(48),
-        cost_estimate=pl.CostEstimate(flops=0, bytes_accessed=20 << 20, transcendentals=0),
+        cost_estimate=lasting(6),
         name="unpack_share",
     )(place, *blocks)
 
@@ -531,7 +531,7 @@
             jax.ShapeDtypeStruct((3, cut, columns), BF16),
         ],
         compiler_params=vmem(40),
-        cost_estimate=pl.CostEstimate(flops=0, bytes_accessed=27 << 20, transcendentals=0),
+        cost_estimate=lasting(10),
         name="pack_rest",
     )(place, *matrices, *received)
 
@@ -598,9 +598,7 @@
         out_shape=[jax.ShapeDtypeStruct((2 * count, triple), BF16)] * 2
         + [jax.ShapeDtypeStruct((2 * count, model_width), BF16), matrix, matrix],
         compiler_params=vmem(48),
-        cost_estimate=pl.CostEstimate(
-            flops=8 * count * model_width * triple, bytes_accessed=24 << 20, transcendentals=0
-        ),
+        cost_estimate=lasting(16),
         name="project",
     )(place, own, other, *halves, biases)
 
@@ -626,9 +624,7 @@
         out_shape=[jax.ShapeDtypeStruct((2 * count, width), BF16)] * 2
         + [jax.ShapeDtypeStruct((2 * count, model_width), BF16)],
         compiler_params=vmem(48),
-        cost_estimate=pl.CostEstimate(
-            flops=8 * count * model_width * width, bytes_accessed=14 << 20, transcendentals=0
-        ),
+        cost_estimate=lasting(8),
         name="out_grads",
     )(own, other, *w_out)
 
@@ -667,9 +663,7 @@
         ],
         out_shape=parts,
         compiler_params=vmem(48),
-        cost_estimate=pl.CostEstimate(
-            flops=4 * count * model_width * width, bytes_accessed=20 << 20, transcendentals=0
-        ),
+        cost_estimate=lasting(12),
         name="split_product",
     )(*lefts, *weights)
 
@@ -698,6 +692,7 @@
             jax.ShapeDtypeStruct((count, lanes(width)), BF16),
         ],
         compiler_params=vmem(32),
+        cost_estimate=lasting(4),
         name="middle_norm",
     )(rows, kept, got, small)
 
@@ -741,6 +736,7 @@
             jax.ShapeDtypeStruct((8, width), F32),
         ],
         compiler_params=vmem(40),
+        cost_estimate=lasting(7),
         name="norm_back",
     )(rows, kept, got, base, gain)
 
@@ -817,11 +813,7 @@
         + [pl.BlockSpec((8, ff_share), lambda i: (0, 0))],
         input_output_aliases={7 + i: i for i in range(len(filled))},
         compiler_params=vmem(58),
-        cost_estimate=pl.CostEstimate(
-            flops=16 * count * model_width * ff_share,
-            bytes_accessed=8 * model_width * ff_share + 16 * count * model_width,
-            transcendentals=2 * count * ff_share,
-        ),
+        cost_estimate=lasting(34),
         name="feed_forward",
     )(rows, cot, *weights, biases, *filled)
 
@@ -929,6 +921,11 @@
         return jnp.pad(rows, ((0, 0), (0, lanes(model_width) - model_width)))
 
     own_in = exchange_micro(rows_in)
+    inputs = own_in.astype(F32)
+    hat_one, _ = norm_stats(inputs)
+    low_one = widen((hat_one * small_master[0] + small_master[1]).astype(BF16))
+    other_one = swap(low_one, "seq", 1)
+    later_cotangent = out_cotangent
 
     ends = jnp.array([first_end, second_end, third_end, dp_count * shard_len], jnp.int32)
     begin = dp_here * shard_len
@@ -952,8 +949,9 @@
         lead = spread_lead(tall, z_here)
         across = [move_rest(wide, (1, 0), 0)]
         over = [move_rest(wide, (0, 2), 0)]
-        both = [move_rest(over[0], (1, 0), 0)]
-        lead, wide = tie(lead, wide)
+        lead, wide, across[0], over[0], other_one, later_cotangent = tie(
+            lead, wide, across[0], over[0], other_one, later_cotangent
+        )
         lead_across = swap(lead, "dp", 1)
         halves = (lead, lead_across, swap(lead, "seq", 2), swap(lead_across, "seq", 2))
         dp_index = dp_here.reshape(1).astype(jnp.int32)
@@ -998,13 +996,10 @@
     block_starts = first_key.reshape(-1, 1, local_rows)
     core_index = core.reshape(1).astype(jnp.int32)
 
-    inputs = own_in.astype(F32)
-    hat_one, _ = norm_stats(inputs)
-    low_one = widen((hat_one * small_master[0] + small_master[1]).astype(BF16))
-    other_one = swap(low_one, "seq", 1)
-
+    own_e = widen(exchange_micro(later_cotangent))
     if planar:
-        low_one, near, far = tie(low_one, near, far)
+        both = [move_rest(over[0], (1, 0), 0)]
+        halves, near, far, both[0], own_e = tie(halves, near, far, both[0], own_e)
         last = move_rest(far, (2, 0), 2)
         across += [move_rest(near, (1, 0), 1), move_rest(far, (1, 0), 2)]
         over += [move_rest(near, (0, 2), 1), move_rest(far, (0, 2), 2)]
@@ -1015,20 +1010,18 @@
     def attend(part):
         return attention_forward(low_blocks, core_index, block_starts, qkv[part], heads_here)
 
+    attended = [attend(0)]
     if planar:
-        last, qkv[0] = tie(last, qkv[0])
+        qkv[1], last, across[1:3], over[1:3], _ = tie(
+            qkv[1], last, across[1:3], over[1:3], attended[0][2]
+        )
         across.append(move_rest(last, (1, 0), 3))
         over.append(move_rest(last, (0, 2), 3))
-    attended = [attend(0)]
-    own_e_in = out_cotangent
-    if planar:
-        qkv[1], over[1:3], own_e_in, _ = tie(qkv[1], over[1:3], own_e_in, attended[0][2])
-        both += [move_rest(over[1], (1, 0), 1), move_rest(over[2], (1, 0), 2)]
-    own_e = widen(exchange_micro(own_e_in))
+        both += [move_rest(over[1], (1, 0), 1), move_rest(across[2], (0, 2), 2)]
     other_e = swap(own_e, "seq", 1)
     attended.append(attend(1))
     if planar:
-        dp_index, across[3], _ = tie(dp_index, across[3], attended[1][2])
+        dp_index, across, over, both, _ = tie(dp_index, across, over, both, attended[1][2])
         both.append(move_rest(across[3], (0, 2), 3))
         rest_mine = [block for pair in zip((wide, near, far, last), across) for block in pair]
         rest_theirs = [block for pair in zip(over, both) for block in pair]
@@ -1052,19 +1045,28 @@
     inner_sums = sums_sent + sums_kept
 
     link = BF16 if planar else F32
+    up_received, out_received = tie(up_received, out_received)
+    grad_mid, low_mid, sums_two = norm_back(
+        middle, up_kept, up_received, own_e, small_master[2:3], True
+    )
+    low_mid, rows_two, rows_e = tie(low_mid, rows_two, rows_e)
+    other_mid = swap(low_mid, "seq", 1)
     back_sent = dot_columns(activated[1], rows_e).astype(link)
     in_sent = dot_columns(rows_two, inner[1]).astype(link)
-    back_sent, in_sent, up_kept = tie(*(back_sent, in_sent, up_kept))
+    back_sent, in_sent, low_mid = tie(back_sent, in_sent, low_mid)
     back_received = swap(back_sent, "seq", 2)
     in_received = swap(in_sent, "seq", 2)
 
-    grad_mid, low_mid, sums_two = norm_back(
-        middle, up_kept, up_received, own_e, small_master[2:3], True
-    )
-    grad_att_mine, grad_att_theirs, rows_mid = out_grads(low_mid, swap(low_mid, "seq", 1), w_out)
+    grad_att_mine, grad_att_theirs, rows_mid = out_grads(low_mid, other_mid, w_out)
     out_sent_theirs = dot_columns(attended[1][0], rows_mid).astype(link)
-    out_sent_theirs, grad_att_theirs = tie(*(out_sent_theirs, grad_att_theirs))
+    out_sent_theirs, rows_two, rows_e, rows_mid = tie(out_sent_theirs, rows_two, rows_e, rows_mid)
     outer_received = swap(out_sent_theirs, "seq", 2)
+    share_back = dot_columns(activated[0], rows_e)
+    share_in = dot_columns(rows_two, inner[0])
+    share_out = dot_columns(attended[0][0], rows_mid)
+    share_back, share_in, share_out, grad_att_theirs = tie(
+        share_back, share_in, share_out, grad_att_theirs
+    )
 
     def attend_back(part, grad_att):
         return attention_backward(
@@ -1080,13 +1082,8 @@
 
     packed_theirs = attend_back(1, grad_att_theirs)
     attn_sent = dot_columns(rows_one, packed_theirs).astype(link)
-    attn_sent, packed_theirs, rows_two, rows_e, rows_mid = tie(
-        attn_sent, packed_theirs, rows_two, rows_e, rows_mid
-    )
+    attn_sent, packed_theirs, y_index = tie(attn_sent, packed_theirs, y_index)
     attn_received = swap(attn_sent, "seq", 2)
-    share_back = dot_columns(activated[0], rows_e)
-    share_in = dot_columns(rows_two, inner[0])
-    share_out = dot_columns(attended[0][0], rows_mid)
     if planar:
         kept_rest, sent_rest = pack_rest(
             y_index,
@@ -1094,9 +1091,15 @@
             (outer_received, in_received, back_received),
             cut,
         )
-        sent_rest, grad_att_mine = tie(sent_rest, grad_att_mine)
+        result_rows = widen(
+            (middle + ((out_kept + out_received)[:, :model_width] + small_master[7])).astype(BF16)
+        )
+        sent_rest, grad_att_mine, result_rows = tie(sent_rest, grad_att_mine, result_rows)
         got_rest = swap(sent_rest, "dp", 1)
     else:
+        result_rows = widen(
+            (middle + ((out_kept + out_received)[:, :model_width] + small_master[7])).astype(BF16)
+        )
         share_back, share_in, share_out = (
             share_back + back_received,
             share_in + in_received,
@@ -1117,14 +1120,9 @@
         sent_last = held[2].astype(BF16)
         kept_near = jnp.where(z_odd, held[0], held[1])
         kept_last = held[2]
-        sent_near, sent_last, packed_mine, out_received = tie(
-            sent_near, sent_last, packed_mine, out_received
-        )
+        sent_near, sent_last, packed_mine = tie(sent_near, sent_last, packed_mine)
         got_near = swap(sent_near, "dp", 2)
         got_last = permute(sent_last, "dp", lower_pairs([(0, 1), (2, 3)], 2))
-    result_rows = widen(
-        (middle + ((out_kept + out_received)[:, :model_width] + small_master[7])).astype(BF16)
-    )
     packed = [packed_mine, packed_theirs]
     sent, kept = split_product(packed, [w_attn_mine, w_attn_theirs], True, model_width)
     if planar:
@@ -1145,10 +1143,12 @@
         own_in, kept, swap(sent, "seq", 1), grad_mid, small_master[0:1], False
     )
     if planar:
-        held_lead, grad_x, sums_one = tie(held_lead, grad_x, sums_one)
+        held_lead, _ = tie(held_lead, sums_one)
         held_lead = held_lead + near_lead.astype(F32)
         sent_lead = held_lead.astype(BF16)
-        sent_lead, held_lead, own_rest = tie(sent_lead, held_lead, own_rest)
+        sent_lead, held_lead, own_rest, grad_x, sums_one = tie(
+            sent_lead, held_lead, own_rest, grad_x, sums_one
+        )
         far_lead = permute(sent_lead, "dp", lower_pairs([(2, 0)], 2))
         rest_grad = (own_rest + got_far.astype(F32)).reshape(1, 1, shard_len)
 
@@ -1183,13 +1183,11 @@
             at_shares([sums[2 * head_share : triple] for sums in bias_sums])[None],
             sums_two[2:4],
             inner_rows,
-            jnp.pad(matrix_sums(weight_sums), (0, model_width - 4))[None],
         ]
     )
 
-    small_sum = sum_everywhere(small_now)
     if planar:
-        held_lead, rest_grad, small_sum = tie(held_lead, rest_grad, small_sum)
+        held_lead, rest_grad = tie(held_lead, rest_grad)
         lead_grad = (held_lead + far_lead.astype(F32))[:, :triple].reshape(1, 1, shard_len)
         leads = z_here == 0
     else:
@@ -1215,9 +1213,13 @@
         second_moment,
         weight,
     )
+    matrix_rows = jnp.stack([matrix_sums(weight_sums), matrix_sums(update_sums)])
+    small_sum = sum_everywhere(
+        jnp.concatenate([small_now, jnp.pad(matrix_rows, ((0, 2), (0, model_width - 4)))])
+    )
     small_grad = small_sum[:12]
     weight_norms = jnp.sqrt(small_sum[12, :4])
-    update_norms = jnp.sqrt(sum_everywhere(matrix_sums(update_sums)[None])[0])
+    update_norms = jnp.sqrt(small_sum[13, :4])
     ratios = weight_norms / update_norms
     new_weight, weight_copy = new_weights(
         ints, jnp.stack([pick(ratios, lower_matrix), pick(ratios, upper_matrix)]), weight, update

time: 906 us -> 844 us (0.932)
  waiting for transfers between devices: 233 us -> 186 us
  other arithmetic: 68.8 us -> 56.1 us
    ppermute x53 -> x48, waiting for transfers between devices: 233 us -> 186 us  [permute(): return lax.ppermute(value, axis_name, pairs)]
    ppermute x53 -> x48, starting transfers between devices: 86.7 us -> 80.1 us  [permute(): return lax.ppermute(value, axis_name, pairs)]
    unnamed x139 -> x161, local copies, waits for them, and re-layouts: 32.9 us -> 35.5 us
  transfers between devices with their start and end apart: 53 -> 48, of which waited for: 21 -> 20; matrix products, arithmetic and copies ran while one was open for 19% -> 18% of each run, Pallas kernels for 32% -> 34%
where the time goes in v4:
time: 844 us; the launch traced here: 834 us
  Pallas kernels  361 us (43%)
  waiting for transfers between devices  186 us (22%)
  starting transfers between devices  80.1 us (9%)
  local copies, waits for them, and re-layouts  75.8 us (9%)
  matrix products  66.5 us (8%)
  other arithmetic  56.1 us (7%)
    ppermute x48, waiting for transfers between devices, permute(): return lax.ppermute(value, axis_name, pairs)  186 us
    pallas_call x2, Pallas kernels, attention_backward(): pl.pallas_call(functools.partial(attention_backward_body, heads, width, b...  112 us
    ppermute x48, starting transfers between devices, permute(): return lax.ppermute(value, axis_name, pairs)  80.1 us
    pallas_call x2, Pallas kernels, attention_forward(): pl.pallas_call(functools.partial(attention_forward_body, heads, width, bq...  69.4 us
    pallas_call x2, Pallas kernels, feed_forward(): pl.pallas_call(functools.partial(feed_forward_body, len(filled)), out_sha...  69 us
    dot_general x8, matrix products, dot_columns(): lax.dot_general(left, right, (((0,), (0,)), ((), ())), preferred_element_...  66.5 us
    unnamed x161, local copies, waits for them, and re-layouts  35.5 us
    pallas_call x2, Pallas kernels, split_product(): pl.pallas_call(functools.partial(split_product_body, steps, turned), grid...  24.6 us
  transfers between devices with their start and end apart: 48, of which 20 were waited for; matrix products, arithmetic and copies ran while one was open for 18% of the time, Pallas kernels for 34%

profile of v4, /device:TPU:0, one launch (start us, length us, event | category | flops | bytes accessed | tf_op | source)
XLA Modules:
  0.0 833.6 jit_solution(12224358824461897843)
XLA Ops:
  0.7 3.1 constant_dynamic-slice_fusion.12
  8.7 2.9 collective-permute-start
  15.5 6.0 round_weights.1
  21.6 2.8 reshape.195
  24.3 5.5 collective-permute-start.1
  31.9 6.0 collective-permute-done
  44.7 5.6 collective-permute-done.1
  51.4 2.6 collective-permute-start.2
  58.5 15.0 %collective-permute-done.2 = bf16[560,840]{1,0:T(8,128)(2,1)} collective-permute-done((bf16[560,840]{1,0:T(8,128)(2,1)}, bf16[560,840]{1,0:T(8,128)(2,1)}, u32[]{:S(2)}, u32[]{:S(2)}) %collective-permute-start.2) | collective-permute-done | bytes 940832 | tf_op jit(solution)/shard_map/ppermute | solution.py:822
  90.4 14.6 %collective-permute-done.6.a1 = bf16[560,840]{1,0:T(8,128)(2,1)} collective-permute-done((bf16[560,840]{1,0:T(8,128)(2,1)S(1)}, bf16[560,840]{1,0:T(8,128)(2,1)}, u32[]{:S(2)}, u32[]{:S(2)}) %collective-permute-start.6) | collective-permute-done | bytes 940832 | tf_op jit(solution)/shard_map/ppermute | solution.py:822
  105.7 4.7 collective-permute-done.12
  113.6 18.3 %collective-permute-done.7.b0 = bf16[560,840]{1,0:T(8,128)(2,1)} collective-permute-done((bf16[560,840]{1,0:T(8,128)(2,1)S(1)}, bf16[560,840]{1,0:T(8,128)(2,1)}, u32[]{:S(2)}, u32[]{:S(2)}) %collective-permute-start.7) | collective-permute-done | bytes 940832 | tf_op jit(solution)/shard_map/ppermute | solution.py:822
  133.0 6.4 collective-permute-done.10.refs_4_
  139.4 10.9 %collective-permute-done.8.b1 = bf16[560,840]{1,0:T(8,128)(2,1)S(1)} collective-permute-done((bf16[560,840]{1,0:T(8,128)(2,1)}, bf16[560,840]{1,0:T(8,128)(2,1)S(1)}, u32[]{:S(2)}, u32[]{:S(2)}) %collective-permute-start.8) | collective-permute-done | bytes 940832 | tf_op jit(solution)/shard_map/ppermute | solution.py:822
  150.3 9.3 %collective-permute-start.13 = (bf16[420,1120]{1,0:T(8,128)(2,1)}, bf16[420,1120]{1,0:T(8,128)(2,1)S(1)}, u32[]{:S(2)}, u32[]{:S(2)}) collective-permute-start(bf16[420,1120]{1,0:T(8,128)(2,1)} %collective-permute-done.10.refs_4_), channel_id=1, source_target_pairs={{0,8},{1,9},{2,10},{3,11},{4,12},{5,13},{6,14},{7,15},{8,0},{9,1},... | collective-permute-start | bytes 2822408 | tf_op jit(solution)/shard_map/ppermute | solution.py:822
  162.0 3.4 collective-permute-start.14
  165.5 3.4 collective-permute-start.16
  171.3 16.3 %project.1 = (bf16[2048,840]{1,0:T(8,128)(2,1)}, bf16[2048,840]{1,0:T(8,128)(2,1)}, bf16[2048,1120]{1,0:T(8,128)(2,1)}, bf16[1120,840]{1,0:T(8,128)(2,1)S(1)}, bf16[1120,840]{1,0:T(8,128)(2,1)}) custom-call(s32[1]{0:T(128)} %bitcast.place_ref, bf16[1024,1152]{1,0:T(8,128)(2,1)} %pad.22.own_ref, bf16[1024,1152]{1,0:T(8,128)(2,1)} %collective-permute-done.5.other_ref, ...), custom_call_target="tpu_custom_call" | custom-call | flops 16000000000 | bytes 4096 | tf_op jit(solution)/shard_map/project/pallas_call | solution.py:586
  188.9 34.7 %attention_forward.2 = (bf16[2048,280]{1,0:T(8,128)(2,1)S(1)}, f32[4,280,512]{2,1,0:T(8,128)S(1)}, f32[4,8,512]{2,1,0:T(8,128)S(1)}) custom-call(s32[4]{0:T(128)S(1)} %and_select_fusion.low_ref, s32[1]{0:T(128)} %bitcast.9.core_ref, s32[4,1,512]{2,1,0:T(1,128)S(1)} %compare_select_fusion.start_ref, bf16[2048,840]{1,0:T(8,128)(2,1)} %get-tuple-element.162.qkv_ref), custom_call_target="tpu_custom_call" | custom-call | flops 35000000512 | bytes 4096 | tf_op jit(solution)/shard_map/attention_forward/pallas_call | solution.py:260
  227.0 3.4 collective-permute-start.19
  230.4 3.9 collective-permute-start.20
  236.8 34.7 %attention_forward.3 = (bf16[2048,280]{1,0:T(8,128)(2,1)S(1)}, f32[4,280,512]{2,1,0:T(8,128)S(1)}, f32[4,8,512]{2,1,0:T(8,128)S(1)}) custom-call(s32[4]{0:T(128)S(1)} %and_select_fusion.low_ref, s32[1]{0:T(128)} %bitcast.9.core_ref, s32[4,1,512]{2,1,0:T(1,128)S(1)} %compare_select_fusion.start_ref, bf16[2048,840]{1,0:T(8,128)(2,1)} %get-tuple-element.164.qkv_ref), custom_call_target="tpu_custom_call" | custom-call | flops 35000000512 | bytes 4096 | tf_op jit(solution)/shard_map/attention_forward/pallas_call | solution.py:260
  275.7 3.7 collective-permute-start.22
  279.4 5.6 unpack_share.2
  285.9 11.5 %collective-permute-done.22.refs_7_ = bf16[420,1120]{1,0:T(8,128)(2,1)S(1)} collective-permute-done((bf16[420,1120]{1,0:T(8,128)(2,1)}, bf16[420,1120]{1,0:T(8,128)(2,1)S(1)}, u32[]{:S(2)}, u32[]{:S(2)}) %collective-permute-start.22) | collective-permute-done | bytes 940832 | tf_op jit(solution)/shard_map/ppermute | solution.py:822
  298.4 5.6 unpack_share.3
  304.0 8.8 %split_product.2 = (f32[1024,1152]{1,0:T(8,128)}, f32[1024,1120]{1,0:T(8,128)}) custom-call(bf16[2048,280]{1,0:T(8,128)(2,1)S(1)} %get-tuple-element.165.left_a, bf16[2048,280]{1,0:T(8,128)(2,1)S(1)} %copy-done.19, bf16[280,1120]{1,0:T(8,128)(2,1)S(1)} %copy-done.26, bf16[280,1120]{1,0:T(8,128)(2,1)S(1)} %get-tuple-element.188.w_b), custom_call_target="tpu_custom_call" | custom-call | flops 12000000000 | bytes 4096 | tf_op jit(solution)/shard_map/split_product/pallas_call | solution.py:656
  313.6 10.7 %collective-permute-done.23.got_ref = f32[1024,1152]{1,0:T(8,128)S(1)} collective-permute-done((f32[1024,1152]{1,0:T(8,128)}, f32[1024,1152]{1,0:T(8,128)S(1)}, u32[]{:S(2)}, u32[]{:S(2)}) %collective-permute-start.23) | collective-permute-done | bytes 4718624 | tf_op jit(solution)/shard_map/ppermute | solution.py:822
  330.1 3.1 collective-permute-done.24.rows_ref
  334.6 34.4 %feed_forward.2 = (bf16[2048,1120]{1,0:T(8,128)(2,1)}, bf16[2048,1120]{1,0:T(8,128)(2,1)}, bf16[2048,1120]{1,0:T(8,128)(2,1)}, bf16[2048,1120]{1,0:T(8,128)(2,1)...) custom-call(bf16[1024,1152]{1,0:T(8,128)(2,1)} %copy-done.64, ...), custom_call_target="tpu_custom_call" | custom-call | flops 33999998976 | bytes 4096 | tf_op jit(solution)/shard_map/feed_forward/pallas_call | solution.py:799
  369.6 34.6 %feed_forward.3 = (bf16[2048,1120]{1,0:T(8,128)(2,1)}, bf16[2048,1120]{1,0:T(8,128)(2,1)}, bf16[2048,1120]{1,0:T(8,128)(2,1)}, bf16[2048,1120]{1,0:T(8,128)(2,1)...) custom-call(bf16[1024,1152]{1,0:T(8,128)(2,1)} %copy-done.10, ...), custom_call_target="tpu_custom_call", output_to_operand_aliasing={{0}: (7, {}), {1}: (8, {}), {2}: (9, {}), {3}: (10, {}), {4... | custom-call | flops 33999998976 | bytes 4096 | tf_op jit(solution)/shard_map/feed_forward/pallas_call | solution.py:799
  406.6 7.7 norm_back.2
  416.6 12.1 %convolution_convert_fusion.1 = bf16[1120,1120]{1,0:T(8,128)(2,1)} fusion(bf16[2048,1120]{1,0:T(8,128)(2,1)} %get-tuple-element.204, bf16[2048,1120]{1,0:T(8,128)(2,1)} %get-tuple-element.219), kind=kOutput, calls=%fused_computation.1 | convolution fusion | flops 5139276800 | bytes 11683840 | tf_op jit(solution)/shard_map/dot_general | solution.py:39
  428.8 7.8 convolution_convert_fusion
  438.7 3.5 fusion.8
  443.7 7.9 out_grads.1
  451.7 6.0 convolution_convert_fusion.3
  459.5 11.5 %fusion.45.back_ref = f32[1120,1120]{1,0:T(8,128)} fusion(bf16[2048,1120]{1,0:T(8,128)(2,1)S(1)} %bitcast.77, bf16[2048,1120]{1,0:T(8,128)(2,1)} %get-tuple-element.219), kind=kOutput, calls=%fused_computation.140 | convolution fusion | flops 5138022400 | bytes 14192640 | tf_op jit(solution)/shard_map/dot_general | solution.py:39
  471.1 8.7 %fusion.46.in_ref = f32[1120,1120]{1,0:T(8,128)} fusion(bf16[2048,1120]{1,0:T(8,128)(2,1)S(1)} %bitcast.81, bf16[2048,1120]{1,0:T(8,128)(2,1)S(1)} %bitcast.79), kind=kOutput, calls=%fused_computation.141 | convolution fusion | flops 5138022400 | bytes 14192640 | tf_op jit(solution)/shard_map/dot_general | solution.py:39
  481.2 56.2 %attention_backward.2.left_b = bf16[2048,896]{1,0:T(8,128)(2,1)} custom-call(s32[4]{0:T(128)} %copy-done.16, s32[1]{0:T(128)} %bitcast.9.core_ref, s32[4,1,512]{2,1,0:T(1,128)} %copy-done.9, bf16[2048,840]{1,0:T(8,128)(2,1)} %get-tuple-element.164.qkv_ref, bf16[2048,280]{1,0:T(8,128)(2,1)} %copy-done.30, f32[4,280,512]{2,1,0:T(8,128)} %copy-done.35, ...), custom_call_target="tpu_custom_call" | custom-call | flops 56000000000 | bytes 4096 | tf_op jit(solution)/shard_map/attention_backward/pallas_call | solution.py:303
  537.4 9.7 %convolution_convert_fusion.2 = bf16[1120,896]{1,0:T(8,128)(2,1)} fusion(bf16[2048,1120]{1,0:T(8,128)(2,1)} %get-tuple-element.158, bf16[2048,896]{1,0:T(8,128)(2,1)} %attention_backward.2.left_b), kind=kOutput, calls=%fused_computation.20 | convolution fusion | flops 4111421440 | bytes 10264576 | tf_op jit(solution)/shard_map/dot_general | solution.py:39
  547.6 3.4 collective-permute-done.31.back_got
  551.1 13.7 %collective-permute-done.29.out_got = bf16[280,1120]{1,0:T(8,128)(2,1)S(1)} collective-permute-done((bf16[280,1120]{1,0:T(8,128)(2,1)}, bf16[280,1120]{1,0:T(8,128)(2,1)S(1)}, u32[]{:S(2)}, u32[]{:S(2)}) %collective-permute-start.29) | collective-permute-done | bytes 627232 | tf_op jit(solution)/shard_map/ppermute | solution.py:822
  564.8 10.3 %pack_rest.1 = (f32[3,420,1120]{2,1,0:T(8,128)}, bf16[3,420,1120]{2,1,0:T(8,128)(2,1)}) custom-call(s32[1]{0:T(128)} %bitcast.place_ref, f32[280,1120]{1,0:T(8,128)S(1)} %fusion.47.out_ref, f32[1120,1120]{1,0:T(8,128)} %fusion.46.in_ref, f32[1120,1120]{1,0:T(8,128)} %fusion.45.back_ref, bf16[280,1120]{1,0:T(8,128)(2,1)S(1)} %collective-permute-done.29.out_got, ...), custom_call_target="tpu_custom_call" | custom-call | flops 10000000000 | bytes 4096 | tf_op jit(solution)/shard_map/pack_rest/pallas_call | solution.py:525
  575.1 55.8 %attention_backward.3.left_a = bf16[2048,896]{1,0:T(8,128)(2,1)} custom-call(s32[4]{0:T(128)} %copy-done.16, s32[1]{0:T(128)} %bitcast.9.core_ref, s32[4,1,512]{2,1,0:T(1,128)} %copy-done.9, bf16[2048,840]{1,0:T(8,128)(2,1)} %get-tuple-element.162.qkv_ref, bf16[2048,280]{1,0:T(8,128)(2,1)} %copy-done.29, f32[4,280,512]{2,1,0:T(8,128)} %copy-done.34, ...), custom_call_target="tpu_custom_call" | custom-call | flops 56000000000 | bytes 4096 | tf_op jit(solution)/shard_map/attention_backward/pallas_call | solution.py:303
  630.9 9.0 %convert_add_fusion = f32[1120,896]{1,0:T(8,128)S(1)} fusion(bf16[1120,896]{1,0:T(8,128)(2,1)} %collective-permute-done.33, bf16[2048,1120]{1,0:T(8,128)(2,1)} %get-tuple-element.158, bf16[2048,896]{1,0:T(8,128)(2,1)} %attention_backward.3.left_a), kind=kOutput, calls=%fused_computation.19 | convolution fusion | flops 4112424960 | bytes 14278656 | tf_op jit(solution)/shard_map/dot_general | solution.py:39
  644.5 2.8 fusion.34
  647.3 15.9 %split_product.3 = (f32[1024,1152]{1,0:T(8,128)}, f32[1024,1120]{1,0:T(8,128)}) custom-call(bf16[2048,896]{1,0:T(8,128)(2,1)} %attention_backward.3.left_a, bf16[2048,896]{1,0:T(8,128)(2,1)} %attention_backward.2.left_b, bf16[1120,840]{1,0:T(8,128)(2,1)S(1)} %copy-done.32, bf16[1120,840]{1,0:T(8,128)(2,1)S(1)} %copy-done.33), custom_call_target="tpu_custom_call" | custom-call | flops 12000000000 | bytes 4096 | tf_op jit(solution)/shard_map/split_product/pallas_call | solution.py:656
  667.5 2.6 convert_reduce_fusion
  672.6 3.6 fusion.37
  677.7 14.5 %collective-permute-done.35 = bf16[560,896]{1,0:T(8,128)(2,1)S(1)} collective-permute-done((bf16[560,896]{1,0:T(8,128)(2,1)S(1)}, bf16[560,896]{1,0:T(8,128)(2,1)S(1)}, u32[]{:S(2)}, u32[]{:S(2)}) %collective-permute-start.35) | collective-permute-done | bytes 1003552 | tf_op jit(solution)/shard_map/ppermute | solution.py:822
  696.9 17.8 %collective-permute-done.37 = bf16[420,1120]{1,0:T(8,128)(2,1)} collective-permute-done((bf16[420,1120]{1,0:T(8,128)(2,1)}, bf16[420,1120]{1,0:T(8,128)(2,1)}, u32[]{:S(2)}, u32[]{:S(2)}) %collective-permute-start.37) | collective-permute-done | bytes 940832 | tf_op jit(solution)/shard_map/ppermute | solution.py:822
  714.7 3.1 fusion.12
  721.5 7.4 norm_back.3
  728.9 2.8 fusion.32
  736.4 4.0 collective-permute-done.41
  741.8 4.3 reshape.201.rest_ref
  746.1 21.5 %collective-permute-done.42 = bf16[560,896]{1,0:T(8,128)(2,1)} collective-permute-done((bf16[560,896]{1,0:T(8,128)(2,1)S(1)}, bf16[560,896]{1,0:T(8,128)(2,1)}, u32[]{:S(2)}, u32[]{:S(2)}) %collective-permute-start.42) | collective-permute-done | bytes 1003552 | tf_op jit(solution)/shard_map/ppermute | solution.py:822
  767.6 3.3 slice_add_fusion.1
  770.8 6.0 reshape.202.lead_ref
  778.4 10.7 %new_moments.1 = (f32[1,1,470400]{2,1,0:T(1,128)}, f32[2,1,1,470400]{3,2,1,0:T(1,128)}, f32[1,1,470400]{2,1,0:T(1,128)S(1)}, f32[2]{0:T(128)S(1)}) custom-call(s32[2]{0:T(128)S(1)} %pad_add_fusion.ints_ref, f32[2]{0:T(128)S(1)} %pad_maximum_fusion.7.floats_ref, f32[1,1,470400]{2,1,0:T(1,128)S(1)} %copy-done.6, f32[1,1,470400]{2,1,0:T(1,128)S(1)} %reshape.201.rest_ref, ...), custom_call_target="tpu_custom_call" | custom-call | flops 10000000000 | bytes 4096 | tf_op jit(solution)/shard_map/new_moments/pallas_call | solution.py:406
  803.6 4.4 copy.53
  816.5 4.4 copy.54
  825.9 6.6 new_weights.1
  (322 shorter events, 135.4 us)
Async XLA Ops:
  8.7 29.2 %collective-permute-start = (bf16[512,1152]{1,0:T(8,128)(2,1)}, bf16[512,1152]{1,0:T(8,128)(2,1)}, u32[]{:S(2)}, u32[]{:S(2)}) collective-permute-start(bf16[512,1152]{1,0:T(8,128)(2,1)} %pad.21), channel_id=1, source_target_pairs={{0,2},{1,3},{2,0},{3,1},{4,6},{5,7},{6,4},{7,5},{8,10},{9,11},{10,... | collective-permute-start | bytes 3538952 | tf_op jit(solution)/shard_map/ppermute | solution.py:822
  24.3 26.0 %collective-permute-start.1 = (bf16[560,840]{1,0:T(8,128)(2,1)}, bf16[560,840]{1,0:T(8,128)(2,1)}, u32[]{:S(2)}, u32[]{:S(2)}) collective-permute-start(bf16[560,840]{1,0:T(8,128)(2,1)} %reshape.195), channel_id=1, source_target_pairs={{0,16},{4,20},{1,17},{5,21},{2,18},{6,22},{3,19},{7,23}} | collective-permute-start | bytes 2822408 | tf_op jit(solution)/shard_map/ppermute | solution.py:822
  44.7 30.2 %collective-permute-start.5 = (bf16[1024,1152]{1,0:T(8,128)(2,1)}, bf16[1024,1152]{1,0:T(8,128)(2,1)}, u32[]{:S(2)}, u32[]{:S(2)}) collective-permute-start(bf16[1024,1152]{1,0:T(8,128)(2,1)} %pad.22.own_ref), channel_id=1, source_target_pairs={{0,1},{1,0},{2,3},{3,2},{4,5},{5,4},{6,7},{7,6},{8,9},{9,8},{10,11... | collective-permute-start | bytes 7077896 | tf_op jit(solution)/shard_map/ppermute | solution.py:822
  51.4 22.1 %collective-permute-start.2 = (bf16[560,840]{1,0:T(8,128)(2,1)}, bf16[560,840]{1,0:T(8,128)(2,1)}, u32[]{:S(2)}, u32[]{:S(2)}) collective-permute-start(bf16[560,840]{1,0:T(8,128)(2,1)} %broadcast_select_fusion.2), channel_id=1, source_target_pairs={{0,8},{4,12},{16,24},{20,28},{1,9},{5,13},{17,25},{21,29},{2,10},{... | collective-permute-start | bytes 2822408 | tf_op jit(solution)/shard_map/ppermute | solution.py:822
  55.2 19.6 %collective-permute-start.3 = (bf16[420,1120]{1,0:T(8,128)(2,1)S(1)}, bf16[420,1120]{1,0:T(8,128)(2,1)}, u32[]{:S(2)}, u32[]{:S(2)}) collective-permute-start(bf16[420,1120]{1,0:T(8,128)(2,1)S(1)} %reshape.196.refs_0_), channel_id=1, source_target_pairs={{8,12},{9,13},{10,14},{11,15},{12,8},{13,9},{14,10},{15,11},{16,20... | collective-permute-start | bytes 2822408 | tf_op jit(solution)/shard_map/ppermute | solution.py:822
  56.9 18.0 %collective-permute-start.4 = (bf16[420,1120]{1,0:T(8,128)(2,1)S(1)}, bf16[420,1120]{1,0:T(8,128)(2,1)}, u32[]{:S(2)}, u32[]{:S(2)}) collective-permute-start(bf16[420,1120]{1,0:T(8,128)(2,1)S(1)} %reshape.196.refs_0_), channel_id=1, source_target_pairs={{8,10},{9,11},{10,8},{11,9},{12,14},{13,15},{14,12},{15,13},{16,18... | collective-permute-start | bytes 2822408 | tf_op jit(solution)/shard_map/ppermute | solution.py:822
  58.5 16.4 %copy-start.52 = (bf16[2,1,512,1120]{2,3,1,0:T(8,128)(2,1)S(1)}, bf16[2,1,512,1120]{2,3,1,0:T(8,128)(2,1)}, u32[]{:S(2)}) copy-start(bf16[2,1,512,1120]{2,3,1,0:T(8,128)(2,1)} %param.14) | copy-start | bytes 6881284
  81.2 29.2 %collective-permute-start.12 = (bf16[512,1152]{1,0:T(8,128)(2,1)}, bf16[512,1152]{1,0:T(8,128)(2,1)}, u32[]{:S(2)}, u32[]{:S(2)}) collective-permute-start(bf16[512,1152]{1,0:T(8,128)(2,1)} %pad.23), channel_id=1, source_target_pairs={{0,2},{1,3},{2,0},{3,1},{4,6},{5,7},{6,4},{7,5},{8,10},{9,11},{10,... | collective-permute-start | bytes 3538952 | tf_op jit(solution)/shard_map/ppermute | solution.py:822
  82.4 22.6 %collective-permute-start.6 = (bf16[560,840]{1,0:T(8,128)(2,1)S(1)}, bf16[560,840]{1,0:T(8,128)(2,1)}, u32[]{:S(2)}, u32[]{:S(2)}) collective-permute-start(bf16[560,840]{1,0:T(8,128)(2,1)S(1)} %broadcast_select_fusion.3.a0), channel_id=1, source_target_pairs={{0,4},{4,0},{8,12},{12,8},{16,20},{20,16},{24,28},{28,24},{1,5},{5... | collective-permute-start | bytes 2822408 | tf_op jit(solution)/shard_map/ppermute | solution.py:822
  84.4 152.4 %copy-start.16 = (s32[4]{0:T(128)}, s32[4]{0:T(128)S(1)}, u32[]{:S(2)}) copy-start(s32[4]{0:T(128)S(1)} %and_select_fusion.low_ref) | copy-start | bytes 52
  84.5 152.4 %copy-start.9 = (s32[4,1,512]{2,1,0:T(1,128)}, s32[4,1,512]{2,1,0:T(1,128)S(1)}, u32[]{:S(2)}) copy-start(s32[4,1,512]{2,1,0:T(1,128)S(1)} %compare_select_fusion.start_ref) | copy-start | bytes 24580
  84.5 47.5 %collective-permute-start.7 = (bf16[560,840]{1,0:T(8,128)(2,1)S(1)}, bf16[560,840]{1,0:T(8,128)(2,1)}, u32[]{:S(2)}, u32[]{:S(2)}) collective-permute-start(bf16[560,840]{1,0:T(8,128)(2,1)S(1)} %broadcast_select_fusion.3.a0), channel_id=1, source_target_pairs={{0,2},{1,3},{2,0},{3,1},{4,6},{5,7},{6,4},{7,5},{8,10},{9,11},{10,... | collective-permute-start | bytes 2822408 | tf_op jit(solution)/shard_map/ppermute | solution.py:822
  85.5 47.6 %collective-permute-start.9 = (bf16[420,1120]{1,0:T(8,128)(2,1)S(1)}, bf16[420,1120]{1,0:T(8,128)(2,1)}, u32[]{:S(2)}, u32[]{:S(2)}) collective-permute-start(bf16[420,1120]{1,0:T(8,128)(2,1)S(1)} %reshape.196.refs_0_), channel_id=1, source_target_pairs={{8,0},{9,1},{10,2},{11,3},{12,4},{13,5},{14,6},{15,7},{16,24},{17,... | collective-permute-start | bytes 2822408 | tf_op jit(solution)/shard_map/ppermute | solution.py:822
  86.7 52.6 %collective-permute-start.10 = (bf16[420,1120]{1,0:T(8,128)(2,1)S(1)}, bf16[420,1120]{1,0:T(8,128)(2,1)}, u32[]{:S(2)}, u32[]{:S(2)}) collective-permute-start(bf16[420,1120]{1,0:T(8,128)(2,1)S(1)} %reshape.196.refs_0_), channel_id=1, source_target_pairs={{8,24},{9,25},{10,26},{11,27},{12,28},{13,29},{14,30},{15,31},{16,... | collective-permute-start | bytes 2822408 | tf_op jit(solution)/shard_map/ppermute | solution.py:822
  105.0 34.4 %collective-permute-start.11 = (bf16[420,1120]{1,0:T(8,128)(2,1)}, bf16[420,1120]{1,0:T(8,128)(2,1)S(1)}, u32[]{:S(2)}, u32[]{:S(2)}) collective-permute-start(bf16[420,1120]{1,0:T(8,128)(2,1)} %collective-permute-done.4.refs_0_), channel_id=1, source_target_pairs={{8,12},{9,13},{10,14},{11,15},{12,8},{13,9},{14,10},{15,11},{16,20... | collective-permute-start | bytes 2822408 | tf_op jit(solution)/shard_map/ppermute | solution.py:822
  110.4 39.9 %collective-permute-start.8 = (bf16[560,840]{1,0:T(8,128)(2,1)}, bf16[560,840]{1,0:T(8,128)(2,1)S(1)}, u32[]{:S(2)}, u32[]{:S(2)}) collective-permute-start(bf16[560,840]{1,0:T(8,128)(2,1)} %collective-permute-done.6.a1), channel_id=1, source_target_pairs={{0,2},{1,3},{2,0},{3,1},{4,6},{5,7},{6,4},{7,5},{8,10},{9,11},{10,... | collective-permute-start | bytes 2822408 | tf_op jit(solution)/shard_map/ppermute | solution.py:822
  113.6 199.4 %copy-start.4 = (bf16[1024,1152]{1,0:T(8,128)(2,1)}, bf16[1024,1152]{1,0:T(8,128)(2,1)S(1)}, u32[]{:S(2)}) copy-start(bf16[1024,1152]{1,0:T(8,128)(2,1)S(1)} %fusion.11.cot_ref.base_ref) | copy-start | bytes 7077892
  150.3 74.7 %collective-permute-start.13 = (bf16[420,1120]{1,0:T(8,128)(2,1)}, bf16[420,1120]{1,0:T(8,128)(2,1)S(1)}, u32[]{:S(2)}, u32[]{:S(2)}) collective-permute-start(bf16[420,1120]{1,0:T(8,128)(2,1)} %collective-permute-done.10.refs_4_), channel_id=1, source_target_pairs={{0,8},{1,9},{2,10},{3,11},{4,12},{5,13},{6,14},{7,15},{8,0},{9,1},... | collective-permute-start | bytes 2822408 | tf_op jit(solution)/shard_map/ppermute | solution.py:822
  159.6 65.4 %collective-permute-start.15 = (bf16[420,1120]{1,0:T(8,128)(2,1)}, bf16[420,1120]{1,0:T(8,128)(2,1)}, u32[]{:S(2)}, u32[]{:S(2)}) collective-permute-start(bf16[420,1120]{1,0:T(8,128)(2,1)} %collective-permute-done.10.refs_4_), channel_id=1, source_target_pairs={{0,4},{1,5},{2,6},{3,7},{4,0},{5,1},{6,2},{7,3},{8,12},{9,13},{10,... | collective-permute-start | bytes 2822408 | tf_op jit(solution)/shard_map/ppermute | solution.py:822
  162.0 63.0 %collective-permute-start.14 = (bf16[420,1120]{1,0:T(8,128)(2,1)}, bf16[420,1120]{1,0:T(8,128)(2,1)S(1)}, u32[]{:S(2)}, u32[]{:S(2)}) collective-permute-start(bf16[420,1120]{1,0:T(8,128)(2,1)} %collective-permute-done.9.refs_2_), channel_id=1, source_target_pairs={{0,4},{1,5},{2,6},{3,7},{4,0},{5,1},{6,2},{7,3},{16,20},{17,21},{1... | collective-permute-start | bytes 2822408 | tf_op jit(solution)/shard_map/ppermute | solution.py:822
  165.5 59.6 %collective-permute-start.16 = (bf16[420,1120]{1,0:T(8,128)(2,1)}, bf16[420,1120]{1,0:T(8,128)(2,1)S(1)}, u32[]{:S(2)}, u32[]{:S(2)}) collective-permute-start(bf16[420,1120]{1,0:T(8,128)(2,1)} %collective-permute-done.9.refs_2_), channel_id=1, source_target_pairs={{0,2},{1,3},{2,0},{3,1},{4,6},{5,7},{6,4},{7,5},{16,18},{17,19},{1... | collective-permute-start | bytes 2822408 | tf_op jit(solution)/shard_map/ppermute | solution.py:822
  168.9 56.2 %collective-permute-start.17 = (bf16[420,1120]{1,0:T(8,128)(2,1)}, bf16[420,1120]{1,0:T(8,128)(2,1)S(1)}, u32[]{:S(2)}, u32[]{:S(2)}) collective-permute-start(bf16[420,1120]{1,0:T(8,128)(2,1)} %collective-permute-done.10.refs_4_), channel_id=1, source_target_pairs={{0,2},{1,3},{2,0},{3,1},{4,6},{5,7},{6,4},{7,5},{8,10},{9,11},{10,... | collective-permute-start | bytes 2822408 | tf_op jit(solution)/shard_map/ppermute | solution.py:822
  225.0 46.5 %copy-start.36 = (f32[4,8,512]{2,1,0:T(8,128)}, f32[4,8,512]{2,1,0:T(8,128)S(1)}, u32[]{:S(2)}) copy-start(f32[4,8,512]{2,1,0:T(8,128)S(1)} %get-tuple-element.163.lse_ref) | copy-start | bytes 196612
  225.0 46.5 %copy-start.65 = (bf16[420,1120]{1,0:T(8,128)(2,1)}, bf16[420,1120]{1,0:T(8,128)(2,1)S(1)}, u32[]{:S(2)}) copy-start(bf16[420,1120]{1,0:T(8,128)(2,1)S(1)} %collective-permute-done.13.refs_6_) | copy-start | bytes 2822404
  225.1 49.6 %collective-permute-start.18 = (bf16[420,1120]{1,0:T(8,128)(2,1)S(1)}, bf16[420,1120]{1,0:T(8,128)(2,1)}, u32[]{:S(2)}, u32[]{:S(2)}) collective-permute-start(bf16[420,1120]{1,0:T(8,128)(2,1)S(1)} %collective-permute-done.13.refs_6_), channel_id=1, source_target_pairs={{0,4},{1,5},{2,6},{3,7},{4,0},{5,1},{6,2},{7,3},{8,12},{9,13},{10,... | collective-permute-start | bytes 2822408 | tf_op jit(solution)/shard_map/ppermute | solution.py:822
  227.0 47.7 %collective-permute-start.19 = (bf16[420,1120]{1,0:T(8,128)(2,1)S(1)}, bf16[420,1120]{1,0:T(8,128)(2,1)}, u32[]{:S(2)}, u32[]{:S(2)}) collective-permute-start(bf16[420,1120]{1,0:T(8,128)(2,1)S(1)} %collective-permute-done.13.refs_6_), channel_id=1, source_target_pairs={{0,2},{1,3},{2,0},{3,1},{4,6},{5,7},{6,4},{7,5},{8,10},{9,11},{10,... | collective-permute-start | bytes 2822408 | tf_op jit(solution)/shard_map/ppermute | solution.py:822
  230.4 44.3 %collective-permute-start.20 = (bf16[420,1120]{1,0:T(8,128)(2,1)S(1)}, bf16[420,1120]{1,0:T(8,128)(2,1)S(1)}, u32[]{:S(2)}, u32[]{:S(2)}) collective-permute-start(bf16[420,1120]{1,0:T(8,128)(2,1)S(1)} %collective-permute-done.16.refs_2_), channel_id=1, source_target_pairs={{0,4},{1,5},{2,6},{3,7},{4,0},{5,1},{6,2},{7,3},{16,20},{17,21},{1... | collective-permute-start | bytes 2822408 | tf_op jit(solution)/shard_map/ppermute | solution.py:822
  234.3 41.4 %collective-permute-start.21 = (bf16[420,1120]{1,0:T(8,128)(2,1)}, bf16[420,1120]{1,0:T(8,128)(2,1)}, u32[]{:S(2)}, u32[]{:S(2)}) collective-permute-start(bf16[420,1120]{1,0:T(8,128)(2,1)} %collective-permute-done.15.refs_5_), channel_id=1, source_target_pairs={{0,2},{1,3},{2,0},{3,1},{4,6},{5,7},{6,4},{7,5},{8,10},{9,11},{10,... | collective-permute-start | bytes 2822408 | tf_op jit(solution)/shard_map/ppermute | solution.py:822
  275.7 22.7 %copy-start.15 = (bf16[420,1120]{1,0:T(8,128)(2,1)S(1)}, bf16[420,1120]{1,0:T(8,128)(2,1)}, u32[]{:S(2)}) copy-start(bf16[420,1120]{1,0:T(8,128)(2,1)} %copy-done.14) | copy-start | bytes 2822404
  275.7 21.7 %collective-permute-start.22 = (bf16[420,1120]{1,0:T(8,128)(2,1)}, bf16[420,1120]{1,0:T(8,128)(2,1)S(1)}, u32[]{:S(2)}, u32[]{:S(2)}) collective-permute-start(bf16[420,1120]{1,0:T(8,128)(2,1)} %collective-permute-done.18.refs_7_), channel_id=1, source_target_pairs={{0,2},{1,3},{2,0},{3,1},{4,6},{5,7},{6,4},{7,5},{8,10},{9,11},{10,... | collective-permute-start | bytes 2822408 | tf_op jit(solution)/shard_map/ppermute | solution.py:822
  285.9 18.1 %copy-start.19 = (bf16[2048,280]{1,0:T(8,128)(2,1)S(1)}, bf16[2048,280]{1,0:T(8,128)(2,1)}, u32[]{:S(2)}) copy-start(bf16[2048,280]{1,0:T(8,128)(2,1)} %copy-done.18) | copy-start | bytes 3440644
  312.8 11.5 %collective-permute-start.23 = (f32[1024,1152]{1,0:T(8,128)}, f32[1024,1152]{1,0:T(8,128)S(1)}, u32[]{:S(2)}, u32[]{:S(2)}) collective-permute-start(f32[1024,1152]{1,0:T(8,128)} %get-tuple-element.190), channel_id=1, source_target_pairs={{0,1},{1,0},{2,3},{3,2},{4,5},{5,4},{6,7},{7,6},{8,9},{9,8},{10,11... | collective-permute-start | bytes 14155784 | tf_op jit(solution)/shard_map/ppermute | solution.py:822
  313.1 16.6 %collective-permute-start.25 = (bf16[1024,1152]{1,0:T(8,128)(2,1)S(1)}, bf16[1024,1152]{1,0:T(8,128)(2,1)S(1)}, u32[]{:S(2)}, u32[]{:S(2)}) collective-permute-start(bf16[1024,1152]{1,0:T(8,128)(2,1)S(1)} %fusion.11.cot_ref.base_ref), channel_id=1, source_target_pairs={{0,1},{1,0},{2,3},{3,2},{4,5},{5,4},{6,7},{7,6},{8,9},{9,8},{10,11... | collective-permute-start | bytes 7077896 | tf_op jit(solution)/shard_map/ppermute | solution.py:822
  328.7 4.5 collective-permute-start.24
  369.0 35.2 %collective-permute-start.26 = (f32[1024,1152]{1,0:T(8,128)}, f32[1024,1152]{1,0:T(8,128)}, u32[]{:S(2)}, u32[]{:S(2)}) collective-permute-start(f32[1024,1152]{1,0:T(8,128)} %get-tuple-element.207), channel_id=1, source_target_pairs={{0,1},{1,0},{2,3},{3,2},{4,5},{5,4},{6,7},{7,6},{8,9},{9,8},{10,11... | collective-permute-start | bytes 14155784 | tf_op jit(solution)/shard_map/ppermute | solution.py:822
  369.2 35.0 %collective-permute-start.27 = (f32[1024,1152]{1,0:T(8,128)}, f32[1024,1152]{1,0:T(8,128)}, u32[]{:S(2)}, u32[]{:S(2)}) collective-permute-start(f32[1024,1152]{1,0:T(8,128)} %get-tuple-element.208), channel_id=1, source_target_pairs={{0,1},{1,0},{2,3},{3,2},{4,5},{5,4},{6,7},{7,6},{8,9},{9,8},{10,11... | collective-permute-start | bytes 14155784 | tf_op jit(solution)/shard_map/ppermute | solution.py:822
  369.6 34.7 %copy-start.5 = (bf16[1024,1152]{1,0:T(8,128)(2,1)S(1)}, bf16[1024,1152]{1,0:T(8,128)(2,1)}, u32[]{:S(2)}) copy-start(bf16[1024,1152]{1,0:T(8,128)(2,1)} %copy-done.4) | copy-start | bytes 7077892
  416.5 27.3 %collective-permute-start.28 = (bf16[1024,1152]{1,0:T(8,128)(2,1)S(1)}, bf16[1024,1152]{1,0:T(8,128)(2,1)}, u32[]{:S(2)}, u32[]{:S(2)}) collective-permute-start(bf16[1024,1152]{1,0:T(8,128)(2,1)S(1)} %get-tuple-element.217.own_ref), channel_id=1, source_target_pairs={{0,1},{1,0},{2,3},{3,2},{4,5},{5,4},{6,7},{7,6},{8,9},{9,8},{10,11... | collective-permute-start | bytes 7077896 | tf_op jit(solution)/shard_map/ppermute | solution.py:822
  436.6 111.0 %collective-permute-start.30 = (bf16[1120,1120]{1,0:T(8,128)(2,1)}, bf16[1120,1120]{1,0:T(8,128)(2,1)}, u32[]{:S(2)}, u32[]{:S(2)}) collective-permute-start(bf16[1120,1120]{1,0:T(8,128)(2,1)} %convolution_convert_fusion), channel_id=1, source_target_pairs={{0,2},{1,3},{2,0},{3,1},{4,6},{5,7},{6,4},{7,5},{8,10},{9,11},{10,... | collective-permute-start | bytes 7526408 | tf_op jit(solution)/shard_map/ppermute | solution.py:822
  438.1 112.9 %collective-permute-start.31 = (bf16[1120,1120]{1,0:T(8,128)(2,1)}, bf16[1120,1120]{1,0:T(8,128)(2,1)}, u32[]{:S(2)}, u32[]{:S(2)}) collective-permute-start(bf16[1120,1120]{1,0:T(8,128)(2,1)} %convolution_convert_fusion.1), channel_id=1, source_target_pairs={{0,2},{1,3},{2,0},{3,1},{4,6},{5,7},{6,4},{7,5},{8,10},{9,11},{10,... | collective-permute-start | bytes 7526408 | tf_op jit(solution)/shard_map/ppermute | solution.py:822
  479.7 85.1 %collective-permute-start.29 = (bf16[280,1120]{1,0:T(8,128)(2,1)}, bf16[280,1120]{1,0:T(8,128)(2,1)S(1)}, u32[]{:S(2)}, u32[]{:S(2)}) collective-permute-start(bf16[280,1120]{1,0:T(8,128)(2,1)} %convolution_convert_fusion.3), channel_id=1, source_target_pairs={{0,2},{1,3},{2,0},{3,1},{4,6},{5,7},{6,4},{7,5},{8,10},{9,11},{10,... | collective-permute-start | bytes 1881608 | tf_op jit(solution)/shard_map/ppermute | solution.py:822
  547.1 83.8 %collective-permute-start.33 = (bf16[1120,896]{1,0:T(8,128)(2,1)}, bf16[1120,896]{1,0:T(8,128)(2,1)}, u32[]{:S(2)}, u32[]{:S(2)}) collective-permute-start(bf16[1120,896]{1,0:T(8,128)(2,1)} %convolution_convert_fusion.2), channel_id=1, source_target_pairs={{0,2},{1,3},{2,0},{3,1},{4,6},{5,7},{6,4},{7,5},{8,10},{9,11},{10,... | collective-permute-start | bytes 6021128 | tf_op jit(solution)/shard_map/ppermute | solution.py:822
  575.1 67.4 %collective-permute-start.34 = (bf16[3,420,1120]{2,1,0:T(8,128)(2,1)}, bf16[3,420,1120]{2,1,0:T(8,128)(2,1)S(1)}, u32[]{:S(2)}, u32[]{:S(2)}) collective-permute-start(bf16[3,420,1120]{2,1,0:T(8,128)(2,1)} %get-tuple-element.244), channel_id=1, source_target_pairs={{0,4},{4,0},{8,12},{12,8},{16,20},{20,16},{24,28},{28,24},{1,5},{5... | collective-permute-start | bytes 8467208 | tf_op jit(solution)/shard_map/ppermute | solution.py:822
  647.2 20.0 %copy-start.57 = (f32[8,1120]{1,0:T(8,128)S(1)}, f32[8,1120]{1,0:T(8,128)}, u32[]{:S(2)}) copy-start(f32[8,1120]{1,0:T(8,128)} %get-tuple-element.279) | copy-start | bytes 107524
  647.3 20.0 %copy-start.58 = (f32[8,1120]{1,0:T(8,128)S(1)}, f32[8,1120]{1,0:T(8,128)}, u32[]{:S(2)}) copy-start(f32[8,1120]{1,0:T(8,128)} %get-tuple-element.280) | copy-start | bytes 107524
  647.3 20.2 %copy-start.53 = (bf16[560,896]{1,0:T(8,128)(2,1)S(1)}, bf16[560,896]{1,0:T(8,128)(2,1)}, u32[]{:S(2)}) copy-start(bf16[560,896]{1,0:T(8,128)(2,1)} %select_convert_fusion) | copy-start | bytes 3010564
  663.2 56.0 %collective-permute-start.38 = (f32[1024,1152]{1,0:T(8,128)}, f32[1024,1152]{1,0:T(8,128)}, u32[]{:S(2)}, u32[]{:S(2)}) collective-permute-start(f32[1024,1152]{1,0:T(8,128)} %get-tuple-element.261), channel_id=1, source_target_pairs={{0,1},{1,0},{2,3},{3,2},{4,5},{5,4},{6,7},{7,6},{8,9},{9,8},{10,11... | collective-permute-start | bytes 14155784 | tf_op jit(solution)/shard_map/ppermute | solution.py:822
  667.5 24.7 %collective-permute-start.35 = (bf16[560,896]{1,0:T(8,128)(2,1)S(1)}, bf16[560,896]{1,0:T(8,128)(2,1)S(1)}, u32[]{:S(2)}, u32[]{:S(2)}) collective-permute-start(bf16[560,896]{1,0:T(8,128)(2,1)S(1)} %copy-done.53), channel_id=1, source_target_pairs={{0,4},{4,0},{8,12},{12,8},{16,20},{20,16},{24,28},{28,24},{1,5},{5... | collective-permute-start | bytes 3010568 | tf_op jit(solution)/shard_map/ppermute | solution.py:822
  670.2 21.9 %copy-start.43 = (f32[560,896]{1,0:T(8,128)S(1)}, f32[560,896]{1,0:T(8,128)}, u32[]{:S(2)}) copy-start(f32[560,896]{1,0:T(8,128)} %slice_select_fusion) | copy-start | bytes 6021124
  670.2 26.6 %collective-permute-start.36 = (bf16[420,1120]{1,0:T(8,128)(2,1)}, bf16[420,1120]{1,0:T(8,128)(2,1)}, u32[]{:S(2)}, u32[]{:S(2)}) collective-permute-start(bf16[420,1120]{1,0:T(8,128)(2,1)} %get-tuple-element.256), channel_id=1, source_target_pairs={{0,8},{4,12},{16,24},{20,28},{1,9},{5,13},{17,25},{21,29},{2,10},{... | collective-permute-start | bytes 2822408 | tf_op jit(solution)/shard_map/ppermute | solution.py:822
  672.6 42.1 %collective-permute-start.37 = (bf16[420,1120]{1,0:T(8,128)(2,1)}, bf16[420,1120]{1,0:T(8,128)(2,1)}, u32[]{:S(2)}, u32[]{:S(2)}) collective-permute-start(bf16[420,1120]{1,0:T(8,128)(2,1)} %get-tuple-element.258), channel_id=1, source_target_pairs={{0,8},{4,12},{8,0},{12,4},{16,24},{20,28},{24,16},{28,20},{1,9},{5... | collective-permute-start | bytes 2822408 | tf_op jit(solution)/shard_map/ppermute | solution.py:822
  676.2 18.8 %copy-start.51 = (bf16[2048,896]{1,0:T(8,128)(2,1)S(1)}, bf16[2048,896]{1,0:T(8,128)(2,1)}, u32[]{:S(2)}) copy-start(bf16[2048,896]{1,0:T(8,128)(2,1)} %attention_backward.3.left_a) | copy-start | bytes 11010052
  676.2 121.0 %collective-permute-start.32 = (bf16[512,1152]{1,0:T(8,128)(2,1)}, bf16[512,1152]{1,0:T(8,128)(2,1)}, u32[]{:S(2)}, u32[]{:S(2)}) collective-permute-start(bf16[512,1152]{1,0:T(8,128)(2,1)} %get-tuple-element.357), channel_id=1, source_target_pairs={{0,2},{1,3},{2,0},{3,1},{4,6},{5,7},{6,4},{7,5},{8,10},{9,11},{10,... | collective-permute-start | bytes 3538952 | tf_op jit(solution)/shard_map/ppermute | solution.py:822
  693.7 35.2 %collective-permute-start.39 = (bf16[560,896]{1,0:T(8,128)(2,1)S(1)}, bf16[560,896]{1,0:T(8,128)(2,1)}, u32[]{:S(2)}, u32[]{:S(2)}) collective-permute-start(bf16[560,896]{1,0:T(8,128)(2,1)S(1)} %get-tuple-element.265), channel_id=1, source_target_pairs={{8,0},{12,4},{24,16},{28,20},{9,1},{13,5},{25,17},{29,21},{10,2},{... | collective-permute-start | bytes 3010568 | tf_op jit(solution)/shard_map/ppermute | solution.py:822
  696.8 22.3 %copy-start.3 = (bf16[1024,1120]{1,0:T(8,128)(2,1)S(1)}, bf16[1024,1120]{1,0:T(8,128)(2,1)}, u32[]{:S(2)}) copy-start(bf16[1024,1120]{1,0:T(8,128)(2,1)} %copy-done.2) | copy-start | bytes 6881284
  717.8 22.6 %collective-permute-start.41 = (bf16[420,1120]{1,0:T(8,128)(2,1)S(1)}, bf16[420,1120]{1,0:T(8,128)(2,1)S(1)}, u32[]{:S(2)}, u32[]{:S(2)}) collective-permute-start(bf16[420,1120]{1,0:T(8,128)(2,1)S(1)} %get-tuple-element.271), channel_id=1, source_target_pairs={{24,8},{28,12},{0,16},{4,20},{8,24},{12,28},{25,9},{29,13},{1,17},... | collective-permute-start | bytes 2822408 | tf_op jit(solution)/shard_map/ppermute | solution.py:822
  731.7 35.9 %collective-permute-start.42 = (bf16[560,896]{1,0:T(8,128)(2,1)S(1)}, bf16[560,896]{1,0:T(8,128)(2,1)}, u32[]{:S(2)}, u32[]{:S(2)}) collective-permute-start(bf16[560,896]{1,0:T(8,128)(2,1)S(1)} %get-tuple-element.273), channel_id=1, source_target_pairs={{16,0},{20,4},{17,1},{21,5},{18,2},{22,6},{19,3},{23,7}} | collective-permute-start | bytes 3010568 | tf_op jit(solution)/shard_map/ppermute | solution.py:822
  734.9 74.1 %collective-permute-start.40 = (bf16[512,1152]{1,0:T(8,128)(2,1)}, bf16[512,1152]{1,0:T(8,128)(2,1)}, u32[]{:S(2)}, u32[]{:S(2)}) collective-permute-start(bf16[512,1152]{1,0:T(8,128)(2,1)} %get-tuple-element.354), channel_id=1, source_target_pairs={{0,2},{1,3},{2,0},{3,1},{4,6},{5,7},{6,4},{7,5},{8,10},{9,11},{10,... | collective-permute-start | bytes 3538952 | tf_op jit(solution)/shard_map/ppermute | solution.py:822
  778.4 18.8 %copy-start.46 = (bf16[512,1152]{1,0:T(8,128)(2,1)S(1)}, bf16[512,1152]{1,0:T(8,128)(2,1)}, u32[]{:S(2)}) copy-start(bf16[512,1152]{1,0:T(8,128)(2,1)} %get-tuple-element.356) | copy-start | bytes 3538948
  793.6 2.0 collective-permute-start.43
  795.6 4.7 collective-permute-start.44
  800.4 7.7 collective-permute-start.45
  808.1 4.4 collective-permute-start.46
  812.5 8.4 %collective-permute-start.47 = (f32[16,1120]{1,0:T(8,128)S(1)}, f32[16,1120]{1,0:T(8,128)S(1)}, u32[]{:S(2)}, u32[]{:S(2)}) collective-permute-start(f32[16,1120]{1,0:T(8,128)S(1)} %add.275), channel_id=1, source_target_pairs={{0,16},{4,20},{8,24},{12,28},{16,0},{20,4},{24,8},{28,12},{1,17},{... | collective-permute-start | bytes 215048 | tf_op jit(solution)/shard_map/ppermute | solution.py:822
  (63 other events, 383.5 us)

commit v5 on v4

--- a/solution.py
+++ b/solution.py
@@ -320,7 +320,7 @@
 
 def put(ref, value):
     width = value.shape[1]
-    ref[:, :width] = value
+    ref[:, :width] = value.astype(ref.dtype)
     if width < ref.shape[1]:
         ref[:, width:] = jnp.zeros((value.shape[0], ref.shape[1] - width), ref.dtype)
 
@@ -629,10 +629,27 @@
     )(own, other, *w_out)
 
 
-def split_product_body(steps, turned, left_a, left_b, w_a, w_b, sent_ref, kept_ref):
-    multiply = dot_transposed if turned else dot_rows
-    inner = w_a.shape[1] if turned else w_a.shape[0]
-    product = multiply(left_a[:, :inner], w_a[...]) + multiply(left_b[:, :inner], w_b[...])
+def row_products(turned, left_refs, weight_refs):
+    product = None
+    for left, weight in zip(left_refs, weight_refs):
+        if turned:
+            term = dot_transposed(left[:, : weight.shape[1]], weight[...])
+        else:
+            term = dot_rows(left[:, : weight.shape[0]], weight[...])
+        product = term if product is None else product + term
+    return product
+
+
+def partial_product_body(left, weight, out_ref):
+    out_ref[...] = row_products(True, [left], [weight])
+
+
+def split_product_body(steps, turned, count, *refs):
+    lefts, weights, rest = refs[:count], refs[count : 2 * count], refs[2 * count :]
+    *partial, sent_ref, kept_ref = rest
+    product = row_products(turned, lefts, weights)
+    if partial:
+        product = product + partial[0][...]
     step = pl.program_id(0)
 
     @pl.when(step < steps)
@@ -641,31 +658,53 @@
 
     @pl.when(step >= steps)
     def own_rows():
-        kept_ref[...] = product
-
-
-def split_product(lefts, weights, turned, model_width):
+        put(kept_ref, product)
+
+
+def other_first(block, width, steps):
+    return pl.BlockSpec((block, width), lambda i: ((i + steps) % (2 * steps), 0))
+
+
+def partial_product(left, weight):
+    count, width = left.shape
+    model_width = weight.shape[0]
+    block = min(512, count // 2)
+    steps = count // 2 // block
+    return pl.pallas_call(
+        partial_product_body,
+        grid=(2 * steps,),
+        in_specs=[other_first(block, width, steps), fixed(weight.shape)],
+        out_specs=pl.BlockSpec((block, model_width), lambda i: (i, 0)),
+        out_shape=jax.ShapeDtypeStruct((count, model_width), F32),
+        compiler_params=vmem(48),
+        cost_estimate=lasting(9),
+        name="partial_product",
+    )(left, weight)
+
+
+def split_product(lefts, weights, turned, model_width, sent_type, partial=()):
     count, width = lefts[0].shape
     block = min(512, count // 2)
     steps = count // 2 // block
-    left = pl.BlockSpec((block, width), lambda i: ((i + steps) % (2 * steps), 0))
     parts = [
-        jax.ShapeDtypeStruct((count // 2, lanes(model_width)), F32),
+        jax.ShapeDtypeStruct((count // 2, lanes(model_width)), sent_type),
         jax.ShapeDtypeStruct((count // 2, model_width), F32),
     ]
     return pl.pallas_call(
-        functools.partial(split_product_body, steps, turned),
+        functools.partial(split_product_body, steps, turned, len(lefts)),
         grid=(2 * steps,),
-        in_specs=[left, left] + [fixed(weights[0].shape)] * 2,
+        in_specs=[other_first(block, width, steps)] * len(lefts)
+        + [fixed(weight.shape) for weight in weights]
+        + [pl.BlockSpec((block, model_width), lambda i: (i, 0))] * len(partial),
         out_specs=[
             pl.BlockSpec((block, lanes(model_width)), lambda i: (jnp.minimum(i, steps - 1), 0)),
             pl.BlockSpec((block, model_width), lambda i: (jnp.maximum(i - steps, 0), 0)),
         ],
         out_shape=parts,
         compiler_params=vmem(48),
-        cost_estimate=lasting(12),
+        cost_estimate=lasting(9),
         name="split_product",
-    )(*lefts, *weights)
+    )(*lefts, *weights, *partial)
 
 
 def middle_body(rows_ref, kept_ref, got_ref, small_ref, middle_ref, low_ref):
@@ -702,7 +741,7 @@
     rows = rows_ref[...].astype(F32)
     hat, scale = norm_stats(rows)
     width = rows.shape[1]
-    upstream = kept_ref[:, :width] + got_ref[:, :width]
+    upstream = kept_ref[:, :width] + got_ref[:, :width].astype(F32)
     base = base_ref[:, :width].astype(F32)
     grad = base + norm_backward(upstream, hat, scale, gain_ref[...])
     low = grad.astype(BF16)
@@ -829,6 +868,12 @@
 
 def tie(*values):
     return lax.optimization_barrier(values)
+
+
+def started(sent, value, mark):
+    sent, mark = tie(sent, mark)
+    value, mark = tie(value, swap(mark, "seq", 1))
+    return sent, value, mark
 
 
 def lower_pairs(pairs, y_count):
@@ -920,12 +965,7 @@
     def widen(rows):
         return jnp.pad(rows, ((0, 0), (0, lanes(model_width) - model_width)))
 
-    own_in = exchange_micro(rows_in)
-    inputs = own_in.astype(F32)
-    hat_one, _ = norm_stats(inputs)
-    low_one = widen((hat_one * small_master[0] + small_master[1]).astype(BF16))
-    other_one = swap(low_one, "seq", 1)
-    later_cotangent = out_cotangent
+    mark = small_master[:8, :128]
 
     ends = jnp.array([first_end, second_end, third_end, dp_count * shard_len], jnp.int32)
     begin = dp_here * shard_len
@@ -941,6 +981,12 @@
 
     weight = weights_master
     low_weight, weight_sums = round_weights(bound, weight)
+    first_rows, low_weight = tie(rows_in, low_weight)
+    own_in = exchange_micro(first_rows)
+    inputs = own_in.astype(F32)
+    hat_one, _ = norm_stats(inputs)
+    low_one = widen((hat_one * small_master[0] + small_master[1]).astype(BF16))
+    other_one = swap(low_one, "seq", 1)
     y_index = y_here.reshape(1).astype(jnp.int32)
     if planar:
         tall = low_weight.reshape(shard_len // triple, triple)
@@ -949,8 +995,8 @@
         lead = spread_lead(tall, z_here)
         across = [move_rest(wide, (1, 0), 0)]
         over = [move_rest(wide, (0, 2), 0)]
-        lead, wide, across[0], over[0], other_one, later_cotangent = tie(
-            lead, wide, across[0], over[0], other_one, later_cotangent
+        lead, wide, across[0], over[0], other_one = tie(
+            lead, wide, across[0], over[0], other_one
         )
         lead_across = swap(lead, "dp", 1)
         halves = (lead, lead_across, swap(lead, "seq", 2), swap(lead_across, "seq", 2))
@@ -996,10 +1042,9 @@
     block_starts = first_key.reshape(-1, 1, local_rows)
     core_index = core.reshape(1).astype(jnp.int32)
 
-    own_e = widen(exchange_micro(later_cotangent))
     if planar:
         both = [move_rest(over[0], (1, 0), 0)]
-        halves, near, far, both[0], own_e = tie(halves, near, far, both[0], own_e)
+        halves, near, far, both[0] = tie(halves, near, far, both[0])
         last = move_rest(far, (2, 0), 2)
         across += [move_rest(near, (1, 0), 1), move_rest(far, (1, 0), 2)]
         over += [move_rest(near, (0, 2), 1), move_rest(far, (0, 2), 2)]
@@ -1010,25 +1055,28 @@
     def attend(part):
         return attention_forward(low_blocks, core_index, block_starts, qkv[part], heads_here)
 
+    later_cotangent = out_cotangent
     attended = [attend(0)]
     if planar:
-        qkv[1], last, across[1:3], over[1:3], _ = tie(
-            qkv[1], last, across[1:3], over[1:3], attended[0][2]
+        qkv[1], last, across[1:3], over[1:3], later_cotangent, _ = tie(
+            qkv[1], last, across[1:3], over[1:3], later_cotangent, attended[0][2]
         )
         across.append(move_rest(last, (1, 0), 3))
         over.append(move_rest(last, (0, 2), 3))
         both += [move_rest(over[1], (1, 0), 1), move_rest(across[2], (0, 2), 2)]
-    other_e = swap(own_e, "seq", 1)
+    own_e = widen(exchange_micro(later_cotangent))
     attended.append(attend(1))
     if planar:
         dp_index, across, over, both, _ = tie(dp_index, across, over, both, attended[1][2])
-        both.append(move_rest(across[3], (0, 2), 3))
+        both.append(move_rest(over[3], (1, 0), 3))
         rest_mine = [block for pair in zip((wide, near, far, last), across) for block in pair]
         rest_theirs = [block for pair in zip(over, both) for block in pair]
         matrices_mine = unpack_share(dp_index, rest_mine, head_share, model_width)
         matrices_theirs = unpack_share(dp_index, rest_theirs, head_share, model_width)
         w_out, w_in, w_back = (list(pair) for pair in zip(matrices_mine, matrices_theirs))
-    sent, kept = split_product([attended[0][0], attended[1][0]], w_out, False, model_width)
+        own_e, w_out[0] = tie(own_e, w_out[0])
+    other_e = swap(own_e, "seq", 1)
+    sent, kept = split_product([attended[0][0], attended[1][0]], w_out, False, model_width, F32)
     middle, low_two = middle_norm(own_in, kept, swap(sent, "seq", 1), small_master)
     other_two = swap(low_two, "seq", 1)
 
@@ -1050,10 +1098,10 @@
         middle, up_kept, up_received, own_e, small_master[2:3], True
     )
     low_mid, rows_two, rows_e = tie(low_mid, rows_two, rows_e)
-    other_mid = swap(low_mid, "seq", 1)
     back_sent = dot_columns(activated[1], rows_e).astype(link)
     in_sent = dot_columns(rows_two, inner[1]).astype(link)
     back_sent, in_sent, low_mid = tie(back_sent, in_sent, low_mid)
+    other_mid = swap(low_mid, "seq", 1)
     back_received = swap(back_sent, "seq", 2)
     in_received = swap(in_sent, "seq", 2)
 
@@ -1067,6 +1115,16 @@
     share_back, share_in, share_out, grad_att_theirs = tie(
         share_back, share_in, share_out, grad_att_theirs
     )
+
+    def place_micro(lower, upper, received):
+        own = jnp.where(chip == 0, lower, upper)[:, :model_width]
+        received = received[:, :model_width]
+        first = jnp.where(chip == 0, own, received)
+        second = jnp.where(chip == 0, received, own)
+        return jnp.stack([first, second])[:, None]
+
+    def return_rows(lower, upper):
+        return swap(jnp.where(chip == 0, upper, lower), "seq", 2)
 
     def attend_back(part, grad_att):
         return attention_backward(
@@ -1082,7 +1140,9 @@
 
     packed_theirs = attend_back(1, grad_att_theirs)
     attn_sent = dot_columns(rows_one, packed_theirs).astype(link)
-    attn_sent, packed_theirs, y_index = tie(attn_sent, packed_theirs, y_index)
+    attn_sent, packed_theirs = tie(attn_sent, packed_theirs)
+    theirs_part = partial_product(packed_theirs, w_attn_theirs)
+    attn_sent, theirs_part, y_index = tie(attn_sent, theirs_part, y_index)
     attn_received = swap(attn_sent, "seq", 2)
     if planar:
         kept_rest, sent_rest = pack_rest(
@@ -1095,11 +1155,15 @@
             (middle + ((out_kept + out_received)[:, :model_width] + small_master[7])).astype(BF16)
         )
         sent_rest, grad_att_mine, result_rows = tie(sent_rest, grad_att_mine, result_rows)
+        result_halves = (result_rows[:local_rows], result_rows[local_rows:])
+        result_received = return_rows(*result_halves)
         got_rest = swap(sent_rest, "dp", 1)
     else:
         result_rows = widen(
             (middle + ((out_kept + out_received)[:, :model_width] + small_master[7])).astype(BF16)
         )
+        result_halves = (result_rows[:local_rows], result_rows[local_rows:])
+        result_received = return_rows(*result_halves)
         share_back, share_in, share_out = (
             share_back + back_received,
             share_in + in_received,
@@ -1107,61 +1171,57 @@
         )
 
     packed_mine = attend_back(0, grad_att_mine)
+    packed_mine, result_received = tie(packed_mine, result_received)
+    sent, kept = split_product(
+        [packed_mine], [w_attn_mine], True, model_width, BF16, [theirs_part]
+    )
+    packed_mine, sent = tie(packed_mine, sent)
     share_attn = dot_columns(rows_one, packed_mine) + attn_received.astype(F32)
     if planar:
         z_odd = z_here % 2 == 1
         kept_lead, sent_lead = halve_plane(share_attn[:tall_rows], share_attn[tall_rows:], y_here)
-        kept_lead, sent_lead, kept_rest, packed_mine = tie(
-            kept_lead, sent_lead, kept_rest, packed_mine
-        )
+        kept_lead, sent_lead, kept_rest = tie(kept_lead, sent_lead, kept_rest)
         got_lead = swap(sent_lead, "dp", 1)
         held = [kept_rest[i] + got_rest[i].astype(F32) for i in range(3)]
         sent_near = jnp.where(z_odd, held[1], held[0]).astype(BF16)
         sent_last = held[2].astype(BF16)
         kept_near = jnp.where(z_odd, held[0], held[1])
         kept_last = held[2]
-        sent_near, sent_last, packed_mine = tie(sent_near, sent_last, packed_mine)
+        (sent_near, sent_last), kept_lead, mark = started(
+            (sent_near, sent_last), kept_lead, mark
+        )
         got_near = swap(sent_near, "dp", 2)
         got_last = permute(sent_last, "dp", lower_pairs([(0, 1), (2, 3)], 2))
     packed = [packed_mine, packed_theirs]
-    sent, kept = split_product(packed, [w_attn_mine, w_attn_theirs], True, model_width)
     if planar:
-        kept_lead, sent = tie(kept_lead, sent)
         held_lead = kept_lead + got_lead.astype(F32)
         sent_lead = held_lead.astype(BF16)
-        sent_lead, held_lead, kept_near, kept_last, kept = tie(
-            sent_lead, held_lead, kept_near, kept_last, kept
-        )
+        sent_lead, held_lead, kept = tie(sent_lead, held_lead, kept)
+        sent_lead, kept, mark = started(sent_lead, kept, mark)
         near_lead = permute(sent_lead, "dp", lower_pairs([(1, 0), (3, 2)], 2))
+    grad_x, sums_one = norm_back(
+        own_in, kept, swap(sent, "seq", 1), grad_mid, small_master[0:1], False
+    )
+    if planar:
+        grad_x, held_lead = tie(grad_x, held_lead)
+        held_lead = held_lead + near_lead.astype(F32)
+        sent_lead = held_lead.astype(BF16)
+        sent_lead, held_lead, kept_near, kept_last = tie(
+            sent_lead, held_lead, kept_near, kept_last
+        )
+        sent_lead, (kept_near, kept_last), mark = started(
+            sent_lead, (kept_near, kept_last), mark
+        )
+        far_lead = permute(sent_lead, "dp", lower_pairs([(2, 0)], 2))
         held_near = kept_near + got_near.astype(F32)
         held_last = kept_last + got_last.astype(F32)
         sent_far = jnp.where(z_here == 1, held_last, held_near).astype(BF16)
         own_rest = jnp.where(z_here == 3, held_last, held_near)
-        sent_far, own_rest, kept = tie(sent_far, own_rest, kept)
         got_far = permute(sent_far, "dp", lower_pairs([(3, 1), (0, 2), (1, 3)], 2))
-    grad_x, sums_one = norm_back(
-        own_in, kept, swap(sent, "seq", 1), grad_mid, small_master[0:1], False
-    )
-    if planar:
-        held_lead, _ = tie(held_lead, sums_one)
-        held_lead = held_lead + near_lead.astype(F32)
-        sent_lead = held_lead.astype(BF16)
-        sent_lead, held_lead, own_rest, grad_x, sums_one = tie(
-            sent_lead, held_lead, own_rest, grad_x, sums_one
-        )
-        far_lead = permute(sent_lead, "dp", lower_pairs([(2, 0)], 2))
-        rest_grad = (own_rest + got_far.astype(F32)).reshape(1, 1, shard_len)
-
-    def return_micro(rows):
-        lower, upper = rows[:local_rows], rows[local_rows:]
-        own = jnp.where(chip == 0, lower, upper)[:, :model_width]
-        received = swap(jnp.where(chip == 0, upper, lower), "seq", 2)[:, :model_width]
-        first = jnp.where(chip == 0, own, received)
-        second = jnp.where(chip == 0, received, own)
-        return jnp.stack([first, second])[:, None]
-
-    result_all = return_micro(result_rows)
-    grad_all = return_micro(grad_x)
+
+    result_all = place_micro(*result_halves, result_received)
+    grad_halves = (grad_x[:local_rows], grad_x[local_rows:])
+    grad_all = place_micro(*grad_halves, return_rows(*grad_halves))
 
     def at_shares(columns):
         row = jnp.zeros((model_width,), F32)
@@ -1187,7 +1247,10 @@
     )
 
     if planar:
-        held_lead, rest_grad = tie(held_lead, rest_grad)
+        rest_grad = (own_rest + got_far.astype(F32)).reshape(1, 1, shard_len)
+        held_lead, rest_grad, result_all, grad_all, small_now = tie(
+            held_lead, rest_grad, result_all, grad_all, small_now
+        )
         lead_grad = (held_lead + far_lead.astype(F32))[:, :triple].reshape(1, 1, shard_len)
         leads = z_here == 0
     else:
@@ -1226,7 +1289,8 @@
     )
     small_one = BETA_ONE * small_first + (1.0 - BETA_ONE) * small_grad
     small_two = BETA_TWO * small_second + (1.0 - BETA_TWO) * small_grad * small_grad
-    small_updated = small_master - SMALL_RATE * (small_one / fix_one) / (
+    small_late = lax.dynamic_update_slice(small_master, mark, (0, 0))
+    small_updated = small_late - SMALL_RATE * (small_one / fix_one) / (
         jnp.sqrt(small_two / fix_two) + ADAM_EPS
     )
     return (

time: 844 us -> 868 us (1.028)
  waiting for transfers between devices: 186 us -> 210 us
    ppermute x48 -> x51, waiting for transfers between devices: 186 us -> 210 us  [permute(): return lax.ppermute(value, axis_name, pairs)]
    ppermute x48 -> x51, starting transfers between devices: 80.1 us -> 82.9 us  [permute(): return lax.ppermute(value, axis_name, pairs)]
    pallas_call x2 -> x3, Pallas kernels: 24.6 us -> 27.4 us  [the longest x2 19.8 us: split_product(): pl.pallas_call(functools.partial(split_product_body, steps, turned, len(l...]
    unnamed x161 -> x172, local copies, waits for them, and re-layouts: 35.5 us -> 34.2 us
  transfers between devices with their start and end apart: 48 -> 51, of which waited for: 20 -> 19; matrix products, arithmetic and copies ran while one was open for 18% -> 14% of each run, Pallas kernels for 34% -> 33%
where the time goes in v5:
time: 868 us; the launch traced here: 858 us
  Pallas kernels  364 us (42%)
  waiting for transfers between devices  210 us (24%)
  starting transfers between devices  82.9 us (10%)
  local copies, waits for them, and re-layouts  75.3 us (9%)
  matrix products  62.6 us (7%)
  other arithmetic  55.3 us (6%)
    ppermute x51, waiting for transfers between devices, permute(): return lax.ppermute(value, axis_name, pairs)  210 us
    pallas_call x2, Pallas kernels, attention_backward(): pl.pallas_call(functools.partial(attention_backward_body, heads, width, b...  112 us
    ppermute x51, starting transfers between devices, permute(): return lax.ppermute(value, axis_name, pairs)  82.9 us
    pallas_call x2, Pallas kernels, attention_forward(): pl.pallas_call(functools.partial(attention_forward_body, heads, width, bq...  69.6 us
    pallas_call x2, Pallas kernels, feed_forward(): pl.pallas_call(functools.partial(feed_forward_body, len(filled)), out_sha...  69.3 us
    dot_general x8, matrix products, dot_columns(): lax.dot_general(left, right, (((0,), (0,)), ((), ())), preferred_element_...  62.6 us
    unnamed x172, local copies, waits for them, and re-layouts  34.2 us
    pallas_call x2, Pallas kernels, split_product(): pl.pallas_call(functools.partial(split_product_body, steps, turned, len(l...  19.8 us
  transfers between devices with their start and end apart: 51, of which 19 were waited for; matrix products, arithmetic and copies ran while one was open for 14% of the time, Pallas kernels for 33%

profile of v5, /device:TPU:0, one launch (start us, length us, event | category | flops | bytes accessed | tf_op | source)
XLA Modules:
  0.0 857.6 jit_solution(1845972063493028949)
XLA Ops:
  8.0 6.0 round_weights.1
  14.1 3.1 constant_dynamic-slice_fusion.12
  20.0 2.9 collective-permute-start
  22.9 2.8 reshape.195
  25.7 5.5 collective-permute-start.1
  34.2 15.0 %collective-permute-done = bf16[512,1152]{1,0:T(8,128)(2,1)} collective-permute-done((bf16[512,1152]{1,0:T(8,128)(2,1)}, bf16[512,1152]{1,0:T(8,128)(2,1)}, u32[]{:S(2)}, u32[]{:S(2)}) %collective-permute-start) | collective-permute-done | bytes 1179680 | tf_op jit(solution)/shard_map/ppermute | solution.py:861
  58.2 5.1 collective-permute-start.2
  67.9 16.6 %collective-permute-done.2 = bf16[560,840]{1,0:T(8,128)(2,1)} collective-permute-done((bf16[560,840]{1,0:T(8,128)(2,1)}, bf16[560,840]{1,0:T(8,128)(2,1)}, u32[]{:S(2)}, u32[]{:S(2)}) %collective-permute-start.2) | collective-permute-done | bytes 940832 | tf_op jit(solution)/shard_map/ppermute | solution.py:861
  93.3 16.5 %collective-permute-done.6.a1 = bf16[560,840]{1,0:T(8,128)(2,1)} collective-permute-done((bf16[560,840]{1,0:T(8,128)(2,1)S(1)}, bf16[560,840]{1,0:T(8,128)(2,1)}, u32[]{:S(2)}, u32[]{:S(2)}) %collective-permute-start.6) | collective-permute-done | bytes 940832 | tf_op jit(solution)/shard_map/ppermute | solution.py:861
  111.8 28.4 %collective-permute-done.10.refs_4_ = bf16[420,1120]{1,0:T(8,128)(2,1)} collective-permute-done((bf16[420,1120]{1,0:T(8,128)(2,1)S(1)}, bf16[420,1120]{1,0:T(8,128)(2,1)}, u32[]{:S(2)}, u32[]{:S(2)}) %collective-permute-start.10) | collective-permute-done | bytes 940832 | tf_op jit(solution)/shard_map/ppermute | solution.py:861
  143.5 3.4 collective-permute-start.14
  151.8 3.4 collective-permute-start.16
  155.2 16.6 %project.1 = (bf16[2048,840]{1,0:T(8,128)(2,1)}, bf16[2048,840]{1,0:T(8,128)(2,1)}, bf16[2048,1120]{1,0:T(8,128)(2,1)}, bf16[1120,840]{1,0:T(8,128)(2,1)S(1)}, bf16[1120,840]{1,0:T(8,128)(2,1)}) custom-call(s32[1]{0:T(128)} %bitcast.4.place_ref, bf16[1024,1152]{1,0:T(8,128)(2,1)} %pad.22.own_ref, bf16[1024,1152]{1,0:T(8,128)(2,1)} %collective-permute-done.5.other_ref, ...), custom_call_target="tpu_custom_call" | custom-call | flops 16000000000 | bytes 4096 | tf_op jit(solution)/shard_map/project/pallas_call | solution.py:586
  173.1 34.9 %attention_forward.2 = (bf16[2048,280]{1,0:T(8,128)(2,1)S(1)}, f32[4,280,512]{2,1,0:T(8,128)S(1)}, f32[4,8,512]{2,1,0:T(8,128)S(1)}) custom-call(s32[4]{0:T(128)S(1)} %and_select_fusion.low_ref, s32[1]{0:T(128)} %bitcast.7.core_ref, s32[4,1,512]{2,1,0:T(1,128)S(1)} %compare_select_fusion.start_ref, bf16[2048,840]{1,0:T(8,128)(2,1)} %get-tuple-element.175.qkv_ref), custom_call_target="tpu_custom_call" | custom-call | flops 35000000512 | bytes 4096 | tf_op jit(solution)/shard_map/attention_forward/pallas_call | solution.py:260
  215.8 3.9 collective-permute-start.20
  219.8 3.9 collective-permute-start.21
  230.2 34.7 %attention_forward.3 = (bf16[2048,280]{1,0:T(8,128)(2,1)S(1)}, f32[4,280,512]{2,1,0:T(8,128)S(1)}, f32[4,8,512]{2,1,0:T(8,128)S(1)}) custom-call(s32[4]{0:T(128)S(1)} %and_select_fusion.low_ref, s32[1]{0:T(128)} %bitcast.7.core_ref, s32[4,1,512]{2,1,0:T(1,128)S(1)} %compare_select_fusion.start_ref, bf16[2048,840]{1,0:T(8,128)(2,1)} %get-tuple-element.180.qkv_ref), custom_call_target="tpu_custom_call" | custom-call | flops 35000000512 | bytes 4096 | tf_op jit(solution)/shard_map/attention_forward/pallas_call | solution.py:260
  273.8 5.7 unpack_share.2
  279.5 3.9 collective-permute-done.17
  285.1 7.4 collective-permute-done.22.refs_7_
  293.4 5.6 unpack_share.3
  299.1 8.8 %split_product.2 = (f32[1024,1152]{1,0:T(8,128)}, f32[1024,1120]{1,0:T(8,128)}) custom-call(bf16[2048,280]{1,0:T(8,128)(2,1)S(1)} %get-tuple-element.181.refs_0_, bf16[2048,280]{1,0:T(8,128)(2,1)S(1)} %copy-done.21, bf16[280,1120]{1,0:T(8,128)(2,1)S(1)} %get-tuple-element.198.refs_2_.w_a, bf16[280,1120]{1,0:T(8,128)(2,1)S(1)} %get-tuple-element.206.refs_3_.w_b), custom_call_target="tpu_custom_call" | custom-call | flops 8999999488 | bytes 4096 | tf_op jit(solution)/shard_map/split_product/pallas_call | solution.py:693
  308.7 10.7 %collective-permute-done.23.got_ref = f32[1024,1152]{1,0:T(8,128)S(1)} collective-permute-done((f32[1024,1152]{1,0:T(8,128)}, f32[1024,1152]{1,0:T(8,128)S(1)}, u32[]{:S(2)}, u32[]{:S(2)}) %collective-permute-start.23) | collective-permute-done | bytes 4718624 | tf_op jit(solution)/shard_map/ppermute | solution.py:861
  325.2 3.1 collective-permute-done.24.rows_ref
  329.7 34.3 %feed_forward.2 = (bf16[2048,1120]{1,0:T(8,128)(2,1)}, bf16[2048,1120]{1,0:T(8,128)(2,1)}, bf16[2048,1120]{1,0:T(8,128)(2,1)}, bf16[2048,1120]{1,0:T(8,128)(2,1)...) custom-call(bf16[1024,1152]{1,0:T(8,128)(2,1)} %copy-done.66, ...), custom_call_target="tpu_custom_call" | custom-call | flops 33999998976 | bytes 4096 | tf_op jit(solution)/shard_map/feed_forward/pallas_call | solution.py:838
  365.4 34.9 %feed_forward.3 = (bf16[2048,1120]{1,0:T(8,128)(2,1)}, bf16[2048,1120]{1,0:T(8,128)(2,1)}, bf16[2048,1120]{1,0:T(8,128)(2,1)}, bf16[2048,1120]{1,0:T(8,128)(2,1)...) custom-call(bf16[1024,1152]{1,0:T(8,128)(2,1)} %copy-done.11, ...), custom_call_target="tpu_custom_call", output_to_operand_aliasing={{0}: (7, {}), {1}: (8, {}), {2}: (9, {}), {3}: (10, {}), {4... | custom-call | flops 33999998976 | bytes 4096 | tf_op jit(solution)/shard_map/feed_forward/pallas_call | solution.py:838
  402.7 7.8 norm_back.2
  410.6 11.8 %convolution_convert_fusion = bf16[1120,1120]{1,0:T(8,128)(2,1)} fusion(bf16[2048,1120]{1,0:T(8,128)(2,1)S(1)} %copy-done.68, bf16[2048,1120]{1,0:T(8,128)(2,1)} %get-tuple-element.233), kind=kOutput, calls=%fused_computation | convolution fusion | flops 5139276800 | bytes 11683840 | tf_op jit(solution)/shard_map/dot_general | solution.py:39
  422.5 7.7 convolution_convert_fusion.1
  431.6 3.0 fusion.24
  434.9 5.8 fusion.8
  445.0 7.9 out_grads.1
  453.0 5.2 convolution_convert_fusion.3
  460.7 8.6 fusion.45.in_ref
  469.3 8.6 %fusion.44.back_ref = f32[1120,1120]{1,0:T(8,128)} fusion(bf16[2048,1120]{1,0:T(8,128)(2,1)S(1)} %bitcast.77, bf16[2048,1120]{1,0:T(8,128)(2,1)S(1)} %bitcast.85), kind=kOutput, calls=%fused_computation.141 | convolution fusion | flops 5138022400 | bytes 14192640 | tf_op jit(solution)/shard_map/dot_general | solution.py:39
  477.9 56.1 %attention_backward.2.left = bf16[2048,896]{1,0:T(8,128)(2,1)} custom-call(s32[4]{0:T(128)} %copy-done.18, s32[1]{0:T(128)} %bitcast.7.core_ref, s32[4,1,512]{2,1,0:T(1,128)} %copy-done.10, bf16[2048,840]{1,0:T(8,128)(2,1)} %get-tuple-element.180.qkv_ref, bf16[2048,280]{1,0:T(8,128)(2,1)} %copy-done.30, f32[4,280,512]{2,1,0:T(8,128)} %copy-done.32, ...), custom_call_target="tpu_custom_call" | custom-call | flops 56000000000 | bytes 4096 | tf_op jit(solution)/shard_map/attention_backward/pallas_call | solution.py:303
  534.0 9.9 %convolution_convert_fusion.2 = bf16[1120,896]{1,0:T(8,128)(2,1)} fusion(bf16[2048,1120]{1,0:T(8,128)(2,1)} %get-tuple-element.174, bf16[2048,896]{1,0:T(8,128)(2,1)} %attention_backward.2.left), kind=kOutput, calls=%fused_computation.20 | convolution fusion | flops 4111421440 | bytes 10264576 | tf_op jit(solution)/shard_map/dot_general | solution.py:39
  543.9 7.6 partial_product.1.refs_2_
  554.2 2.6 collective-permute-done.31.back_got
  556.7 13.7 %collective-permute-done.29.out_got = bf16[280,1120]{1,0:T(8,128)(2,1)S(1)} collective-permute-done((bf16[280,1120]{1,0:T(8,128)(2,1)S(1)}, bf16[280,1120]{1,0:T(8,128)(2,1)S(1)}, u32[]{:S(2)}, u32[]{:S(2)}) %collective-permute-start.29) | collective-permute-done | bytes 627232 | tf_op jit(solution)/shard_map/ppermute | solution.py:861
  570.5 10.4 %pack_rest.1 = (f32[3,420,1120]{2,1,0:T(8,128)}, bf16[3,420,1120]{2,1,0:T(8,128)(2,1)}) custom-call(s32[1]{0:T(128)} %bitcast.4.place_ref, f32[280,1120]{1,0:T(8,128)S(1)} %fusion.46.out_ref, f32[1120,1120]{1,0:T(8,128)} %fusion.45.in_ref, f32[1120,1120]{1,0:T(8,128)} %fusion.44.back_ref, bf16[280,1120]{1,0:T(8,128)(2,1)S(1)} %collective-permute-done.29.out_got, ...), custom_call_target="tpu_custom_call" | custom-call | flops 10000000000 | bytes 4096 | tf_op jit(solution)/shard_map/pack_rest/pallas_call | solution.py:525
  582.9 55.9 %attention_backward.3.refs_0_ = bf16[2048,896]{1,0:T(8,128)(2,1)} custom-call(s32[4]{0:T(128)} %copy-done.18, s32[1]{0:T(128)} %bitcast.7.core_ref, s32[4,1,512]{2,1,0:T(1,128)} %copy-done.10, bf16[2048,840]{1,0:T(8,128)(2,1)} %get-tuple-element.175.qkv_ref, bf16[2048,280]{1,0:T(8,128)(2,1)} %copy-done.29, f32[4,280,512]{2,1,0:T(8,128)} %copy-done.31, ...), custom_call_target="tpu_custom_call" | custom-call | flops 56000000000 | bytes 4096 | tf_op jit(solution)/shard_map/attention_backward/pallas_call | solution.py:303
  638.8 11.1 %split_product.3 = (bf16[1024,1152]{1,0:T(8,128)(2,1)S(1)}, f32[1024,1120]{1,0:T(8,128)}) custom-call(bf16[2048,896]{1,0:T(8,128)(2,1)} %attention_backward.3.refs_0_, bf16[1120,840]{1,0:T(8,128)(2,1)S(1)} %copy-done.25, f32[2048,1120]{1,0:T(8,128)} %partial_product.1.refs_2_), custom_call_target="tpu_custom_call" | custom-call | flops 8999999488 | bytes 4096 | tf_op jit(solution)/shard_map/split_product/pallas_call | solution.py:693
  651.8 9.1 %convert_add_fusion = f32[1120,896]{1,0:T(8,128)S(1)} fusion(bf16[1120,896]{1,0:T(8,128)(2,1)} %collective-permute-done.33, bf16[2048,1120]{1,0:T(8,128)(2,1)} %get-tuple-element.174, bf16[2048,896]{1,0:T(8,128)(2,1)} %attention_backward.3.refs_0_), kind=kOutput, calls=%fused_computation.19 | convolution fusion | flops 4112424960 | bytes 14278656 | tf_op jit(solution)/shard_map/dot_general | solution.py:39
  661.5 4.8 fusion.33
  668.5 17.5 %collective-permute-done.36 = bf16[560,896]{1,0:T(8,128)(2,1)S(1)} collective-permute-done((bf16[560,896]{1,0:T(8,128)(2,1)S(1)}, bf16[560,896]{1,0:T(8,128)(2,1)S(1)}, u32[]{:S(2)}, u32[]{:S(2)}) %collective-permute-start.36) | collective-permute-done | bytes 1003552 | tf_op jit(solution)/shard_map/ppermute | solution.py:861
  690.6 6.6 norm_back.3
  699.2 35.6 %collective-permute-done.39 = bf16[560,896]{1,0:T(8,128)(2,1)S(1)} collective-permute-done((bf16[560,896]{1,0:T(8,128)(2,1)S(1)}, bf16[560,896]{1,0:T(8,128)(2,1)S(1)}, u32[]{:S(2)}, u32[]{:S(2)}) %collective-permute-start.39) | collective-permute-done | bytes 1003552 | tf_op jit(solution)/shard_map/ppermute | solution.py:861
  739.4 2.6 select_convert_fusion.1
  742.0 6.8 collective-permute-start.43
  752.0 18.0 %collective-permute-done.43 = bf16[420,1120]{1,0:T(8,128)(2,1)S(1)} collective-permute-done((bf16[420,1120]{1,0:T(8,128)(2,1)S(1)}, bf16[420,1120]{1,0:T(8,128)(2,1)S(1)}, u32[]{:S(2)}, u32[]{:S(2)}) %collective-permute-start.43) | collective-permute-done | bytes 940832 | tf_op jit(solution)/shard_map/ppermute | solution.py:861
  770.0 3.2 convert_add_fusion.3
  773.2 4.3 reshape.199.rest_ref
  777.5 9.5 %collective-permute-done.45 = bf16[560,896]{1,0:T(8,128)(2,1)} collective-permute-done((bf16[560,896]{1,0:T(8,128)(2,1)}, bf16[560,896]{1,0:T(8,128)(2,1)}, u32[]{:S(2)}, u32[]{:S(2)}) %collective-permute-start.45) | collective-permute-done | bytes 1003552 | tf_op jit(solution)/shard_map/ppermute | solution.py:861
  786.9 3.3 slice_add_fusion.1
  790.2 6.0 reshape.202.lead_ref
  797.8 10.4 %new_moments.1 = (f32[1,1,470400]{2,1,0:T(1,128)}, f32[2,1,1,470400]{3,2,1,0:T(1,128)}, f32[1,1,470400]{2,1,0:T(1,128)S(1)}, f32[2]{0:T(128)S(1)}) custom-call(s32[2]{0:T(128)S(1)} %pad_add_fusion.ints_ref, f32[2]{0:T(128)S(1)} %pad_maximum_fusion.8.floats_ref, f32[1,1,470400]{2,1,0:T(1,128)S(1)} %copy-done.7, f32[1,1,470400]{2,1,0:T(1,128)S(1)} %reshape.199.rest_ref, ...), custom_call_target="tpu_custom_call" | custom-call | flops 10000000000 | bytes 4096 | tf_op jit(solution)/shard_map/new_moments/pallas_call | solution.py:406
  814.0 4.3 collective-permute-done.47
  818.7 4.1 collective-permute-done.48
  822.8 7.4 collective-permute-start.49
  832.5 3.8 collective-permute-start.50
  836.3 4.3 copy.53
  840.6 4.4 copy.54
  850.6 6.5 new_weights.1
  (345 shorter events, 126.7 us)
Async XLA Ops:
  1.5 428.9 %copy-start.8 = (f32[12,1120]{1,0:T(8,128)}, f32[12,1120]{1,0:T(8,128)S(1)}, u32[]{:S(2)}) copy-start(f32[12,1120]{1,0:T(8,128)S(1)} %copy.71.small_ref) | copy-start | bytes 161284
  20.0 29.2 %collective-permute-start = (bf16[512,1152]{1,0:T(8,128)(2,1)}, bf16[512,1152]{1,0:T(8,128)(2,1)}, u32[]{:S(2)}, u32[]{:S(2)}) collective-permute-start(bf16[512,1152]{1,0:T(8,128)(2,1)} %pad.21), channel_id=1, source_target_pairs={{0,2},{1,3},{2,0},{3,1},{4,6},{5,7},{6,4},{7,5},{8,10},{9,11},{10,... | collective-permute-start | bytes 3538952 | tf_op jit(solution)/shard_map/ppermute | solution.py:861
  25.7 30.3 %collective-permute-start.1 = (bf16[560,840]{1,0:T(8,128)(2,1)}, bf16[560,840]{1,0:T(8,128)(2,1)}, u32[]{:S(2)}, u32[]{:S(2)}) collective-permute-start(bf16[560,840]{1,0:T(8,128)(2,1)} %reshape.195), channel_id=1, source_target_pairs={{0,16},{4,20},{1,17},{5,21},{2,18},{6,22},{3,19},{7,23}} | collective-permute-start | bytes 2822408 | tf_op jit(solution)/shard_map/ppermute | solution.py:861
  56.0 29.9 %collective-permute-start.5 = (bf16[1024,1152]{1,0:T(8,128)(2,1)}, bf16[1024,1152]{1,0:T(8,128)(2,1)}, u32[]{:S(2)}, u32[]{:S(2)}) collective-permute-start(bf16[1024,1152]{1,0:T(8,128)(2,1)} %pad.22.own_ref), channel_id=1, source_target_pairs={{0,1},{1,0},{2,3},{3,2},{4,5},{5,4},{6,7},{7,6},{8,9},{9,8},{10,11... | collective-permute-start | bytes 7077896 | tf_op jit(solution)/shard_map/ppermute | solution.py:861
  58.2 53.2 %copy-start.63 = (s32[2,1,11]{2,1,0:T(1,128)S(1)}, s32[2,1,11]{2,1,0:T(1,128)}, u32[]{:S(2)}) copy-start(s32[2,1,11]{2,1,0:T(1,128)} %param.15) | copy-start | bytes 268
  58.2 53.2 %copy-start.64 = (s32[2,1,11]{2,1,0:T(1,128)S(1)}, s32[2,1,11]{2,1,0:T(1,128)}, u32[]{:S(2)}) copy-start(s32[2,1,11]{2,1,0:T(1,128)} %param.16) | copy-start | bytes 268
  58.2 26.3 %collective-permute-start.2 = (bf16[560,840]{1,0:T(8,128)(2,1)}, bf16[560,840]{1,0:T(8,128)(2,1)}, u32[]{:S(2)}, u32[]{:S(2)}) collective-permute-start(bf16[560,840]{1,0:T(8,128)(2,1)} %broadcast_select_fusion.2), channel_id=1, source_target_pairs={{0,8},{4,12},{16,24},{20,28},{1,9},{5,13},{17,25},{21,29},{2,10},{... | collective-permute-start | bytes 2822408 | tf_op jit(solution)/shard_map/ppermute | solution.py:861
  64.6 21.2 %collective-permute-start.3 = (bf16[420,1120]{1,0:T(8,128)(2,1)S(1)}, bf16[420,1120]{1,0:T(8,128)(2,1)}, u32[]{:S(2)}, u32[]{:S(2)}) collective-permute-start(bf16[420,1120]{1,0:T(8,128)(2,1)S(1)} %reshape.196.refs_0_), channel_id=1, source_target_pairs={{8,12},{9,13},{10,14},{11,15},{12,8},{13,9},{14,10},{15,11},{16,20... | collective-permute-start | bytes 2822408 | tf_op jit(solution)/shard_map/ppermute | solution.py:861
  66.3 19.6 %collective-permute-start.4 = (bf16[420,1120]{1,0:T(8,128)(2,1)S(1)}, bf16[420,1120]{1,0:T(8,128)(2,1)}, u32[]{:S(2)}, u32[]{:S(2)}) collective-permute-start(bf16[420,1120]{1,0:T(8,128)(2,1)S(1)} %reshape.196.refs_0_), channel_id=1, source_target_pairs={{8,10},{9,11},{10,8},{11,9},{12,14},{13,15},{14,12},{15,13},{16,18... | collective-permute-start | bytes 2822408 | tf_op jit(solution)/shard_map/ppermute | solution.py:861
  85.9 24.0 %collective-permute-start.6 = (bf16[560,840]{1,0:T(8,128)(2,1)S(1)}, bf16[560,840]{1,0:T(8,128)(2,1)}, u32[]{:S(2)}, u32[]{:S(2)}) collective-permute-start(bf16[560,840]{1,0:T(8,128)(2,1)S(1)} %broadcast_select_fusion.3.a0), channel_id=1, source_target_pairs={{0,4},{4,0},{8,12},{12,8},{16,20},{20,16},{24,28},{28,24},{1,5},{5... | collective-permute-start | bytes 2822408 | tf_op jit(solution)/shard_map/ppermute | solution.py:861
  87.6 24.3 %collective-permute-start.7 = (bf16[560,840]{1,0:T(8,128)(2,1)S(1)}, bf16[560,840]{1,0:T(8,128)(2,1)}, u32[]{:S(2)}, u32[]{:S(2)}) collective-permute-start(bf16[560,840]{1,0:T(8,128)(2,1)S(1)} %broadcast_select_fusion.3.a0), channel_id=1, source_target_pairs={{0,2},{1,3},{2,0},{3,1},{4,6},{5,7},{6,4},{7,5},{8,10},{9,11},{10,... | collective-permute-start | bytes 2822408 | tf_op jit(solution)/shard_map/ppermute | solution.py:861
  89.1 51.1 %collective-permute-start.10 = (bf16[420,1120]{1,0:T(8,128)(2,1)S(1)}, bf16[420,1120]{1,0:T(8,128)(2,1)}, u32[]{:S(2)}, u32[]{:S(2)}) collective-permute-start(bf16[420,1120]{1,0:T(8,128)(2,1)S(1)} %reshape.196.refs_0_), channel_id=1, source_target_pairs={{8,24},{9,25},{10,26},{11,27},{12,28},{13,29},{14,30},{15,31},{16,... | collective-permute-start | bytes 2822408 | tf_op jit(solution)/shard_map/ppermute | solution.py:861
  90.4 51.1 %collective-permute-start.9 = (bf16[420,1120]{1,0:T(8,128)(2,1)S(1)}, bf16[420,1120]{1,0:T(8,128)(2,1)}, u32[]{:S(2)}, u32[]{:S(2)}) collective-permute-start(bf16[420,1120]{1,0:T(8,128)(2,1)S(1)} %reshape.196.refs_0_), channel_id=1, source_target_pairs={{8,0},{9,1},{10,2},{11,3},{12,4},{13,5},{14,6},{15,7},{16,24},{17,... | collective-permute-start | bytes 2822408 | tf_op jit(solution)/shard_map/ppermute | solution.py:861
  91.7 48.5 %collective-permute-start.11 = (bf16[420,1120]{1,0:T(8,128)(2,1)}, bf16[420,1120]{1,0:T(8,128)(2,1)}, u32[]{:S(2)}, u32[]{:S(2)}) collective-permute-start(bf16[420,1120]{1,0:T(8,128)(2,1)} %collective-permute-done.4.refs_0_), channel_id=1, source_target_pairs={{8,12},{9,13},{10,14},{11,15},{12,8},{13,9},{14,10},{15,11},{16,20... | collective-permute-start | bytes 2822408 | tf_op jit(solution)/shard_map/ppermute | solution.py:861
  109.9 31.7 %collective-permute-start.8 = (bf16[560,840]{1,0:T(8,128)(2,1)}, bf16[560,840]{1,0:T(8,128)(2,1)}, u32[]{:S(2)}, u32[]{:S(2)}) collective-permute-start(bf16[560,840]{1,0:T(8,128)(2,1)} %collective-permute-done.6.a1), channel_id=1, source_target_pairs={{0,2},{1,3},{2,0},{3,1},{4,6},{5,7},{6,4},{7,5},{8,10},{9,11},{10,... | collective-permute-start | bytes 2822408 | tf_op jit(solution)/shard_map/ppermute | solution.py:861
  111.8 118.4 %copy-start.18 = (s32[4]{0:T(128)}, s32[4]{0:T(128)S(1)}, u32[]{:S(2)}) copy-start(s32[4]{0:T(128)S(1)} %and_select_fusion.low_ref) | copy-start | bytes 52
  111.8 118.3 %copy-start.10 = (s32[4,1,512]{2,1,0:T(1,128)}, s32[4,1,512]{2,1,0:T(1,128)S(1)}, u32[]{:S(2)}) copy-start(s32[4,1,512]{2,1,0:T(1,128)S(1)} %compare_select_fusion.start_ref) | copy-start | bytes 24580
  141.5 68.5 %collective-permute-start.12 = (bf16[420,1120]{1,0:T(8,128)(2,1)}, bf16[420,1120]{1,0:T(8,128)(2,1)}, u32[]{:S(2)}, u32[]{:S(2)}) collective-permute-start(bf16[420,1120]{1,0:T(8,128)(2,1)} %collective-permute-done.10.refs_4_), channel_id=1, source_target_pairs={{0,8},{1,9},{2,10},{3,11},{4,12},{5,13},{6,14},{7,15},{8,0},{9,1},... | collective-permute-start | bytes 2822408 | tf_op jit(solution)/shard_map/ppermute | solution.py:861
  143.5 67.5 %collective-permute-start.14 = (bf16[420,1120]{1,0:T(8,128)(2,1)}, bf16[420,1120]{1,0:T(8,128)(2,1)}, u32[]{:S(2)}, u32[]{:S(2)}) collective-permute-start(bf16[420,1120]{1,0:T(8,128)(2,1)} %collective-permute-done.10.refs_4_), channel_id=1, source_target_pairs={{0,4},{1,5},{2,6},{3,7},{4,0},{5,1},{6,2},{7,3},{8,12},{9,13},{10,... | collective-permute-start | bytes 2822408 | tf_op jit(solution)/shard_map/ppermute | solution.py:861
  146.9 63.1 %collective-permute-start.13 = (bf16[420,1120]{1,0:T(8,128)(2,1)}, bf16[420,1120]{1,0:T(8,128)(2,1)S(1)}, u32[]{:S(2)}, u32[]{:S(2)}) collective-permute-start(bf16[420,1120]{1,0:T(8,128)(2,1)} %collective-permute-done.9.refs_2_), channel_id=1, source_target_pairs={{0,4},{1,5},{2,6},{3,7},{4,0},{5,1},{6,2},{7,3},{16,20},{17,21},{1... | collective-permute-start | bytes 2822408 | tf_op jit(solution)/shard_map/ppermute | solution.py:861
  149.3 61.7 %collective-permute-start.15 = (bf16[420,1120]{1,0:T(8,128)(2,1)}, bf16[420,1120]{1,0:T(8,128)(2,1)}, u32[]{:S(2)}, u32[]{:S(2)}) collective-permute-start(bf16[420,1120]{1,0:T(8,128)(2,1)} %collective-permute-done.9.refs_2_), channel_id=1, source_target_pairs={{0,2},{1,3},{2,0},{3,1},{4,6},{5,7},{6,4},{7,5},{16,18},{17,19},{1... | collective-permute-start | bytes 2822408 | tf_op jit(solution)/shard_map/ppermute | solution.py:861
  151.8 59.2 %collective-permute-start.16 = (bf16[420,1120]{1,0:T(8,128)(2,1)}, bf16[420,1120]{1,0:T(8,128)(2,1)S(1)}, u32[]{:S(2)}, u32[]{:S(2)}) collective-permute-start(bf16[420,1120]{1,0:T(8,128)(2,1)} %collective-permute-done.10.refs_4_), channel_id=1, source_target_pairs={{0,2},{1,3},{2,0},{3,1},{4,6},{5,7},{6,4},{7,5},{8,10},{9,11},{10,... | collective-permute-start | bytes 2822408 | tf_op jit(solution)/shard_map/ppermute | solution.py:861
  173.1 50.6 %copy-start.49 = (bf16[2,1,512,1120]{2,3,1,0:T(8,128)(2,1)S(1)}, bf16[2,1,512,1120]{2,3,1,0:T(8,128)(2,1)}, u32[]{:S(2)}) copy-start(bf16[2,1,512,1120]{2,3,1,0:T(8,128)(2,1)} %param.14) | copy-start | bytes 6881284
  212.0 58.5 %collective-permute-start.18 = (bf16[420,1120]{1,0:T(8,128)(2,1)}, bf16[420,1120]{1,0:T(8,128)(2,1)}, u32[]{:S(2)}, u32[]{:S(2)}) collective-permute-start(bf16[420,1120]{1,0:T(8,128)(2,1)} %collective-permute-done.12.refs_6_), channel_id=1, source_target_pairs={{0,4},{1,5},{2,6},{3,7},{4,0},{5,1},{6,2},{7,3},{8,12},{9,13},{10,... | collective-permute-start | bytes 2822408 | tf_op jit(solution)/shard_map/ppermute | solution.py:861
  213.9 56.5 %collective-permute-start.19 = (bf16[420,1120]{1,0:T(8,128)(2,1)}, bf16[420,1120]{1,0:T(8,128)(2,1)}, u32[]{:S(2)}, u32[]{:S(2)}) collective-permute-start(bf16[420,1120]{1,0:T(8,128)(2,1)} %collective-permute-done.12.refs_6_), channel_id=1, source_target_pairs={{0,2},{1,3},{2,0},{3,1},{4,6},{5,7},{6,4},{7,5},{8,10},{9,11},{10,... | collective-permute-start | bytes 2822408 | tf_op jit(solution)/shard_map/ppermute | solution.py:861
  215.8 54.6 %collective-permute-start.20 = (bf16[420,1120]{1,0:T(8,128)(2,1)}, bf16[420,1120]{1,0:T(8,128)(2,1)}, u32[]{:S(2)}, u32[]{:S(2)}) collective-permute-start(bf16[420,1120]{1,0:T(8,128)(2,1)} %collective-permute-done.15.refs_2_), channel_id=1, source_target_pairs={{0,4},{1,5},{2,6},{3,7},{4,0},{5,1},{6,2},{7,3},{16,20},{17,21},{1... | collective-permute-start | bytes 2822408 | tf_op jit(solution)/shard_map/ppermute | solution.py:861
  219.8 50.7 %collective-permute-start.21 = (bf16[420,1120]{1,0:T(8,128)(2,1)}, bf16[420,1120]{1,0:T(8,128)(2,1)}, u32[]{:S(2)}, u32[]{:S(2)}) collective-permute-start(bf16[420,1120]{1,0:T(8,128)(2,1)} %collective-permute-done.14.refs_5_), channel_id=1, source_target_pairs={{0,2},{1,3},{2,0},{3,1},{4,6},{5,7},{6,4},{7,5},{8,10},{9,11},{10,... | collective-permute-start | bytes 2822408 | tf_op jit(solution)/shard_map/ppermute | solution.py:861
  230.1 53.2 %collective-permute-start.17 = (bf16[512,1152]{1,0:T(8,128)(2,1)}, bf16[512,1152]{1,0:T(8,128)(2,1)}, u32[]{:S(2)}, u32[]{:S(2)}) collective-permute-start(bf16[512,1152]{1,0:T(8,128)(2,1)} %pad.23), channel_id=1, source_target_pairs={{0,2},{1,3},{2,0},{3,1},{4,6},{5,7},{6,4},{7,5},{8,10},{9,11},{10,... | collective-permute-start | bytes 3538952 | tf_op jit(solution)/shard_map/ppermute | solution.py:861
  270.5 22.0 %collective-permute-start.22 = (bf16[420,1120]{1,0:T(8,128)(2,1)}, bf16[420,1120]{1,0:T(8,128)(2,1)S(1)}, u32[]{:S(2)}, u32[]{:S(2)}) collective-permute-start(bf16[420,1120]{1,0:T(8,128)(2,1)} %collective-permute-done.19.refs_6_), channel_id=1, source_target_pairs={{0,4},{1,5},{2,6},{3,7},{4,0},{5,1},{6,2},{7,3},{8,12},{9,13},{10,... | collective-permute-start | bytes 2822408 | tf_op jit(solution)/shard_map/ppermute | solution.py:861
  307.9 11.5 %collective-permute-start.23 = (f32[1024,1152]{1,0:T(8,128)}, f32[1024,1152]{1,0:T(8,128)S(1)}, u32[]{:S(2)}, u32[]{:S(2)}) collective-permute-start(f32[1024,1152]{1,0:T(8,128)} %get-tuple-element.208), channel_id=1, source_target_pairs={{0,1},{1,0},{2,3},{3,2},{4,5},{5,4},{6,7},{7,6},{8,9},{9,8},{10,11... | collective-permute-start | bytes 14155784 | tf_op jit(solution)/shard_map/ppermute | solution.py:861
  308.1 16.5 %collective-permute-start.25 = (bf16[1024,1152]{1,0:T(8,128)(2,1)S(1)}, bf16[1024,1152]{1,0:T(8,128)(2,1)S(1)}, u32[]{:S(2)}, u32[]{:S(2)}) collective-permute-start(bf16[1024,1152]{1,0:T(8,128)(2,1)S(1)} %fusion.11.cot_ref.base_ref), channel_id=1, source_target_pairs={{0,1},{1,0},{2,3},{3,2},{4,5},{5,4},{6,7},{7,6},{8,9},{9,8},{10,11... | collective-permute-start | bytes 7077896 | tf_op jit(solution)/shard_map/ppermute | solution.py:861
  323.7 4.5 collective-permute-start.24
  364.0 36.3 %collective-permute-start.26 = (f32[1024,1152]{1,0:T(8,128)}, f32[1024,1152]{1,0:T(8,128)}, u32[]{:S(2)}, u32[]{:S(2)}) collective-permute-start(f32[1024,1152]{1,0:T(8,128)} %get-tuple-element.225), channel_id=1, source_target_pairs={{0,1},{1,0},{2,3},{3,2},{4,5},{5,4},{6,7},{7,6},{8,9},{9,8},{10,11... | collective-permute-start | bytes 14155784 | tf_op jit(solution)/shard_map/ppermute | solution.py:861
  364.2 36.1 %collective-permute-start.27 = (f32[1024,1152]{1,0:T(8,128)}, f32[1024,1152]{1,0:T(8,128)}, u32[]{:S(2)}, u32[]{:S(2)}) collective-permute-start(f32[1024,1152]{1,0:T(8,128)} %get-tuple-element.226), channel_id=1, source_target_pairs={{0,1},{1,0},{2,3},{3,2},{4,5},{5,4},{6,7},{7,6},{8,9},{9,8},{10,11... | collective-permute-start | bytes 14155784 | tf_op jit(solution)/shard_map/ppermute | solution.py:861
  365.4 35.0 %copy-start.6 = (bf16[1024,1152]{1,0:T(8,128)(2,1)S(1)}, bf16[1024,1152]{1,0:T(8,128)(2,1)}, u32[]{:S(2)}) copy-start(bf16[1024,1152]{1,0:T(8,128)(2,1)} %copy-done.5) | copy-start | bytes 7077892
  430.2 14.7 %collective-permute-start.28 = (bf16[1024,1152]{1,0:T(8,128)(2,1)}, bf16[1024,1152]{1,0:T(8,128)(2,1)}, u32[]{:S(2)}, u32[]{:S(2)}) collective-permute-start(bf16[1024,1152]{1,0:T(8,128)(2,1)} %get-tuple-element.235.own_ref), channel_id=1, source_target_pairs={{0,1},{1,0},{2,3},{3,2},{4,5},{5,4},{6,7},{7,6},{8,9},{9,8},{10,11... | collective-permute-start | bytes 7077896 | tf_op jit(solution)/shard_map/ppermute | solution.py:861
  442.3 111.9 %collective-permute-start.30 = (bf16[1120,1120]{1,0:T(8,128)(2,1)}, bf16[1120,1120]{1,0:T(8,128)(2,1)}, u32[]{:S(2)}, u32[]{:S(2)}) collective-permute-start(bf16[1120,1120]{1,0:T(8,128)(2,1)} %convolution_convert_fusion), channel_id=1, source_target_pairs={{0,2},{1,3},{2,0},{3,1},{4,6},{5,7},{6,4},{7,5},{8,10},{9,11},{10,... | collective-permute-start | bytes 7526408 | tf_op jit(solution)/shard_map/ppermute | solution.py:861
  442.3 114.4 %collective-permute-start.31 = (bf16[1120,1120]{1,0:T(8,128)(2,1)}, bf16[1120,1120]{1,0:T(8,128)(2,1)}, u32[]{:S(2)}, u32[]{:S(2)}) collective-permute-start(bf16[1120,1120]{1,0:T(8,128)(2,1)} %convolution_convert_fusion.1), channel_id=1, source_target_pairs={{0,2},{1,3},{2,0},{3,1},{4,6},{5,7},{6,4},{7,5},{8,10},{9,11},{10,... | collective-permute-start | bytes 7526408 | tf_op jit(solution)/shard_map/ppermute | solution.py:861
  543.9 26.6 %collective-permute-start.29 = (bf16[280,1120]{1,0:T(8,128)(2,1)S(1)}, bf16[280,1120]{1,0:T(8,128)(2,1)S(1)}, u32[]{:S(2)}, u32[]{:S(2)}) collective-permute-start(bf16[280,1120]{1,0:T(8,128)(2,1)S(1)} %convolution_convert_fusion.3), channel_id=1, source_target_pairs={{0,2},{1,3},{2,0},{3,1},{4,6},{5,7},{6,4},{7,5},{8,10},{9,11},{10,... | collective-permute-start | bytes 1881608 | tf_op jit(solution)/shard_map/ppermute | solution.py:861
  552.1 99.7 %collective-permute-start.33 = (bf16[1120,896]{1,0:T(8,128)(2,1)}, bf16[1120,896]{1,0:T(8,128)(2,1)}, u32[]{:S(2)}, u32[]{:S(2)}) collective-permute-start(bf16[1120,896]{1,0:T(8,128)(2,1)} %convolution_convert_fusion.2), channel_id=1, source_target_pairs={{0,2},{1,3},{2,0},{3,1},{4,6},{5,7},{6,4},{7,5},{8,10},{9,11},{10,... | collective-permute-start | bytes 6021128 | tf_op jit(solution)/shard_map/ppermute | solution.py:861
  582.7 56.1 %collective-permute-start.32 = (bf16[512,1152]{1,0:T(8,128)(2,1)}, bf16[512,1152]{1,0:T(8,128)(2,1)S(1)}, u32[]{:S(2)}, u32[]{:S(2)}) collective-permute-start(bf16[512,1152]{1,0:T(8,128)(2,1)} %get-tuple-element.385), channel_id=1, source_target_pairs={{0,2},{1,3},{2,0},{3,1},{4,6},{5,7},{6,4},{7,5},{8,10},{9,11},{10,... | collective-permute-start | bytes 3538952 | tf_op jit(solution)/shard_map/ppermute | solution.py:861
  582.8 78.6 %collective-permute-start.34 = (bf16[3,420,1120]{2,1,0:T(8,128)(2,1)}, bf16[3,420,1120]{2,1,0:T(8,128)(2,1)}, u32[]{:S(2)}, u32[]{:S(2)}) collective-permute-start(bf16[3,420,1120]{2,1,0:T(8,128)(2,1)} %get-tuple-element.270), channel_id=1, source_target_pairs={{0,4},{4,0},{8,12},{12,8},{16,20},{20,16},{24,28},{28,24},{1,5},{5... | collective-permute-start | bytes 8467208 | tf_op jit(solution)/shard_map/ppermute | solution.py:861
  582.9 55.9 %copy-start.25 = (bf16[1120,840]{1,0:T(8,128)(2,1)S(1)}, bf16[1120,840]{1,0:T(8,128)(2,1)}, u32[]{:S(2)}) copy-start(bf16[1120,840]{1,0:T(8,128)(2,1)} %copy-done.24) | copy-start | bytes 5644804
  649.9 40.6 %collective-permute-start.38 = (bf16[1024,1152]{1,0:T(8,128)(2,1)S(1)}, bf16[1024,1152]{1,0:T(8,128)(2,1)S(1)}, u32[]{:S(2)}, u32[]{:S(2)}) collective-permute-start(bf16[1024,1152]{1,0:T(8,128)(2,1)S(1)} %get-tuple-element.280), channel_id=1, source_target_pairs={{0,1},{1,0},{2,3},{3,2},{4,5},{5,4},{6,7},{7,6},{8,9},{9,8},{10,11... | collective-permute-start | bytes 7077896 | tf_op jit(solution)/shard_map/ppermute | solution.py:861
  661.3 24.6 %collective-permute-start.36 = (bf16[560,896]{1,0:T(8,128)(2,1)S(1)}, bf16[560,896]{1,0:T(8,128)(2,1)S(1)}, u32[]{:S(2)}, u32[]{:S(2)}) collective-permute-start(bf16[560,896]{1,0:T(8,128)(2,1)S(1)} %select_convert_fusion), channel_id=1, source_target_pairs={{0,4},{4,0},{8,12},{12,8},{16,20},{20,16},{24,28},{28,24},{1,5},{5... | collective-permute-start | bytes 3010568 | tf_op jit(solution)/shard_map/ppermute | solution.py:861
  666.2 2.3 collective-permute-start.35
  686.2 4.3 collective-permute-start.37
  686.9 52.5 %collective-permute-start.41 = (bf16[420,1120]{1,0:T(8,128)(2,1)}, bf16[420,1120]{1,0:T(8,128)(2,1)}, u32[]{:S(2)}, u32[]{:S(2)}) collective-permute-start(bf16[420,1120]{1,0:T(8,128)(2,1)} %get-tuple-element.293), channel_id=1, source_target_pairs={{0,8},{4,12},{16,24},{20,28},{1,9},{5,13},{17,25},{21,29},{2,10},{... | collective-permute-start | bytes 2822408 | tf_op jit(solution)/shard_map/ppermute | solution.py:861
  689.2 50.1 %collective-permute-start.42 = (bf16[420,1120]{1,0:T(8,128)(2,1)}, bf16[420,1120]{1,0:T(8,128)(2,1)}, u32[]{:S(2)}, u32[]{:S(2)}) collective-permute-start(bf16[420,1120]{1,0:T(8,128)(2,1)} %get-tuple-element.295), channel_id=1, source_target_pairs={{0,8},{4,12},{8,0},{12,4},{16,24},{20,28},{24,16},{28,20},{1,9},{5... | collective-permute-start | bytes 2822408 | tf_op jit(solution)/shard_map/ppermute | solution.py:861
  689.2 45.6 %collective-permute-start.39 = (bf16[560,896]{1,0:T(8,128)(2,1)S(1)}, bf16[560,896]{1,0:T(8,128)(2,1)S(1)}, u32[]{:S(2)}, u32[]{:S(2)}) collective-permute-start(bf16[560,896]{1,0:T(8,128)(2,1)S(1)} %get-tuple-element.285), channel_id=1, source_target_pairs={{8,0},{12,4},{24,16},{28,20},{9,1},{13,5},{25,17},{29,21},{10,2},{... | collective-permute-start | bytes 3010568 | tf_op jit(solution)/shard_map/ppermute | solution.py:861
  699.1 38.7 %copy-start.55 = (f32[4,1120]{1,0:T(4,128)S(1)}, f32[4,1120]{1,0:T(4,128)}, u32[]{:S(2)}) copy-start(f32[4,1120]{1,0:T(4,128)} %copy-done.54) | copy-start | bytes 53764
  699.1 38.7 %copy-start.58 = (f32[2,1120]{1,0:T(2,128)S(1)}, f32[2,1120]{1,0:T(2,128)}, u32[]{:S(2)}) copy-start(f32[2,1120]{1,0:T(2,128)} %get-tuple-element.411) | copy-start | bytes 26884
  699.1 38.7 %copy-start.59 = (f32[2,1120]{1,0:T(2,128)S(1)}, f32[2,1120]{1,0:T(2,128)}, u32[]{:S(2)}) copy-start(f32[2,1120]{1,0:T(2,128)} %get-tuple-element.412) | copy-start | bytes 26884
  699.1 40.3 %copy-start.39 = (f32[420,1120]{1,0:T(8,128)S(1)}, f32[420,1120]{1,0:T(8,128)}, u32[]{:S(2)}) copy-start(f32[420,1120]{1,0:T(8,128)} %get-tuple-element.292) | copy-start | bytes 5644804
  699.1 49.6 %collective-permute-start.44 = (bf16[512,1152]{1,0:T(8,128)(2,1)}, bf16[512,1152]{1,0:T(8,128)(2,1)}, u32[]{:S(2)}, u32[]{:S(2)}) collective-permute-start(bf16[512,1152]{1,0:T(8,128)(2,1)} %get-tuple-element.382), channel_id=1, source_target_pairs={{0,2},{1,3},{2,0},{3,1},{4,6},{5,7},{6,4},{7,5},{8,10},{9,11},{10,... | collective-permute-start | bytes 3538952 | tf_op jit(solution)/shard_map/ppermute | solution.py:861
  736.7 2.6 collective-permute-start.40
  737.9 49.0 %collective-permute-start.45 = (bf16[560,896]{1,0:T(8,128)(2,1)}, bf16[560,896]{1,0:T(8,128)(2,1)}, u32[]{:S(2)}, u32[]{:S(2)}) collective-permute-start(bf16[560,896]{1,0:T(8,128)(2,1)} %get-tuple-element.305), channel_id=1, source_target_pairs={{16,0},{20,4},{17,1},{21,5},{18,2},{22,6},{19,3},{23,7}} | collective-permute-start | bytes 3010568 | tf_op jit(solution)/shard_map/ppermute | solution.py:861
  742.0 28.0 %collective-permute-start.43 = (bf16[420,1120]{1,0:T(8,128)(2,1)S(1)}, bf16[420,1120]{1,0:T(8,128)(2,1)S(1)}, u32[]{:S(2)}, u32[]{:S(2)}) collective-permute-start(bf16[420,1120]{1,0:T(8,128)(2,1)S(1)} %select_convert_fusion.1), channel_id=1, source_target_pairs={{24,8},{28,12},{0,16},{4,20},{8,24},{12,28},{25,9},{29,13},{1,17},... | collective-permute-start | bytes 2822408 | tf_op jit(solution)/shard_map/ppermute | solution.py:861
  797.8 38.6 %copy-start.9 = (f32[12,1120]{1,0:T(8,128)S(1)}, f32[12,1120]{1,0:T(8,128)}, u32[]{:S(2)}) copy-start(f32[12,1120]{1,0:T(8,128)} %copy-done.8) | copy-start | bytes 161284
  812.6 1.3 collective-permute-start.46
  813.9 4.4 collective-permute-start.47
  818.3 4.4 collective-permute-start.48
  822.8 9.7 %collective-permute-start.49 = (f32[16,1120]{1,0:T(8,128)S(1)}, f32[16,1120]{1,0:T(8,128)S(1)}, u32[]{:S(2)}, u32[]{:S(2)}) collective-permute-start(f32[16,1120]{1,0:T(8,128)S(1)} %add.274), channel_id=1, source_target_pairs={{0,8},{4,12},{8,0},{12,4},{16,24},{20,28},{24,16},{28,20},{1,9},{5... | collective-permute-start | bytes 215048 | tf_op jit(solution)/shard_map/ppermute | solution.py:861
  832.5 12.5 %collective-permute-start.50 = (f32[16,1120]{1,0:T(8,128)S(1)}, f32[16,1120]{1,0:T(8,128)S(1)}, u32[]{:S(2)}, u32[]{:S(2)}) collective-permute-start(f32[16,1120]{1,0:T(8,128)S(1)} %add.275), channel_id=1, source_target_pairs={{0,16},{4,20},{8,24},{12,28},{16,0},{20,4},{24,8},{28,12},{1,17},{... | collective-permute-start | bytes 215048 | tf_op jit(solution)/shard_map/ppermute | solution.py:861
  (71 other events, 588.7 us)

commit v6 on v5

--- a/solution.py
+++ b/solution.py
@@ -337,31 +337,21 @@
     return pl.BlockSpec(memory_space=pl.ANY)
 
 
-def round_weights_body(bound_ref, weight_ref, low_ref, sums_ref):
-    values = weight_ref[...]
-    low_ref[...] = values[0, 0].astype(BF16)
-    place = lax.broadcasted_iota(jnp.int32, values.shape, 2)
-    squares = values * values
-    lower = jnp.sum(jnp.where(place < bound_ref[0], squares, 0.0))
-    sums_ref[0] = lower
-    sums_ref[1] = jnp.sum(squares) - lower
-
-
-def round_weights(bound, weight):
-    smem = pl.BlockSpec(memory_space=pltpu.SMEM)
+def round_weights_body(weight_ref, low_ref):
+    low_ref[...] = weight_ref[0, 0, :].astype(BF16)
+
+
+def round_weights(weight):
     whole = pl.BlockSpec(memory_space=pltpu.VMEM)
     return pl.pallas_call(
         round_weights_body,
-        in_specs=[smem, whole],
-        out_specs=[whole, smem],
-        out_shape=[
-            jax.ShapeDtypeStruct(weight.shape[2:], BF16),
-            jax.ShapeDtypeStruct((2,), F32),
-        ],
+        in_specs=[whole],
+        out_specs=whole,
+        out_shape=jax.ShapeDtypeStruct(weight.shape[2:], BF16),
         compiler_params=vmem(32),
         cost_estimate=lasting(6),
         name="round_weights",
-    )(bound, weight)
+    )(weight)
 
 
 def moments_body(
@@ -380,17 +370,17 @@
     update_ref[...] = update
     count = grad.shape[2]
     place = step * count + lax.broadcasted_iota(jnp.int32, grad.shape, 2)
-    squares = update * update
-    lower = jnp.sum(jnp.where(place < ints_ref[0], squares, 0.0))
-    upper = jnp.sum(squares) - lower
 
     @pl.when(step == 0)
     def clear():
-        sums_ref[0] = 0.0
-        sums_ref[1] = 0.0
-
-    sums_ref[0] += lower
-    sums_ref[1] += upper
+        for index in range(4):
+            sums_ref[index] = 0.0
+
+    for index, values in enumerate((weight_ref[...], update)):
+        squares = values * values
+        lower = jnp.sum(jnp.where(place < ints_ref[0], squares, 0.0))
+        sums_ref[2 * index] += lower
+        sums_ref[2 * index + 1] += jnp.sum(squares) - lower
 
 
 def flat_steps(count):
@@ -412,7 +402,7 @@
             jax.ShapeDtypeStruct(weight.shape, F32),
             jax.ShapeDtypeStruct((2,) + weight.shape, F32),
             jax.ShapeDtypeStruct(weight.shape, F32),
-            jax.ShapeDtypeStruct((2,), F32),
+            jax.ShapeDtypeStruct((4,), F32),
         ],
         compiler_params=vmem(48),
         cost_estimate=lasting(10),
@@ -734,6 +724,75 @@
         cost_estimate=lasting(4),
         name="middle_norm",
     )(rows, kept, got, small)
+
+
+def turn(block):
+    return block.astype(F32).T.astype(BF16)
+
+
+def take_rows_body(chip_ref, array_ref, own_ref, sent_ref):
+    rows = turn(array_ref[0, 0])
+
+    @pl.when(pl.program_id(0) == 0)
+    def other_micro():
+        put(sent_ref, rows)
+
+    @pl.when(pl.program_id(0) == 1)
+    def own_micro():
+        put(own_ref, rows)
+
+
+def take_rows(chip, array):
+    turned = jnp.swapaxes(array, 2, 3)
+    _, _, width, count = turned.shape
+    out = pl.BlockSpec((count, lanes(width)), lambda i, chip_ref: (0, 0))
+    return pl.pallas_call(
+        take_rows_body,
+        grid_spec=pltpu.PrefetchScalarGridSpec(
+            num_scalar_prefetch=1,
+            grid=(2,),
+            in_specs=[
+                pl.BlockSpec(
+                    (1, 1, width, count),
+                    lambda i, chip_ref: (jnp.where(i == 0, 1 - chip_ref[0], chip_ref[0]), 0, 0, 0),
+                )
+            ],
+            out_specs=[out, out],
+        ),
+        out_shape=[jax.ShapeDtypeStruct((count, lanes(width)), BF16)] * 2,
+        compiler_params=vmem(32),
+        cost_estimate=lasting(4),
+        name="take_rows",
+    )(chip, turned)
+
+
+def place_rows_body(chip_ref, rows_ref, received_ref, out_ref):
+    width = out_ref.shape[2]
+    rows = jnp.where(
+        pl.program_id(0) == chip_ref[0], rows_ref[:, :width], received_ref[:, :width]
+    )
+    out_ref[0, 0] = turn(rows)
+
+
+def place_rows(chip, rows, received, width):
+    count, sent_width = received.shape
+    turned = pl.pallas_call(
+        place_rows_body,
+        grid_spec=pltpu.PrefetchScalarGridSpec(
+            num_scalar_prefetch=1,
+            grid=(2,),
+            in_specs=[
+                pl.BlockSpec((count, sent_width), lambda i, chip_ref: (chip_ref[0], 0)),
+                pl.BlockSpec((count, sent_width), lambda i, chip_ref: (0, 0)),
+            ],
+            out_specs=pl.BlockSpec((1, 1, width, count), lambda i, chip_ref: (i, 0, 0, 0)),
+        ),
+        out_shape=jax.ShapeDtypeStruct((2, 1, width, count), BF16),
+        compiler_params=vmem(32),
+        cost_estimate=lasting(4),
+        name="place_rows",
+    )(chip, rows, received)
+    return jnp.swapaxes(turned, 2, 3)
 
 
 def norm_back_body(wide_out, rows_ref, kept_ref, got_ref, base_ref, gain_ref, *outs):
@@ -955,9 +1014,10 @@
     planar = dp_count == 8 and shard_len * 2 == first_end
     shares = (core + 2 * chip, core + 2 * (1 - chip))
 
-    def exchange_micro(array):
-        own = pick(array[:, 0], chip)
-        received = swap(widen(pick(array[:, 0], 1 - chip)), "seq", 2)[:, :model_width]
+    chip_index = chip.reshape(1).astype(jnp.int32)
+
+    def exchange_micro(own, sent):
+        received = swap(sent, "seq", 2)
         first = jnp.where(chip == 0, own, received)
         second = jnp.where(chip == 0, received, own)
         return jnp.concatenate([first, second], axis=0)
@@ -980,23 +1040,25 @@
         )
 
     weight = weights_master
-    low_weight, weight_sums = round_weights(bound, weight)
-    first_rows, low_weight = tie(rows_in, low_weight)
-    own_in = exchange_micro(first_rows)
+    low_weight = round_weights(weight)
+    if planar:
+        tall = low_weight.reshape(shard_len // triple, triple)
+    own_first, sent_rows = take_rows(chip_index, rows_in)
+    own_in = exchange_micro(own_first, sent_rows)[:, :model_width]
+    own_cotangent, sent_cotangent = take_rows(chip_index, out_cotangent)
     inputs = own_in.astype(F32)
     hat_one, _ = norm_stats(inputs)
     low_one = widen((hat_one * small_master[0] + small_master[1]).astype(BF16))
     other_one = swap(low_one, "seq", 1)
     y_index = y_here.reshape(1).astype(jnp.int32)
     if planar:
-        tall = low_weight.reshape(shard_len // triple, triple)
         wide = low_weight.reshape(shard_len // model_width, model_width)
         cut, tall_rows = wide.shape[0], tall.shape[0]
         lead = spread_lead(tall, z_here)
         across = [move_rest(wide, (1, 0), 0)]
         over = [move_rest(wide, (0, 2), 0)]
-        lead, wide, across[0], over[0], other_one = tie(
-            lead, wide, across[0], over[0], other_one
+        lead, wide, across[0], over[0], other_one, sent_cotangent = tie(
+            lead, wide, across[0], over[0], other_one, sent_cotangent
         )
         lead_across = swap(lead, "dp", 1)
         halves = (lead, lead_across, swap(lead, "seq", 2), swap(lead_across, "seq", 2))
@@ -1055,16 +1117,15 @@
     def attend(part):
         return attention_forward(low_blocks, core_index, block_starts, qkv[part], heads_here)
 
-    later_cotangent = out_cotangent
     attended = [attend(0)]
     if planar:
-        qkv[1], last, across[1:3], over[1:3], later_cotangent, _ = tie(
-            qkv[1], last, across[1:3], over[1:3], later_cotangent, attended[0][2]
+        qkv[1], last, across[1:3], over[1:3], sent_cotangent, _ = tie(
+            qkv[1], last, across[1:3], over[1:3], sent_cotangent, attended[0][2]
         )
         across.append(move_rest(last, (1, 0), 3))
         over.append(move_rest(last, (0, 2), 3))
         both += [move_rest(over[1], (1, 0), 1), move_rest(across[2], (0, 2), 2)]
-    own_e = widen(exchange_micro(later_cotangent))
+    own_e = exchange_micro(own_cotangent, sent_cotangent)
     attended.append(attend(1))
     if planar:
         dp_index, across, over, both, _ = tie(dp_index, across, over, both, attended[1][2])
@@ -1093,7 +1154,6 @@
     inner_sums = sums_sent + sums_kept
 
     link = BF16 if planar else F32
-    up_received, out_received = tie(up_received, out_received)
     grad_mid, low_mid, sums_two = norm_back(
         middle, up_kept, up_received, own_e, small_master[2:3], True
     )
@@ -1115,13 +1175,6 @@
     share_back, share_in, share_out, grad_att_theirs = tie(
         share_back, share_in, share_out, grad_att_theirs
     )
-
-    def place_micro(lower, upper, received):
-        own = jnp.where(chip == 0, lower, upper)[:, :model_width]
-        received = received[:, :model_width]
-        first = jnp.where(chip == 0, own, received)
-        second = jnp.where(chip == 0, received, own)
-        return jnp.stack([first, second])[:, None]
 
     def return_rows(lower, upper):
         return swap(jnp.where(chip == 0, upper, lower), "seq", 2)
@@ -1142,7 +1195,9 @@
     attn_sent = dot_columns(rows_one, packed_theirs).astype(link)
     attn_sent, packed_theirs = tie(attn_sent, packed_theirs)
     theirs_part = partial_product(packed_theirs, w_attn_theirs)
-    attn_sent, theirs_part, y_index = tie(attn_sent, theirs_part, y_index)
+    attn_sent, theirs_part, y_index, out_received = tie(
+        attn_sent, theirs_part, y_index, out_received
+    )
     attn_received = swap(attn_sent, "seq", 2)
     if planar:
         kept_rest, sent_rest = pack_rest(
@@ -1187,41 +1242,37 @@
         sent_last = held[2].astype(BF16)
         kept_near = jnp.where(z_odd, held[0], held[1])
         kept_last = held[2]
-        (sent_near, sent_last), kept_lead, mark = started(
-            (sent_near, sent_last), kept_lead, mark
-        )
+        sent_near, sent_last, kept_lead = tie(sent_near, sent_last, kept_lead)
         got_near = swap(sent_near, "dp", 2)
         got_last = permute(sent_last, "dp", lower_pairs([(0, 1), (2, 3)], 2))
     packed = [packed_mine, packed_theirs]
     if planar:
         held_lead = kept_lead + got_lead.astype(F32)
         sent_lead = held_lead.astype(BF16)
-        sent_lead, held_lead, kept = tie(sent_lead, held_lead, kept)
-        sent_lead, kept, mark = started(sent_lead, kept, mark)
-        near_lead = permute(sent_lead, "dp", lower_pairs([(1, 0), (3, 2)], 2))
-    grad_x, sums_one = norm_back(
-        own_in, kept, swap(sent, "seq", 1), grad_mid, small_master[0:1], False
-    )
-    if planar:
-        grad_x, held_lead = tie(grad_x, held_lead)
-        held_lead = held_lead + near_lead.astype(F32)
-        sent_lead = held_lead.astype(BF16)
         sent_lead, held_lead, kept_near, kept_last = tie(
             sent_lead, held_lead, kept_near, kept_last
         )
-        sent_lead, (kept_near, kept_last), mark = started(
-            sent_lead, (kept_near, kept_last), mark
-        )
-        far_lead = permute(sent_lead, "dp", lower_pairs([(2, 0)], 2))
+        near_lead = permute(sent_lead, "dp", lower_pairs([(1, 0), (3, 2)], 2))
         held_near = kept_near + got_near.astype(F32)
         held_last = kept_last + got_last.astype(F32)
         sent_far = jnp.where(z_here == 1, held_last, held_near).astype(BF16)
         own_rest = jnp.where(z_here == 3, held_last, held_near)
+        sent_far, own_rest, kept = tie(sent_far, own_rest, kept)
         got_far = permute(sent_far, "dp", lower_pairs([(3, 1), (0, 2), (1, 3)], 2))
-
-    result_all = place_micro(*result_halves, result_received)
+    grad_x, sums_one = norm_back(
+        own_in, kept, swap(sent, "seq", 1), grad_mid, small_master[0:1], False
+    )
+    if planar:
+        sums_one, held_lead = tie(sums_one, held_lead)
+        held_lead = held_lead + near_lead.astype(F32)
+        sent_lead = held_lead.astype(BF16)
+        sent_lead, held_lead, own_rest, grad_x = tie(sent_lead, held_lead, own_rest, grad_x)
+        sent_lead, own_rest, mark = started(sent_lead, own_rest, mark)
+        far_lead = permute(sent_lead, "dp", lower_pairs([(2, 0)], 2))
+
+    result_all = place_rows(chip_index, result_rows, result_received, model_width)
     grad_halves = (grad_x[:local_rows], grad_x[local_rows:])
-    grad_all = place_micro(*grad_halves, return_rows(*grad_halves))
+    grad_all = place_rows(chip_index, grad_x, return_rows(*grad_halves), model_width)
 
     def at_shares(columns):
         row = jnp.zeros((model_width,), F32)
@@ -1267,7 +1318,7 @@
     fix_one = 1.0 - jnp.exp(steps_done * math.log(BETA_ONE))
     fix_two = 1.0 - jnp.exp(steps_done * math.log(BETA_TWO))
     ints = jnp.concatenate([bound, leads.astype(jnp.int32).reshape(1)])
-    reduced, moments, update, update_sums = new_moments(
+    reduced, moments, update, matrix_squares = new_moments(
         ints,
         jnp.stack([fix_one, fix_two]),
         lead_grad,
@@ -1276,7 +1327,7 @@
         second_moment,
         weight,
     )
-    matrix_rows = jnp.stack([matrix_sums(weight_sums), matrix_sums(update_sums)])
+    matrix_rows = jnp.stack([matrix_sums(matrix_squares[:2]), matrix_sums(matrix_squares[2:])])
     small_sum = sum_everywhere(
         jnp.concatenate([small_now, jnp.pad(matrix_rows, ((0, 2), (0, model_width - 4)))])
     )

time: 868 us -> 816 us (0.940)
  local copies, waits for them, and re-layouts: 75.3 us -> 47.8 us
  waiting for transfers between devices: 210 us -> 189 us
  other arithmetic: 55.3 us -> 43.7 us
    ppermute x51 -> x49, waiting for transfers between devices: 210 us -> 189 us  [permute(): return lax.ppermute(value, axis_name, pairs)]
    dynamic_slice x8 -> x2, local copies, waits for them, and re-layouts: 15.4 us -> 1.24 us  [pick(): return lax.dynamic_index_in_dim(stacked, index, axis, keepdims=False)]
    unnamed x172 -> x174, local copies, waits for them, and re-layouts: 34.2 us -> 24.1 us
    ppermute x51 -> x49, starting transfers between devices: 82.9 us -> 85.9 us  [permute(): return lax.ppermute(value, axis_name, pairs)]
  transfers between devices with their start and end apart: 51 -> 49, of which waited for: 19 -> 20; matrix products, arithmetic and copies ran while one was open for 14% -> 11% of each run, Pallas kernels for 33% -> 36%
where the time goes in v6:
time: 816 us; the launch traced here: 807 us
  Pallas kernels  370 us (45%)
  waiting for transfers between devices  189 us (23%)
  starting transfers between devices  85.9 us (11%)
  matrix products  63.3 us (8%)
  local copies, waits for them, and re-layouts  47.8 us (6%)
  other arithmetic  43.7 us (5%)
    ppermute x49, waiting for transfers between devices, permute(): return lax.ppermute(value, axis_name, pairs)  189 us
    pallas_call x2, Pallas kernels, attention_backward(): pl.pallas_call(functools.partial(attention_backward_body, heads, width, b...  112 us
    ppermute x49, starting transfers between devices, permute(): return lax.ppermute(value, axis_name, pairs)  85.9 us
    pallas_call x2, Pallas kernels, attention_forward(): pl.pallas_call(functools.partial(attention_forward_body, heads, width, bq...  70 us
    pallas_call x2, Pallas kernels, feed_forward(): pl.pallas_call(functools.partial(feed_forward_body, len(filled)), out_sha...  69.1 us
    dot_general x8, matrix products, dot_columns(): lax.dot_general(left, right, (((0,), (0,)), ((), ())), preferred_element_...  63.3 us
    unnamed x174, local copies, waits for them, and re-layouts  24.1 us
    pallas_call x2, Pallas kernels, split_product(): pl.pallas_call(functools.partial(split_product_body, steps, turned, len(l...  19.5 us
  transfers between devices with their start and end apart: 49, of which 20 were waited for; matrix products, arithmetic and copies ran while one was open for 11% of the time, Pallas kernels for 36%

profile of v6, /device:TPU:0, one launch (start us, length us, event | category | flops | bytes accessed | tf_op | source)
XLA Modules:
  0.0 807.3 jit_solution(1309912998254114627)
XLA Ops:
  5.3 2.9 collective-permute-start
  9.1 2.8 reshape.190
  11.9 5.5 collective-permute-start.1
  18.0 16.5 %collective-permute-done = bf16[512,1152]{1,0:T(8,128)(2,1)} collective-permute-done((bf16[512,1152]{1,0:T(8,128)(2,1)}, bf16[512,1152]{1,0:T(8,128)(2,1)}, u32[]{:S(2)}, u32[]{:S(2)}) %collective-permute-start) | collective-permute-done | bytes 1179680 | tf_op jit(solution)/shard_map/ppermute | solution.py:920
  41.9 5.9 collective-permute-start.2
  56.0 13.2 %collective-permute-done.2 = bf16[560,840]{1,0:T(8,128)(2,1)} collective-permute-done((bf16[560,840]{1,0:T(8,128)(2,1)}, bf16[560,840]{1,0:T(8,128)(2,1)}, u32[]{:S(2)}, u32[]{:S(2)}) %collective-permute-start.2) | collective-permute-done | bytes 940832 | tf_op jit(solution)/shard_map/ppermute | solution.py:920
  78.1 16.5 %collective-permute-done.6.a1 = bf16[560,840]{1,0:T(8,128)(2,1)} collective-permute-done((bf16[560,840]{1,0:T(8,128)(2,1)S(1)}, bf16[560,840]{1,0:T(8,128)(2,1)}, u32[]{:S(2)}, u32[]{:S(2)}) %collective-permute-start.6) | collective-permute-done | bytes 940832 | tf_op jit(solution)/shard_map/ppermute | solution.py:920
  96.6 29.4 %collective-permute-done.10.refs_4_ = bf16[420,1120]{1,0:T(8,128)(2,1)} collective-permute-done((bf16[420,1120]{1,0:T(8,128)(2,1)}, bf16[420,1120]{1,0:T(8,128)(2,1)}, u32[]{:S(2)}, u32[]{:S(2)}) %collective-permute-start.10) | collective-permute-done | bytes 940832 | tf_op jit(solution)/shard_map/ppermute | solution.py:920
  129.2 3.4 collective-permute-start.14
  132.7 2.4 collective-permute-start.13
  135.1 2.4 collective-permute-start.15
  137.6 3.9 collective-permute-start.16
  141.4 16.6 %project.1 = (bf16[2048,840]{1,0:T(8,128)(2,1)}, bf16[2048,840]{1,0:T(8,128)(2,1)}, bf16[2048,1120]{1,0:T(8,128)(2,1)}, bf16[1120,840]{1,0:T(8,128)(2,1)S(1)}, bf16[1120,840]{1,0:T(8,128)(2,1)}) custom-call(s32[1]{0:T(128)} %bitcast.2.place_ref, bf16[1024,1152]{1,0:T(8,128)(2,1)} %pad.11.own_ref, bf16[1024,1152]{1,0:T(8,128)(2,1)} %collective-permute-done.5.other_ref, ...), custom_call_target="tpu_custom_call" | custom-call | flops 16000000000 | bytes 4096 | tf_op jit(solution)/shard_map/project/pallas_call | solution.py:576
  158.1 35.3 %attention_forward.2 = (bf16[2048,280]{1,0:T(8,128)(2,1)S(1)}, f32[4,280,512]{2,1,0:T(8,128)S(1)}, f32[4,8,512]{2,1,0:T(8,128)S(1)}) custom-call(s32[4]{0:T(128)S(1)} %and_select_fusion.low_ref, s32[1]{0:T(128)} %bitcast.6.core_ref, s32[4,1,512]{2,1,0:T(1,128)S(1)} %compare_select_fusion.start_ref, bf16[2048,840]{1,0:T(8,128)(2,1)} %get-tuple-element.172.qkv_ref), custom_call_target="tpu_custom_call" | custom-call | flops 35000000512 | bytes 4096 | tf_op jit(solution)/shard_map/attention_forward/pallas_call | solution.py:260
  195.4 2.5 collective-permute-start.19
  197.8 3.9 collective-permute-start.20
  201.7 3.4 collective-permute-start.21
  205.8 34.7 %attention_forward.3 = (bf16[2048,280]{1,0:T(8,128)(2,1)S(1)}, f32[4,280,512]{2,1,0:T(8,128)S(1)}, f32[4,8,512]{2,1,0:T(8,128)S(1)}) custom-call(s32[4]{0:T(128)S(1)} %and_select_fusion.low_ref, s32[1]{0:T(128)} %bitcast.6.core_ref, s32[4,1,512]{2,1,0:T(1,128)S(1)} %compare_select_fusion.start_ref, bf16[2048,840]{1,0:T(8,128)(2,1)} %get-tuple-element.178.qkv_ref), custom_call_target="tpu_custom_call" | custom-call | flops 35000000512 | bytes 4096 | tf_op jit(solution)/shard_map/attention_forward/pallas_call | solution.py:260
  244.6 2.4 collective-permute-start.22
  247.0 5.6 unpack_share.2
  252.7 12.1 %collective-permute-done.17 = bf16[512,1152]{1,0:T(8,128)(2,1)} collective-permute-done((bf16[512,1152]{1,0:T(8,128)(2,1)S(1)}, bf16[512,1152]{1,0:T(8,128)(2,1)}, u32[]{:S(2)}, u32[]{:S(2)}) %collective-permute-start.17) | collective-permute-done | bytes 1179680 | tf_op jit(solution)/shard_map/ppermute | solution.py:920
  267.7 5.4 unpack_share.3
  273.2 8.8 %split_product.2 = (f32[1024,1152]{1,0:T(8,128)}, f32[1024,1120]{1,0:T(8,128)}) custom-call(bf16[2048,280]{1,0:T(8,128)(2,1)S(1)} %get-tuple-element.179.refs_0_, bf16[2048,280]{1,0:T(8,128)(2,1)S(1)} %copy-done.24, bf16[280,1120]{1,0:T(8,128)(2,1)S(1)} %get-tuple-element.197.refs_2_.w_a, bf16[280,1120]{1,0:T(8,128)(2,1)S(1)} %get-tuple-element.205.refs_3_.w_b), custom_call_target="tpu_custom_call" | custom-call | flops 8999999488 | bytes 4096 | tf_op jit(solution)/shard_map/split_product/pallas_call | solution.py:683
  282.7 10.7 %collective-permute-done.23.got_ref = f32[1024,1152]{1,0:T(8,128)S(1)} collective-permute-done((f32[1024,1152]{1,0:T(8,128)}, f32[1024,1152]{1,0:T(8,128)S(1)}, u32[]{:S(2)}, u32[]{:S(2)}) %collective-permute-start.23) | collective-permute-done | bytes 4718624 | tf_op jit(solution)/shard_map/ppermute | solution.py:920
  299.3 3.1 collective-permute-done.24.rows_ref
  303.8 34.4 %feed_forward.2 = (bf16[2048,1120]{1,0:T(8,128)(2,1)}, bf16[2048,1120]{1,0:T(8,128)(2,1)}, bf16[2048,1120]{1,0:T(8,128)(2,1)}, bf16[2048,1120]{1,0:T(8,128)(2,1)...) custom-call(bf16[1024,1152]{1,0:T(8,128)(2,1)} %copy-done.66, ...), custom_call_target="tpu_custom_call" | custom-call | flops 33999998976 | bytes 4096 | tf_op jit(solution)/shard_map/feed_forward/pallas_call | solution.py:897
  338.4 34.6 %feed_forward.3 = (bf16[2048,1120]{1,0:T(8,128)(2,1)}, bf16[2048,1120]{1,0:T(8,128)(2,1)}, bf16[2048,1120]{1,0:T(8,128)(2,1)}, bf16[2048,1120]{1,0:T(8,128)(2,1)...) custom-call(bf16[1024,1152]{1,0:T(8,128)(2,1)} %copy-done.12, ...), custom_call_target="tpu_custom_call", output_to_operand_aliasing={{0}: (7, {}), {1}: (8, {}), {2}: (9, {}), {3}: (10, {}), {4... | custom-call | flops 33999998976 | bytes 4096 | tf_op jit(solution)/shard_map/feed_forward/pallas_call | solution.py:897
  373.1 2.3 copy-done.1
  375.5 8.1 %norm_back.2 = (f32[1024,1120]{1,0:T(8,128)S(1)}, bf16[1024,1152]{1,0:T(8,128)(2,1)}, f32[8,1120]{1,0:T(8,128)S(1)}) custom-call(f32[1024,1120]{1,0:T(8,128)S(1)} %copy-done.1, f32[1024,1152]{1,0:T(8,128)} %get-tuple-element.223.kept_ref, f32[1024,1152]{1,0:T(8,128)} %collective-permute-done.26.got_ref, bf16[1024,1152]{1,0:T(8,128)(2,1)S(1)} %copy-done.6, ...), custom_call_target="tpu_custom_call" | custom-call | flops 7000000000 | bytes 4096 | tf_op jit(solution)/shard_map/norm_back/pallas_call | solution.py:825
  383.6 13.2 %convolution_convert_fusion = bf16[1120,1120]{1,0:T(8,128)(2,1)} fusion(bf16[2048,1120]{1,0:T(8,128)(2,1)} %get-tuple-element.235, bf16[2048,1120]{1,0:T(8,128)(2,1)} %get-tuple-element.230), kind=kOutput, calls=%fused_computation | convolution fusion | flops 5139276800 | bytes 11683840 | tf_op jit(solution)/shard_map/dot_general | solution.py:39
  396.8 7.8 convolution_convert_fusion.1
  414.7 7.8 out_grads.1
  422.6 6.0 convolution_convert_fusion.3
  430.6 8.5 %fusion.40.in_ref = f32[1120,1120]{1,0:T(8,128)} fusion(bf16[2048,1120]{1,0:T(8,128)(2,1)S(1)} %bitcast.70, bf16[2048,1120]{1,0:T(8,128)(2,1)S(1)} %bitcast.68), kind=kOutput, calls=%fused_computation.125 | convolution fusion | flops 5138022400 | bytes 14192640 | tf_op jit(solution)/shard_map/dot_general | solution.py:39
  439.0 8.8 %fusion.39.back_ref = f32[1120,1120]{1,0:T(8,128)} fusion(bf16[2048,1120]{1,0:T(8,128)(2,1)S(1)} %bitcast.66, bf16[2048,1120]{1,0:T(8,128)(2,1)S(1)} %bitcast.74), kind=kOutput, calls=%fused_computation.124 | convolution fusion | flops 5138022400 | bytes 14192640 | tf_op jit(solution)/shard_map/dot_general | solution.py:39
  447.9 56.1 %attention_backward.2.left = bf16[2048,896]{1,0:T(8,128)(2,1)} custom-call(s32[4]{0:T(128)} %copy-done.21, s32[1]{0:T(128)} %bitcast.6.core_ref, s32[4,1,512]{2,1,0:T(1,128)} %copy-done.11, bf16[2048,840]{1,0:T(8,128)(2,1)} %get-tuple-element.178.qkv_ref, bf16[2048,280]{1,0:T(8,128)(2,1)} %copy-done.37, f32[4,280,512]{2,1,0:T(8,128)} %copy-done.39, ...), custom_call_target="tpu_custom_call" | custom-call | flops 56000000000 | bytes 4096 | tf_op jit(solution)/shard_map/attention_backward/pallas_call | solution.py:303
  503.9 9.9 %convolution_convert_fusion.2 = bf16[1120,896]{1,0:T(8,128)(2,1)} fusion(bf16[2048,1120]{1,0:T(8,128)(2,1)} %get-tuple-element.171, bf16[2048,896]{1,0:T(8,128)(2,1)} %attention_backward.2.left), kind=kOutput, calls=%fused_computation.17 | convolution fusion | flops 4111421440 | bytes 10264576 | tf_op jit(solution)/shard_map/dot_general | solution.py:39
  513.8 7.7 partial_product.1.refs_2_
  522.1 4.9 fusion.8
  529.3 9.7 %collective-permute-done.29.out_got = bf16[280,1120]{1,0:T(8,128)(2,1)S(1)} collective-permute-done((bf16[280,1120]{1,0:T(8,128)(2,1)S(1)}, bf16[280,1120]{1,0:T(8,128)(2,1)S(1)}, u32[]{:S(2)}, u32[]{:S(2)}) %collective-permute-start.29) | collective-permute-done | bytes 627232 | tf_op jit(solution)/shard_map/ppermute | solution.py:920
  539.0 10.4 %pack_rest.1 = (f32[3,420,1120]{2,1,0:T(8,128)}, bf16[3,420,1120]{2,1,0:T(8,128)(2,1)}) custom-call(s32[1]{0:T(128)} %bitcast.2.place_ref, f32[280,1120]{1,0:T(8,128)S(1)} %fusion.41.out_ref, f32[1120,1120]{1,0:T(8,128)} %fusion.40.in_ref, f32[1120,1120]{1,0:T(8,128)} %fusion.39.back_ref, bf16[280,1120]{1,0:T(8,128)(2,1)S(1)} %collective-permute-done.29.out_got, ...), custom_call_target="tpu_custom_call" | custom-call | flops 10000000000 | bytes 4096 | tf_op jit(solution)/shard_map/pack_rest/pallas_call | solution.py:515
  552.6 55.8 %attention_backward.3.refs_0_ = bf16[2048,896]{1,0:T(8,128)(2,1)} custom-call(s32[4]{0:T(128)} %copy-done.21, s32[1]{0:T(128)} %bitcast.6.core_ref, s32[4,1,512]{2,1,0:T(1,128)} %copy-done.11, bf16[2048,840]{1,0:T(8,128)(2,1)} %get-tuple-element.172.qkv_ref, bf16[2048,280]{1,0:T(8,128)(2,1)} %copy-done.36, f32[4,280,512]{2,1,0:T(8,128)} %copy-done.38, ...), custom_call_target="tpu_custom_call" | custom-call | flops 56000000000 | bytes 4096 | tf_op jit(solution)/shard_map/attention_backward/pallas_call | solution.py:303
  610.0 10.7 %split_product.3 = (bf16[1024,1152]{1,0:T(8,128)(2,1)S(1)}, f32[1024,1120]{1,0:T(8,128)}) custom-call(bf16[2048,896]{1,0:T(8,128)(2,1)} %attention_backward.3.refs_0_, bf16[1120,840]{1,0:T(8,128)(2,1)S(1)} %copy-done.28, f32[2048,1120]{1,0:T(8,128)} %partial_product.1.refs_2_), custom_call_target="tpu_custom_call" | custom-call | flops 8999999488 | bytes 4096 | tf_op jit(solution)/shard_map/split_product/pallas_call | solution.py:683
  620.8 7.5 fusion.42
  631.1 3.8 fusion.31
  638.2 17.4 %collective-permute-done.35 = bf16[560,896]{1,0:T(8,128)(2,1)S(1)} collective-permute-done((bf16[560,896]{1,0:T(8,128)(2,1)S(1)}, bf16[560,896]{1,0:T(8,128)(2,1)S(1)}, u32[]{:S(2)}, u32[]{:S(2)}) %collective-permute-start.35) | collective-permute-done | bytes 1003552 | tf_op jit(solution)/shard_map/ppermute | solution.py:920
  658.5 20.7 %collective-permute-done.37 = bf16[420,1120]{1,0:T(8,128)(2,1)S(1)} collective-permute-done((bf16[420,1120]{1,0:T(8,128)(2,1)}, bf16[420,1120]{1,0:T(8,128)(2,1)S(1)}, u32[]{:S(2)}, u32[]{:S(2)}) %collective-permute-start.37) | collective-permute-done | bytes 940832 | tf_op jit(solution)/shard_map/ppermute | solution.py:920
  681.3 6.5 norm_back.3
  698.1 12.6 %collective-permute-done.41 = bf16[420,1120]{1,0:T(8,128)(2,1)} collective-permute-done((bf16[420,1120]{1,0:T(8,128)(2,1)}, bf16[420,1120]{1,0:T(8,128)(2,1)}, u32[]{:S(2)}, u32[]{:S(2)}) %collective-permute-start.41) | collective-permute-done | bytes 940832 | tf_op jit(solution)/shard_map/ppermute | solution.py:920
  710.7 3.2 convert_add_fusion.3
  713.9 5.5 reshape.194.rest_ref
  721.3 3.0 place_rows.3
  724.3 13.3 %collective-permute-done.43 = bf16[560,896]{1,0:T(8,128)(2,1)} collective-permute-done((bf16[560,896]{1,0:T(8,128)(2,1)}, bf16[560,896]{1,0:T(8,128)(2,1)}, u32[]{:S(2)}, u32[]{:S(2)}) %collective-permute-start.43) | collective-permute-done | bytes 1003552 | tf_op jit(solution)/shard_map/ppermute | solution.py:920
  737.7 2.7 slice_add_fusion.1
  740.4 6.2 reshape.198.lead_ref
  748.1 13.4 %new_moments.1 = (f32[1,1,470400]{2,1,0:T(1,128)}, f32[2,1,1,470400]{3,2,1,0:T(1,128)}, f32[1,1,470400]{2,1,0:T(1,128)S(1)}, f32[4]{0:T(128)S(1)}) custom-call(s32[2]{0:T(128)S(1)} %pad_add_fusion.ints_ref, f32[2]{0:T(128)S(1)} %pad_maximum_fusion.9.floats_ref, f32[1,1,470400]{2,1,0:T(1,128)S(1)} %copy-done.8, f32[1,1,470400]{2,1,0:T(1,128)S(1)} %copy-done.7, ...), custom_call_target="tpu_custom_call" | custom-call | flops 10000000000 | bytes 4096 | tf_op jit(solution)/shard_map/new_moments/pallas_call | solution.py:396
  763.3 2.6 fusion.22
  766.0 2.6 fusion.23
  771.6 2.8 collective-permute-done.45
  776.0 2.8 collective-permute-done.46
  778.9 7.4 collective-permute-start.47
  788.6 3.9 collective-permute-start.48
  792.4 2.3 collective-permute-done.48
  800.3 6.5 new_weights.1
  (336 shorter events, 106.5 us)
Async XLA Ops:
  1.5 403.5 %copy-start.9 = (f32[12,1120]{1,0:T(8,128)}, f32[12,1120]{1,0:T(8,128)S(1)}, u32[]{:S(2)}) copy-start(f32[12,1120]{1,0:T(8,128)S(1)} %copy.47.small_ref) | copy-start | bytes 161284
  5.3 29.2 %collective-permute-start = (bf16[512,1152]{1,0:T(8,128)(2,1)}, bf16[512,1152]{1,0:T(8,128)(2,1)}, u32[]{:S(2)}, u32[]{:S(2)}) collective-permute-start(bf16[512,1152]{1,0:T(8,128)(2,1)} %get-tuple-element.161), channel_id=1, source_target_pairs={{0,2},{1,3},{2,0},{3,1},{4,6},{5,7},{6,4},{7,5},{8,10},{9,11},{10,... | collective-permute-start | bytes 3538952 | tf_op jit(solution)/shard_map/ppermute | solution.py:920
  11.9 28.9 %collective-permute-start.1 = (bf16[560,840]{1,0:T(8,128)(2,1)}, bf16[560,840]{1,0:T(8,128)(2,1)}, u32[]{:S(2)}, u32[]{:S(2)}) collective-permute-start(bf16[560,840]{1,0:T(8,128)(2,1)} %reshape.190), channel_id=1, source_target_pairs={{0,16},{4,20},{1,17},{5,21},{2,18},{6,22},{3,19},{7,23}} | collective-permute-start | bytes 2822408 | tf_op jit(solution)/shard_map/ppermute | solution.py:920
  40.8 29.8 %collective-permute-start.5 = (bf16[1024,1152]{1,0:T(8,128)(2,1)}, bf16[1024,1152]{1,0:T(8,128)(2,1)}, u32[]{:S(2)}, u32[]{:S(2)}) collective-permute-start(bf16[1024,1152]{1,0:T(8,128)(2,1)} %pad.11.own_ref), channel_id=1, source_target_pairs={{0,1},{1,0},{2,3},{3,2},{4,5},{5,4},{6,7},{7,6},{8,9},{9,8},{10,11... | collective-permute-start | bytes 7077896 | tf_op jit(solution)/shard_map/ppermute | solution.py:920
  41.9 27.3 %collective-permute-start.2 = (bf16[560,840]{1,0:T(8,128)(2,1)}, bf16[560,840]{1,0:T(8,128)(2,1)}, u32[]{:S(2)}, u32[]{:S(2)}) collective-permute-start(bf16[560,840]{1,0:T(8,128)(2,1)} %broadcast_select_fusion.4), channel_id=1, source_target_pairs={{0,8},{4,12},{16,24},{20,28},{1,9},{5,13},{17,25},{21,29},{2,10},{... | collective-permute-start | bytes 2822408 | tf_op jit(solution)/shard_map/ppermute | solution.py:920
  50.0 20.6 %collective-permute-start.3 = (bf16[420,1120]{1,0:T(8,128)(2,1)}, bf16[420,1120]{1,0:T(8,128)(2,1)}, u32[]{:S(2)}, u32[]{:S(2)}) collective-permute-start(bf16[420,1120]{1,0:T(8,128)(2,1)} %reshape.191.refs_0_), channel_id=1, source_target_pairs={{8,12},{9,13},{10,14},{11,15},{12,8},{13,9},{14,10},{15,11},{16,20... | collective-permute-start | bytes 2822408 | tf_op jit(solution)/shard_map/ppermute | solution.py:920
  51.6 19.0 %collective-permute-start.4 = (bf16[420,1120]{1,0:T(8,128)(2,1)}, bf16[420,1120]{1,0:T(8,128)(2,1)}, u32[]{:S(2)}, u32[]{:S(2)}) collective-permute-start(bf16[420,1120]{1,0:T(8,128)(2,1)} %reshape.191.refs_0_), channel_id=1, source_target_pairs={{8,10},{9,11},{10,8},{11,9},{12,14},{13,15},{14,12},{15,13},{16,18... | collective-permute-start | bytes 2822408 | tf_op jit(solution)/shard_map/ppermute | solution.py:920
  56.0 40.2 %copy-start.63 = (s32[2,1,11]{2,1,0:T(1,128)S(1)}, s32[2,1,11]{2,1,0:T(1,128)}, u32[]{:S(2)}) copy-start(s32[2,1,11]{2,1,0:T(1,128)} %param.15) | copy-start | bytes 268
  56.0 40.2 %copy-start.64 = (s32[2,1,11]{2,1,0:T(1,128)S(1)}, s32[2,1,11]{2,1,0:T(1,128)}, u32[]{:S(2)}) copy-start(s32[2,1,11]{2,1,0:T(1,128)} %param.16) | copy-start | bytes 268
  70.6 24.0 %collective-permute-start.6 = (bf16[560,840]{1,0:T(8,128)(2,1)S(1)}, bf16[560,840]{1,0:T(8,128)(2,1)}, u32[]{:S(2)}, u32[]{:S(2)}) collective-permute-start(bf16[560,840]{1,0:T(8,128)(2,1)S(1)} %broadcast_select_fusion.5.a0), channel_id=1, source_target_pairs={{0,4},{4,0},{8,12},{12,8},{16,20},{20,16},{24,28},{28,24},{1,5},{5... | collective-permute-start | bytes 2822408 | tf_op jit(solution)/shard_map/ppermute | solution.py:920
  72.3 24.3 %collective-permute-start.7 = (bf16[560,840]{1,0:T(8,128)(2,1)S(1)}, bf16[560,840]{1,0:T(8,128)(2,1)}, u32[]{:S(2)}, u32[]{:S(2)}) collective-permute-start(bf16[560,840]{1,0:T(8,128)(2,1)S(1)} %broadcast_select_fusion.5.a0), channel_id=1, source_target_pairs={{0,2},{1,3},{2,0},{3,1},{4,6},{5,7},{6,4},{7,5},{8,10},{9,11},{10,... | collective-permute-start | bytes 2822408 | tf_op jit(solution)/shard_map/ppermute | solution.py:920
  73.9 52.1 %collective-permute-start.10 = (bf16[420,1120]{1,0:T(8,128)(2,1)}, bf16[420,1120]{1,0:T(8,128)(2,1)}, u32[]{:S(2)}, u32[]{:S(2)}) collective-permute-start(bf16[420,1120]{1,0:T(8,128)(2,1)} %reshape.191.refs_0_), channel_id=1, source_target_pairs={{8,24},{9,25},{10,26},{11,27},{12,28},{13,29},{14,30},{15,31},{16,... | collective-permute-start | bytes 2822408 | tf_op jit(solution)/shard_map/ppermute | solution.py:920
  75.2 52.2 %collective-permute-start.9 = (bf16[420,1120]{1,0:T(8,128)(2,1)}, bf16[420,1120]{1,0:T(8,128)(2,1)}, u32[]{:S(2)}, u32[]{:S(2)}) collective-permute-start(bf16[420,1120]{1,0:T(8,128)(2,1)} %reshape.191.refs_0_), channel_id=1, source_target_pairs={{8,0},{9,1},{10,2},{11,3},{12,4},{13,5},{14,6},{15,7},{16,24},{17,... | collective-permute-start | bytes 2822408 | tf_op jit(solution)/shard_map/ppermute | solution.py:920
  76.5 49.5 %collective-permute-start.11 = (bf16[420,1120]{1,0:T(8,128)(2,1)}, bf16[420,1120]{1,0:T(8,128)(2,1)}, u32[]{:S(2)}, u32[]{:S(2)}) collective-permute-start(bf16[420,1120]{1,0:T(8,128)(2,1)} %collective-permute-done.4.refs_0_), channel_id=1, source_target_pairs={{8,12},{9,13},{10,14},{11,15},{12,8},{13,9},{14,10},{15,11},{16,20... | collective-permute-start | bytes 2822408 | tf_op jit(solution)/shard_map/ppermute | solution.py:920
  94.6 32.7 %collective-permute-start.8 = (bf16[560,840]{1,0:T(8,128)(2,1)}, bf16[560,840]{1,0:T(8,128)(2,1)}, u32[]{:S(2)}, u32[]{:S(2)}) collective-permute-start(bf16[560,840]{1,0:T(8,128)(2,1)} %collective-permute-done.6.a1), channel_id=1, source_target_pairs={{0,2},{1,3},{2,0},{3,1},{4,6},{5,7},{6,4},{7,5},{8,10},{9,11},{10,... | collective-permute-start | bytes 2822408 | tf_op jit(solution)/shard_map/ppermute | solution.py:920
  96.5 109.2 %copy-start.21 = (s32[4]{0:T(128)}, s32[4]{0:T(128)S(1)}, u32[]{:S(2)}) copy-start(s32[4]{0:T(128)S(1)} %and_select_fusion.low_ref) | copy-start | bytes 52
  96.6 109.2 %copy-start.11 = (s32[4,1,512]{2,1,0:T(1,128)}, s32[4,1,512]{2,1,0:T(1,128)S(1)}, u32[]{:S(2)}) copy-start(s32[4,1,512]{2,1,0:T(1,128)S(1)} %compare_select_fusion.start_ref) | copy-start | bytes 24580
  127.3 66.1 %collective-permute-start.12 = (bf16[420,1120]{1,0:T(8,128)(2,1)}, bf16[420,1120]{1,0:T(8,128)(2,1)}, u32[]{:S(2)}, u32[]{:S(2)}) collective-permute-start(bf16[420,1120]{1,0:T(8,128)(2,1)} %collective-permute-done.10.refs_4_), channel_id=1, source_target_pairs={{0,8},{1,9},{2,10},{3,11},{4,12},{5,13},{6,14},{7,15},{8,0},{9,1},... | collective-permute-start | bytes 2822408 | tf_op jit(solution)/shard_map/ppermute | solution.py:920
  129.2 64.2 %collective-permute-start.14 = (bf16[420,1120]{1,0:T(8,128)(2,1)}, bf16[420,1120]{1,0:T(8,128)(2,1)}, u32[]{:S(2)}, u32[]{:S(2)}) collective-permute-start(bf16[420,1120]{1,0:T(8,128)(2,1)} %collective-permute-done.10.refs_4_), channel_id=1, source_target_pairs={{0,4},{1,5},{2,6},{3,7},{4,0},{5,1},{6,2},{7,3},{8,12},{9,13},{10,... | collective-permute-start | bytes 2822408 | tf_op jit(solution)/shard_map/ppermute | solution.py:920
  132.7 60.7 %collective-permute-start.13 = (bf16[420,1120]{1,0:T(8,128)(2,1)}, bf16[420,1120]{1,0:T(8,128)(2,1)S(1)}, u32[]{:S(2)}, u32[]{:S(2)}) collective-permute-start(bf16[420,1120]{1,0:T(8,128)(2,1)} %collective-permute-done.9.refs_2_), channel_id=1, source_target_pairs={{0,4},{1,5},{2,6},{3,7},{4,0},{5,1},{6,2},{7,3},{16,20},{17,21},{1... | collective-permute-start | bytes 2822408 | tf_op jit(solution)/shard_map/ppermute | solution.py:920
  135.1 58.3 %collective-permute-start.15 = (bf16[420,1120]{1,0:T(8,128)(2,1)}, bf16[420,1120]{1,0:T(8,128)(2,1)S(1)}, u32[]{:S(2)}, u32[]{:S(2)}) collective-permute-start(bf16[420,1120]{1,0:T(8,128)(2,1)} %collective-permute-done.9.refs_2_), channel_id=1, source_target_pairs={{0,2},{1,3},{2,0},{3,1},{4,6},{5,7},{6,4},{7,5},{16,18},{17,19},{1... | collective-permute-start | bytes 2822408 | tf_op jit(solution)/shard_map/ppermute | solution.py:920
  137.6 55.9 %collective-permute-start.16 = (bf16[420,1120]{1,0:T(8,128)(2,1)}, bf16[420,1120]{1,0:T(8,128)(2,1)S(1)}, u32[]{:S(2)}, u32[]{:S(2)}) collective-permute-start(bf16[420,1120]{1,0:T(8,128)(2,1)} %collective-permute-done.10.refs_4_), channel_id=1, source_target_pairs={{0,2},{1,3},{2,0},{3,1},{4,6},{5,7},{6,4},{7,5},{8,10},{9,11},{10,... | collective-permute-start | bytes 2822408 | tf_op jit(solution)/shard_map/ppermute | solution.py:920
  158.0 35.3 %copy-start.27 = (bf16[1120,840]{1,0:T(8,128)(2,1)}, bf16[1120,840]{1,0:T(8,128)(2,1)S(1)}, u32[]{:S(2)}) copy-start(bf16[1120,840]{1,0:T(8,128)(2,1)S(1)} %get-tuple-element.260.refs_1_) | copy-start | bytes 5644804
  158.0 47.1 %copy-start.18 = (bf16[512,1152]{1,0:T(8,128)(2,1)S(1)}, bf16[512,1152]{1,0:T(8,128)(2,1)}, u32[]{:S(2)}) copy-start(bf16[512,1152]{1,0:T(8,128)(2,1)} %copy-done.17) | copy-start | bytes 3538948
  193.3 47.2 %copy-start.38 = (f32[4,280,512]{2,1,0:T(8,128)}, f32[4,280,512]{2,1,0:T(8,128)S(1)}, u32[]{:S(2)}) copy-start(f32[4,280,512]{2,1,0:T(8,128)S(1)} %get-tuple-element.257.outt_ref) | copy-start | bytes 6881284
  193.4 47.2 %copy-start.40 = (f32[4,8,512]{2,1,0:T(8,128)}, f32[4,8,512]{2,1,0:T(8,128)S(1)}, u32[]{:S(2)}) copy-start(f32[4,8,512]{2,1,0:T(8,128)S(1)} %get-tuple-element.177.lse_ref) | copy-start | bytes 196612
  193.4 50.3 %collective-permute-start.18 = (bf16[420,1120]{1,0:T(8,128)(2,1)}, bf16[420,1120]{1,0:T(8,128)(2,1)}, u32[]{:S(2)}, u32[]{:S(2)}) collective-permute-start(bf16[420,1120]{1,0:T(8,128)(2,1)} %collective-permute-done.12.refs_6_), channel_id=1, source_target_pairs={{0,4},{1,5},{2,6},{3,7},{4,0},{5,1},{6,2},{7,3},{8,12},{9,13},{10,... | collective-permute-start | bytes 2822408 | tf_op jit(solution)/shard_map/ppermute | solution.py:920
  195.4 48.3 %collective-permute-start.19 = (bf16[420,1120]{1,0:T(8,128)(2,1)}, bf16[420,1120]{1,0:T(8,128)(2,1)}, u32[]{:S(2)}, u32[]{:S(2)}) collective-permute-start(bf16[420,1120]{1,0:T(8,128)(2,1)} %collective-permute-done.12.refs_6_), channel_id=1, source_target_pairs={{0,2},{1,3},{2,0},{3,1},{4,6},{5,7},{6,4},{7,5},{8,10},{9,11},{10,... | collective-permute-start | bytes 2822408 | tf_op jit(solution)/shard_map/ppermute | solution.py:920
  197.8 45.9 %collective-permute-start.20 = (bf16[420,1120]{1,0:T(8,128)(2,1)S(1)}, bf16[420,1120]{1,0:T(8,128)(2,1)S(1)}, u32[]{:S(2)}, u32[]{:S(2)}) collective-permute-start(bf16[420,1120]{1,0:T(8,128)(2,1)S(1)} %collective-permute-done.15.refs_2_), channel_id=1, source_target_pairs={{0,4},{1,5},{2,6},{3,7},{4,0},{5,1},{6,2},{7,3},{16,20},{17,21},{1... | collective-permute-start | bytes 2822408 | tf_op jit(solution)/shard_map/ppermute | solution.py:920
  201.7 42.9 %collective-permute-start.21 = (bf16[420,1120]{1,0:T(8,128)(2,1)}, bf16[420,1120]{1,0:T(8,128)(2,1)S(1)}, u32[]{:S(2)}, u32[]{:S(2)}) collective-permute-start(bf16[420,1120]{1,0:T(8,128)(2,1)} %collective-permute-done.14.refs_5_), channel_id=1, source_target_pairs={{0,2},{1,3},{2,0},{3,1},{4,6},{5,7},{6,4},{7,5},{8,10},{9,11},{10,... | collective-permute-start | bytes 2822408 | tf_op jit(solution)/shard_map/ppermute | solution.py:920
  205.2 59.6 %collective-permute-start.17 = (bf16[512,1152]{1,0:T(8,128)(2,1)S(1)}, bf16[512,1152]{1,0:T(8,128)(2,1)}, u32[]{:S(2)}, u32[]{:S(2)}) collective-permute-start(bf16[512,1152]{1,0:T(8,128)(2,1)S(1)} %copy-done.18), channel_id=1, source_target_pairs={{0,2},{1,3},{2,0},{3,1},{4,6},{5,7},{6,4},{7,5},{8,10},{9,11},{10,... | collective-permute-start | bytes 3538952 | tf_op jit(solution)/shard_map/ppermute | solution.py:920
  244.6 21.9 %collective-permute-start.22 = (bf16[420,1120]{1,0:T(8,128)(2,1)}, bf16[420,1120]{1,0:T(8,128)(2,1)}, u32[]{:S(2)}, u32[]{:S(2)}) collective-permute-start(bf16[420,1120]{1,0:T(8,128)(2,1)} %collective-permute-done.19.refs_6_), channel_id=1, source_target_pairs={{0,4},{1,5},{2,6},{3,7},{4,0},{5,1},{6,2},{7,3},{8,12},{9,13},{10,... | collective-permute-start | bytes 2822408 | tf_op jit(solution)/shard_map/ppermute | solution.py:920
  282.0 11.5 %collective-permute-start.23 = (f32[1024,1152]{1,0:T(8,128)}, f32[1024,1152]{1,0:T(8,128)S(1)}, u32[]{:S(2)}, u32[]{:S(2)}) collective-permute-start(f32[1024,1152]{1,0:T(8,128)} %get-tuple-element.207), channel_id=1, source_target_pairs={{0,1},{1,0},{2,3},{3,2},{4,5},{5,4},{6,7},{7,6},{8,9},{9,8},{10,11... | collective-permute-start | bytes 14155784 | tf_op jit(solution)/shard_map/ppermute | solution.py:920
  282.2 16.6 %collective-permute-start.25 = (bf16[1024,1152]{1,0:T(8,128)(2,1)S(1)}, bf16[1024,1152]{1,0:T(8,128)(2,1)S(1)}, u32[]{:S(2)}, u32[]{:S(2)}) collective-permute-start(bf16[1024,1152]{1,0:T(8,128)(2,1)S(1)} %pad_maximum_fusion.1.cot_ref.base_ref), channel_id=1, source_target_pairs={{0,1},{1,0},{2,3},{3,2},{4,5},{5,4},{6,7},{7,6},{8,9},{9,8},{10,11... | collective-permute-start | bytes 7077896 | tf_op jit(solution)/shard_map/ppermute | solution.py:920
  297.9 4.5 collective-permute-start.24
  338.2 34.9 %collective-permute-start.26 = (f32[1024,1152]{1,0:T(8,128)}, f32[1024,1152]{1,0:T(8,128)}, u32[]{:S(2)}, u32[]{:S(2)}) collective-permute-start(f32[1024,1152]{1,0:T(8,128)} %get-tuple-element.224), channel_id=1, source_target_pairs={{0,1},{1,0},{2,3},{3,2},{4,5},{5,4},{6,7},{7,6},{8,9},{9,8},{10,11... | collective-permute-start | bytes 14155784 | tf_op jit(solution)/shard_map/ppermute | solution.py:920
  404.6 8.9 %collective-permute-start.27 = (bf16[1024,1152]{1,0:T(8,128)(2,1)}, bf16[1024,1152]{1,0:T(8,128)(2,1)}, u32[]{:S(2)}, u32[]{:S(2)}) collective-permute-start(bf16[1024,1152]{1,0:T(8,128)(2,1)} %get-tuple-element.232.own_ref), channel_id=1, source_target_pairs={{0,1},{1,0},{2,3},{3,2},{4,5},{5,4},{6,7},{7,6},{8,9},{9,8},{10,11... | collective-permute-start | bytes 7077896 | tf_op jit(solution)/shard_map/ppermute | solution.py:920
  410.4 111.1 %collective-permute-start.28 = (f32[1024,1152]{1,0:T(8,128)}, f32[1024,1152]{1,0:T(8,128)}, u32[]{:S(2)}, u32[]{:S(2)}) collective-permute-start(f32[1024,1152]{1,0:T(8,128)} %get-tuple-element.244), channel_id=1, source_target_pairs={{0,1},{1,0},{2,3},{3,2},{4,5},{5,4},{6,7},{7,6},{8,9},{9,8},{10,11... | collective-permute-start | bytes 14155784 | tf_op jit(solution)/shard_map/ppermute | solution.py:920
  410.8 118.5 %collective-permute-start.30 = (bf16[1120,1120]{1,0:T(8,128)(2,1)}, bf16[1120,1120]{1,0:T(8,128)(2,1)}, u32[]{:S(2)}, u32[]{:S(2)}) collective-permute-start(bf16[1120,1120]{1,0:T(8,128)(2,1)} %convolution_convert_fusion), channel_id=1, source_target_pairs={{0,2},{1,3},{2,0},{3,1},{4,6},{5,7},{6,4},{7,5},{8,10},{9,11},{10,... | collective-permute-start | bytes 7526408 | tf_op jit(solution)/shard_map/ppermute | solution.py:920
  411.4 117.9 %collective-permute-start.31 = (bf16[1120,1120]{1,0:T(8,128)(2,1)}, bf16[1120,1120]{1,0:T(8,128)(2,1)}, u32[]{:S(2)}, u32[]{:S(2)}) collective-permute-start(bf16[1120,1120]{1,0:T(8,128)(2,1)} %convolution_convert_fusion.1), channel_id=1, source_target_pairs={{0,2},{1,3},{2,0},{3,1},{4,6},{5,7},{6,4},{7,5},{8,10},{9,11},{10,... | collective-permute-start | bytes 7526408 | tf_op jit(solution)/shard_map/ppermute | solution.py:920
  521.5 17.5 %collective-permute-start.29 = (bf16[280,1120]{1,0:T(8,128)(2,1)S(1)}, bf16[280,1120]{1,0:T(8,128)(2,1)S(1)}, u32[]{:S(2)}, u32[]{:S(2)}) collective-permute-start(bf16[280,1120]{1,0:T(8,128)(2,1)S(1)} %copy-done.68), channel_id=1, source_target_pairs={{0,2},{1,3},{2,0},{3,1},{4,6},{5,7},{6,4},{7,5},{8,10},{9,11},{10,... | collective-permute-start | bytes 1881608 | tf_op jit(solution)/shard_map/ppermute | solution.py:920
  527.1 101.2 %collective-permute-start.33 = (bf16[1120,896]{1,0:T(8,128)(2,1)}, bf16[1120,896]{1,0:T(8,128)(2,1)}, u32[]{:S(2)}, u32[]{:S(2)}) collective-permute-start(bf16[1120,896]{1,0:T(8,128)(2,1)} %convolution_convert_fusion.2), channel_id=1, source_target_pairs={{0,2},{1,3},{2,0},{3,1},{4,6},{5,7},{6,4},{7,5},{8,10},{9,11},{10,... | collective-permute-start | bytes 6021128 | tf_op jit(solution)/shard_map/ppermute | solution.py:920
  550.5 57.9 %collective-permute-start.32 = (bf16[512,1152]{1,0:T(8,128)(2,1)}, bf16[512,1152]{1,0:T(8,128)(2,1)S(1)}, u32[]{:S(2)}, u32[]{:S(2)}) collective-permute-start(bf16[512,1152]{1,0:T(8,128)(2,1)} %slice_select_fusion.2), channel_id=1, source_target_pairs={{0,2},{1,3},{2,0},{3,1},{4,6},{5,7},{6,4},{7,5},{8,10},{9,11},{10,... | collective-permute-start | bytes 3538952 | tf_op jit(solution)/shard_map/ppermute | solution.py:920
  551.1 80.0 %collective-permute-start.34 = (bf16[3,420,1120]{2,1,0:T(8,128)(2,1)}, bf16[3,420,1120]{2,1,0:T(8,128)(2,1)}, u32[]{:S(2)}, u32[]{:S(2)}) collective-permute-start(bf16[3,420,1120]{2,1,0:T(8,128)(2,1)} %get-tuple-element.267), channel_id=1, source_target_pairs={{0,4},{4,0},{8,12},{12,8},{16,20},{20,16},{24,28},{28,24},{1,5},{5... | collective-permute-start | bytes 8467208 | tf_op jit(solution)/shard_map/ppermute | solution.py:920
  620.7 60.5 %collective-permute-start.38 = (bf16[1024,1152]{1,0:T(8,128)(2,1)S(1)}, bf16[1024,1152]{1,0:T(8,128)(2,1)S(1)}, u32[]{:S(2)}, u32[]{:S(2)}) collective-permute-start(bf16[1024,1152]{1,0:T(8,128)(2,1)S(1)} %get-tuple-element.277), channel_id=1, source_target_pairs={{0,1},{1,0},{2,3},{3,2},{4,5},{5,4},{6,7},{7,6},{8,9},{9,8},{10,11... | collective-permute-start | bytes 7077896 | tf_op jit(solution)/shard_map/ppermute | solution.py:920
  630.9 24.6 %collective-permute-start.35 = (bf16[560,896]{1,0:T(8,128)(2,1)S(1)}, bf16[560,896]{1,0:T(8,128)(2,1)S(1)}, u32[]{:S(2)}, u32[]{:S(2)}) collective-permute-start(bf16[560,896]{1,0:T(8,128)(2,1)S(1)} %select_convert_fusion), channel_id=1, source_target_pairs={{0,4},{4,0},{8,12},{12,8},{16,20},{20,16},{24,28},{28,24},{1,5},{5... | collective-permute-start | bytes 3010568 | tf_op jit(solution)/shard_map/ppermute | solution.py:920
  634.9 23.6 %collective-permute-start.36 = (bf16[420,1120]{1,0:T(8,128)(2,1)}, bf16[420,1120]{1,0:T(8,128)(2,1)S(1)}, u32[]{:S(2)}, u32[]{:S(2)}) collective-permute-start(bf16[420,1120]{1,0:T(8,128)(2,1)} %get-tuple-element.272), channel_id=1, source_target_pairs={{0,8},{4,12},{16,24},{20,28},{1,9},{5,13},{17,25},{21,29},{2,10},{... | collective-permute-start | bytes 2822408 | tf_op jit(solution)/shard_map/ppermute | solution.py:920
  636.2 42.9 %collective-permute-start.37 = (bf16[420,1120]{1,0:T(8,128)(2,1)}, bf16[420,1120]{1,0:T(8,128)(2,1)S(1)}, u32[]{:S(2)}, u32[]{:S(2)}) collective-permute-start(bf16[420,1120]{1,0:T(8,128)(2,1)} %get-tuple-element.274), channel_id=1, source_target_pairs={{0,8},{4,12},{8,0},{12,4},{16,24},{20,28},{24,16},{28,20},{1,9},{5... | collective-permute-start | bytes 2822408 | tf_op jit(solution)/shard_map/ppermute | solution.py:920
  636.4 44.9 %slice-start.2 = ((s8[4718592]{0:T(1024)(128)(4,1)}), s8[4194304]{0:T(1024)(128)(4,1)S(1)}, s32[]{:S(2)}) async-start(s8[4718592]{0:T(1024)(128)(4,1)} %bitcast.58), calls=%async_computation.2 | async-start | bytes 8388608
  638.2 43.1 %slice-start.3 = ((s8[4718592]{0:T(1024)(128)(4,1)}), s8[524288]{0:T(1024)(128)(4,1)S(1)}, s32[]{:S(2)}) async-start(s8[4718592]{0:T(1024)(128)(4,1)} %bitcast.58), calls=%async_computation.3 | async-start | bytes 1048576
  655.9 34.3 %collective-permute-start.39 = (bf16[560,896]{1,0:T(8,128)(2,1)S(1)}, bf16[560,896]{1,0:T(8,128)(2,1)S(1)}, u32[]{:S(2)}, u32[]{:S(2)}) collective-permute-start(bf16[560,896]{1,0:T(8,128)(2,1)S(1)} %get-tuple-element.282), channel_id=1, source_target_pairs={{8,0},{12,4},{24,16},{28,20},{9,1},{13,5},{25,17},{29,21},{10,2},{... | collective-permute-start | bytes 3010568 | tf_op jit(solution)/shard_map/ppermute | solution.py:920
  687.8 22.8 %collective-permute-start.41 = (bf16[420,1120]{1,0:T(8,128)(2,1)}, bf16[420,1120]{1,0:T(8,128)(2,1)}, u32[]{:S(2)}, u32[]{:S(2)}) collective-permute-start(bf16[420,1120]{1,0:T(8,128)(2,1)} %get-tuple-element.290), channel_id=1, source_target_pairs={{24,8},{28,12},{0,16},{4,20},{8,24},{12,28},{25,9},{29,13},{1,17},... | collective-permute-start | bytes 2822408 | tf_op jit(solution)/shard_map/ppermute | solution.py:920
  693.2 28.1 %collective-permute-start.42 = (bf16[512,1152]{1,0:T(8,128)(2,1)}, bf16[512,1152]{1,0:T(8,128)(2,1)}, u32[]{:S(2)}, u32[]{:S(2)}) collective-permute-start(bf16[512,1152]{1,0:T(8,128)(2,1)} %slice_select_fusion.1), channel_id=1, source_target_pairs={{0,2},{1,3},{2,0},{3,1},{4,6},{5,7},{6,4},{7,5},{8,10},{9,11},{10,... | collective-permute-start | bytes 3538952 | tf_op jit(solution)/shard_map/ppermute | solution.py:920
  695.3 2.8 collective-permute-start.40
  696.5 41.1 %collective-permute-start.43 = (bf16[560,896]{1,0:T(8,128)(2,1)}, bf16[560,896]{1,0:T(8,128)(2,1)}, u32[]{:S(2)}, u32[]{:S(2)}) collective-permute-start(bf16[560,896]{1,0:T(8,128)(2,1)} %get-tuple-element.300), channel_id=1, source_target_pairs={{16,0},{20,4},{17,1},{21,5},{18,2},{22,6},{19,3},{23,7}} | collective-permute-start | bytes 3010568 | tf_op jit(solution)/shard_map/ppermute | solution.py:920
  748.1 44.4 %copy-start.10 = (f32[12,1120]{1,0:T(8,128)S(1)}, f32[12,1120]{1,0:T(8,128)}, u32[]{:S(2)}) copy-start(f32[12,1120]{1,0:T(8,128)} %copy-done.9) | copy-start | bytes 161284
  748.1 46.7 %copy-start.51 = (f32[12,1120]{1,0:T(8,128)S(1)}, f32[12,1120]{1,0:T(8,128)}, u32[]{:S(2)}) copy-start(f32[12,1120]{1,0:T(8,128)} %param.21) | copy-start | bytes 161284
  748.1 46.8 %copy-start.52 = (f32[12,1120]{1,0:T(8,128)S(1)}, f32[12,1120]{1,0:T(8,128)}, u32[]{:S(2)}) copy-start(f32[12,1120]{1,0:T(8,128)} %param.22) | copy-start | bytes 161284
  762.8 36.1 %copy-start.16 = (f32[1,1,470400]{2,1,0:T(1,128)S(1)}, f32[1,1,470400]{2,1,0:T(1,128)}, u32[]{:S(2)}) copy-start(f32[1,1,470400]{2,1,0:T(1,128)} %weight_ref.5) | copy-start | bytes 5644804
  768.6 1.3 collective-permute-start.44
  770.0 4.4 collective-permute-start.45
  774.4 4.4 collective-permute-start.46
  778.9 9.7 %collective-permute-start.47 = (f32[16,1120]{1,0:T(8,128)S(1)}, f32[16,1120]{1,0:T(8,128)S(1)}, u32[]{:S(2)}, u32[]{:S(2)}) collective-permute-start(f32[16,1120]{1,0:T(8,128)S(1)} %add.259), channel_id=1, source_target_pairs={{0,8},{4,12},{8,0},{12,4},{16,24},{20,28},{24,16},{28,20},{1,9},{5... | collective-permute-start | bytes 215048 | tf_op jit(solution)/shard_map/ppermute | solution.py:920
  788.6 6.2 collective-permute-start.48
  (71 other events, 545.4 us)

commit v7 on v6

--- a/solution.py
+++ b/solution.py
@@ -192,24 +192,38 @@
         ]
         dqt[...] = jnp.zeros_like(dqt)
 
+        def attend(key_block, key_part, query_part):
+            key_count = key_part.stop - key_part.start
+            count = query_part.stop - query_part.start
+            k0 = pl.multiple_of(key_block * bq + key_part.start, key_count)
+            keys = pl.ds(k0, key_count)
+            rows = pl.ds(pl.multiple_of(q0 + query_part.start, count), count)
+            key_place = k0 + lax.broadcasted_iota(jnp.int32, (key_count, count), 0)
+            allowed = (key_place <= query_place[:, query_part]) & (
+                key_place >= start[:, query_part]
+            )
+            for h in range(heads):
+                scores = dot_transposed(ks[h, keys], qs[h, rows]) * factor
+                weights = jnp.exp2(
+                    jnp.where(allowed, scores - lse_ref[qb, h : h + 1, query_part], MASKED)
+                )
+                dweights = dot_transposed(vs[h, keys], ds[h, rows])
+                dscores = (weights * (dweights - inners[h][:, query_part])).astype(BF16)
+                dv[h, keys] += dot_rows(weights.astype(BF16), ds[h, rows])
+                dk[h, keys] += dot_rows(dscores, qs[h, rows])
+                dqt[h * width : (h + 1) * width, query_part] += dot_rows(
+                    kt[h, key_block, :, key_part], dscores
+                )
+
+        every = slice(0, bq)
+
         def key_step(kb, inner_carry):
-            k0 = pl.multiple_of(kb * bq, bq)
-            keys = pl.ds(k0, bq)
-            key_place = k0 + lax.broadcasted_iota(jnp.int32, (bq, bq), 0)
-            allowed = (key_place <= query_place) & (key_place >= start)
-            for h in range(heads):
-                scores = dot_transposed(ks[h, keys], qs[h, queries]) * factor
-                weights = jnp.exp2(
-                    jnp.where(allowed, scores - lse_ref[qb, h : h + 1, :], MASKED)
-                )
-                dweights = dot_transposed(vs[h, keys], ds[h, queries])
-                dscores = (weights * (dweights - inners[h])).astype(BF16)
-                dv[h, keys] += dot_rows(weights.astype(BF16), ds[h, queries])
-                dk[h, keys] += dot_rows(dscores, qs[h, queries])
-                dqt[h * width : (h + 1) * width] += dot_rows(kt[h, kb], dscores)
+            attend(kb, every, every)
             return inner_carry
 
-        lax.fori_loop(low_ref[qb], qb + 1, key_step, 0)
+        lax.fori_loop(low_ref[qb], qb, key_step, 0)
+        attend(qb, slice(0, bq // 2), every)
+        attend(qb, slice(bq // 2, bq), slice(bq // 2, bq))
         grad_ref[here, 0:flat] = (dqt[...] * score_scale).T.astype(BF16)
         return carry
 
@@ -354,6 +368,33 @@
     )(weight)
 
 
+def add_squares(sums_ref, values, in_lower):
+    squares = values * values
+    lower = jnp.sum(jnp.where(in_lower, squares, 0.0))
+    sums_ref[0] += lower
+    sums_ref[1] += jnp.sum(squares) - lower
+
+
+def square_sums_body(bound_ref, weight_ref, sums_ref):
+    sums_ref[0] = 0.0
+    sums_ref[1] = 0.0
+    place = lax.broadcasted_iota(jnp.int32, weight_ref.shape, 2)
+    add_squares(sums_ref, weight_ref[...], place < bound_ref[0])
+
+
+def square_sums(bound, weight):
+    smem = pl.BlockSpec(memory_space=pltpu.SMEM)
+    return pl.pallas_call(
+        square_sums_body,
+        in_specs=[smem, pl.BlockSpec(memory_space=pltpu.VMEM)],
+        out_specs=smem,
+        out_shape=jax.ShapeDtypeStruct((2,), F32),
+        compiler_params=vmem(32),
+        cost_estimate=lasting(6),
+        name="square_sums",
+    )(bound, weight)
+
+
 def moments_body(
     ints_ref, floats_ref, lead_ref, rest_ref, first_ref, second_ref, weight_ref,
     grad_ref, moments_ref, update_ref, sums_ref,
@@ -373,14 +414,10 @@
 
     @pl.when(step == 0)
     def clear():
-        for index in range(4):
-            sums_ref[index] = 0.0
-
-    for index, values in enumerate((weight_ref[...], update)):
-        squares = values * values
-        lower = jnp.sum(jnp.where(place < ints_ref[0], squares, 0.0))
-        sums_ref[2 * index] += lower
-        sums_ref[2 * index + 1] += jnp.sum(squares) - lower
+        sums_ref[0] = 0.0
+        sums_ref[1] = 0.0
+
+    add_squares(sums_ref, update, place < ints_ref[0])
 
 
 def flat_steps(count):
@@ -402,7 +439,7 @@
             jax.ShapeDtypeStruct(weight.shape, F32),
             jax.ShapeDtypeStruct((2,) + weight.shape, F32),
             jax.ShapeDtypeStruct(weight.shape, F32),
-            jax.ShapeDtypeStruct((4,), F32),
+            jax.ShapeDtypeStruct((2,), F32),
         ],
         compiler_params=vmem(48),
         cost_estimate=lasting(10),
@@ -1050,6 +1087,7 @@
     hat_one, _ = norm_stats(inputs)
     low_one = widen((hat_one * small_master[0] + small_master[1]).astype(BF16))
     other_one = swap(low_one, "seq", 1)
+    weight_squares = square_sums(bound, weight)
     y_index = y_here.reshape(1).astype(jnp.int32)
     if planar:
         wide = low_weight.reshape(shard_len // model_width, model_width)
@@ -1106,7 +1144,9 @@
 
     if planar:
         both = [move_rest(over[0], (1, 0), 0)]
-        halves, near, far, both[0] = tie(halves, near, far, both[0])
+        halves, near, far, both[0], weight_squares = tie(
+            halves, near, far, both[0], weight_squares
+        )
         last = move_rest(far, (2, 0), 2)
         across += [move_rest(near, (1, 0), 1), move_rest(far, (1, 0), 2)]
         over += [move_rest(near, (0, 2), 1), move_rest(far, (0, 2), 2)]
@@ -1157,11 +1197,13 @@
     grad_mid, low_mid, sums_two = norm_back(
         middle, up_kept, up_received, own_e, small_master[2:3], True
     )
-    low_mid, rows_two, rows_e = tie(low_mid, rows_two, rows_e)
+    low_mid, rows_e = tie(low_mid, rows_e)
     back_sent = dot_columns(activated[1], rows_e).astype(link)
+    back_sent, low_mid = tie(back_sent, low_mid)
+    other_mid = swap(low_mid, "seq", 1)
+    rows_two, other_mid = tie(rows_two, other_mid)
     in_sent = dot_columns(rows_two, inner[1]).astype(link)
-    back_sent, in_sent, low_mid = tie(back_sent, in_sent, low_mid)
-    other_mid = swap(low_mid, "seq", 1)
+    in_sent, low_mid = tie(in_sent, low_mid)
     back_received = swap(back_sent, "seq", 2)
     in_received = swap(in_sent, "seq", 2)
 
@@ -1318,7 +1360,7 @@
     fix_one = 1.0 - jnp.exp(steps_done * math.log(BETA_ONE))
     fix_two = 1.0 - jnp.exp(steps_done * math.log(BETA_TWO))
     ints = jnp.concatenate([bound, leads.astype(jnp.int32).reshape(1)])
-    reduced, moments, update, matrix_squares = new_moments(
+    reduced, moments, update, update_squares = new_moments(
         ints,
         jnp.stack([fix_one, fix_two]),
         lead_grad,
@@ -1327,7 +1369,7 @@
         second_moment,
         weight,
     )
-    matrix_rows = jnp.stack([matrix_sums(matrix_squares[:2]), matrix_sums(matrix_squares[2:])])
+    matrix_rows = jnp.stack([matrix_sums(weight_squares), matrix_sums(update_squares)])
     small_sum = sum_everywhere(
         jnp.concatenate([small_now, jnp.pad(matrix_rows, ((0, 2), (0, model_width - 4)))])
     )

time: 816 us -> 805 us (0.987)
    unnamed x174 -> x168, local copies, waits for them, and re-layouts: 24.1 us -> 24.5 us
  transfers between devices with their start and end apart: 49 -> 49, of which waited for: 20 -> 22; matrix products, arithmetic and copies ran while one was open for 11% -> 13% of each run, Pallas kernels for 36% -> 36%
where the time goes in v7:
time: 805 us; the launch traced here: 796 us
  Pallas kernels  364 us (45%)
  waiting for transfers between devices  186 us (23%)
  starting transfers between devices  81.1 us (10%)
  matrix products  66.7 us (8%)
  local copies, waits for them, and re-layouts  48.7 us (6%)
  other arithmetic  42.7 us (5%)
    ppermute x49, waiting for transfers between devices, permute(): return lax.ppermute(value, axis_name, pairs)  186 us
    pallas_call x2, Pallas kernels, attention_backward(): pl.pallas_call(functools.partial(attention_backward_body, heads, width, b...  104 us
    ppermute x49, starting transfers between devices, permute(): return lax.ppermute(value, axis_name, pairs)  81.1 us
    pallas_call x2, Pallas kernels, attention_forward(): pl.pallas_call(functools.partial(attention_forward_body, heads, width, bq...  69.9 us
    pallas_call x2, Pallas kernels, feed_forward(): pl.pallas_call(functools.partial(feed_forward_body, len(filled)), out_sha...  69.4 us
    dot_general x8, matrix products, dot_columns(): lax.dot_general(left, right, (((0,), (0,)), ((), ())), preferred_element_...  66.7 us
    unnamed x168, local copies, waits for them, and re-layouts  24.5 us
    pallas_call x2, Pallas kernels, split_product(): pl.pallas_call(functools.partial(split_product_body, steps, turned, len(l...  19.3 us
  transfers between devices with their start and end apart: 49, of which 22 were waited for; matrix products, arithmetic and copies ran while one was open for 13% of the time, Pallas kernels for 36%

profile of v7, /device:TPU:0, one launch (start us, length us, event | category | flops | bytes accessed | tf_op | source)
XLA Modules:
  0.0 796.2 jit_solution(17624238024192456348)
XLA Ops:
  5.3 2.9 collective-permute-start
  10.9 5.5 collective-permute-start.1
  17.1 17.4 %collective-permute-done = bf16[512,1152]{1,0:T(8,128)(2,1)} collective-permute-done((bf16[512,1152]{1,0:T(8,128)(2,1)}, bf16[512,1152]{1,0:T(8,128)(2,1)}, u32[]{:S(2)}, u32[]{:S(2)}) %collective-permute-start) | collective-permute-done | bytes 1179680 | tf_op jit(solution)/shard_map/ppermute | solution.py:957
  41.9 5.9 collective-permute-start.2
  56.0 13.2 %collective-permute-done.2 = bf16[560,840]{1,0:T(8,128)(2,1)} collective-permute-done((bf16[560,840]{1,0:T(8,128)(2,1)}, bf16[560,840]{1,0:T(8,128)(2,1)}, u32[]{:S(2)}, u32[]{:S(2)}) %collective-permute-start.2) | collective-permute-done | bytes 940832 | tf_op jit(solution)/shard_map/ppermute | solution.py:957
  78.6 16.0 %collective-permute-done.6.a1 = bf16[560,840]{1,0:T(8,128)(2,1)} collective-permute-done((bf16[560,840]{1,0:T(8,128)(2,1)S(1)}, bf16[560,840]{1,0:T(8,128)(2,1)}, u32[]{:S(2)}, u32[]{:S(2)}) %collective-permute-start.6) | collective-permute-done | bytes 940832 | tf_op jit(solution)/shard_map/ppermute | solution.py:957
  101.5 4.7 square_sums.1
  106.2 20.2 %collective-permute-done.10.refs_4_ = bf16[420,1120]{1,0:T(8,128)(2,1)} collective-permute-done((bf16[420,1120]{1,0:T(8,128)(2,1)}, bf16[420,1120]{1,0:T(8,128)(2,1)}, u32[]{:S(2)}, u32[]{:S(2)}) %collective-permute-start.10) | collective-permute-done | bytes 940832 | tf_op jit(solution)/shard_map/ppermute | solution.py:957
  129.6 3.4 collective-permute-start.14
  133.1 2.4 collective-permute-start.13
  135.5 2.4 collective-permute-start.15
  137.9 3.4 collective-permute-start.16
  141.3 16.6 %project.1 = (bf16[2048,840]{1,0:T(8,128)(2,1)}, bf16[2048,840]{1,0:T(8,128)(2,1)}, bf16[2048,1120]{1,0:T(8,128)(2,1)}, bf16[1120,840]{1,0:T(8,128)(2,1)S(1)}, bf16[1120,840]{1,0:T(8,128)(2,1)}) custom-call(s32[1]{0:T(128)} %bitcast.2.place_ref, bf16[1024,1152]{1,0:T(8,128)(2,1)} %pad.11.own_ref, bf16[1024,1152]{1,0:T(8,128)(2,1)} %collective-permute-done.5.other_ref, ...), custom_call_target="tpu_custom_call" | custom-call | flops 16000000000 | bytes 4096 | tf_op jit(solution)/shard_map/project/pallas_call | solution.py:613
  158.0 35.2 %attention_forward.2 = (bf16[2048,280]{1,0:T(8,128)(2,1)S(1)}, f32[4,280,512]{2,1,0:T(8,128)S(1)}, f32[4,8,512]{2,1,0:T(8,128)S(1)}) custom-call(s32[4]{0:T(128)S(1)} %and_select_fusion.low_ref, s32[1]{0:T(128)} %bitcast.8.core_ref, s32[4,1,512]{2,1,0:T(1,128)S(1)} %compare_select_fusion.start_ref, bf16[2048,840]{1,0:T(8,128)(2,1)} %get-tuple-element.175.qkv_ref), custom_call_target="tpu_custom_call" | custom-call | flops 35000000512 | bytes 4096 | tf_op jit(solution)/shard_map/attention_forward/pallas_call | solution.py:274
  197.2 3.9 collective-permute-start.20
  201.1 3.9 collective-permute-start.21
  205.1 34.7 %attention_forward.3 = (bf16[2048,280]{1,0:T(8,128)(2,1)S(1)}, f32[4,280,512]{2,1,0:T(8,128)S(1)}, f32[4,8,512]{2,1,0:T(8,128)S(1)}) custom-call(s32[4]{0:T(128)S(1)} %and_select_fusion.low_ref, s32[1]{0:T(128)} %bitcast.8.core_ref, s32[4,1,512]{2,1,0:T(1,128)S(1)} %compare_select_fusion.start_ref, bf16[2048,840]{1,0:T(8,128)(2,1)} %get-tuple-element.181.qkv_ref), custom_call_target="tpu_custom_call" | custom-call | flops 35000000512 | bytes 4096 | tf_op jit(solution)/shard_map/attention_forward/pallas_call | solution.py:274
  244.0 3.0 collective-permute-start.22
  247.1 5.7 unpack_share.2
  252.8 11.8 %collective-permute-done.17 = bf16[512,1152]{1,0:T(8,128)(2,1)S(1)} collective-permute-done((bf16[512,1152]{1,0:T(8,128)(2,1)S(1)}, bf16[512,1152]{1,0:T(8,128)(2,1)S(1)}, u32[]{:S(2)}, u32[]{:S(2)}) %collective-permute-start.17) | collective-permute-done | bytes 1179680 | tf_op jit(solution)/shard_map/ppermute | solution.py:957
  267.1 5.4 unpack_share.3
  272.6 8.7 %split_product.2 = (f32[1024,1152]{1,0:T(8,128)}, f32[1024,1120]{1,0:T(8,128)}) custom-call(bf16[2048,280]{1,0:T(8,128)(2,1)S(1)} %get-tuple-element.182.refs_0_, bf16[2048,280]{1,0:T(8,128)(2,1)S(1)} %copy-done.25, bf16[280,1120]{1,0:T(8,128)(2,1)S(1)} %get-tuple-element.200.refs_2_.w_a, bf16[280,1120]{1,0:T(8,128)(2,1)S(1)} %get-tuple-element.208.refs_3_.w_b), custom_call_target="tpu_custom_call" | custom-call | flops 8999999488 | bytes 4096 | tf_op jit(solution)/shard_map/split_product/pallas_call | solution.py:720
  282.0 10.7 %collective-permute-done.23.got_ref = f32[1024,1152]{1,0:T(8,128)S(1)} collective-permute-done((f32[1024,1152]{1,0:T(8,128)}, f32[1024,1152]{1,0:T(8,128)S(1)}, u32[]{:S(2)}, u32[]{:S(2)}) %collective-permute-start.23) | collective-permute-done | bytes 4718624 | tf_op jit(solution)/shard_map/ppermute | solution.py:957
  298.6 3.1 collective-permute-done.24.rows_ref
  303.1 34.4 %feed_forward.2 = (bf16[2048,1120]{1,0:T(8,128)(2,1)}, bf16[2048,1120]{1,0:T(8,128)(2,1)}, bf16[2048,1120]{1,0:T(8,128)(2,1)}, bf16[2048,1120]{1,0:T(8,128)(2,1)...) custom-call(bf16[1024,1152]{1,0:T(8,128)(2,1)} %copy-done.65, ...), custom_call_target="tpu_custom_call" | custom-call | flops 33999998976 | bytes 4096 | tf_op jit(solution)/shard_map/feed_forward/pallas_call | solution.py:934
  337.7 34.9 %feed_forward.3 = (bf16[2048,1120]{1,0:T(8,128)(2,1)}, bf16[2048,1120]{1,0:T(8,128)(2,1)}, bf16[2048,1120]{1,0:T(8,128)(2,1)}, bf16[2048,1120]{1,0:T(8,128)(2,1)...) custom-call(bf16[1024,1152]{1,0:T(8,128)(2,1)} %copy-done.12, ...), custom_call_target="tpu_custom_call", output_to_operand_aliasing={{0}: (7, {}), {1}: (8, {}), {2}: (9, {}), {3}: (10, {}), {4... | custom-call | flops 33999998976 | bytes 4096 | tf_op jit(solution)/shard_map/feed_forward/pallas_call | solution.py:934
  372.7 2.3 copy-done.1
  375.0 7.9 norm_back.2
  383.0 11.7 %convolution_convert_fusion.1 = bf16[1120,1120]{1,0:T(8,128)(2,1)} fusion(bf16[2048,1120]{1,0:T(8,128)(2,1)} %get-tuple-element.225, bf16[2048,1120]{1,0:T(8,128)(2,1)S(1)} %copy-done.68), kind=kOutput, calls=%fused_computation.1 | convolution fusion | flops 5139276800 | bytes 11683840 | tf_op jit(solution)/shard_map/dot_general | solution.py:39
  397.3 3.0 fusion.22
  401.5 11.6 %convolution_convert_fusion = bf16[1120,1120]{1,0:T(8,128)(2,1)} fusion(bf16[2048,1120]{1,0:T(8,128)(2,1)} %get-tuple-element.240, bf16[2048,1120]{1,0:T(8,128)(2,1)} %get-tuple-element.235), kind=kOutput, calls=%fused_computation | convolution fusion | flops 5139276800 | bytes 11683840 | tf_op jit(solution)/shard_map/dot_general | solution.py:39
  413.1 8.3 %out_grads.1 = (bf16[2048,280]{1,0:T(8,128)(2,1)S(1)}, bf16[2048,280]{1,0:T(8,128)(2,1)S(1)}, bf16[2048,1120]{1,0:T(8,128)(2,1)}) custom-call(bf16[1024,1152]{1,0:T(8,128)(2,1)} %get-tuple-element.236.own_ref, bf16[1024,1152]{1,0:T(8,128)(2,1)} %collective-permute-done.27.other_ref, bf16[280,1120]{1,0:T(8,128)(2,1)S(1)} %copy-done.34, ...), custom_call_target="tpu_custom_call" | custom-call | flops 8000000000 | bytes 4096 | tf_op jit(solution)/shard_map/out_grads/pallas_call | solution.py:646
  421.5 6.0 convolution_convert_fusion.3
  429.4 8.5 %fusion.41.in_ref = f32[1120,1120]{1,0:T(8,128)} fusion(bf16[2048,1120]{1,0:T(8,128)(2,1)S(1)} %bitcast.70, bf16[2048,1120]{1,0:T(8,128)(2,1)S(1)} %bitcast.68), kind=kOutput, calls=%fused_computation.126 | convolution fusion | flops 5138022400 | bytes 14192640 | tf_op jit(solution)/shard_map/dot_general | solution.py:39
  437.9 8.7 %fusion.40.back_ref = f32[1120,1120]{1,0:T(8,128)} fusion(bf16[2048,1120]{1,0:T(8,128)(2,1)S(1)} %bitcast.66, bf16[2048,1120]{1,0:T(8,128)(2,1)S(1)} %bitcast.72), kind=kOutput, calls=%fused_computation.125 | convolution fusion | flops 5138022400 | bytes 14192640 | tf_op jit(solution)/shard_map/dot_general | solution.py:39
  448.6 52.0 %attention_backward.2.left = bf16[2048,896]{1,0:T(8,128)(2,1)} custom-call(s32[4]{0:T(128)} %copy-done.22, s32[1]{0:T(128)} %bitcast.8.core_ref, s32[4,1,512]{2,1,0:T(1,128)} %copy-done.11, bf16[2048,840]{1,0:T(8,128)(2,1)} %get-tuple-element.181.qkv_ref, bf16[2048,280]{1,0:T(8,128)(2,1)} %copy-done.38, f32[4,280,512]{2,1,0:T(8,128)} %copy-done.40, ...), custom_call_target="tpu_custom_call" | custom-call | flops 56000000000 | bytes 4096 | tf_op jit(solution)/shard_map/attention_backward/pallas_call | solution.py:317
  500.6 9.9 %convolution_convert_fusion.2 = bf16[1120,896]{1,0:T(8,128)(2,1)} fusion(bf16[2048,1120]{1,0:T(8,128)(2,1)} %get-tuple-element.174, bf16[2048,896]{1,0:T(8,128)(2,1)} %attention_backward.2.left), kind=kOutput, calls=%fused_computation.17 | convolution fusion | flops 4111421440 | bytes 10264576 | tf_op jit(solution)/shard_map/dot_general | solution.py:39
  510.5 8.0 partial_product.1.refs_2_
  518.5 4.5 fusion.8
  525.8 10.1 %collective-permute-done.29.out_got = bf16[280,1120]{1,0:T(8,128)(2,1)S(1)} collective-permute-done((bf16[280,1120]{1,0:T(8,128)(2,1)S(1)}, bf16[280,1120]{1,0:T(8,128)(2,1)S(1)}, u32[]{:S(2)}, u32[]{:S(2)}) %collective-permute-start.29) | collective-permute-done | bytes 627232 | tf_op jit(solution)/shard_map/ppermute | solution.py:957
  535.9 10.4 %pack_rest.1 = (f32[3,420,1120]{2,1,0:T(8,128)}, bf16[3,420,1120]{2,1,0:T(8,128)(2,1)}) custom-call(s32[1]{0:T(128)} %bitcast.2.place_ref, f32[280,1120]{1,0:T(8,128)S(1)} %fusion.42.out_ref, f32[1120,1120]{1,0:T(8,128)} %fusion.41.in_ref, f32[1120,1120]{1,0:T(8,128)} %fusion.40.back_ref, bf16[280,1120]{1,0:T(8,128)(2,1)S(1)} %collective-permute-done.29.out_got, ...), custom_call_target="tpu_custom_call" | custom-call | flops 10000000000 | bytes 4096 | tf_op jit(solution)/shard_map/pack_rest/pallas_call | solution.py:552
  547.5 51.9 %attention_backward.3.refs_0_ = bf16[2048,896]{1,0:T(8,128)(2,1)} custom-call(s32[4]{0:T(128)} %copy-done.22, s32[1]{0:T(128)} %bitcast.8.core_ref, s32[4,1,512]{2,1,0:T(1,128)} %copy-done.11, bf16[2048,840]{1,0:T(8,128)(2,1)} %get-tuple-element.175.qkv_ref, bf16[2048,280]{1,0:T(8,128)(2,1)} %copy-done.37, f32[4,280,512]{2,1,0:T(8,128)} %copy-done.39, ...), custom_call_target="tpu_custom_call" | custom-call | flops 56000000000 | bytes 4096 | tf_op jit(solution)/shard_map/attention_backward/pallas_call | solution.py:317
  599.4 3.6 collective-permute-done.32.received_ref
  604.5 10.6 %split_product.3 = (bf16[1024,1152]{1,0:T(8,128)(2,1)S(1)}, f32[1024,1120]{1,0:T(8,128)}) custom-call(bf16[2048,896]{1,0:T(8,128)(2,1)} %attention_backward.3.refs_0_, bf16[1120,840]{1,0:T(8,128)(2,1)S(1)} %copy-done.29, f32[2048,1120]{1,0:T(8,128)} %partial_product.1.refs_2_), custom_call_target="tpu_custom_call" | custom-call | flops 8999999488 | bytes 4096 | tf_op jit(solution)/shard_map/split_product/pallas_call | solution.py:720
  615.1 8.6 %fusion.43 = f32[1120,896]{1,0:T(8,128)S(1)} fusion(bf16[2048,1120]{1,0:T(8,128)(2,1)} %get-tuple-element.174, bf16[2048,896]{1,0:T(8,128)(2,1)} %attention_backward.3.refs_0_), kind=kOutput, calls=%fused_computation.128 | convolution fusion | flops 4110417920 | bytes 12271616 | tf_op jit(solution)/shard_map/dot_general | solution.py:39
  626.5 3.6 fusion.31
  633.5 16.1 %collective-permute-done.35 = bf16[560,896]{1,0:T(8,128)(2,1)} collective-permute-done((bf16[560,896]{1,0:T(8,128)(2,1)S(1)}, bf16[560,896]{1,0:T(8,128)(2,1)}, u32[]{:S(2)}, u32[]{:S(2)}) %collective-permute-start.35) | collective-permute-done | bytes 1003552 | tf_op jit(solution)/shard_map/ppermute | solution.py:957
  653.8 20.7 %collective-permute-done.37 = bf16[420,1120]{1,0:T(8,128)(2,1)S(1)} collective-permute-done((bf16[420,1120]{1,0:T(8,128)(2,1)}, bf16[420,1120]{1,0:T(8,128)(2,1)S(1)}, u32[]{:S(2)}, u32[]{:S(2)}) %collective-permute-start.37) | collective-permute-done | bytes 940832 | tf_op jit(solution)/shard_map/ppermute | solution.py:957
  676.6 6.5 norm_back.3
  683.1 2.2 collective-permute-start.41
  691.9 14.1 %collective-permute-done.41 = bf16[420,1120]{1,0:T(8,128)(2,1)} collective-permute-done((bf16[420,1120]{1,0:T(8,128)(2,1)}, bf16[420,1120]{1,0:T(8,128)(2,1)}, u32[]{:S(2)}, u32[]{:S(2)}) %collective-permute-start.41) | collective-permute-done | bytes 940832 | tf_op jit(solution)/shard_map/ppermute | solution.py:957
  706.0 3.2 convert_add_fusion.3
  709.2 5.5 reshape.195.rest_ref
  716.1 3.0 place_rows.3
  719.2 13.8 %collective-permute-done.43 = bf16[560,896]{1,0:T(8,128)(2,1)} collective-permute-done((bf16[560,896]{1,0:T(8,128)(2,1)S(1)}, bf16[560,896]{1,0:T(8,128)(2,1)}, u32[]{:S(2)}, u32[]{:S(2)}) %collective-permute-start.43) | collective-permute-done | bytes 1003552 | tf_op jit(solution)/shard_map/ppermute | solution.py:957
  733.0 2.7 slice_add_fusion.1
  735.6 6.2 reshape.198.lead_ref
  743.3 10.4 %new_moments.1 = (f32[1,1,470400]{2,1,0:T(1,128)}, f32[2,1,1,470400]{3,2,1,0:T(1,128)}, f32[1,1,470400]{2,1,0:T(1,128)S(1)}, f32[2]{0:T(128)S(1)}) custom-call(s32[2]{0:T(128)S(1)} %pad_add_fusion.ints_ref, f32[2]{0:T(128)S(1)} %pad_maximum_fusion.9.floats_ref, f32[1,1,470400]{2,1,0:T(1,128)S(1)} %copy-done.8, f32[1,1,470400]{2,1,0:T(1,128)S(1)} %copy-done.7, ...), custom_call_target="tpu_custom_call" | custom-call | flops 10000000000 | bytes 4096 | tf_op jit(solution)/shard_map/new_moments/pallas_call | solution.py:433
  755.6 2.5 fusion.23
  759.8 4.1 collective-permute-done.45
  765.9 2.4 collective-permute-done.46
  768.3 7.4 collective-permute-start.47
  778.1 3.6 collective-permute-start.48
  789.5 6.5 new_weights.1
  (331 shorter events, 107.2 us)
Async XLA Ops:
  1.5 393.6 %copy-start.9 = (f32[12,1120]{1,0:T(8,128)}, f32[12,1120]{1,0:T(8,128)S(1)}, u32[]{:S(2)}) copy-start(f32[12,1120]{1,0:T(8,128)S(1)} %copy.47.small_ref) | copy-start | bytes 161284
  5.3 29.2 %collective-permute-start = (bf16[512,1152]{1,0:T(8,128)(2,1)}, bf16[512,1152]{1,0:T(8,128)(2,1)}, u32[]{:S(2)}, u32[]{:S(2)}) collective-permute-start(bf16[512,1152]{1,0:T(8,128)(2,1)} %get-tuple-element.164), channel_id=1, source_target_pairs={{0,2},{1,3},{2,0},{3,1},{4,6},{5,7},{6,4},{7,5},{8,10},{9,11},{10,... | collective-permute-start | bytes 3538952 | tf_op jit(solution)/shard_map/ppermute | solution.py:957
  10.9 29.8 %collective-permute-start.1 = (bf16[560,840]{1,0:T(8,128)(2,1)S(1)}, bf16[560,840]{1,0:T(8,128)(2,1)}, u32[]{:S(2)}, u32[]{:S(2)}) collective-permute-start(bf16[560,840]{1,0:T(8,128)(2,1)S(1)} %reshape.190), channel_id=1, source_target_pairs={{0,16},{4,20},{1,17},{5,21},{2,18},{6,22},{3,19},{7,23}} | collective-permute-start | bytes 2822408 | tf_op jit(solution)/shard_map/ppermute | solution.py:957
  40.8 29.8 %collective-permute-start.5 = (bf16[1024,1152]{1,0:T(8,128)(2,1)}, bf16[1024,1152]{1,0:T(8,128)(2,1)}, u32[]{:S(2)}, u32[]{:S(2)}) collective-permute-start(bf16[1024,1152]{1,0:T(8,128)(2,1)} %pad.11.own_ref), channel_id=1, source_target_pairs={{0,1},{1,0},{2,3},{3,2},{4,5},{5,4},{6,7},{7,6},{8,9},{9,8},{10,11... | collective-permute-start | bytes 7077896 | tf_op jit(solution)/shard_map/ppermute | solution.py:957
  41.9 27.4 %collective-permute-start.2 = (bf16[560,840]{1,0:T(8,128)(2,1)}, bf16[560,840]{1,0:T(8,128)(2,1)}, u32[]{:S(2)}, u32[]{:S(2)}) collective-permute-start(bf16[560,840]{1,0:T(8,128)(2,1)} %broadcast_select_fusion.4), channel_id=1, source_target_pairs={{0,8},{4,12},{16,24},{20,28},{1,9},{5,13},{17,25},{21,29},{2,10},{... | collective-permute-start | bytes 2822408 | tf_op jit(solution)/shard_map/ppermute | solution.py:957
  50.0 20.5 %collective-permute-start.3 = (bf16[420,1120]{1,0:T(8,128)(2,1)}, bf16[420,1120]{1,0:T(8,128)(2,1)}, u32[]{:S(2)}, u32[]{:S(2)}) collective-permute-start(bf16[420,1120]{1,0:T(8,128)(2,1)} %reshape.191.refs_0_), channel_id=1, source_target_pairs={{8,12},{9,13},{10,14},{11,15},{12,8},{13,9},{14,10},{15,11},{16,20... | collective-permute-start | bytes 2822408 | tf_op jit(solution)/shard_map/ppermute | solution.py:957
  51.6 18.9 %collective-permute-start.4 = (bf16[420,1120]{1,0:T(8,128)(2,1)}, bf16[420,1120]{1,0:T(8,128)(2,1)}, u32[]{:S(2)}, u32[]{:S(2)}) collective-permute-start(bf16[420,1120]{1,0:T(8,128)(2,1)} %reshape.191.refs_0_), channel_id=1, source_target_pairs={{8,10},{9,11},{10,8},{11,9},{12,14},{13,15},{14,12},{15,13},{16,18... | collective-permute-start | bytes 2822408 | tf_op jit(solution)/shard_map/ppermute | solution.py:957
  56.0 40.1 %copy-start.61 = (s32[4]{0:T(128)S(1)}, s32[4]{0:T(128)}, u32[]{:S(2)}) copy-start(s32[4]{0:T(128)} %constant.164.clone) | copy-start | bytes 52
  70.6 24.0 %collective-permute-start.6 = (bf16[560,840]{1,0:T(8,128)(2,1)S(1)}, bf16[560,840]{1,0:T(8,128)(2,1)}, u32[]{:S(2)}, u32[]{:S(2)}) collective-permute-start(bf16[560,840]{1,0:T(8,128)(2,1)S(1)} %broadcast_select_fusion.5.a0), channel_id=1, source_target_pairs={{0,4},{4,0},{8,12},{12,8},{16,20},{20,16},{24,28},{28,24},{1,5},{5... | collective-permute-start | bytes 2822408 | tf_op jit(solution)/shard_map/ppermute | solution.py:957
  72.7 132.5 %copy-start.22 = (s32[4]{0:T(128)}, s32[4]{0:T(128)S(1)}, u32[]{:S(2)}) copy-start(s32[4]{0:T(128)S(1)} %and_select_fusion.low_ref) | copy-start | bytes 52
  72.7 33.5 %collective-permute-start.7 = (bf16[560,840]{1,0:T(8,128)(2,1)S(1)}, bf16[560,840]{1,0:T(8,128)(2,1)}, u32[]{:S(2)}, u32[]{:S(2)}) collective-permute-start(bf16[560,840]{1,0:T(8,128)(2,1)S(1)} %broadcast_select_fusion.5.a0), channel_id=1, source_target_pairs={{0,2},{1,3},{2,0},{3,1},{4,6},{5,7},{6,4},{7,5},{8,10},{9,11},{10,... | collective-permute-start | bytes 2822408 | tf_op jit(solution)/shard_map/ppermute | solution.py:957
  74.2 52.1 %collective-permute-start.10 = (bf16[420,1120]{1,0:T(8,128)(2,1)}, bf16[420,1120]{1,0:T(8,128)(2,1)}, u32[]{:S(2)}, u32[]{:S(2)}) collective-permute-start(bf16[420,1120]{1,0:T(8,128)(2,1)} %reshape.191.refs_0_), channel_id=1, source_target_pairs={{8,24},{9,25},{10,26},{11,27},{12,28},{13,29},{14,30},{15,31},{16,... | collective-permute-start | bytes 2822408 | tf_op jit(solution)/shard_map/ppermute | solution.py:957
  75.5 52.2 %collective-permute-start.9 = (bf16[420,1120]{1,0:T(8,128)(2,1)}, bf16[420,1120]{1,0:T(8,128)(2,1)}, u32[]{:S(2)}, u32[]{:S(2)}) collective-permute-start(bf16[420,1120]{1,0:T(8,128)(2,1)} %reshape.191.refs_0_), channel_id=1, source_target_pairs={{8,0},{9,1},{10,2},{11,3},{12,4},{13,5},{14,6},{15,7},{16,24},{17,... | collective-permute-start | bytes 2822408 | tf_op jit(solution)/shard_map/ppermute | solution.py:957
  76.8 49.5 %collective-permute-start.11 = (bf16[420,1120]{1,0:T(8,128)(2,1)}, bf16[420,1120]{1,0:T(8,128)(2,1)}, u32[]{:S(2)}, u32[]{:S(2)}) collective-permute-start(bf16[420,1120]{1,0:T(8,128)(2,1)} %collective-permute-done.4.refs_0_), channel_id=1, source_target_pairs={{8,12},{9,13},{10,14},{11,15},{12,8},{13,9},{14,10},{15,11},{16,20... | collective-permute-start | bytes 2822408 | tf_op jit(solution)/shard_map/ppermute | solution.py:957
  94.6 33.1 %collective-permute-start.8 = (bf16[560,840]{1,0:T(8,128)(2,1)}, bf16[560,840]{1,0:T(8,128)(2,1)}, u32[]{:S(2)}, u32[]{:S(2)}) collective-permute-start(bf16[560,840]{1,0:T(8,128)(2,1)} %collective-permute-done.6.a1), channel_id=1, source_target_pairs={{0,2},{1,3},{2,0},{3,1},{4,6},{5,7},{6,4},{7,5},{8,10},{9,11},{10,... | collective-permute-start | bytes 2822408 | tf_op jit(solution)/shard_map/ppermute | solution.py:957
  100.0 105.2 %copy-start.11 = (s32[4,1,512]{2,1,0:T(1,128)}, s32[4,1,512]{2,1,0:T(1,128)S(1)}, u32[]{:S(2)}) copy-start(s32[4,1,512]{2,1,0:T(1,128)S(1)} %compare_select_fusion.start_ref) | copy-start | bytes 24580
  127.7 65.6 %collective-permute-start.12 = (bf16[420,1120]{1,0:T(8,128)(2,1)}, bf16[420,1120]{1,0:T(8,128)(2,1)}, u32[]{:S(2)}, u32[]{:S(2)}) collective-permute-start(bf16[420,1120]{1,0:T(8,128)(2,1)} %collective-permute-done.10.refs_4_), channel_id=1, source_target_pairs={{0,8},{1,9},{2,10},{3,11},{4,12},{5,13},{6,14},{7,15},{8,0},{9,1},... | collective-permute-start | bytes 2822408 | tf_op jit(solution)/shard_map/ppermute | solution.py:957
  129.6 63.7 %collective-permute-start.14 = (bf16[420,1120]{1,0:T(8,128)(2,1)}, bf16[420,1120]{1,0:T(8,128)(2,1)}, u32[]{:S(2)}, u32[]{:S(2)}) collective-permute-start(bf16[420,1120]{1,0:T(8,128)(2,1)} %collective-permute-done.10.refs_4_), channel_id=1, source_target_pairs={{0,4},{1,5},{2,6},{3,7},{4,0},{5,1},{6,2},{7,3},{8,12},{9,13},{10,... | collective-permute-start | bytes 2822408 | tf_op jit(solution)/shard_map/ppermute | solution.py:957
  133.1 60.2 %collective-permute-start.13 = (bf16[420,1120]{1,0:T(8,128)(2,1)}, bf16[420,1120]{1,0:T(8,128)(2,1)S(1)}, u32[]{:S(2)}, u32[]{:S(2)}) collective-permute-start(bf16[420,1120]{1,0:T(8,128)(2,1)} %collective-permute-done.9.refs_2_), channel_id=1, source_target_pairs={{0,4},{1,5},{2,6},{3,7},{4,0},{5,1},{6,2},{7,3},{16,20},{17,21},{1... | collective-permute-start | bytes 2822408 | tf_op jit(solution)/shard_map/ppermute | solution.py:957
  135.5 57.8 %collective-permute-start.15 = (bf16[420,1120]{1,0:T(8,128)(2,1)}, bf16[420,1120]{1,0:T(8,128)(2,1)S(1)}, u32[]{:S(2)}, u32[]{:S(2)}) collective-permute-start(bf16[420,1120]{1,0:T(8,128)(2,1)} %collective-permute-done.9.refs_2_), channel_id=1, source_target_pairs={{0,2},{1,3},{2,0},{3,1},{4,6},{5,7},{6,4},{7,5},{16,18},{17,19},{1... | collective-permute-start | bytes 2822408 | tf_op jit(solution)/shard_map/ppermute | solution.py:957
  137.9 55.4 %collective-permute-start.16 = (bf16[420,1120]{1,0:T(8,128)(2,1)}, bf16[420,1120]{1,0:T(8,128)(2,1)S(1)}, u32[]{:S(2)}, u32[]{:S(2)}) collective-permute-start(bf16[420,1120]{1,0:T(8,128)(2,1)} %collective-permute-done.10.refs_4_), channel_id=1, source_target_pairs={{0,2},{1,3},{2,0},{3,1},{4,6},{5,7},{6,4},{7,5},{8,10},{9,11},{10,... | collective-permute-start | bytes 2822408 | tf_op jit(solution)/shard_map/ppermute | solution.py:957
  158.0 35.3 %copy-start.28 = (bf16[1120,840]{1,0:T(8,128)(2,1)}, bf16[1120,840]{1,0:T(8,128)(2,1)S(1)}, u32[]{:S(2)}) copy-start(bf16[1120,840]{1,0:T(8,128)(2,1)S(1)} %get-tuple-element.265.refs_1_) | copy-start | bytes 5644804
  158.0 47.1 %copy-start.19 = (bf16[512,1152]{1,0:T(8,128)(2,1)S(1)}, bf16[512,1152]{1,0:T(8,128)(2,1)}, u32[]{:S(2)}) copy-start(bf16[512,1152]{1,0:T(8,128)(2,1)} %copy-done.18) | copy-start | bytes 3538948
  193.2 46.6 %copy-start.39 = (f32[4,280,512]{2,1,0:T(8,128)}, f32[4,280,512]{2,1,0:T(8,128)S(1)}, u32[]{:S(2)}) copy-start(f32[4,280,512]{2,1,0:T(8,128)S(1)} %get-tuple-element.262.outt_ref) | copy-start | bytes 6881284
  193.2 46.6 %copy-start.41 = (f32[4,8,512]{2,1,0:T(8,128)}, f32[4,8,512]{2,1,0:T(8,128)S(1)}, u32[]{:S(2)}) copy-start(f32[4,8,512]{2,1,0:T(8,128)S(1)} %get-tuple-element.180.lse_ref) | copy-start | bytes 196612
  193.3 49.7 %collective-permute-start.18 = (bf16[420,1120]{1,0:T(8,128)(2,1)}, bf16[420,1120]{1,0:T(8,128)(2,1)}, u32[]{:S(2)}, u32[]{:S(2)}) collective-permute-start(bf16[420,1120]{1,0:T(8,128)(2,1)} %collective-permute-done.12.refs_6_), channel_id=1, source_target_pairs={{0,4},{1,5},{2,6},{3,7},{4,0},{5,1},{6,2},{7,3},{8,12},{9,13},{10,... | collective-permute-start | bytes 2822408 | tf_op jit(solution)/shard_map/ppermute | solution.py:957
  195.2 47.8 %collective-permute-start.19 = (bf16[420,1120]{1,0:T(8,128)(2,1)}, bf16[420,1120]{1,0:T(8,128)(2,1)}, u32[]{:S(2)}, u32[]{:S(2)}) collective-permute-start(bf16[420,1120]{1,0:T(8,128)(2,1)} %collective-permute-done.12.refs_6_), channel_id=1, source_target_pairs={{0,2},{1,3},{2,0},{3,1},{4,6},{5,7},{6,4},{7,5},{8,10},{9,11},{10,... | collective-permute-start | bytes 2822408 | tf_op jit(solution)/shard_map/ppermute | solution.py:957
  197.2 45.9 %collective-permute-start.20 = (bf16[420,1120]{1,0:T(8,128)(2,1)S(1)}, bf16[420,1120]{1,0:T(8,128)(2,1)S(1)}, u32[]{:S(2)}, u32[]{:S(2)}) collective-permute-start(bf16[420,1120]{1,0:T(8,128)(2,1)S(1)} %collective-permute-done.15.refs_2_), channel_id=1, source_target_pairs={{0,4},{1,5},{2,6},{3,7},{4,0},{5,1},{6,2},{7,3},{16,20},{17,21},{1... | collective-permute-start | bytes 2822408 | tf_op jit(solution)/shard_map/ppermute | solution.py:957
  201.1 43.0 %collective-permute-start.21 = (bf16[420,1120]{1,0:T(8,128)(2,1)}, bf16[420,1120]{1,0:T(8,128)(2,1)}, u32[]{:S(2)}, u32[]{:S(2)}) collective-permute-start(bf16[420,1120]{1,0:T(8,128)(2,1)} %collective-permute-done.14.refs_5_), channel_id=1, source_target_pairs={{0,2},{1,3},{2,0},{3,1},{4,6},{5,7},{6,4},{7,5},{8,10},{9,11},{10,... | collective-permute-start | bytes 2822408 | tf_op jit(solution)/shard_map/ppermute | solution.py:957
  205.0 59.5 %collective-permute-start.17 = (bf16[512,1152]{1,0:T(8,128)(2,1)S(1)}, bf16[512,1152]{1,0:T(8,128)(2,1)S(1)}, u32[]{:S(2)}, u32[]{:S(2)}) collective-permute-start(bf16[512,1152]{1,0:T(8,128)(2,1)S(1)} %copy-done.19), channel_id=1, source_target_pairs={{0,2},{1,3},{2,0},{3,1},{4,6},{5,7},{6,4},{7,5},{8,10},{9,11},{10,... | collective-permute-start | bytes 3538952 | tf_op jit(solution)/shard_map/ppermute | solution.py:957
  244.0 22.0 %collective-permute-start.22 = (bf16[420,1120]{1,0:T(8,128)(2,1)}, bf16[420,1120]{1,0:T(8,128)(2,1)S(1)}, u32[]{:S(2)}, u32[]{:S(2)}) collective-permute-start(bf16[420,1120]{1,0:T(8,128)(2,1)} %collective-permute-done.19.refs_6_), channel_id=1, source_target_pairs={{0,4},{1,5},{2,6},{3,7},{4,0},{5,1},{6,2},{7,3},{8,12},{9,13},{10,... | collective-permute-start | bytes 2822408 | tf_op jit(solution)/shard_map/ppermute | solution.py:957
  281.2 11.5 %collective-permute-start.23 = (f32[1024,1152]{1,0:T(8,128)}, f32[1024,1152]{1,0:T(8,128)S(1)}, u32[]{:S(2)}, u32[]{:S(2)}) collective-permute-start(f32[1024,1152]{1,0:T(8,128)} %get-tuple-element.210), channel_id=1, source_target_pairs={{0,1},{1,0},{2,3},{3,2},{4,5},{5,4},{6,7},{7,6},{8,9},{9,8},{10,11... | collective-permute-start | bytes 14155784 | tf_op jit(solution)/shard_map/ppermute | solution.py:957
  281.5 16.6 %collective-permute-start.25 = (bf16[1024,1152]{1,0:T(8,128)(2,1)S(1)}, bf16[1024,1152]{1,0:T(8,128)(2,1)S(1)}, u32[]{:S(2)}, u32[]{:S(2)}) collective-permute-start(bf16[1024,1152]{1,0:T(8,128)(2,1)S(1)} %pad_maximum_fusion.1.cot_ref.base_ref), channel_id=1, source_target_pairs={{0,1},{1,0},{2,3},{3,2},{4,5},{5,4},{6,7},{7,6},{8,9},{9,8},{10,11... | collective-permute-start | bytes 7077896 | tf_op jit(solution)/shard_map/ppermute | solution.py:957
  297.1 4.5 collective-permute-start.24
  337.5 35.1 %collective-permute-start.26 = (f32[1024,1152]{1,0:T(8,128)}, f32[1024,1152]{1,0:T(8,128)}, u32[]{:S(2)}, u32[]{:S(2)}) collective-permute-start(f32[1024,1152]{1,0:T(8,128)} %get-tuple-element.228), channel_id=1, source_target_pairs={{0,1},{1,0},{2,3},{3,2},{4,5},{5,4},{6,7},{7,6},{8,9},{9,8},{10,11... | collective-permute-start | bytes 14155784 | tf_op jit(solution)/shard_map/ppermute | solution.py:957
  337.7 35.0 %copy-start.6 = (bf16[1024,1152]{1,0:T(8,128)(2,1)S(1)}, bf16[1024,1152]{1,0:T(8,128)(2,1)}, u32[]{:S(2)}) copy-start(bf16[1024,1152]{1,0:T(8,128)(2,1)} %copy-done.5) | copy-start | bytes 7077892
  394.7 6.8 collective-permute-start.27
  400.3 118.2 %collective-permute-start.28 = (f32[1024,1152]{1,0:T(8,128)}, f32[1024,1152]{1,0:T(8,128)}, u32[]{:S(2)}, u32[]{:S(2)}) collective-permute-start(f32[1024,1152]{1,0:T(8,128)} %get-tuple-element.249), channel_id=1, source_target_pairs={{0,1},{1,0},{2,3},{3,2},{4,5},{5,4},{6,7},{7,6},{8,9},{9,8},{10,11... | collective-permute-start | bytes 14155784 | tf_op jit(solution)/shard_map/ppermute | solution.py:957
  400.9 124.9 %collective-permute-start.31 = (bf16[1120,1120]{1,0:T(8,128)(2,1)}, bf16[1120,1120]{1,0:T(8,128)(2,1)}, u32[]{:S(2)}, u32[]{:S(2)}) collective-permute-start(bf16[1120,1120]{1,0:T(8,128)(2,1)} %convolution_convert_fusion.1), channel_id=1, source_target_pairs={{0,2},{1,3},{2,0},{3,1},{4,6},{5,7},{6,4},{7,5},{8,10},{9,11},{10,... | collective-permute-start | bytes 7526408 | tf_op jit(solution)/shard_map/ppermute | solution.py:957
  446.6 89.3 %collective-permute-start.30 = (bf16[1120,1120]{1,0:T(8,128)(2,1)}, bf16[1120,1120]{1,0:T(8,128)(2,1)}, u32[]{:S(2)}, u32[]{:S(2)}) collective-permute-start(bf16[1120,1120]{1,0:T(8,128)(2,1)} %convolution_convert_fusion), channel_id=1, source_target_pairs={{0,2},{1,3},{2,0},{3,1},{4,6},{5,7},{6,4},{7,5},{8,10},{9,11},{10,... | collective-permute-start | bytes 7526408 | tf_op jit(solution)/shard_map/ppermute | solution.py:957
  518.5 17.4 %collective-permute-start.29 = (bf16[280,1120]{1,0:T(8,128)(2,1)S(1)}, bf16[280,1120]{1,0:T(8,128)(2,1)S(1)}, u32[]{:S(2)}, u32[]{:S(2)}) collective-permute-start(bf16[280,1120]{1,0:T(8,128)(2,1)S(1)} %copy-done.67), channel_id=1, source_target_pairs={{0,2},{1,3},{2,0},{3,1},{4,6},{5,7},{6,4},{7,5},{8,10},{9,11},{10,... | collective-permute-start | bytes 1881608 | tf_op jit(solution)/shard_map/ppermute | solution.py:957
  523.2 100.6 %collective-permute-start.33 = (bf16[1120,896]{1,0:T(8,128)(2,1)}, bf16[1120,896]{1,0:T(8,128)(2,1)}, u32[]{:S(2)}, u32[]{:S(2)}) collective-permute-start(bf16[1120,896]{1,0:T(8,128)(2,1)} %convolution_convert_fusion.2), channel_id=1, source_target_pairs={{0,2},{1,3},{2,0},{3,1},{4,6},{5,7},{6,4},{7,5},{8,10},{9,11},{10,... | collective-permute-start | bytes 6021128 | tf_op jit(solution)/shard_map/ppermute | solution.py:957
  547.5 55.5 %collective-permute-start.32 = (bf16[512,1152]{1,0:T(8,128)(2,1)}, bf16[512,1152]{1,0:T(8,128)(2,1)S(1)}, u32[]{:S(2)}, u32[]{:S(2)}) collective-permute-start(bf16[512,1152]{1,0:T(8,128)(2,1)} %slice_select_fusion.2), channel_id=1, source_target_pairs={{0,2},{1,3},{2,0},{3,1},{4,6},{5,7},{6,4},{7,5},{8,10},{9,11},{10,... | collective-permute-start | bytes 3538952 | tf_op jit(solution)/shard_map/ppermute | solution.py:957
  547.5 79.0 %collective-permute-start.34 = (bf16[3,420,1120]{2,1,0:T(8,128)(2,1)}, bf16[3,420,1120]{2,1,0:T(8,128)(2,1)}, u32[]{:S(2)}, u32[]{:S(2)}) collective-permute-start(bf16[3,420,1120]{2,1,0:T(8,128)(2,1)} %get-tuple-element.272), channel_id=1, source_target_pairs={{0,4},{4,0},{8,12},{12,8},{16,20},{20,16},{24,28},{28,24},{1,5},{5... | collective-permute-start | bytes 8467208 | tf_op jit(solution)/shard_map/ppermute | solution.py:957
  626.3 23.3 %collective-permute-start.35 = (bf16[560,896]{1,0:T(8,128)(2,1)S(1)}, bf16[560,896]{1,0:T(8,128)(2,1)}, u32[]{:S(2)}, u32[]{:S(2)}) collective-permute-start(bf16[560,896]{1,0:T(8,128)(2,1)S(1)} %select_convert_fusion), channel_id=1, source_target_pairs={{0,4},{4,0},{8,12},{12,8},{16,20},{20,16},{24,28},{28,24},{1,5},{5... | collective-permute-start | bytes 3010568 | tf_op jit(solution)/shard_map/ppermute | solution.py:957
  626.4 50.1 %collective-permute-start.38 = (bf16[1024,1152]{1,0:T(8,128)(2,1)S(1)}, bf16[1024,1152]{1,0:T(8,128)(2,1)S(1)}, u32[]{:S(2)}, u32[]{:S(2)}) collective-permute-start(bf16[1024,1152]{1,0:T(8,128)(2,1)S(1)} %get-tuple-element.282), channel_id=1, source_target_pairs={{0,1},{1,0},{2,3},{3,2},{4,5},{5,4},{6,7},{7,6},{8,9},{9,8},{10,11... | collective-permute-start | bytes 7077896 | tf_op jit(solution)/shard_map/ppermute | solution.py:957
  630.2 23.6 %collective-permute-start.36 = (bf16[420,1120]{1,0:T(8,128)(2,1)}, bf16[420,1120]{1,0:T(8,128)(2,1)S(1)}, u32[]{:S(2)}, u32[]{:S(2)}) collective-permute-start(bf16[420,1120]{1,0:T(8,128)(2,1)} %get-tuple-element.277), channel_id=1, source_target_pairs={{0,8},{4,12},{16,24},{20,28},{1,9},{5,13},{17,25},{21,29},{2,10},{... | collective-permute-start | bytes 2822408 | tf_op jit(solution)/shard_map/ppermute | solution.py:957
  631.5 43.0 %collective-permute-start.37 = (bf16[420,1120]{1,0:T(8,128)(2,1)}, bf16[420,1120]{1,0:T(8,128)(2,1)S(1)}, u32[]{:S(2)}, u32[]{:S(2)}) collective-permute-start(bf16[420,1120]{1,0:T(8,128)(2,1)} %get-tuple-element.279), channel_id=1, source_target_pairs={{0,8},{4,12},{8,0},{12,4},{16,24},{20,28},{24,16},{28,20},{1,9},{5... | collective-permute-start | bytes 2822408 | tf_op jit(solution)/shard_map/ppermute | solution.py:957
  631.7 44.9 %slice-start.2 = ((s8[4718592]{0:T(1024)(128)(4,1)}), s8[4194304]{0:T(1024)(128)(4,1)S(1)}, s32[]{:S(2)}) async-start(s8[4718592]{0:T(1024)(128)(4,1)} %bitcast.58), calls=%async_computation.2 | async-start | bytes 8388608
  633.5 43.1 %slice-start.3 = ((s8[4718592]{0:T(1024)(128)(4,1)}), s8[524288]{0:T(1024)(128)(4,1)S(1)}, s32[]{:S(2)}) async-start(s8[4718592]{0:T(1024)(128)(4,1)} %bitcast.58), calls=%async_computation.3 | async-start | bytes 1048576
  651.1 34.2 %collective-permute-start.39 = (bf16[560,896]{1,0:T(8,128)(2,1)S(1)}, bf16[560,896]{1,0:T(8,128)(2,1)S(1)}, u32[]{:S(2)}, u32[]{:S(2)}) collective-permute-start(bf16[560,896]{1,0:T(8,128)(2,1)S(1)} %get-tuple-element.287), channel_id=1, source_target_pairs={{8,0},{12,4},{24,16},{28,20},{9,1},{13,5},{25,17},{29,21},{10,2},{... | collective-permute-start | bytes 3010568 | tf_op jit(solution)/shard_map/ppermute | solution.py:957
  683.1 22.9 %collective-permute-start.41 = (bf16[420,1120]{1,0:T(8,128)(2,1)}, bf16[420,1120]{1,0:T(8,128)(2,1)}, u32[]{:S(2)}, u32[]{:S(2)}) collective-permute-start(bf16[420,1120]{1,0:T(8,128)(2,1)} %get-tuple-element.295), channel_id=1, source_target_pairs={{24,8},{28,12},{0,16},{4,20},{8,24},{12,28},{25,9},{29,13},{1,17},... | collective-permute-start | bytes 2822408 | tf_op jit(solution)/shard_map/ppermute | solution.py:957
  688.0 28.1 %collective-permute-start.42 = (bf16[512,1152]{1,0:T(8,128)(2,1)}, bf16[512,1152]{1,0:T(8,128)(2,1)}, u32[]{:S(2)}, u32[]{:S(2)}) collective-permute-start(bf16[512,1152]{1,0:T(8,128)(2,1)} %slice_select_fusion.1), channel_id=1, source_target_pairs={{0,2},{1,3},{2,0},{3,1},{4,6},{5,7},{6,4},{7,5},{8,10},{9,11},{10,... | collective-permute-start | bytes 3538952 | tf_op jit(solution)/shard_map/ppermute | solution.py:957
  689.1 2.8 collective-permute-start.40
  690.3 42.6 %collective-permute-start.43 = (bf16[560,896]{1,0:T(8,128)(2,1)S(1)}, bf16[560,896]{1,0:T(8,128)(2,1)}, u32[]{:S(2)}, u32[]{:S(2)}) collective-permute-start(bf16[560,896]{1,0:T(8,128)(2,1)S(1)} %get-tuple-element.305), channel_id=1, source_target_pairs={{16,0},{20,4},{17,1},{21,5},{18,2},{22,6},{19,3},{23,7}} | collective-permute-start | bytes 3010568 | tf_op jit(solution)/shard_map/ppermute | solution.py:957
  743.3 38.4 %copy-start.10 = (f32[12,1120]{1,0:T(8,128)S(1)}, f32[12,1120]{1,0:T(8,128)}, u32[]{:S(2)}) copy-start(f32[12,1120]{1,0:T(8,128)} %copy-done.9) | copy-start | bytes 161284
  743.3 40.7 %copy-start.50 = (f32[12,1120]{1,0:T(8,128)S(1)}, f32[12,1120]{1,0:T(8,128)}, u32[]{:S(2)}) copy-start(f32[12,1120]{1,0:T(8,128)} %param.21) | copy-start | bytes 161284
  743.3 40.7 %copy-start.51 = (f32[12,1120]{1,0:T(8,128)S(1)}, f32[12,1120]{1,0:T(8,128)}, u32[]{:S(2)}) copy-start(f32[12,1120]{1,0:T(8,128)} %param.22) | copy-start | bytes 161284
  755.0 32.9 %copy-start.17 = (f32[1,1,470400]{2,1,0:T(1,128)S(1)}, f32[1,1,470400]{2,1,0:T(1,128)}, u32[]{:S(2)}) copy-start(f32[1,1,470400]{2,1,0:T(1,128)} %weight_ref.7) | copy-start | bytes 5644804
  758.1 1.3 collective-permute-start.44
  759.5 4.4 collective-permute-start.45
  763.9 4.4 collective-permute-start.46
  768.3 9.7 %collective-permute-start.47 = (f32[16,1120]{1,0:T(8,128)S(1)}, f32[16,1120]{1,0:T(8,128)S(1)}, u32[]{:S(2)}, u32[]{:S(2)}) collective-permute-start(f32[16,1120]{1,0:T(8,128)S(1)} %add.259), channel_id=1, source_target_pairs={{0,8},{4,12},{8,0},{12,4},{16,24},{20,28},{24,16},{28,20},{1,9},{5... | collective-permute-start | bytes 215048 | tf_op jit(solution)/shard_map/ppermute | solution.py:957
  778.1 5.9 collective-permute-start.48
  (68 other events, 506.9 us)

commit v8 on v7

--- a/solution.py
+++ b/solution.py
@@ -736,7 +736,7 @@
 
 def middle_body(rows_ref, kept_ref, got_ref, small_ref, middle_ref, low_ref):
     middle = rows_ref[...].astype(F32) + (
-        kept_ref[...] + got_ref[:, : kept_ref.shape[1]] + small_ref[6:7]
+        kept_ref[...] + got_ref[:, : kept_ref.shape[1]].astype(F32) + small_ref[6:7]
     )
     middle_ref[...] = middle
     hat, _ = norm_stats(middle)
@@ -1177,7 +1177,7 @@
         w_out, w_in, w_back = (list(pair) for pair in zip(matrices_mine, matrices_theirs))
         own_e, w_out[0] = tie(own_e, w_out[0])
     other_e = swap(own_e, "seq", 1)
-    sent, kept = split_product([attended[0][0], attended[1][0]], w_out, False, model_width, F32)
+    sent, kept = split_product([attended[0][0], attended[1][0]], w_out, False, model_width, BF16)
     middle, low_two = middle_norm(own_in, kept, swap(sent, "seq", 1), small_master)
     other_two = swap(low_two, "seq", 1)
 
@@ -1235,7 +1235,7 @@
 
     packed_theirs = attend_back(1, grad_att_theirs)
     attn_sent = dot_columns(rows_one, packed_theirs).astype(link)
-    attn_sent, packed_theirs = tie(attn_sent, packed_theirs)
+    attn_sent, packed_theirs, outer_received = tie(attn_sent, packed_theirs, outer_received)
     theirs_part = partial_product(packed_theirs, w_attn_theirs)
     attn_sent, theirs_part, y_index, out_received = tie(
         attn_sent, theirs_part, y_index, out_received
@@ -1299,18 +1299,16 @@
         held_last = kept_last + got_last.astype(F32)
         sent_far = jnp.where(z_here == 1, held_last, held_near).astype(BF16)
         own_rest = jnp.where(z_here == 3, held_last, held_near)
-        sent_far, own_rest, kept = tie(sent_far, own_rest, kept)
+        sent_far, own_rest, held_lead = tie(sent_far, own_rest, held_lead)
+        held_lead = held_lead + near_lead.astype(F32)
+        sent_lead = held_lead.astype(BF16)
+        sent_lead, held_lead, sent_far, kept = tie(sent_lead, held_lead, sent_far, kept)
+        sent_lead, (kept, sent_far), mark = started(sent_lead, (kept, sent_far), mark)
+        far_lead = permute(sent_lead, "dp", lower_pairs([(2, 0)], 2))
         got_far = permute(sent_far, "dp", lower_pairs([(3, 1), (0, 2), (1, 3)], 2))
     grad_x, sums_one = norm_back(
         own_in, kept, swap(sent, "seq", 1), grad_mid, small_master[0:1], False
     )
-    if planar:
-        sums_one, held_lead = tie(sums_one, held_lead)
-        held_lead = held_lead + near_lead.astype(F32)
-        sent_lead = held_lead.astype(BF16)
-        sent_lead, held_lead, own_rest, grad_x = tie(sent_lead, held_lead, own_rest, grad_x)
-        sent_lead, own_rest, mark = started(sent_lead, own_rest, mark)
-        far_lead = permute(sent_lead, "dp", lower_pairs([(2, 0)], 2))
 
     result_all = place_rows(chip_index, result_rows, result_received, model_width)
     grad_halves = (grad_x[:local_rows], grad_x[local_rows:])
@@ -1340,11 +1338,11 @@
     )
 
     if planar:
+        lead_grad = (held_lead + far_lead.astype(F32))[:, :triple].reshape(1, 1, shard_len)
+        own_rest, lead_grad, result_all, grad_all, small_now = tie(
+            own_rest, lead_grad, result_all, grad_all, small_now
+        )
         rest_grad = (own_rest + got_far.astype(F32)).reshape(1, 1, shard_len)
-        held_lead, rest_grad, result_all, grad_all, small_now = tie(
-            held_lead, rest_grad, result_all, grad_all, small_now
-        )
-        lead_grad = (held_lead + far_lead.astype(F32))[:, :triple].reshape(1, 1, shard_len)
         leads = z_here == 0
     else:
         flat_here = jnp.concatenate(

time: 805 us -> 794 us (0.986)
    unnamed x168 -> x172, local copies, waits for them, and re-layouts: 24.5 us -> 24.4 us
  transfers between devices with their start and end apart: 49 -> 49, of which waited for: 22 -> 20; matrix products, arithmetic and copies ran while one was open for 13% -> 13% of each run, Pallas kernels for 36% -> 37%
where the time goes in v8:
time: 794 us; the launch traced here: 786 us
  Pallas kernels  366 us (46%)
  waiting for transfers between devices  178 us (22%)
  starting transfers between devices  77.4 us (10%)
  matrix products  67.2 us (8%)
  local copies, waits for them, and re-layouts  47 us (6%)
  other arithmetic  42.7 us (5%)
    ppermute x49, waiting for transfers between devices, permute(): return lax.ppermute(value, axis_name, pairs)  178 us
    pallas_call x2, Pallas kernels, attention_backward(): pl.pallas_call(functools.partial(attention_backward_body, heads, width, b...  104 us
    ppermute x49, starting transfers between devices, permute(): return lax.ppermute(value, axis_name, pairs)  77.4 us
    pallas_call x2, Pallas kernels, attention_forward(): pl.pallas_call(functools.partial(attention_forward_body, heads, width, bq...  70 us
    pallas_call x2, Pallas kernels, feed_forward(): pl.pallas_call(functools.partial(feed_forward_body, len(filled)), out_sha...  69.3 us
    dot_general x8, matrix products, dot_columns(): lax.dot_general(left, right, (((0,), (0,)), ((), ())), preferred_element_...  67.2 us
    unnamed x172, local copies, waits for them, and re-layouts  24.4 us
    pallas_call x2, Pallas kernels, split_product(): pl.pallas_call(functools.partial(split_product_body, steps, turned, len(l...  19.2 us
  transfers between devices with their start and end apart: 49, of which 20 were waited for; matrix products, arithmetic and copies ran while one was open for 13% of the time, Pallas kernels for 37%

profile of v8, /device:TPU:0, one launch (start us, length us, event | category | flops | bytes accessed | tf_op | source)
XLA Modules:
  0.0 785.6 jit_solution(12357662784390592958)
XLA Ops:
  5.3 2.9 collective-permute-start
  9.1 2.8 reshape.190
  11.9 5.5 collective-permute-start.1
  18.0 16.5 %collective-permute-done = bf16[512,1152]{1,0:T(8,128)(2,1)} collective-permute-done((bf16[512,1152]{1,0:T(8,128)(2,1)}, bf16[512,1152]{1,0:T(8,128)(2,1)}, u32[]{:S(2)}, u32[]{:S(2)}) %collective-permute-start) | collective-permute-done | bytes 1179680 | tf_op jit(solution)/shard_map/ppermute | solution.py:957
  42.0 5.9 collective-permute-start.2
  56.2 13.2 %collective-permute-done.2 = bf16[560,840]{1,0:T(8,128)(2,1)} collective-permute-done((bf16[560,840]{1,0:T(8,128)(2,1)}, bf16[560,840]{1,0:T(8,128)(2,1)}, u32[]{:S(2)}, u32[]{:S(2)}) %collective-permute-start.2) | collective-permute-done | bytes 940832 | tf_op jit(solution)/shard_map/ppermute | solution.py:957
  78.7 16.0 %collective-permute-done.6.a1 = bf16[560,840]{1,0:T(8,128)(2,1)} collective-permute-done((bf16[560,840]{1,0:T(8,128)(2,1)S(1)}, bf16[560,840]{1,0:T(8,128)(2,1)}, u32[]{:S(2)}, u32[]{:S(2)}) %collective-permute-start.6) | collective-permute-done | bytes 940832 | tf_op jit(solution)/shard_map/ppermute | solution.py:957
  101.4 4.7 square_sums.1
  106.1 20.4 %collective-permute-done.10.refs_4_ = bf16[420,1120]{1,0:T(8,128)(2,1)} collective-permute-done((bf16[420,1120]{1,0:T(8,128)(2,1)}, bf16[420,1120]{1,0:T(8,128)(2,1)}, u32[]{:S(2)}, u32[]{:S(2)}) %collective-permute-start.10) | collective-permute-done | bytes 940832 | tf_op jit(solution)/shard_map/ppermute | solution.py:957
  129.8 3.4 collective-permute-start.14
  135.6 2.4 collective-permute-start.15
  138.1 3.4 collective-permute-start.16
  141.5 16.6 %project.1 = (bf16[2048,840]{1,0:T(8,128)(2,1)}, bf16[2048,840]{1,0:T(8,128)(2,1)}, bf16[2048,1120]{1,0:T(8,128)(2,1)}, bf16[1120,840]{1,0:T(8,128)(2,1)S(1)}, bf16[1120,840]{1,0:T(8,128)(2,1)}) custom-call(s32[1]{0:T(128)} %bitcast.place_ref, bf16[1024,1152]{1,0:T(8,128)(2,1)} %pad.11.own_ref, bf16[1024,1152]{1,0:T(8,128)(2,1)} %collective-permute-done.5.other_ref, ...), custom_call_target="tpu_custom_call" | custom-call | flops 16000000000 | bytes 4096 | tf_op jit(solution)/shard_map/project/pallas_call | solution.py:613
  158.1 35.3 %attention_forward.2 = (bf16[2048,280]{1,0:T(8,128)(2,1)S(1)}, f32[4,280,512]{2,1,0:T(8,128)S(1)}, f32[4,8,512]{2,1,0:T(8,128)S(1)}) custom-call(s32[4]{0:T(128)S(1)} %and_select_fusion.low_ref, s32[1]{0:T(128)} %bitcast.8.core_ref, s32[4,1,512]{2,1,0:T(1,128)S(1)} %compare_select_fusion.start_ref, bf16[2048,840]{1,0:T(8,128)(2,1)} %get-tuple-element.175.qkv_ref), custom_call_target="tpu_custom_call" | custom-call | flops 35000000512 | bytes 4096 | tf_op jit(solution)/shard_map/attention_forward/pallas_call | solution.py:274
  195.4 2.4 collective-permute-start.19
  197.9 3.9 collective-permute-start.20
  201.8 3.4 collective-permute-start.21
  205.8 34.7 %attention_forward.3 = (bf16[2048,280]{1,0:T(8,128)(2,1)S(1)}, f32[4,280,512]{2,1,0:T(8,128)S(1)}, f32[4,8,512]{2,1,0:T(8,128)S(1)}) custom-call(s32[4]{0:T(128)S(1)} %and_select_fusion.low_ref, s32[1]{0:T(128)} %bitcast.8.core_ref, s32[4,1,512]{2,1,0:T(1,128)S(1)} %compare_select_fusion.start_ref, bf16[2048,840]{1,0:T(8,128)(2,1)} %get-tuple-element.181.qkv_ref), custom_call_target="tpu_custom_call" | custom-call | flops 35000000512 | bytes 4096 | tf_op jit(solution)/shard_map/attention_forward/pallas_call | solution.py:274
  244.7 2.4 collective-permute-start.22
  247.1 5.7 unpack_share.2
  252.9 12.0 %collective-permute-done.17 = bf16[512,1152]{1,0:T(8,128)(2,1)} collective-permute-done((bf16[512,1152]{1,0:T(8,128)(2,1)S(1)}, bf16[512,1152]{1,0:T(8,128)(2,1)}, u32[]{:S(2)}, u32[]{:S(2)}) %collective-permute-start.17) | collective-permute-done | bytes 1179680 | tf_op jit(solution)/shard_map/ppermute | solution.py:957
  267.7 5.6 unpack_share.3
  273.4 8.5 %split_product.2 = (bf16[1024,1152]{1,0:T(8,128)(2,1)}, f32[1024,1120]{1,0:T(8,128)}) custom-call(bf16[2048,280]{1,0:T(8,128)(2,1)S(1)} %get-tuple-element.182.refs_0_, bf16[2048,280]{1,0:T(8,128)(2,1)S(1)} %copy-done.27, bf16[280,1120]{1,0:T(8,128)(2,1)S(1)} %get-tuple-element.200.refs_2_.w_a, bf16[280,1120]{1,0:T(8,128)(2,1)S(1)} %get-tuple-element.208.refs_3_.w_b), custom_call_target="tpu_custom_call" | custom-call | flops 8999999488 | bytes 4096 | tf_op jit(solution)/shard_map/split_product/pallas_call | solution.py:720
  282.7 4.3 collective-permute-done.23.got_ref
  293.0 3.1 collective-permute-done.24.rows_ref
  297.4 34.4 %feed_forward.2 = (bf16[2048,1120]{1,0:T(8,128)(2,1)}, bf16[2048,1120]{1,0:T(8,128)(2,1)}, bf16[2048,1120]{1,0:T(8,128)(2,1)}, bf16[2048,1120]{1,0:T(8,128)(2,1)...) custom-call(bf16[1024,1152]{1,0:T(8,128)(2,1)} %copy-done.68, ...), custom_call_target="tpu_custom_call" | custom-call | flops 33999998976 | bytes 4096 | tf_op jit(solution)/shard_map/feed_forward/pallas_call | solution.py:934
  332.0 34.9 %feed_forward.3 = (bf16[2048,1120]{1,0:T(8,128)(2,1)}, bf16[2048,1120]{1,0:T(8,128)(2,1)}, bf16[2048,1120]{1,0:T(8,128)(2,1)}, bf16[2048,1120]{1,0:T(8,128)(2,1)...) custom-call(bf16[1024,1152]{1,0:T(8,128)(2,1)} %copy-done.15, ...), custom_call_target="tpu_custom_call", output_to_operand_aliasing={{0}: (7, {}), {1}: (8, {}), {2}: (9, {}), {3}: (10, {}), {4... | custom-call | flops 33999998976 | bytes 4096 | tf_op jit(solution)/shard_map/feed_forward/pallas_call | solution.py:934
  369.3 7.8 norm_back.2
  377.1 13.1 %convolution_convert_fusion.1 = bf16[1120,1120]{1,0:T(8,128)(2,1)} fusion(bf16[2048,1120]{1,0:T(8,128)(2,1)} %get-tuple-element.225, bf16[2048,1120]{1,0:T(8,128)(2,1)} %get-tuple-element.239), kind=kOutput, calls=%fused_computation.1 | convolution fusion | flops 5139276800 | bytes 11683840 | tf_op jit(solution)/shard_map/dot_general | solution.py:39
  392.7 2.9 fusion.22
  397.2 11.6 %convolution_convert_fusion = bf16[1120,1120]{1,0:T(8,128)(2,1)} fusion(bf16[2048,1120]{1,0:T(8,128)(2,1)} %get-tuple-element.240, bf16[2048,1120]{1,0:T(8,128)(2,1)} %get-tuple-element.235), kind=kOutput, calls=%fused_computation | convolution fusion | flops 5139276800 | bytes 11683840 | tf_op jit(solution)/shard_map/dot_general | solution.py:39
  408.8 8.2 %out_grads.1 = (bf16[2048,280]{1,0:T(8,128)(2,1)S(1)}, bf16[2048,280]{1,0:T(8,128)(2,1)S(1)}, bf16[2048,1120]{1,0:T(8,128)(2,1)}) custom-call(bf16[1024,1152]{1,0:T(8,128)(2,1)} %get-tuple-element.236.own_ref, bf16[1024,1152]{1,0:T(8,128)(2,1)} %collective-permute-done.27.other_ref, bf16[280,1120]{1,0:T(8,128)(2,1)S(1)} %get-tuple-element.200.refs_2_.w_a, ...), custom_call_target="tpu_custom_call" | custom-call | flops 8000000000 | bytes 4096 | tf_op jit(solution)/shard_map/out_grads/pallas_call | solution.py:646
  417.1 5.2 convolution_convert_fusion.3
  422.4 2.7 fusion.42.out_ref
  425.1 8.5 %fusion.41.in_ref = f32[1120,1120]{1,0:T(8,128)} fusion(bf16[2048,1120]{1,0:T(8,128)(2,1)S(1)} %bitcast.70, bf16[2048,1120]{1,0:T(8,128)(2,1)S(1)} %bitcast.68), kind=kOutput, calls=%fused_computation.126 | convolution fusion | flops 5138022400 | bytes 14192640 | tf_op jit(solution)/shard_map/dot_general | solution.py:39
  433.6 8.8 %fusion.40.back_ref = f32[1120,1120]{1,0:T(8,128)} fusion(bf16[2048,1120]{1,0:T(8,128)(2,1)S(1)} %bitcast.66, bf16[2048,1120]{1,0:T(8,128)(2,1)S(1)} %bitcast.72), kind=kOutput, calls=%fused_computation.125 | convolution fusion | flops 5138022400 | bytes 14192640 | tf_op jit(solution)/shard_map/dot_general | solution.py:39
  444.4 51.9 %attention_backward.2.left = bf16[2048,896]{1,0:T(8,128)(2,1)} custom-call(s32[4]{0:T(128)} %copy-done.25, s32[1]{0:T(128)} %bitcast.8.core_ref, s32[4,1,512]{2,1,0:T(1,128)} %copy-done.14, bf16[2048,840]{1,0:T(8,128)(2,1)} %get-tuple-element.181.qkv_ref, bf16[2048,280]{1,0:T(8,128)(2,1)} %copy-done.39, f32[4,280,512]{2,1,0:T(8,128)} %copy-done.41, ...), custom_call_target="tpu_custom_call" | custom-call | flops 56000000000 | bytes 4096 | tf_op jit(solution)/shard_map/attention_backward/pallas_call | solution.py:317
  496.4 9.9 %convolution_convert_fusion.2 = bf16[1120,896]{1,0:T(8,128)(2,1)} fusion(bf16[2048,1120]{1,0:T(8,128)(2,1)} %get-tuple-element.174, bf16[2048,896]{1,0:T(8,128)(2,1)} %attention_backward.2.left), kind=kOutput, calls=%fused_computation.17 | convolution fusion | flops 4111421440 | bytes 10264576 | tf_op jit(solution)/shard_map/dot_general | solution.py:39
  506.3 8.0 %partial_product.1.refs_2_ = f32[2048,1120]{1,0:T(8,128)} custom-call(bf16[2048,896]{1,0:T(8,128)(2,1)S(1)} %copy-done.2, bf16[1120,840]{1,0:T(8,128)(2,1)S(1)} %copy-done.33), custom_call_target="tpu_custom_call" | custom-call | flops 8999999488 | bytes 4096 | tf_op jit(solution)/shard_map/partial_product/pallas_call | solution.py:700
  514.3 4.9 fusion.8
  520.6 4.0 collective-permute-done.30.in_got
  524.5 10.4 %pack_rest.1 = (f32[3,420,1120]{2,1,0:T(8,128)}, bf16[3,420,1120]{2,1,0:T(8,128)(2,1)}) custom-call(s32[1]{0:T(128)} %bitcast.place_ref, f32[280,1120]{1,0:T(8,128)S(1)} %copy-done.11, f32[1120,1120]{1,0:T(8,128)} %fusion.41.in_ref, f32[1120,1120]{1,0:T(8,128)} %fusion.40.back_ref, bf16[280,1120]{1,0:T(8,128)(2,1)S(1)} %collective-permute-done.28.out_got, ...), custom_call_target="tpu_custom_call" | custom-call | flops 10000000000 | bytes 4096 | tf_op jit(solution)/shard_map/pack_rest/pallas_call | solution.py:552
  538.1 51.9 %attention_backward.3.refs_0_ = bf16[2048,896]{1,0:T(8,128)(2,1)} custom-call(s32[4]{0:T(128)} %copy-done.25, s32[1]{0:T(128)} %bitcast.8.core_ref, s32[4,1,512]{2,1,0:T(1,128)} %copy-done.14, bf16[2048,840]{1,0:T(8,128)(2,1)} %get-tuple-element.175.qkv_ref, bf16[2048,280]{1,0:T(8,128)(2,1)} %copy-done.38, f32[4,280,512]{2,1,0:T(8,128)} %copy-done.40, ...), custom_call_target="tpu_custom_call" | custom-call | flops 56000000000 | bytes 4096 | tf_op jit(solution)/shard_map/attention_backward/pallas_call | solution.py:317
  593.8 10.8 %split_product.3 = (bf16[1024,1152]{1,0:T(8,128)(2,1)S(1)}, f32[1024,1120]{1,0:T(8,128)}) custom-call(bf16[2048,896]{1,0:T(8,128)(2,1)} %attention_backward.3.refs_0_, bf16[1120,840]{1,0:T(8,128)(2,1)S(1)} %copy-done.32, f32[2048,1120]{1,0:T(8,128)} %partial_product.1.refs_2_), custom_call_target="tpu_custom_call" | custom-call | flops 8999999488 | bytes 4096 | tf_op jit(solution)/shard_map/split_product/pallas_call | solution.py:720
  604.6 7.6 fusion.43
  616.5 2.5 fusion.31
  620.5 17.9 %collective-permute-done.35 = bf16[560,896]{1,0:T(8,128)(2,1)S(1)} collective-permute-done((bf16[560,896]{1,0:T(8,128)(2,1)S(1)}, bf16[560,896]{1,0:T(8,128)(2,1)S(1)}, u32[]{:S(2)}, u32[]{:S(2)}) %collective-permute-start.35) | collective-permute-done | bytes 1003552 | tf_op jit(solution)/shard_map/ppermute | solution.py:957
  642.3 20.7 %collective-permute-done.37 = bf16[420,1120]{1,0:T(8,128)(2,1)S(1)} collective-permute-done((bf16[420,1120]{1,0:T(8,128)(2,1)S(1)}, bf16[420,1120]{1,0:T(8,128)(2,1)S(1)}, u32[]{:S(2)}, u32[]{:S(2)}) %collective-permute-start.37) | collective-permute-done | bytes 940832 | tf_op jit(solution)/shard_map/ppermute | solution.py:957
  669.3 6.7 norm_back.3
  679.6 7.3 collective-permute-start.43
  686.9 3.3 place_rows.2
  690.2 26.4 %collective-permute-done.39 = bf16[560,896]{1,0:T(8,128)(2,1)} collective-permute-done((bf16[560,896]{1,0:T(8,128)(2,1)}, bf16[560,896]{1,0:T(8,128)(2,1)}, u32[]{:S(2)}, u32[]{:S(2)}) %collective-permute-start.39) | collective-permute-done | bytes 1003552 | tf_op jit(solution)/shard_map/ppermute | solution.py:957
  716.6 3.3 slice_add_fusion.1
  719.9 6.2 reshape.195.lead_ref
  726.1 3.2 place_rows.3
  729.3 2.7 convert_add_fusion.3
  732.0 4.3 reshape.198.rest_ref
  737.9 10.5 %new_moments.1 = (f32[1,1,470400]{2,1,0:T(1,128)}, f32[2,1,1,470400]{3,2,1,0:T(1,128)}, f32[1,1,470400]{2,1,0:T(1,128)S(1)}, f32[2]{0:T(128)S(1)}) custom-call(s32[2]{0:T(128)S(1)} %pad_add_fusion.ints_ref, f32[2]{0:T(128)S(1)} %pad_maximum_fusion.9.floats_ref, f32[1,1,470400]{2,1,0:T(1,128)S(1)} %copy-done.10, f32[1,1,470400]{2,1,0:T(1,128)S(1)} %reshape.198.rest_ref, ...), custom_call_target="tpu_custom_call" | custom-call | flops 10000000000 | bytes 4096 | tf_op jit(solution)/shard_map/new_moments/pallas_call | solution.py:433
  750.1 2.5 fusion.23
  754.6 3.8 collective-permute-done.45
  758.8 4.0 collective-permute-done.46
  764.8 2.5 collective-permute-done.47
  767.4 5.9 collective-permute-done.48
  778.8 6.5 new_weights.1
  (335 shorter events, 105.7 us)
Async XLA Ops:
  1.5 389.1 %copy-start.12 = (f32[12,1120]{1,0:T(8,128)}, f32[12,1120]{1,0:T(8,128)S(1)}, u32[]{:S(2)}) copy-start(f32[12,1120]{1,0:T(8,128)S(1)} %copy.47.small_ref) | copy-start | bytes 161284
  5.3 29.2 %collective-permute-start = (bf16[512,1152]{1,0:T(8,128)(2,1)}, bf16[512,1152]{1,0:T(8,128)(2,1)}, u32[]{:S(2)}, u32[]{:S(2)}) collective-permute-start(bf16[512,1152]{1,0:T(8,128)(2,1)} %get-tuple-element.164), channel_id=1, source_target_pairs={{0,2},{1,3},{2,0},{3,1},{4,6},{5,7},{6,4},{7,5},{8,10},{9,11},{10,... | collective-permute-start | bytes 3538952 | tf_op jit(solution)/shard_map/ppermute | solution.py:957
  11.9 29.1 %collective-permute-start.1 = (bf16[560,840]{1,0:T(8,128)(2,1)}, bf16[560,840]{1,0:T(8,128)(2,1)}, u32[]{:S(2)}, u32[]{:S(2)}) collective-permute-start(bf16[560,840]{1,0:T(8,128)(2,1)} %reshape.190), channel_id=1, source_target_pairs={{0,16},{4,20},{1,17},{5,21},{2,18},{6,22},{3,19},{7,23}} | collective-permute-start | bytes 2822408 | tf_op jit(solution)/shard_map/ppermute | solution.py:957
  40.9 29.8 %collective-permute-start.5 = (bf16[1024,1152]{1,0:T(8,128)(2,1)}, bf16[1024,1152]{1,0:T(8,128)(2,1)}, u32[]{:S(2)}, u32[]{:S(2)}) collective-permute-start(bf16[1024,1152]{1,0:T(8,128)(2,1)} %pad.11.own_ref), channel_id=1, source_target_pairs={{0,1},{1,0},{2,3},{3,2},{4,5},{5,4},{6,7},{7,6},{8,9},{9,8},{10,11... | collective-permute-start | bytes 7077896 | tf_op jit(solution)/shard_map/ppermute | solution.py:957
  42.0 27.3 %collective-permute-start.2 = (bf16[560,840]{1,0:T(8,128)(2,1)}, bf16[560,840]{1,0:T(8,128)(2,1)}, u32[]{:S(2)}, u32[]{:S(2)}) collective-permute-start(bf16[560,840]{1,0:T(8,128)(2,1)} %broadcast_select_fusion.4), channel_id=1, source_target_pairs={{0,8},{4,12},{16,24},{20,28},{1,9},{5,13},{17,25},{21,29},{2,10},{... | collective-permute-start | bytes 2822408 | tf_op jit(solution)/shard_map/ppermute | solution.py:957
  50.2 20.5 %collective-permute-start.3 = (bf16[420,1120]{1,0:T(8,128)(2,1)}, bf16[420,1120]{1,0:T(8,128)(2,1)}, u32[]{:S(2)}, u32[]{:S(2)}) collective-permute-start(bf16[420,1120]{1,0:T(8,128)(2,1)} %reshape.191.refs_0_), channel_id=1, source_target_pairs={{8,12},{9,13},{10,14},{11,15},{12,8},{13,9},{14,10},{15,11},{16,20... | collective-permute-start | bytes 2822408 | tf_op jit(solution)/shard_map/ppermute | solution.py:957
  51.8 19.0 %collective-permute-start.4 = (bf16[420,1120]{1,0:T(8,128)(2,1)}, bf16[420,1120]{1,0:T(8,128)(2,1)}, u32[]{:S(2)}, u32[]{:S(2)}) collective-permute-start(bf16[420,1120]{1,0:T(8,128)(2,1)} %reshape.191.refs_0_), channel_id=1, source_target_pairs={{8,10},{9,11},{10,8},{11,9},{12,14},{13,15},{14,12},{15,13},{16,18... | collective-permute-start | bytes 2822408 | tf_op jit(solution)/shard_map/ppermute | solution.py:957
  56.2 40.1 %copy-start.64 = (s32[4]{0:T(128)S(1)}, s32[4]{0:T(128)}, u32[]{:S(2)}) copy-start(s32[4]{0:T(128)} %constant.164.clone) | copy-start | bytes 52
  70.7 24.0 %collective-permute-start.6 = (bf16[560,840]{1,0:T(8,128)(2,1)S(1)}, bf16[560,840]{1,0:T(8,128)(2,1)}, u32[]{:S(2)}, u32[]{:S(2)}) collective-permute-start(bf16[560,840]{1,0:T(8,128)(2,1)S(1)} %broadcast_select_fusion.5.a0), channel_id=1, source_target_pairs={{0,4},{4,0},{8,12},{12,8},{16,20},{20,16},{24,28},{28,24},{1,5},{5... | collective-permute-start | bytes 2822408 | tf_op jit(solution)/shard_map/ppermute | solution.py:957
  72.8 133.0 %copy-start.25 = (s32[4]{0:T(128)}, s32[4]{0:T(128)S(1)}, u32[]{:S(2)}) copy-start(s32[4]{0:T(128)S(1)} %and_select_fusion.low_ref) | copy-start | bytes 52
  72.8 33.3 %collective-permute-start.7 = (bf16[560,840]{1,0:T(8,128)(2,1)S(1)}, bf16[560,840]{1,0:T(8,128)(2,1)}, u32[]{:S(2)}, u32[]{:S(2)}) collective-permute-start(bf16[560,840]{1,0:T(8,128)(2,1)S(1)} %broadcast_select_fusion.5.a0), channel_id=1, source_target_pairs={{0,2},{1,3},{2,0},{3,1},{4,6},{5,7},{6,4},{7,5},{8,10},{9,11},{10,... | collective-permute-start | bytes 2822408 | tf_op jit(solution)/shard_map/ppermute | solution.py:957
  74.4 52.1 %collective-permute-start.10 = (bf16[420,1120]{1,0:T(8,128)(2,1)}, bf16[420,1120]{1,0:T(8,128)(2,1)}, u32[]{:S(2)}, u32[]{:S(2)}) collective-permute-start(bf16[420,1120]{1,0:T(8,128)(2,1)} %reshape.191.refs_0_), channel_id=1, source_target_pairs={{8,24},{9,25},{10,26},{11,27},{12,28},{13,29},{14,30},{15,31},{16,... | collective-permute-start | bytes 2822408 | tf_op jit(solution)/shard_map/ppermute | solution.py:957
  75.7 52.2 %collective-permute-start.9 = (bf16[420,1120]{1,0:T(8,128)(2,1)}, bf16[420,1120]{1,0:T(8,128)(2,1)}, u32[]{:S(2)}, u32[]{:S(2)}) collective-permute-start(bf16[420,1120]{1,0:T(8,128)(2,1)} %reshape.191.refs_0_), channel_id=1, source_target_pairs={{8,0},{9,1},{10,2},{11,3},{12,4},{13,5},{14,6},{15,7},{16,24},{17,... | collective-permute-start | bytes 2822408 | tf_op jit(solution)/shard_map/ppermute | solution.py:957
  77.0 49.5 %collective-permute-start.11 = (bf16[420,1120]{1,0:T(8,128)(2,1)}, bf16[420,1120]{1,0:T(8,128)(2,1)}, u32[]{:S(2)}, u32[]{:S(2)}) collective-permute-start(bf16[420,1120]{1,0:T(8,128)(2,1)} %collective-permute-done.4.refs_0_), channel_id=1, source_target_pairs={{8,12},{9,13},{10,14},{11,15},{12,8},{13,9},{14,10},{15,11},{16,20... | collective-permute-start | bytes 2822408 | tf_op jit(solution)/shard_map/ppermute | solution.py:957
  94.7 33.1 %collective-permute-start.8 = (bf16[560,840]{1,0:T(8,128)(2,1)}, bf16[560,840]{1,0:T(8,128)(2,1)}, u32[]{:S(2)}, u32[]{:S(2)}) collective-permute-start(bf16[560,840]{1,0:T(8,128)(2,1)} %collective-permute-done.6.a1), channel_id=1, source_target_pairs={{0,2},{1,3},{2,0},{3,1},{4,6},{5,7},{6,4},{7,5},{8,10},{9,11},{10,... | collective-permute-start | bytes 2822408 | tf_op jit(solution)/shard_map/ppermute | solution.py:957
  99.9 105.9 %copy-start.14 = (s32[4,1,512]{2,1,0:T(1,128)}, s32[4,1,512]{2,1,0:T(1,128)S(1)}, u32[]{:S(2)}) copy-start(s32[4,1,512]{2,1,0:T(1,128)S(1)} %compare_select_fusion.start_ref) | copy-start | bytes 24580
  127.8 65.6 %collective-permute-start.12 = (bf16[420,1120]{1,0:T(8,128)(2,1)}, bf16[420,1120]{1,0:T(8,128)(2,1)}, u32[]{:S(2)}, u32[]{:S(2)}) collective-permute-start(bf16[420,1120]{1,0:T(8,128)(2,1)} %collective-permute-done.10.refs_4_), channel_id=1, source_target_pairs={{0,8},{1,9},{2,10},{3,11},{4,12},{5,13},{6,14},{7,15},{8,0},{9,1},... | collective-permute-start | bytes 2822408 | tf_op jit(solution)/shard_map/ppermute | solution.py:957
  129.8 63.7 %collective-permute-start.14 = (bf16[420,1120]{1,0:T(8,128)(2,1)}, bf16[420,1120]{1,0:T(8,128)(2,1)}, u32[]{:S(2)}, u32[]{:S(2)}) collective-permute-start(bf16[420,1120]{1,0:T(8,128)(2,1)} %collective-permute-done.10.refs_4_), channel_id=1, source_target_pairs={{0,4},{1,5},{2,6},{3,7},{4,0},{5,1},{6,2},{7,3},{8,12},{9,13},{10,... | collective-permute-start | bytes 2822408 | tf_op jit(solution)/shard_map/ppermute | solution.py:957
  133.2 60.2 %collective-permute-start.13 = (bf16[420,1120]{1,0:T(8,128)(2,1)}, bf16[420,1120]{1,0:T(8,128)(2,1)S(1)}, u32[]{:S(2)}, u32[]{:S(2)}) collective-permute-start(bf16[420,1120]{1,0:T(8,128)(2,1)} %collective-permute-done.9.refs_2_), channel_id=1, source_target_pairs={{0,4},{1,5},{2,6},{3,7},{4,0},{5,1},{6,2},{7,3},{16,20},{17,21},{1... | collective-permute-start | bytes 2822408 | tf_op jit(solution)/shard_map/ppermute | solution.py:957
  135.6 57.8 %collective-permute-start.15 = (bf16[420,1120]{1,0:T(8,128)(2,1)}, bf16[420,1120]{1,0:T(8,128)(2,1)S(1)}, u32[]{:S(2)}, u32[]{:S(2)}) collective-permute-start(bf16[420,1120]{1,0:T(8,128)(2,1)} %collective-permute-done.9.refs_2_), channel_id=1, source_target_pairs={{0,2},{1,3},{2,0},{3,1},{4,6},{5,7},{6,4},{7,5},{16,18},{17,19},{1... | collective-permute-start | bytes 2822408 | tf_op jit(solution)/shard_map/ppermute | solution.py:957
  138.1 55.4 %collective-permute-start.16 = (bf16[420,1120]{1,0:T(8,128)(2,1)}, bf16[420,1120]{1,0:T(8,128)(2,1)S(1)}, u32[]{:S(2)}, u32[]{:S(2)}) collective-permute-start(bf16[420,1120]{1,0:T(8,128)(2,1)} %collective-permute-done.10.refs_4_), channel_id=1, source_target_pairs={{0,2},{1,3},{2,0},{3,1},{4,6},{5,7},{6,4},{7,5},{8,10},{9,11},{10,... | collective-permute-start | bytes 2822408 | tf_op jit(solution)/shard_map/ppermute | solution.py:957
  158.1 35.3 %copy-start.31 = (bf16[1120,840]{1,0:T(8,128)(2,1)}, bf16[1120,840]{1,0:T(8,128)(2,1)S(1)}, u32[]{:S(2)}) copy-start(bf16[1120,840]{1,0:T(8,128)(2,1)S(1)} %get-tuple-element.266.refs_1_) | copy-start | bytes 5644804
  158.1 47.1 %copy-start.22 = (bf16[512,1152]{1,0:T(8,128)(2,1)S(1)}, bf16[512,1152]{1,0:T(8,128)(2,1)}, u32[]{:S(2)}) copy-start(bf16[512,1152]{1,0:T(8,128)(2,1)} %copy-done.21) | copy-start | bytes 3538948
  193.4 47.1 %copy-start.40 = (f32[4,280,512]{2,1,0:T(8,128)}, f32[4,280,512]{2,1,0:T(8,128)S(1)}, u32[]{:S(2)}) copy-start(f32[4,280,512]{2,1,0:T(8,128)S(1)} %get-tuple-element.263.outt_ref) | copy-start | bytes 6881284
  193.4 47.1 %copy-start.42 = (f32[4,8,512]{2,1,0:T(8,128)}, f32[4,8,512]{2,1,0:T(8,128)S(1)}, u32[]{:S(2)}) copy-start(f32[4,8,512]{2,1,0:T(8,128)S(1)} %get-tuple-element.180.lse_ref) | copy-start | bytes 196612
  193.5 50.2 %collective-permute-start.18 = (bf16[420,1120]{1,0:T(8,128)(2,1)}, bf16[420,1120]{1,0:T(8,128)(2,1)}, u32[]{:S(2)}, u32[]{:S(2)}) collective-permute-start(bf16[420,1120]{1,0:T(8,128)(2,1)} %collective-permute-done.12.refs_6_), channel_id=1, source_target_pairs={{0,4},{1,5},{2,6},{3,7},{4,0},{5,1},{6,2},{7,3},{8,12},{9,13},{10,... | collective-permute-start | bytes 2822408 | tf_op jit(solution)/shard_map/ppermute | solution.py:957
  195.4 48.3 %collective-permute-start.19 = (bf16[420,1120]{1,0:T(8,128)(2,1)}, bf16[420,1120]{1,0:T(8,128)(2,1)}, u32[]{:S(2)}, u32[]{:S(2)}) collective-permute-start(bf16[420,1120]{1,0:T(8,128)(2,1)} %collective-permute-done.12.refs_6_), channel_id=1, source_target_pairs={{0,2},{1,3},{2,0},{3,1},{4,6},{5,7},{6,4},{7,5},{8,10},{9,11},{10,... | collective-permute-start | bytes 2822408 | tf_op jit(solution)/shard_map/ppermute | solution.py:957
  197.9 45.9 %collective-permute-start.20 = (bf16[420,1120]{1,0:T(8,128)(2,1)S(1)}, bf16[420,1120]{1,0:T(8,128)(2,1)S(1)}, u32[]{:S(2)}, u32[]{:S(2)}) collective-permute-start(bf16[420,1120]{1,0:T(8,128)(2,1)S(1)} %collective-permute-done.15.refs_2_), channel_id=1, source_target_pairs={{0,4},{1,5},{2,6},{3,7},{4,0},{5,1},{6,2},{7,3},{16,20},{17,21},{1... | collective-permute-start | bytes 2822408 | tf_op jit(solution)/shard_map/ppermute | solution.py:957
  201.8 42.9 %collective-permute-start.21 = (bf16[420,1120]{1,0:T(8,128)(2,1)}, bf16[420,1120]{1,0:T(8,128)(2,1)S(1)}, u32[]{:S(2)}, u32[]{:S(2)}) collective-permute-start(bf16[420,1120]{1,0:T(8,128)(2,1)} %collective-permute-done.14.refs_5_), channel_id=1, source_target_pairs={{0,2},{1,3},{2,0},{3,1},{4,6},{5,7},{6,4},{7,5},{8,10},{9,11},{10,... | collective-permute-start | bytes 2822408 | tf_op jit(solution)/shard_map/ppermute | solution.py:957
  205.2 59.6 %collective-permute-start.17 = (bf16[512,1152]{1,0:T(8,128)(2,1)S(1)}, bf16[512,1152]{1,0:T(8,128)(2,1)}, u32[]{:S(2)}, u32[]{:S(2)}) collective-permute-start(bf16[512,1152]{1,0:T(8,128)(2,1)S(1)} %copy-done.22), channel_id=1, source_target_pairs={{0,2},{1,3},{2,0},{3,1},{4,6},{5,7},{6,4},{7,5},{8,10},{9,11},{10,... | collective-permute-start | bytes 3538952 | tf_op jit(solution)/shard_map/ppermute | solution.py:957
  244.7 21.9 %collective-permute-start.22 = (bf16[420,1120]{1,0:T(8,128)(2,1)}, bf16[420,1120]{1,0:T(8,128)(2,1)S(1)}, u32[]{:S(2)}, u32[]{:S(2)}) collective-permute-start(bf16[420,1120]{1,0:T(8,128)(2,1)} %collective-permute-done.19.refs_6_), channel_id=1, source_target_pairs={{0,4},{1,5},{2,6},{3,7},{4,0},{5,1},{6,2},{7,3},{8,12},{9,13},{10,... | collective-permute-start | bytes 2822408 | tf_op jit(solution)/shard_map/ppermute | solution.py:957
  281.9 5.1 collective-permute-start.23
  282.1 10.3 %collective-permute-start.25 = (bf16[1024,1152]{1,0:T(8,128)(2,1)S(1)}, bf16[1024,1152]{1,0:T(8,128)(2,1)S(1)}, u32[]{:S(2)}, u32[]{:S(2)}) collective-permute-start(bf16[1024,1152]{1,0:T(8,128)(2,1)S(1)} %pad_maximum_fusion.1.cot_ref.base_ref), channel_id=1, source_target_pairs={{0,1},{1,0},{2,3},{3,2},{4,5},{5,4},{6,7},{7,6},{8,9},{9,8},{10,11... | collective-permute-start | bytes 7077896 | tf_op jit(solution)/shard_map/ppermute | solution.py:957
  291.5 4.5 collective-permute-start.24
  331.8 35.1 %collective-permute-start.26 = (f32[1024,1152]{1,0:T(8,128)}, f32[1024,1152]{1,0:T(8,128)}, u32[]{:S(2)}, u32[]{:S(2)}) collective-permute-start(f32[1024,1152]{1,0:T(8,128)} %get-tuple-element.228), channel_id=1, source_target_pairs={{0,1},{1,0},{2,3},{3,2},{4,5},{5,4},{6,7},{7,6},{8,9},{9,8},{10,11... | collective-permute-start | bytes 14155784 | tf_op jit(solution)/shard_map/ppermute | solution.py:957
  332.0 34.9 %copy-start.7 = (bf16[1024,1152]{1,0:T(8,128)(2,1)S(1)}, bf16[1024,1152]{1,0:T(8,128)(2,1)}, u32[]{:S(2)}) copy-start(bf16[1024,1152]{1,0:T(8,128)(2,1)} %copy-done.6) | copy-start | bytes 7077892
  390.2 7.0 collective-permute-start.27
  395.6 118.7 %collective-permute-start.29 = (f32[1024,1152]{1,0:T(8,128)}, f32[1024,1152]{1,0:T(8,128)}, u32[]{:S(2)}, u32[]{:S(2)}) collective-permute-start(f32[1024,1152]{1,0:T(8,128)} %get-tuple-element.250), channel_id=1, source_target_pairs={{0,1},{1,0},{2,3},{3,2},{4,5},{5,4},{6,7},{7,6},{8,9},{9,8},{10,11... | collective-permute-start | bytes 14155784 | tf_op jit(solution)/shard_map/ppermute | solution.py:957
  396.2 124.4 %collective-permute-start.31 = (bf16[1120,1120]{1,0:T(8,128)(2,1)}, bf16[1120,1120]{1,0:T(8,128)(2,1)}, u32[]{:S(2)}, u32[]{:S(2)}) collective-permute-start(bf16[1120,1120]{1,0:T(8,128)(2,1)} %convolution_convert_fusion.1), channel_id=1, source_target_pairs={{0,2},{1,3},{2,0},{3,1},{4,6},{5,7},{6,4},{7,5},{8,10},{9,11},{10,... | collective-permute-start | bytes 7526408 | tf_op jit(solution)/shard_map/ppermute | solution.py:957
  442.4 63.8 %collective-permute-start.28 = (bf16[280,1120]{1,0:T(8,128)(2,1)S(1)}, bf16[280,1120]{1,0:T(8,128)(2,1)S(1)}, u32[]{:S(2)}, u32[]{:S(2)}) collective-permute-start(bf16[280,1120]{1,0:T(8,128)(2,1)S(1)} %convolution_convert_fusion.3), channel_id=1, source_target_pairs={{0,2},{1,3},{2,0},{3,1},{4,6},{5,7},{6,4},{7,5},{8,10},{9,11},{10,... | collective-permute-start | bytes 1881608 | tf_op jit(solution)/shard_map/ppermute | solution.py:957
  443.4 81.1 %collective-permute-start.30 = (bf16[1120,1120]{1,0:T(8,128)(2,1)}, bf16[1120,1120]{1,0:T(8,128)(2,1)}, u32[]{:S(2)}, u32[]{:S(2)}) collective-permute-start(bf16[1120,1120]{1,0:T(8,128)(2,1)} %convolution_convert_fusion), channel_id=1, source_target_pairs={{0,2},{1,3},{2,0},{3,1},{4,6},{5,7},{6,4},{7,5},{8,10},{9,11},{10,... | collective-permute-start | bytes 7526408 | tf_op jit(solution)/shard_map/ppermute | solution.py:957
  519.4 92.7 %collective-permute-start.33 = (bf16[1120,896]{1,0:T(8,128)(2,1)}, bf16[1120,896]{1,0:T(8,128)(2,1)}, u32[]{:S(2)}, u32[]{:S(2)}) collective-permute-start(bf16[1120,896]{1,0:T(8,128)(2,1)} %convolution_convert_fusion.2), channel_id=1, source_target_pairs={{0,2},{1,3},{2,0},{3,1},{4,6},{5,7},{6,4},{7,5},{8,10},{9,11},{10,... | collective-permute-start | bytes 6021128 | tf_op jit(solution)/shard_map/ppermute | solution.py:957
  536.0 56.2 %collective-permute-start.32 = (bf16[512,1152]{1,0:T(8,128)(2,1)}, bf16[512,1152]{1,0:T(8,128)(2,1)}, u32[]{:S(2)}, u32[]{:S(2)}) collective-permute-start(bf16[512,1152]{1,0:T(8,128)(2,1)} %slice_select_fusion.2), channel_id=1, source_target_pairs={{0,2},{1,3},{2,0},{3,1},{4,6},{5,7},{6,4},{7,5},{8,10},{9,11},{10,... | collective-permute-start | bytes 3538952 | tf_op jit(solution)/shard_map/ppermute | solution.py:957
  537.0 79.5 %collective-permute-start.34 = (bf16[3,420,1120]{2,1,0:T(8,128)(2,1)}, bf16[3,420,1120]{2,1,0:T(8,128)(2,1)}, u32[]{:S(2)}, u32[]{:S(2)}) collective-permute-start(bf16[3,420,1120]{2,1,0:T(8,128)(2,1)} %get-tuple-element.273), channel_id=1, source_target_pairs={{0,4},{4,0},{8,12},{12,8},{16,20},{20,16},{24,28},{28,24},{1,5},{5... | collective-permute-start | bytes 8467208 | tf_op jit(solution)/shard_map/ppermute | solution.py:957
  614.7 23.7 %collective-permute-start.35 = (bf16[560,896]{1,0:T(8,128)(2,1)S(1)}, bf16[560,896]{1,0:T(8,128)(2,1)S(1)}, u32[]{:S(2)}, u32[]{:S(2)}) collective-permute-start(bf16[560,896]{1,0:T(8,128)(2,1)S(1)} %select_convert_fusion), channel_id=1, source_target_pairs={{0,4},{4,0},{8,12},{12,8},{16,20},{20,16},{24,28},{28,24},{1,5},{5... | collective-permute-start | bytes 3010568 | tf_op jit(solution)/shard_map/ppermute | solution.py:957
  616.5 52.8 %collective-permute-start.41 = (bf16[1024,1152]{1,0:T(8,128)(2,1)S(1)}, bf16[1024,1152]{1,0:T(8,128)(2,1)S(1)}, u32[]{:S(2)}, u32[]{:S(2)}) collective-permute-start(bf16[1024,1152]{1,0:T(8,128)(2,1)S(1)} %get-tuple-element.295), channel_id=1, source_target_pairs={{0,1},{1,0},{2,3},{3,2},{4,5},{5,4},{6,7},{7,6},{8,9},{9,8},{10,11... | collective-permute-start | bytes 7077896 | tf_op jit(solution)/shard_map/ppermute | solution.py:957
  619.1 23.3 %collective-permute-start.36 = (bf16[420,1120]{1,0:T(8,128)(2,1)S(1)}, bf16[420,1120]{1,0:T(8,128)(2,1)S(1)}, u32[]{:S(2)}, u32[]{:S(2)}) collective-permute-start(bf16[420,1120]{1,0:T(8,128)(2,1)S(1)} %get-tuple-element.278), channel_id=1, source_target_pairs={{0,8},{4,12},{16,24},{20,28},{1,9},{5,13},{17,25},{21,29},{2,10},{... | collective-permute-start | bytes 2822408 | tf_op jit(solution)/shard_map/ppermute | solution.py:957
  620.4 42.7 %collective-permute-start.37 = (bf16[420,1120]{1,0:T(8,128)(2,1)S(1)}, bf16[420,1120]{1,0:T(8,128)(2,1)S(1)}, u32[]{:S(2)}, u32[]{:S(2)}) collective-permute-start(bf16[420,1120]{1,0:T(8,128)(2,1)S(1)} %get-tuple-element.280), channel_id=1, source_target_pairs={{0,8},{4,12},{8,0},{12,4},{16,24},{20,28},{24,16},{28,20},{1,9},{5... | collective-permute-start | bytes 2822408 | tf_op jit(solution)/shard_map/ppermute | solution.py:957
  638.7 27.3 %collective-permute-start.38 = (bf16[560,896]{1,0:T(8,128)(2,1)S(1)}, bf16[560,896]{1,0:T(8,128)(2,1)S(1)}, u32[]{:S(2)}, u32[]{:S(2)}) collective-permute-start(bf16[560,896]{1,0:T(8,128)(2,1)S(1)} %get-tuple-element.284), channel_id=1, source_target_pairs={{8,0},{12,4},{24,16},{28,20},{9,1},{13,5},{25,17},{29,21},{10,2},{... | collective-permute-start | bytes 3010568 | tf_op jit(solution)/shard_map/ppermute | solution.py:957
  640.0 29.3 %slice-start.2 = ((s8[4718592]{0:T(1024)(128)(4,1)}), s8[4194304]{0:T(1024)(128)(4,1)S(1)}, s32[]{:S(2)}) async-start(s8[4718592]{0:T(1024)(128)(4,1)} %bitcast.58), calls=%async_computation.2 | async-start | bytes 8388608
  640.6 28.7 %slice-start.3 = ((s8[4718592]{0:T(1024)(128)(4,1)}), s8[524288]{0:T(1024)(128)(4,1)S(1)}, s32[]{:S(2)}) async-start(s8[4718592]{0:T(1024)(128)(4,1)} %bitcast.58), calls=%async_computation.3 | async-start | bytes 1048576
  667.9 1.4 collective-permute-start.40
  668.0 48.6 %collective-permute-start.39 = (bf16[560,896]{1,0:T(8,128)(2,1)}, bf16[560,896]{1,0:T(8,128)(2,1)}, u32[]{:S(2)}, u32[]{:S(2)}) collective-permute-start(bf16[560,896]{1,0:T(8,128)(2,1)} %get-tuple-element.289), channel_id=1, source_target_pairs={{16,0},{20,4},{17,1},{21,5},{18,2},{22,6},{19,3},{23,7}} | collective-permute-start | bytes 3010568 | tf_op jit(solution)/shard_map/ppermute | solution.py:957
  677.4 48.7 %collective-permute-start.42 = (bf16[512,1152]{1,0:T(8,128)(2,1)}, bf16[512,1152]{1,0:T(8,128)(2,1)}, u32[]{:S(2)}, u32[]{:S(2)}) collective-permute-start(bf16[512,1152]{1,0:T(8,128)(2,1)} %slice_select_fusion.1), channel_id=1, source_target_pairs={{0,2},{1,3},{2,0},{3,1},{4,6},{5,7},{6,4},{7,5},{8,10},{9,11},{10,... | collective-permute-start | bytes 3538952 | tf_op jit(solution)/shard_map/ppermute | solution.py:957
  679.6 49.8 %collective-permute-start.43 = (bf16[420,1120]{1,0:T(8,128)(2,1)S(1)}, bf16[420,1120]{1,0:T(8,128)(2,1)}, u32[]{:S(2)}, u32[]{:S(2)}) collective-permute-start(bf16[420,1120]{1,0:T(8,128)(2,1)S(1)} %copy-done.53), channel_id=1, source_target_pairs={{24,8},{28,12},{0,16},{4,20},{8,24},{12,28},{25,9},{29,13},{1,17},... | collective-permute-start | bytes 2822408 | tf_op jit(solution)/shard_map/ppermute | solution.py:957
  737.8 29.5 %copy-start.13 = (f32[12,1120]{1,0:T(8,128)S(1)}, f32[12,1120]{1,0:T(8,128)}, u32[]{:S(2)}) copy-start(f32[12,1120]{1,0:T(8,128)} %copy-done.12) | copy-start | bytes 161284
  737.8 35.5 %copy-start.54 = (f32[12,1120]{1,0:T(8,128)S(1)}, f32[12,1120]{1,0:T(8,128)}, u32[]{:S(2)}) copy-start(f32[12,1120]{1,0:T(8,128)} %param.21) | copy-start | bytes 161284
  737.8 35.5 %copy-start.55 = (f32[12,1120]{1,0:T(8,128)S(1)}, f32[12,1120]{1,0:T(8,128)}, u32[]{:S(2)}) copy-start(f32[12,1120]{1,0:T(8,128)} %param.22) | copy-start | bytes 161284
  749.6 27.7 %copy-start.20 = (f32[1,1,470400]{2,1,0:T(1,128)S(1)}, f32[1,1,470400]{2,1,0:T(1,128)}, u32[]{:S(2)}) copy-start(f32[1,1,470400]{2,1,0:T(1,128)} %weight_ref.7) | copy-start | bytes 5644804
  752.7 1.3 collective-permute-start.44
  754.0 4.4 collective-permute-start.45
  758.4 4.4 collective-permute-start.46
  762.9 4.4 collective-permute-start.47
  767.3 6.0 collective-permute-start.48
  (70 other events, 473.8 us)

commit v9 on v8

--- a/solution.py
+++ b/solution.py
@@ -476,8 +476,8 @@
     )(ints, ratios, weight, update)
 
 
-def unpack_body(cut, out_rows, in_rows, place_ref, *refs):
-    blocks, (w_out, w_in, w_back, held, sems) = refs[:8], refs[8:]
+def unpack_body(cut, rows, skipped, place_ref, *refs):
+    blocks, (w_out, w_in, w_back, held, sems) = refs[:8], refs[8 + skipped :]
     here = place_ref[0]
     copies = [
         pltpu.make_async_copy(block, held.at[index ^ here], sems.at[index])
@@ -487,37 +487,52 @@
         copy.start()
     for copy in copies:
         copy.wait()
-    begin = 2 * cut
-    for target, rows in ((w_out, out_rows), (w_in, in_rows), (w_back, in_rows)):
+    begin, columns = 2 * cut, held.shape[2]
+    for target, count_rows in zip((w_out, w_in, w_back), rows):
         done = 0
-        while done < rows:
+        while done < count_rows:
             block, offset = divmod(begin + done, cut)
-            count = min(cut - offset, rows - done)
-            target[done : done + count] = held[block, offset : offset + count]
+            count = min(cut - offset, count_rows - done)
+            target[done : done + count, :columns] = held[block, offset : offset + count]
             done += count
-        begin += rows
-
-
-def unpack_share(place, blocks, out_rows, in_rows):
+        begin += count_rows
+        if target.shape[1] > columns:
+            target[:, columns:] = jnp.zeros((count_rows, target.shape[1] - columns), BF16)
+    rest = w_back.shape[0] - rows[2]
+    if rest:
+        w_back[rows[2] :] = jnp.zeros((rest, w_back.shape[1]), BF16)
+
+
+def unpack_share(place, blocks, out_rows, in_rows, part, joined):
     cut, columns = blocks[0].shape
-    shapes = [(out_rows, columns), (in_rows, columns), (in_rows, columns)]
-    return pl.pallas_call(
-        functools.partial(unpack_body, cut, out_rows, in_rows),
+    wide = lanes(columns)
+    joined = () if joined is None else tuple(joined)
+    return pl.pallas_call(
+        functools.partial(unpack_body, cut, (out_rows, in_rows, columns), len(joined)),
         grid_spec=pltpu.PrefetchScalarGridSpec(
             num_scalar_prefetch=1,
             grid=(1,),
-            in_specs=[hbm()] * 8,
-            out_specs=[whole_block(shape) for shape in shapes],
+            in_specs=[hbm()] * (8 + len(joined)),
+            out_specs=[
+                whole_block((out_rows, columns)),
+                pl.BlockSpec((in_rows, wide), lambda i, place_ref: (0, part)),
+                pl.BlockSpec((wide, columns), lambda i, place_ref: (part, 0)),
+            ],
             scratch_shapes=[
                 pltpu.VMEM((8, cut, columns), BF16),
                 pltpu.SemaphoreType.DMA((8,)),
             ],
         ),
-        out_shape=[jax.ShapeDtypeStruct(shape, BF16) for shape in shapes],
+        out_shape=[
+            jax.ShapeDtypeStruct((out_rows, columns), BF16),
+            jax.ShapeDtypeStruct((in_rows, 2 * wide), BF16),
+            jax.ShapeDtypeStruct((2 * wide, columns), BF16),
+        ],
+        input_output_aliases={9 + i: 1 + i for i in range(len(joined))},
         compiler_params=vmem(48),
         cost_estimate=lasting(6),
         name="unpack_share",
-    )(place, *blocks)
+    )(place, *blocks, *joined)
 
 
 def pack_rest_body(
@@ -876,17 +891,7 @@
     )(rows, kept, got, base, gain)
 
 
-def feed_forward_body(
-    skipped,
-    rows_ref,
-    cot_ref,
-    w_in_mine,
-    w_in_theirs,
-    w_back_mine,
-    w_back_theirs,
-    bias_ref,
-    *refs,
-):
+def feed_forward_body(skipped, rows_ref, cot_ref, w_in, w_back, bias_ref, *refs):
     (
         act_mine, act_theirs, inner_mine, inner_theirs, rows_out, cot_out, out_ref, up_ref, sums_ref
     ) = refs[skipped:]
@@ -899,30 +904,27 @@
     def clear():
         sums_ref[...] = jnp.zeros_like(sums_ref)
 
-    out, up = None, None
-    shares = (
-        (w_in_mine, w_back_mine, act_mine, inner_mine),
-        (w_in_theirs, w_back_theirs, act_theirs, inner_theirs),
-    )
-    for part, (w_in, w_back, act_ref, inner_ref) in enumerate(shares):
-        hidden = dot_rows(rows, w_in[...]) + bias_ref[part : part + 1]
-        value, slope = gelu_parts(hidden)
-        act = value.astype(BF16)
-        act_ref[...] = act
-        inner = (dot_transposed(cot, w_back[...]) * slope).astype(BF16)
-        inner_ref[...] = inner
-        sums_ref[part : part + 1] += jnp.sum(inner.astype(F32), axis=0, keepdims=True)
-        one_out = dot_rows(act, w_back[...])
-        one_up = dot_transposed(inner, w_in[...])
-        out = one_out if out is None else out + one_out
-        up = one_up if up is None else up + one_up
-    put(out_ref, out)
-    put(up_ref, up)
+    width = act_mine.shape[1]
+    wide = w_in.shape[1] // 2
+    value, slope = gelu_parts(dot_rows(rows, w_in[...]) + bias_ref[0:1])
+    act = value.astype(BF16)
+    inner = (dot_transposed(cot, w_back[...]) * slope).astype(BF16)
+    sums_ref[0:1] += jnp.sum(inner.astype(F32), axis=0, keepdims=True)
+    for part, (act_ref, inner_ref) in enumerate(
+        ((act_mine, inner_mine), (act_theirs, inner_theirs))
+    ):
+        act_ref[...] = act[:, part * wide : part * wide + width]
+        inner_ref[...] = inner[:, part * wide : part * wide + width]
+    put(out_ref, dot_rows(act, w_back[...]))
+    put(up_ref, dot_transposed(inner, w_in[...]))
 
 
 def feed_forward(rows, cot, half, weights, biases, filled):
     count, sent_width = rows.shape
-    model_width, ff_share = weights[0].shape
+    model_width, both_wide = weights[0].shape
+    ff_share = biases.shape[1]
+    pad = both_wide // 2 - ff_share
+    biases = jnp.pad(biases, ((0, 0), (0, pad))).reshape(1, both_wide)
     block = min(FF_ROWS, count)
     steps = count // block
     row_spec = pl.BlockSpec((block, sent_width), lambda i: (i, 0))
@@ -936,17 +938,17 @@
         out_shape=[act_shape] * 4
         + [row_shape] * 2
         + [part_shape] * 2
-        + [jax.ShapeDtypeStruct((8, ff_share), F32)],
+        + [jax.ShapeDtypeStruct((8, both_wide), F32)],
         grid=(steps,),
         in_specs=[row_spec, row_spec]
         + [fixed(matrix.shape) for matrix in weights]
-        + [fixed((2, ff_share))]
+        + [fixed((1, both_wide))]
         + [hbm()] * len(filled),
         out_specs=[joined(ff_share)] * 4
         + [joined(model_width)] * 2
         + [row_spec] * 2
-        + [pl.BlockSpec((8, ff_share), lambda i: (0, 0))],
-        input_output_aliases={7 + i: i for i in range(len(filled))},
+        + [pl.BlockSpec((8, both_wide), lambda i: (0, 0))],
+        input_output_aliases={5 + i: i for i in range(len(filled))},
         compiler_params=vmem(58),
         cost_estimate=lasting(34),
         name="feed_forward",
@@ -1114,8 +1116,23 @@
             second = jnp.where(y_here == 0, matrix[model_width // 2 :], matrix[: model_width // 2])
             halves += [first, second]
         w_out = [flat[first_end:second_end].reshape(head_share, model_width) for flat in per_share]
-        w_in = [flat[second_end:third_end].reshape(model_width, model_width) for flat in per_share]
-        w_back = [flat[third_end:].reshape(model_width, model_width) for flat in per_share]
+        beyond = lanes(model_width) - model_width
+        w_in = jnp.concatenate(
+            [
+                jnp.pad(
+                    flat[second_end:third_end].reshape(model_width, model_width),
+                    ((0, 0), (0, beyond)),
+                )
+                for flat in per_share
+            ],
+            axis=1,
+        )
+        w_back = jnp.concatenate(
+            [
+                jnp.pad(flat[third_end:].reshape(model_width, model_width), ((0, beyond), (0, 0)))
+                for flat in per_share
+            ]
+        )
 
     def share_columns(vector, share):
         return lax.dynamic_slice_in_dim(vector, share * head_share, head_share)
@@ -1172,16 +1189,18 @@
         both.append(move_rest(over[3], (1, 0), 3))
         rest_mine = [block for pair in zip((wide, near, far, last), across) for block in pair]
         rest_theirs = [block for pair in zip(over, both) for block in pair]
-        matrices_mine = unpack_share(dp_index, rest_mine, head_share, model_width)
-        matrices_theirs = unpack_share(dp_index, rest_theirs, head_share, model_width)
-        w_out, w_in, w_back = (list(pair) for pair in zip(matrices_mine, matrices_theirs))
+        out_mine, *joined = unpack_share(dp_index, rest_mine, head_share, model_width, 0, None)
+        out_theirs, w_in, w_back = unpack_share(
+            dp_index, rest_theirs, head_share, model_width, 1, joined
+        )
+        w_out = [out_mine, out_theirs]
         own_e, w_out[0] = tie(own_e, w_out[0])
     other_e = swap(own_e, "seq", 1)
     sent, kept = split_product([attended[0][0], attended[1][0]], w_out, False, model_width, BF16)
     middle, low_two = middle_norm(own_in, kept, swap(sent, "seq", 1), small_master)
     other_two = swap(low_two, "seq", 1)
 
-    weights = (w_in[0], w_in[1], w_back[0], w_back[1])
+    weights = (w_in, w_back)
     *filled, out_sent, up_sent, sums_sent = feed_forward(
         other_two, other_e, 1, weights, ff_biases, None
     )
@@ -1323,8 +1342,9 @@
     bias_sums = [jnp.sum(packed[part].astype(F32), axis=0) for part in range(2)]
     inner_rows = jnp.zeros((4, model_width), F32)
     for part in range(2):
+        first = part * lanes(model_width)
         inner_rows = lax.dynamic_update_slice(
-            inner_rows, inner_sums[part : part + 1], (shares[part], 0)
+            inner_rows, inner_sums[0:1, first : first + model_width], (shares[part], 0)
         )
     small_now = jnp.concatenate(
         [

time: 794 us -> 789 us (level)
    unnamed x172 -> x173, local copies, waits for them, and re-layouts: 24.4 us -> 26.1 us
  transfers between devices with their start and end apart: 49 -> 49, of which waited for: 20 -> 21; matrix products, arithmetic and copies ran while one was open for 13% -> 14% of each run, Pallas kernels for 37% -> 37%
where the time goes in v9:
time: 789 us; the launch traced here: 780 us
  Pallas kernels  360 us (46%)
  waiting for transfers between devices  181 us (23%)
  starting transfers between devices  73.7 us (9%)
  matrix products  67.2 us (9%)
  local copies, waits for them, and re-layouts  48.7 us (6%)
  other arithmetic  42 us (5%)
    ppermute x49, waiting for transfers between devices, permute(): return lax.ppermute(value, axis_name, pairs)  181 us
    pallas_call x2, Pallas kernels, attention_backward(): pl.pallas_call(functools.partial(attention_backward_body, heads, width, b...  104 us
    ppermute x49, starting transfers between devices, permute(): return lax.ppermute(value, axis_name, pairs)  73.7 us
    pallas_call x2, Pallas kernels, attention_forward(): pl.pallas_call(functools.partial(attention_forward_body, heads, width, bq...  70 us
    dot_general x8, matrix products, dot_columns(): lax.dot_general(left, right, (((0,), (0,)), ((), ())), preferred_element_...  67.2 us
    pallas_call x2, Pallas kernels, feed_forward(): pl.pallas_call(functools.partial(feed_forward_body, len(filled)), out_sha...  64 us
    unnamed x173, local copies, waits for them, and re-layouts  26.1 us
    pallas_call x2, Pallas kernels, split_product(): pl.pallas_call(functools.partial(split_product_body, steps, turned, len(l...  19.1 us
  transfers between devices with their start and end apart: 49, of which 21 were waited for; matrix products, arithmetic and copies ran while one was open for 14% of the time, Pallas kernels for 37%

profile of v9, /device:TPU:0, one launch (start us, length us, event | category | flops | bytes accessed | tf_op | source)
XLA Modules:
  0.0 780.4 jit_solution(6541398713599921055)
XLA Ops:
  5.3 2.9 collective-permute-start
  9.1 2.8 reshape.194
  11.9 5.4 collective-permute-start.1
  17.9 16.6 %collective-permute-done = bf16[512,1152]{1,0:T(8,128)(2,1)} collective-permute-done((bf16[512,1152]{1,0:T(8,128)(2,1)}, bf16[512,1152]{1,0:T(8,128)(2,1)}, u32[]{:S(2)}, u32[]{:S(2)}) %collective-permute-start) | collective-permute-done | bytes 1179680 | tf_op jit(solution)/shard_map/ppermute | solution.py:959
  42.1 5.9 collective-permute-start.2
  56.2 13.3 %collective-permute-done.2 = bf16[560,840]{1,0:T(8,128)(2,1)} collective-permute-done((bf16[560,840]{1,0:T(8,128)(2,1)}, bf16[560,840]{1,0:T(8,128)(2,1)}, u32[]{:S(2)}, u32[]{:S(2)}) %collective-permute-start.2) | collective-permute-done | bytes 940832 | tf_op jit(solution)/shard_map/ppermute | solution.py:959
  78.8 16.0 %collective-permute-done.6.a1 = bf16[560,840]{1,0:T(8,128)(2,1)} collective-permute-done((bf16[560,840]{1,0:T(8,128)(2,1)S(1)}, bf16[560,840]{1,0:T(8,128)(2,1)}, u32[]{:S(2)}, u32[]{:S(2)}) %collective-permute-start.6) | collective-permute-done | bytes 940832 | tf_op jit(solution)/shard_map/ppermute | solution.py:959
  101.4 4.7 square_sums.1
  106.1 20.4 %collective-permute-done.10.refs_4_ = bf16[420,1120]{1,0:T(8,128)(2,1)} collective-permute-done((bf16[420,1120]{1,0:T(8,128)(2,1)}, bf16[420,1120]{1,0:T(8,128)(2,1)}, u32[]{:S(2)}, u32[]{:S(2)}) %collective-permute-start.10) | collective-permute-done | bytes 940832 | tf_op jit(solution)/shard_map/ppermute | solution.py:959
  129.8 3.4 collective-permute-start.14
  135.6 2.4 collective-permute-start.15
  138.1 3.4 collective-permute-start.16
  141.5 16.6 %project.1 = (bf16[2048,840]{1,0:T(8,128)(2,1)}, bf16[2048,840]{1,0:T(8,128)(2,1)}, bf16[2048,1120]{1,0:T(8,128)(2,1)}, bf16[1120,840]{1,0:T(8,128)(2,1)S(1)}, bf16[1120,840]{1,0:T(8,128)(2,1)}) custom-call(s32[1]{0:T(128)} %bitcast.place_ref, bf16[1024,1152]{1,0:T(8,128)(2,1)} %pad.16.own_ref, bf16[1024,1152]{1,0:T(8,128)(2,1)} %collective-permute-done.5.other_ref, ...), custom_call_target="tpu_custom_call" | custom-call | flops 16000000000 | bytes 4096 | tf_op jit(solution)/shard_map/project/pallas_call | solution.py:628
  158.1 35.3 %attention_forward.2 = (bf16[2048,280]{1,0:T(8,128)(2,1)S(1)}, f32[4,280,512]{2,1,0:T(8,128)S(1)}, f32[4,8,512]{2,1,0:T(8,128)S(1)}) custom-call(s32[4]{0:T(128)S(1)} %and_select_fusion.low_ref, s32[1]{0:T(128)} %bitcast.8.core_ref, s32[4,1,512]{2,1,0:T(1,128)S(1)} %compare_select_fusion.start_ref, bf16[2048,840]{1,0:T(8,128)(2,1)} %get-tuple-element.175.qkv_ref), custom_call_target="tpu_custom_call" | custom-call | flops 35000000512 | bytes 4096 | tf_op jit(solution)/shard_map/attention_forward/pallas_call | solution.py:274
  197.4 3.9 collective-permute-start.20
  201.3 4.1 collective-permute-start.21
  205.5 34.7 %attention_forward.3 = (bf16[2048,280]{1,0:T(8,128)(2,1)S(1)}, f32[4,280,512]{2,1,0:T(8,128)S(1)}, f32[4,8,512]{2,1,0:T(8,128)S(1)}) custom-call(s32[4]{0:T(128)S(1)} %and_select_fusion.low_ref, s32[1]{0:T(128)} %bitcast.8.core_ref, s32[4,1,512]{2,1,0:T(1,128)S(1)} %compare_select_fusion.start_ref, bf16[2048,840]{1,0:T(8,128)(2,1)} %get-tuple-element.181.qkv_ref), custom_call_target="tpu_custom_call" | custom-call | flops 35000000512 | bytes 4096 | tf_op jit(solution)/shard_map/attention_forward/pallas_call | solution.py:274
  245.4 2.5 collective-permute-start.22
  247.9 5.8 unpack_share.2
  253.7 11.1 %collective-permute-done.17 = bf16[512,1152]{1,0:T(8,128)(2,1)} collective-permute-done((bf16[512,1152]{1,0:T(8,128)(2,1)S(1)}, bf16[512,1152]{1,0:T(8,128)(2,1)}, u32[]{:S(2)}, u32[]{:S(2)}) %collective-permute-start.17) | collective-permute-done | bytes 1179680 | tf_op jit(solution)/shard_map/ppermute | solution.py:959
  268.4 5.6 unpack_share.3
  274.0 8.3 %split_product.2 = (bf16[1024,1152]{1,0:T(8,128)(2,1)}, f32[1024,1120]{1,0:T(8,128)}) custom-call(bf16[2048,280]{1,0:T(8,128)(2,1)S(1)} %get-tuple-element.182.refs_0_, bf16[2048,280]{1,0:T(8,128)(2,1)S(1)} %copy-done.27, bf16[280,1120]{1,0:T(8,128)(2,1)S(1)} %get-tuple-element.200.refs_2_.w_a, bf16[280,1120]{1,0:T(8,128)(2,1)S(1)} %get-tuple-element.210.refs_3_.w_b), custom_call_target="tpu_custom_call" | custom-call | flops 8999999488 | bytes 4096 | tf_op jit(solution)/shard_map/split_product/pallas_call | solution.py:735
  283.2 4.4 collective-permute-done.23.got_ref
  293.6 3.1 collective-permute-done.24.rows_ref
  298.1 31.7 %feed_forward.2 = (bf16[2048,1120]{1,0:T(8,128)(2,1)}, bf16[2048,1120]{1,0:T(8,128)(2,1)}, bf16[2048,1120]{1,0:T(8,128)(2,1)}, bf16[2048,1120]{1,0:T(8,128)(2,1)...) custom-call(bf16[1024,1152]{1,0:T(8,128)(2,1)} %copy-done.68, ...), custom_call_target="tpu_custom_call" | custom-call | flops 33999998976 | bytes 4096 | tf_op jit(solution)/shard_map/feed_forward/pallas_call | solution.py:936
  330.1 32.2 %feed_forward.3 = (bf16[2048,1120]{1,0:T(8,128)(2,1)}, bf16[2048,1120]{1,0:T(8,128)(2,1)}, bf16[2048,1120]{1,0:T(8,128)(2,1)}, bf16[2048,1120]{1,0:T(8,128)(2,1)...) custom-call(bf16[1024,1152]{1,0:T(8,128)(2,1)} %copy-done.15, ...), custom_call_target="tpu_custom_call", output_to_operand_aliasing={{0}: (5, {}), {1}: (6, {}), {2}: (7, {}), {3}: (8, {}), {4}... | custom-call | flops 33999998976 | bytes 4096 | tf_op jit(solution)/shard_map/feed_forward/pallas_call | solution.py:936
  364.7 7.8 norm_back.2
  372.5 13.1 %convolution_convert_fusion.1 = bf16[1120,1120]{1,0:T(8,128)(2,1)} fusion(bf16[2048,1120]{1,0:T(8,128)(2,1)} %get-tuple-element.225, bf16[2048,1120]{1,0:T(8,128)(2,1)} %get-tuple-element.239), kind=kOutput, calls=%fused_computation.1 | convolution fusion | flops 5139276800 | bytes 11683840 | tf_op jit(solution)/shard_map/dot_general | solution.py:39
  388.1 3.0 fusion.23
  391.8 11.5 %convolution_convert_fusion = bf16[1120,1120]{1,0:T(8,128)(2,1)} fusion(bf16[2048,1120]{1,0:T(8,128)(2,1)} %get-tuple-element.240, bf16[2048,1120]{1,0:T(8,128)(2,1)} %get-tuple-element.235), kind=kOutput, calls=%fused_computation | convolution fusion | flops 5139276800 | bytes 11683840 | tf_op jit(solution)/shard_map/dot_general | solution.py:39
  403.3 8.2 %out_grads.1 = (bf16[2048,280]{1,0:T(8,128)(2,1)S(1)}, bf16[2048,280]{1,0:T(8,128)(2,1)S(1)}, bf16[2048,1120]{1,0:T(8,128)(2,1)}) custom-call(bf16[1024,1152]{1,0:T(8,128)(2,1)} %get-tuple-element.236.own_ref, bf16[1024,1152]{1,0:T(8,128)(2,1)} %collective-permute-done.27.other_ref, bf16[280,1120]{1,0:T(8,128)(2,1)S(1)} %copy-done.37, ...), custom_call_target="tpu_custom_call" | custom-call | flops 8000000000 | bytes 4096 | tf_op jit(solution)/shard_map/out_grads/pallas_call | solution.py:661
  411.6 5.2 convolution_convert_fusion.3
  416.8 2.7 fusion.43.out_ref
  419.6 8.5 %fusion.42.in_ref = f32[1120,1120]{1,0:T(8,128)} fusion(bf16[2048,1120]{1,0:T(8,128)(2,1)S(1)} %bitcast.76, bf16[2048,1120]{1,0:T(8,128)(2,1)S(1)} %bitcast.74), kind=kOutput, calls=%fused_computation.127 | convolution fusion | flops 5138022400 | bytes 14192640 | tf_op jit(solution)/shard_map/dot_general | solution.py:39
  428.1 8.8 %fusion.41.back_ref = f32[1120,1120]{1,0:T(8,128)} fusion(bf16[2048,1120]{1,0:T(8,128)(2,1)S(1)} %bitcast.72, bf16[2048,1120]{1,0:T(8,128)(2,1)S(1)} %bitcast.78), kind=kOutput, calls=%fused_computation.126 | convolution fusion | flops 5138022400 | bytes 14192640 | tf_op jit(solution)/shard_map/dot_general | solution.py:39
  439.0 51.9 %attention_backward.2.left = bf16[2048,896]{1,0:T(8,128)(2,1)} custom-call(s32[4]{0:T(128)} %copy-done.25, s32[1]{0:T(128)} %bitcast.8.core_ref, s32[4,1,512]{2,1,0:T(1,128)} %copy-done.14, bf16[2048,840]{1,0:T(8,128)(2,1)} %get-tuple-element.181.qkv_ref, bf16[2048,280]{1,0:T(8,128)(2,1)} %copy-done.39, f32[4,280,512]{2,1,0:T(8,128)} %copy-done.41, ...), custom_call_target="tpu_custom_call" | custom-call | flops 56000000000 | bytes 4096 | tf_op jit(solution)/shard_map/attention_backward/pallas_call | solution.py:317
  490.9 9.9 %convolution_convert_fusion.2 = bf16[1120,896]{1,0:T(8,128)(2,1)} fusion(bf16[2048,1120]{1,0:T(8,128)(2,1)} %get-tuple-element.174, bf16[2048,896]{1,0:T(8,128)(2,1)} %attention_backward.2.left), kind=kOutput, calls=%fused_computation.17 | convolution fusion | flops 4111421440 | bytes 10264576 | tf_op jit(solution)/shard_map/dot_general | solution.py:39
  500.8 8.0 %partial_product.1.refs_2_ = f32[2048,1120]{1,0:T(8,128)} custom-call(bf16[2048,896]{1,0:T(8,128)(2,1)S(1)} %copy-done.2, bf16[1120,840]{1,0:T(8,128)(2,1)S(1)} %copy-done.33), custom_call_target="tpu_custom_call" | custom-call | flops 8999999488 | bytes 4096 | tf_op jit(solution)/shard_map/partial_product/pallas_call | solution.py:715
  508.8 4.9 fusion.8
  514.0 6.0 collective-permute-done.30.in_got
  520.0 10.4 %pack_rest.1 = (f32[3,420,1120]{2,1,0:T(8,128)}, bf16[3,420,1120]{2,1,0:T(8,128)(2,1)}) custom-call(s32[1]{0:T(128)} %bitcast.place_ref, f32[280,1120]{1,0:T(8,128)S(1)} %copy-done.11, f32[1120,1120]{1,0:T(8,128)} %fusion.42.in_ref, f32[1120,1120]{1,0:T(8,128)} %fusion.41.back_ref, bf16[280,1120]{1,0:T(8,128)(2,1)S(1)} %collective-permute-done.28.out_got, ...), custom_call_target="tpu_custom_call" | custom-call | flops 10000000000 | bytes 4096 | tf_op jit(solution)/shard_map/pack_rest/pallas_call | solution.py:567
  532.8 51.9 %attention_backward.3.refs_0_ = bf16[2048,896]{1,0:T(8,128)(2,1)} custom-call(s32[4]{0:T(128)} %copy-done.25, s32[1]{0:T(128)} %bitcast.8.core_ref, s32[4,1,512]{2,1,0:T(1,128)} %copy-done.14, bf16[2048,840]{1,0:T(8,128)(2,1)} %get-tuple-element.175.qkv_ref, bf16[2048,280]{1,0:T(8,128)(2,1)} %copy-done.38, f32[4,280,512]{2,1,0:T(8,128)} %copy-done.40, ...), custom_call_target="tpu_custom_call" | custom-call | flops 56000000000 | bytes 4096 | tf_op jit(solution)/shard_map/attention_backward/pallas_call | solution.py:317
  584.7 3.1 collective-permute-done.32.received_ref
  589.3 10.7 %split_product.3 = (bf16[1024,1152]{1,0:T(8,128)(2,1)S(1)}, f32[1024,1120]{1,0:T(8,128)}) custom-call(bf16[2048,896]{1,0:T(8,128)(2,1)} %attention_backward.3.refs_0_, bf16[1120,840]{1,0:T(8,128)(2,1)S(1)} %copy-done.32, f32[2048,1120]{1,0:T(8,128)} %partial_product.1.refs_2_), custom_call_target="tpu_custom_call" | custom-call | flops 8999999488 | bytes 4096 | tf_op jit(solution)/shard_map/split_product/pallas_call | solution.py:735
  600.1 7.6 fusion.44
  611.4 2.5 fusion.32
  615.4 18.5 %collective-permute-done.35 = bf16[560,896]{1,0:T(8,128)(2,1)S(1)} collective-permute-done((bf16[560,896]{1,0:T(8,128)(2,1)S(1)}, bf16[560,896]{1,0:T(8,128)(2,1)S(1)}, u32[]{:S(2)}, u32[]{:S(2)}) %collective-permute-start.35) | collective-permute-done | bytes 1003552 | tf_op jit(solution)/shard_map/ppermute | solution.py:959
  637.2 20.7 %collective-permute-done.37 = bf16[420,1120]{1,0:T(8,128)(2,1)S(1)} collective-permute-done((bf16[420,1120]{1,0:T(8,128)(2,1)S(1)}, bf16[420,1120]{1,0:T(8,128)(2,1)S(1)}, u32[]{:S(2)}, u32[]{:S(2)}) %collective-permute-start.37) | collective-permute-done | bytes 940832 | tf_op jit(solution)/shard_map/ppermute | solution.py:959
  664.2 6.7 norm_back.3
  674.2 7.3 collective-permute-start.43
  681.5 3.3 place_rows.2
  684.8 26.6 %collective-permute-done.39 = bf16[560,896]{1,0:T(8,128)(2,1)} collective-permute-done((bf16[560,896]{1,0:T(8,128)(2,1)}, bf16[560,896]{1,0:T(8,128)(2,1)}, u32[]{:S(2)}, u32[]{:S(2)}) %collective-permute-start.39) | collective-permute-done | bytes 1003552 | tf_op jit(solution)/shard_map/ppermute | solution.py:959
  711.5 3.3 slice_add_fusion.1
  714.8 6.2 reshape.200.lead_ref
  720.9 3.2 place_rows.3
  724.2 2.7 convert_add_fusion.3
  726.9 4.3 reshape.203.rest_ref
  732.7 10.5 %new_moments.1 = (f32[1,1,470400]{2,1,0:T(1,128)}, f32[2,1,1,470400]{3,2,1,0:T(1,128)}, f32[1,1,470400]{2,1,0:T(1,128)S(1)}, f32[2]{0:T(128)S(1)}) custom-call(s32[2]{0:T(128)S(1)} %pad_add_fusion.ints_ref, f32[2]{0:T(128)S(1)} %pad_maximum_fusion.8.floats_ref, f32[1,1,470400]{2,1,0:T(1,128)S(1)} %copy-done.10, f32[1,1,470400]{2,1,0:T(1,128)S(1)} %reshape.203.rest_ref, ...), custom_call_target="tpu_custom_call" | custom-call | flops 10000000000 | bytes 4096 | tf_op jit(solution)/shard_map/new_moments/pallas_call | solution.py:433
  745.0 2.5 fusion.24
  749.2 4.1 collective-permute-done.45
  754.3 3.4 collective-permute-done.46
  759.6 2.5 collective-permute-done.47
  762.2 5.9 collective-permute-done.48
  773.7 6.5 new_weights.1
  (336 shorter events, 102.6 us)
Async XLA Ops:
  1.5 384.5 %copy-start.12 = (f32[12,1120]{1,0:T(8,128)}, f32[12,1120]{1,0:T(8,128)S(1)}, u32[]{:S(2)}) copy-start(f32[12,1120]{1,0:T(8,128)S(1)} %copy.52.small_ref) | copy-start | bytes 161284
  5.3 29.2 %collective-permute-start = (bf16[512,1152]{1,0:T(8,128)(2,1)}, bf16[512,1152]{1,0:T(8,128)(2,1)}, u32[]{:S(2)}, u32[]{:S(2)}) collective-permute-start(bf16[512,1152]{1,0:T(8,128)(2,1)} %get-tuple-element.164), channel_id=1, source_target_pairs={{0,2},{1,3},{2,0},{3,1},{4,6},{5,7},{6,4},{7,5},{8,10},{9,11},{10,... | collective-permute-start | bytes 3538952 | tf_op jit(solution)/shard_map/ppermute | solution.py:959
  11.9 29.1 %collective-permute-start.1 = (bf16[560,840]{1,0:T(8,128)(2,1)}, bf16[560,840]{1,0:T(8,128)(2,1)}, u32[]{:S(2)}, u32[]{:S(2)}) collective-permute-start(bf16[560,840]{1,0:T(8,128)(2,1)} %reshape.194), channel_id=1, source_target_pairs={{0,16},{4,20},{1,17},{5,21},{2,18},{6,22},{3,19},{7,23}} | collective-permute-start | bytes 2822408 | tf_op jit(solution)/shard_map/ppermute | solution.py:959
  40.9 29.8 %collective-permute-start.5 = (bf16[1024,1152]{1,0:T(8,128)(2,1)}, bf16[1024,1152]{1,0:T(8,128)(2,1)}, u32[]{:S(2)}, u32[]{:S(2)}) collective-permute-start(bf16[1024,1152]{1,0:T(8,128)(2,1)} %pad.16.own_ref), channel_id=1, source_target_pairs={{0,1},{1,0},{2,3},{3,2},{4,5},{5,4},{6,7},{7,6},{8,9},{9,8},{10,11... | collective-permute-start | bytes 7077896 | tf_op jit(solution)/shard_map/ppermute | solution.py:959
  42.1 27.3 %collective-permute-start.2 = (bf16[560,840]{1,0:T(8,128)(2,1)}, bf16[560,840]{1,0:T(8,128)(2,1)}, u32[]{:S(2)}, u32[]{:S(2)}) collective-permute-start(bf16[560,840]{1,0:T(8,128)(2,1)} %broadcast_select_fusion.4), channel_id=1, source_target_pairs={{0,8},{4,12},{16,24},{20,28},{1,9},{5,13},{17,25},{21,29},{2,10},{... | collective-permute-start | bytes 2822408 | tf_op jit(solution)/shard_map/ppermute | solution.py:959
  50.2 20.6 %collective-permute-start.3 = (bf16[420,1120]{1,0:T(8,128)(2,1)}, bf16[420,1120]{1,0:T(8,128)(2,1)}, u32[]{:S(2)}, u32[]{:S(2)}) collective-permute-start(bf16[420,1120]{1,0:T(8,128)(2,1)} %reshape.195.refs_0_), channel_id=1, source_target_pairs={{8,12},{9,13},{10,14},{11,15},{12,8},{13,9},{14,10},{15,11},{16,20... | collective-permute-start | bytes 2822408 | tf_op jit(solution)/shard_map/ppermute | solution.py:959
  51.8 19.0 %collective-permute-start.4 = (bf16[420,1120]{1,0:T(8,128)(2,1)}, bf16[420,1120]{1,0:T(8,128)(2,1)}, u32[]{:S(2)}, u32[]{:S(2)}) collective-permute-start(bf16[420,1120]{1,0:T(8,128)(2,1)} %reshape.195.refs_0_), channel_id=1, source_target_pairs={{8,10},{9,11},{10,8},{11,9},{12,14},{13,15},{14,12},{15,13},{16,18... | collective-permute-start | bytes 2822408 | tf_op jit(solution)/shard_map/ppermute | solution.py:959
  56.1 40.1 %copy-start.64 = (s32[4]{0:T(128)S(1)}, s32[4]{0:T(128)}, u32[]{:S(2)}) copy-start(s32[4]{0:T(128)} %constant.164.clone) | copy-start | bytes 52
  70.8 24.0 %collective-permute-start.6 = (bf16[560,840]{1,0:T(8,128)(2,1)S(1)}, bf16[560,840]{1,0:T(8,128)(2,1)}, u32[]{:S(2)}, u32[]{:S(2)}) collective-permute-start(bf16[560,840]{1,0:T(8,128)(2,1)S(1)} %broadcast_select_fusion.5.a0), channel_id=1, source_target_pairs={{0,4},{4,0},{8,12},{12,8},{16,20},{20,16},{24,28},{28,24},{1,5},{5... | collective-permute-start | bytes 2822408 | tf_op jit(solution)/shard_map/ppermute | solution.py:959
  72.9 132.7 %copy-start.25 = (s32[4]{0:T(128)}, s32[4]{0:T(128)S(1)}, u32[]{:S(2)}) copy-start(s32[4]{0:T(128)S(1)} %and_select_fusion.low_ref) | copy-start | bytes 52
  72.9 33.3 %collective-permute-start.7 = (bf16[560,840]{1,0:T(8,128)(2,1)S(1)}, bf16[560,840]{1,0:T(8,128)(2,1)}, u32[]{:S(2)}, u32[]{:S(2)}) collective-permute-start(bf16[560,840]{1,0:T(8,128)(2,1)S(1)} %broadcast_select_fusion.5.a0), channel_id=1, source_target_pairs={{0,2},{1,3},{2,0},{3,1},{4,6},{5,7},{6,4},{7,5},{8,10},{9,11},{10,... | collective-permute-start | bytes 2822408 | tf_op jit(solution)/shard_map/ppermute | solution.py:959
  74.4 52.1 %collective-permute-start.10 = (bf16[420,1120]{1,0:T(8,128)(2,1)}, bf16[420,1120]{1,0:T(8,128)(2,1)}, u32[]{:S(2)}, u32[]{:S(2)}) collective-permute-start(bf16[420,1120]{1,0:T(8,128)(2,1)} %reshape.195.refs_0_), channel_id=1, source_target_pairs={{8,24},{9,25},{10,26},{11,27},{12,28},{13,29},{14,30},{15,31},{16,... | collective-permute-start | bytes 2822408 | tf_op jit(solution)/shard_map/ppermute | solution.py:959
  75.7 52.1 %collective-permute-start.9 = (bf16[420,1120]{1,0:T(8,128)(2,1)}, bf16[420,1120]{1,0:T(8,128)(2,1)}, u32[]{:S(2)}, u32[]{:S(2)}) collective-permute-start(bf16[420,1120]{1,0:T(8,128)(2,1)} %reshape.195.refs_0_), channel_id=1, source_target_pairs={{8,0},{9,1},{10,2},{11,3},{12,4},{13,5},{14,6},{15,7},{16,24},{17,... | collective-permute-start | bytes 2822408 | tf_op jit(solution)/shard_map/ppermute | solution.py:959
  77.0 49.5 %collective-permute-start.11 = (bf16[420,1120]{1,0:T(8,128)(2,1)}, bf16[420,1120]{1,0:T(8,128)(2,1)}, u32[]{:S(2)}, u32[]{:S(2)}) collective-permute-start(bf16[420,1120]{1,0:T(8,128)(2,1)} %collective-permute-done.4.refs_0_), channel_id=1, source_target_pairs={{8,12},{9,13},{10,14},{11,15},{12,8},{13,9},{14,10},{15,11},{16,20... | collective-permute-start | bytes 2822408 | tf_op jit(solution)/shard_map/ppermute | solution.py:959
  94.8 33.1 %collective-permute-start.8 = (bf16[560,840]{1,0:T(8,128)(2,1)}, bf16[560,840]{1,0:T(8,128)(2,1)}, u32[]{:S(2)}, u32[]{:S(2)}) collective-permute-start(bf16[560,840]{1,0:T(8,128)(2,1)} %collective-permute-done.6.a1), channel_id=1, source_target_pairs={{0,2},{1,3},{2,0},{3,1},{4,6},{5,7},{6,4},{7,5},{8,10},{9,11},{10,... | collective-permute-start | bytes 2822408 | tf_op jit(solution)/shard_map/ppermute | solution.py:959
  99.9 105.6 %copy-start.14 = (s32[4,1,512]{2,1,0:T(1,128)}, s32[4,1,512]{2,1,0:T(1,128)S(1)}, u32[]{:S(2)}) copy-start(s32[4,1,512]{2,1,0:T(1,128)S(1)} %compare_select_fusion.start_ref) | copy-start | bytes 24580
  127.9 65.6 %collective-permute-start.12 = (bf16[420,1120]{1,0:T(8,128)(2,1)}, bf16[420,1120]{1,0:T(8,128)(2,1)}, u32[]{:S(2)}, u32[]{:S(2)}) collective-permute-start(bf16[420,1120]{1,0:T(8,128)(2,1)} %collective-permute-done.10.refs_4_), channel_id=1, source_target_pairs={{0,8},{1,9},{2,10},{3,11},{4,12},{5,13},{6,14},{7,15},{8,0},{9,1},... | collective-permute-start | bytes 2822408 | tf_op jit(solution)/shard_map/ppermute | solution.py:959
  129.8 63.7 %collective-permute-start.14 = (bf16[420,1120]{1,0:T(8,128)(2,1)}, bf16[420,1120]{1,0:T(8,128)(2,1)}, u32[]{:S(2)}, u32[]{:S(2)}) collective-permute-start(bf16[420,1120]{1,0:T(8,128)(2,1)} %collective-permute-done.10.refs_4_), channel_id=1, source_target_pairs={{0,4},{1,5},{2,6},{3,7},{4,0},{5,1},{6,2},{7,3},{8,12},{9,13},{10,... | collective-permute-start | bytes 2822408 | tf_op jit(solution)/shard_map/ppermute | solution.py:959
  133.2 60.2 %collective-permute-start.13 = (bf16[420,1120]{1,0:T(8,128)(2,1)}, bf16[420,1120]{1,0:T(8,128)(2,1)S(1)}, u32[]{:S(2)}, u32[]{:S(2)}) collective-permute-start(bf16[420,1120]{1,0:T(8,128)(2,1)} %collective-permute-done.9.refs_2_), channel_id=1, source_target_pairs={{0,4},{1,5},{2,6},{3,7},{4,0},{5,1},{6,2},{7,3},{16,20},{17,21},{1... | collective-permute-start | bytes 2822408 | tf_op jit(solution)/shard_map/ppermute | solution.py:959
  135.6 57.8 %collective-permute-start.15 = (bf16[420,1120]{1,0:T(8,128)(2,1)}, bf16[420,1120]{1,0:T(8,128)(2,1)S(1)}, u32[]{:S(2)}, u32[]{:S(2)}) collective-permute-start(bf16[420,1120]{1,0:T(8,128)(2,1)} %collective-permute-done.9.refs_2_), channel_id=1, source_target_pairs={{0,2},{1,3},{2,0},{3,1},{4,6},{5,7},{6,4},{7,5},{16,18},{17,19},{1... | collective-permute-start | bytes 2822408 | tf_op jit(solution)/shard_map/ppermute | solution.py:959
  138.1 55.4 %collective-permute-start.16 = (bf16[420,1120]{1,0:T(8,128)(2,1)}, bf16[420,1120]{1,0:T(8,128)(2,1)S(1)}, u32[]{:S(2)}, u32[]{:S(2)}) collective-permute-start(bf16[420,1120]{1,0:T(8,128)(2,1)} %collective-permute-done.10.refs_4_), channel_id=1, source_target_pairs={{0,2},{1,3},{2,0},{3,1},{4,6},{5,7},{6,4},{7,5},{8,10},{9,11},{10,... | collective-permute-start | bytes 2822408 | tf_op jit(solution)/shard_map/ppermute | solution.py:959
  158.1 35.3 %copy-start.31 = (bf16[1120,840]{1,0:T(8,128)(2,1)}, bf16[1120,840]{1,0:T(8,128)(2,1)S(1)}, u32[]{:S(2)}) copy-start(bf16[1120,840]{1,0:T(8,128)(2,1)S(1)} %get-tuple-element.266.refs_1_) | copy-start | bytes 5644804
  158.1 47.3 %copy-start.22 = (bf16[512,1152]{1,0:T(8,128)(2,1)S(1)}, bf16[512,1152]{1,0:T(8,128)(2,1)}, u32[]{:S(2)}) copy-start(bf16[512,1152]{1,0:T(8,128)(2,1)} %copy-done.21) | copy-start | bytes 3538948
  193.4 46.9 %copy-start.40 = (f32[4,280,512]{2,1,0:T(8,128)}, f32[4,280,512]{2,1,0:T(8,128)S(1)}, u32[]{:S(2)}) copy-start(f32[4,280,512]{2,1,0:T(8,128)S(1)} %get-tuple-element.263.outt_ref) | copy-start | bytes 6881284
  193.4 46.8 %copy-start.42 = (f32[4,8,512]{2,1,0:T(8,128)}, f32[4,8,512]{2,1,0:T(8,128)S(1)}, u32[]{:S(2)}) copy-start(f32[4,8,512]{2,1,0:T(8,128)S(1)} %get-tuple-element.180.lse_ref) | copy-start | bytes 196612
  193.5 49.9 %collective-permute-start.18 = (bf16[420,1120]{1,0:T(8,128)(2,1)}, bf16[420,1120]{1,0:T(8,128)(2,1)}, u32[]{:S(2)}, u32[]{:S(2)}) collective-permute-start(bf16[420,1120]{1,0:T(8,128)(2,1)} %collective-permute-done.12.refs_6_), channel_id=1, source_target_pairs={{0,4},{1,5},{2,6},{3,7},{4,0},{5,1},{6,2},{7,3},{8,12},{9,13},{10,... | collective-permute-start | bytes 2822408 | tf_op jit(solution)/shard_map/ppermute | solution.py:959
  195.4 48.0 %collective-permute-start.19 = (bf16[420,1120]{1,0:T(8,128)(2,1)}, bf16[420,1120]{1,0:T(8,128)(2,1)}, u32[]{:S(2)}, u32[]{:S(2)}) collective-permute-start(bf16[420,1120]{1,0:T(8,128)(2,1)} %collective-permute-done.12.refs_6_), channel_id=1, source_target_pairs={{0,2},{1,3},{2,0},{3,1},{4,6},{5,7},{6,4},{7,5},{8,10},{9,11},{10,... | collective-permute-start | bytes 2822408 | tf_op jit(solution)/shard_map/ppermute | solution.py:959
  197.4 46.1 %collective-permute-start.20 = (bf16[420,1120]{1,0:T(8,128)(2,1)S(1)}, bf16[420,1120]{1,0:T(8,128)(2,1)S(1)}, u32[]{:S(2)}, u32[]{:S(2)}) collective-permute-start(bf16[420,1120]{1,0:T(8,128)(2,1)S(1)} %collective-permute-done.15.refs_2_), channel_id=1, source_target_pairs={{0,4},{1,5},{2,6},{3,7},{4,0},{5,1},{6,2},{7,3},{16,20},{17,21},{1... | collective-permute-start | bytes 2822408 | tf_op jit(solution)/shard_map/ppermute | solution.py:959
  201.3 43.2 %collective-permute-start.21 = (bf16[420,1120]{1,0:T(8,128)(2,1)}, bf16[420,1120]{1,0:T(8,128)(2,1)S(1)}, u32[]{:S(2)}, u32[]{:S(2)}) collective-permute-start(bf16[420,1120]{1,0:T(8,128)(2,1)} %collective-permute-done.14.refs_5_), channel_id=1, source_target_pairs={{0,2},{1,3},{2,0},{3,1},{4,6},{5,7},{6,4},{7,5},{8,10},{9,11},{10,... | collective-permute-start | bytes 2822408 | tf_op jit(solution)/shard_map/ppermute | solution.py:959
  205.4 59.4 %collective-permute-start.17 = (bf16[512,1152]{1,0:T(8,128)(2,1)S(1)}, bf16[512,1152]{1,0:T(8,128)(2,1)}, u32[]{:S(2)}, u32[]{:S(2)}) collective-permute-start(bf16[512,1152]{1,0:T(8,128)(2,1)S(1)} %copy-done.22), channel_id=1, source_target_pairs={{0,2},{1,3},{2,0},{3,1},{4,6},{5,7},{6,4},{7,5},{8,10},{9,11},{10,... | collective-permute-start | bytes 3538952 | tf_op jit(solution)/shard_map/ppermute | solution.py:959
  245.4 22.0 %collective-permute-start.22 = (bf16[420,1120]{1,0:T(8,128)(2,1)}, bf16[420,1120]{1,0:T(8,128)(2,1)S(1)}, u32[]{:S(2)}, u32[]{:S(2)}) collective-permute-start(bf16[420,1120]{1,0:T(8,128)(2,1)} %collective-permute-done.19.refs_6_), channel_id=1, source_target_pairs={{0,4},{1,5},{2,6},{3,7},{4,0},{5,1},{6,2},{7,3},{8,12},{9,13},{10,... | collective-permute-start | bytes 2822408 | tf_op jit(solution)/shard_map/ppermute | solution.py:959
  282.4 5.2 collective-permute-start.23
  282.6 10.5 %collective-permute-start.25 = (bf16[1024,1152]{1,0:T(8,128)(2,1)S(1)}, bf16[1024,1152]{1,0:T(8,128)(2,1)S(1)}, u32[]{:S(2)}, u32[]{:S(2)}) collective-permute-start(bf16[1024,1152]{1,0:T(8,128)(2,1)S(1)} %pad_maximum_fusion.1.cot_ref.base_ref), channel_id=1, source_target_pairs={{0,1},{1,0},{2,3},{3,2},{4,5},{5,4},{6,7},{7,6},{8,9},{9,8},{10,11... | collective-permute-start | bytes 7077896 | tf_op jit(solution)/shard_map/ppermute | solution.py:959
  292.1 4.5 collective-permute-start.24
  329.9 32.4 %collective-permute-start.26 = (f32[1024,1152]{1,0:T(8,128)}, f32[1024,1152]{1,0:T(8,128)}, u32[]{:S(2)}, u32[]{:S(2)}) collective-permute-start(f32[1024,1152]{1,0:T(8,128)} %get-tuple-element.228), channel_id=1, source_target_pairs={{0,1},{1,0},{2,3},{3,2},{4,5},{5,4},{6,7},{7,6},{8,9},{9,8},{10,11... | collective-permute-start | bytes 14155784 | tf_op jit(solution)/shard_map/ppermute | solution.py:959
  330.1 32.2 %copy-start.7 = (bf16[1024,1152]{1,0:T(8,128)(2,1)S(1)}, bf16[1024,1152]{1,0:T(8,128)(2,1)}, u32[]{:S(2)}) copy-start(bf16[1024,1152]{1,0:T(8,128)(2,1)} %copy-done.6) | copy-start | bytes 7077892
  385.6 6.2 collective-permute-start.27
  391.1 117.7 %collective-permute-start.29 = (f32[1024,1152]{1,0:T(8,128)}, f32[1024,1152]{1,0:T(8,128)}, u32[]{:S(2)}, u32[]{:S(2)}) collective-permute-start(f32[1024,1152]{1,0:T(8,128)} %get-tuple-element.250), channel_id=1, source_target_pairs={{0,1},{1,0},{2,3},{3,2},{4,5},{5,4},{6,7},{7,6},{8,9},{9,8},{10,11... | collective-permute-start | bytes 14155784 | tf_op jit(solution)/shard_map/ppermute | solution.py:959
  391.7 122.3 %collective-permute-start.31 = (bf16[1120,1120]{1,0:T(8,128)(2,1)}, bf16[1120,1120]{1,0:T(8,128)(2,1)}, u32[]{:S(2)}, u32[]{:S(2)}) collective-permute-start(bf16[1120,1120]{1,0:T(8,128)(2,1)} %convolution_convert_fusion.1), channel_id=1, source_target_pairs={{0,2},{1,3},{2,0},{3,1},{4,6},{5,7},{6,4},{7,5},{8,10},{9,11},{10,... | collective-permute-start | bytes 7526408 | tf_op jit(solution)/shard_map/ppermute | solution.py:959
  436.9 63.8 %collective-permute-start.28 = (bf16[280,1120]{1,0:T(8,128)(2,1)S(1)}, bf16[280,1120]{1,0:T(8,128)(2,1)S(1)}, u32[]{:S(2)}, u32[]{:S(2)}) collective-permute-start(bf16[280,1120]{1,0:T(8,128)(2,1)S(1)} %convolution_convert_fusion.3), channel_id=1, source_target_pairs={{0,2},{1,3},{2,0},{3,1},{4,6},{5,7},{6,4},{7,5},{8,10},{9,11},{10,... | collective-permute-start | bytes 1881608 | tf_op jit(solution)/shard_map/ppermute | solution.py:959
  439.0 81.1 %collective-permute-start.30 = (bf16[1120,1120]{1,0:T(8,128)(2,1)}, bf16[1120,1120]{1,0:T(8,128)(2,1)}, u32[]{:S(2)}, u32[]{:S(2)}) collective-permute-start(bf16[1120,1120]{1,0:T(8,128)(2,1)} %convolution_convert_fusion), channel_id=1, source_target_pairs={{0,2},{1,3},{2,0},{3,1},{4,6},{5,7},{6,4},{7,5},{8,10},{9,11},{10,... | collective-permute-start | bytes 7526408 | tf_op jit(solution)/shard_map/ppermute | solution.py:959
  513.9 93.7 %collective-permute-start.33 = (bf16[1120,896]{1,0:T(8,128)(2,1)}, bf16[1120,896]{1,0:T(8,128)(2,1)}, u32[]{:S(2)}, u32[]{:S(2)}) collective-permute-start(bf16[1120,896]{1,0:T(8,128)(2,1)} %convolution_convert_fusion.2), channel_id=1, source_target_pairs={{0,2},{1,3},{2,0},{3,1},{4,6},{5,7},{6,4},{7,5},{8,10},{9,11},{10,... | collective-permute-start | bytes 6021128 | tf_op jit(solution)/shard_map/ppermute | solution.py:959
  531.5 56.2 %collective-permute-start.32 = (bf16[512,1152]{1,0:T(8,128)(2,1)}, bf16[512,1152]{1,0:T(8,128)(2,1)}, u32[]{:S(2)}, u32[]{:S(2)}) collective-permute-start(bf16[512,1152]{1,0:T(8,128)(2,1)} %slice_select_fusion.2), channel_id=1, source_target_pairs={{0,2},{1,3},{2,0},{3,1},{4,6},{5,7},{6,4},{7,5},{8,10},{9,11},{10,... | collective-permute-start | bytes 3538952 | tf_op jit(solution)/shard_map/ppermute | solution.py:959
  531.6 79.8 %collective-permute-start.34 = (bf16[3,420,1120]{2,1,0:T(8,128)(2,1)}, bf16[3,420,1120]{2,1,0:T(8,128)(2,1)}, u32[]{:S(2)}, u32[]{:S(2)}) collective-permute-start(bf16[3,420,1120]{2,1,0:T(8,128)(2,1)} %get-tuple-element.273), channel_id=1, source_target_pairs={{0,4},{4,0},{8,12},{12,8},{16,20},{20,16},{24,28},{28,24},{1,5},{5... | collective-permute-start | bytes 8467208 | tf_op jit(solution)/shard_map/ppermute | solution.py:959
  610.2 23.7 %collective-permute-start.35 = (bf16[560,896]{1,0:T(8,128)(2,1)S(1)}, bf16[560,896]{1,0:T(8,128)(2,1)S(1)}, u32[]{:S(2)}, u32[]{:S(2)}) collective-permute-start(bf16[560,896]{1,0:T(8,128)(2,1)S(1)} %select_convert_fusion), channel_id=1, source_target_pairs={{0,4},{4,0},{8,12},{12,8},{16,20},{20,16},{24,28},{28,24},{1,5},{5... | collective-permute-start | bytes 3010568 | tf_op jit(solution)/shard_map/ppermute | solution.py:959
  611.4 52.8 %collective-permute-start.41 = (bf16[1024,1152]{1,0:T(8,128)(2,1)S(1)}, bf16[1024,1152]{1,0:T(8,128)(2,1)S(1)}, u32[]{:S(2)}, u32[]{:S(2)}) collective-permute-start(bf16[1024,1152]{1,0:T(8,128)(2,1)S(1)} %get-tuple-element.295), channel_id=1, source_target_pairs={{0,1},{1,0},{2,3},{3,2},{4,5},{5,4},{6,7},{7,6},{8,9},{9,8},{10,11... | collective-permute-start | bytes 7077896 | tf_op jit(solution)/shard_map/ppermute | solution.py:959
  613.9 23.3 %collective-permute-start.36 = (bf16[420,1120]{1,0:T(8,128)(2,1)S(1)}, bf16[420,1120]{1,0:T(8,128)(2,1)S(1)}, u32[]{:S(2)}, u32[]{:S(2)}) collective-permute-start(bf16[420,1120]{1,0:T(8,128)(2,1)S(1)} %get-tuple-element.278), channel_id=1, source_target_pairs={{0,8},{4,12},{16,24},{20,28},{1,9},{5,13},{17,25},{21,29},{2,10},{... | collective-permute-start | bytes 2822408 | tf_op jit(solution)/shard_map/ppermute | solution.py:959
  615.3 42.7 %collective-permute-start.37 = (bf16[420,1120]{1,0:T(8,128)(2,1)S(1)}, bf16[420,1120]{1,0:T(8,128)(2,1)S(1)}, u32[]{:S(2)}, u32[]{:S(2)}) collective-permute-start(bf16[420,1120]{1,0:T(8,128)(2,1)S(1)} %get-tuple-element.280), channel_id=1, source_target_pairs={{0,8},{4,12},{8,0},{12,4},{16,24},{20,28},{24,16},{28,20},{1,9},{5... | collective-permute-start | bytes 2822408 | tf_op jit(solution)/shard_map/ppermute | solution.py:959
  634.2 26.7 %collective-permute-start.38 = (bf16[560,896]{1,0:T(8,128)(2,1)S(1)}, bf16[560,896]{1,0:T(8,128)(2,1)S(1)}, u32[]{:S(2)}, u32[]{:S(2)}) collective-permute-start(bf16[560,896]{1,0:T(8,128)(2,1)S(1)} %get-tuple-element.284), channel_id=1, source_target_pairs={{8,0},{12,4},{24,16},{28,20},{9,1},{13,5},{25,17},{29,21},{10,2},{... | collective-permute-start | bytes 3010568 | tf_op jit(solution)/shard_map/ppermute | solution.py:959
  635.5 28.7 %slice-start.2 = ((s8[4718592]{0:T(1024)(128)(4,1)}), s8[4194304]{0:T(1024)(128)(4,1)S(1)}, s32[]{:S(2)}) async-start(s8[4718592]{0:T(1024)(128)(4,1)} %bitcast.62), calls=%async_computation.2 | async-start | bytes 8388608
  636.1 28.1 %slice-start.3 = ((s8[4718592]{0:T(1024)(128)(4,1)}), s8[524288]{0:T(1024)(128)(4,1)S(1)}, s32[]{:S(2)}) async-start(s8[4718592]{0:T(1024)(128)(4,1)} %bitcast.62), calls=%async_computation.3 | async-start | bytes 1048576
  662.8 1.4 collective-permute-start.40
  662.8 48.6 %collective-permute-start.39 = (bf16[560,896]{1,0:T(8,128)(2,1)}, bf16[560,896]{1,0:T(8,128)(2,1)}, u32[]{:S(2)}, u32[]{:S(2)}) collective-permute-start(bf16[560,896]{1,0:T(8,128)(2,1)} %get-tuple-element.289), channel_id=1, source_target_pairs={{16,0},{20,4},{17,1},{21,5},{18,2},{22,6},{19,3},{23,7}} | collective-permute-start | bytes 3010568 | tf_op jit(solution)/shard_map/ppermute | solution.py:959
  672.2 48.7 %collective-permute-start.42 = (bf16[512,1152]{1,0:T(8,128)(2,1)}, bf16[512,1152]{1,0:T(8,128)(2,1)}, u32[]{:S(2)}, u32[]{:S(2)}) collective-permute-start(bf16[512,1152]{1,0:T(8,128)(2,1)} %slice_select_fusion.1), channel_id=1, source_target_pairs={{0,2},{1,3},{2,0},{3,1},{4,6},{5,7},{6,4},{7,5},{8,10},{9,11},{10,... | collective-permute-start | bytes 3538952 | tf_op jit(solution)/shard_map/ppermute | solution.py:959
  674.2 50.0 %collective-permute-start.43 = (bf16[420,1120]{1,0:T(8,128)(2,1)S(1)}, bf16[420,1120]{1,0:T(8,128)(2,1)}, u32[]{:S(2)}, u32[]{:S(2)}) collective-permute-start(bf16[420,1120]{1,0:T(8,128)(2,1)S(1)} %copy-done.53), channel_id=1, source_target_pairs={{24,8},{28,12},{0,16},{4,20},{8,24},{12,28},{25,9},{29,13},{1,17},... | collective-permute-start | bytes 2822408 | tf_op jit(solution)/shard_map/ppermute | solution.py:959
  732.7 29.5 %copy-start.13 = (f32[12,1120]{1,0:T(8,128)S(1)}, f32[12,1120]{1,0:T(8,128)}, u32[]{:S(2)}) copy-start(f32[12,1120]{1,0:T(8,128)} %copy-done.12) | copy-start | bytes 161284
  732.7 35.5 %copy-start.54 = (f32[12,1120]{1,0:T(8,128)S(1)}, f32[12,1120]{1,0:T(8,128)}, u32[]{:S(2)}) copy-start(f32[12,1120]{1,0:T(8,128)} %param.21) | copy-start | bytes 161284
  732.7 35.5 %copy-start.55 = (f32[12,1120]{1,0:T(8,128)S(1)}, f32[12,1120]{1,0:T(8,128)}, u32[]{:S(2)}) copy-start(f32[12,1120]{1,0:T(8,128)} %param.22) | copy-start | bytes 161284
  744.4 27.7 %copy-start.20 = (f32[1,1,470400]{2,1,0:T(1,128)S(1)}, f32[1,1,470400]{2,1,0:T(1,128)}, u32[]{:S(2)}) copy-start(f32[1,1,470400]{2,1,0:T(1,128)} %weight_ref.7) | copy-start | bytes 5644804
  747.5 1.3 collective-permute-start.44
  748.8 4.4 collective-permute-start.45
  753.3 4.4 collective-permute-start.46
  757.7 4.4 collective-permute-start.47
  762.1 6.0 collective-permute-start.48
  (70 other events, 477.1 us)

commit v10 on v9

--- a/solution.py
+++ b/solution.py
@@ -1359,8 +1359,8 @@
 
     if planar:
         lead_grad = (held_lead + far_lead.astype(F32))[:, :triple].reshape(1, 1, shard_len)
-        own_rest, lead_grad, result_all, grad_all, small_now = tie(
-            own_rest, lead_grad, result_all, grad_all, small_now
+        own_rest, lead_grad, result_all, small_now = tie(
+            own_rest, lead_grad, result_all, small_now
         )
         rest_grad = (own_rest + got_far.astype(F32)).reshape(1, 1, shard_len)
         leads = z_here == 0

time: 789 us -> 787 us (level)
    unnamed x173 -> x177, local copies, waits for them, and re-layouts: 26.1 us -> 30 us
  transfers between devices with their start and end apart: 49 -> 49, of which waited for: 21 -> 21; matrix products, arithmetic and copies ran while one was open for 14% -> 15% of each run, Pallas kernels for 37% -> 38%
where the time goes in v10:
time: 787 us; the launch traced here: 778 us
  Pallas kernels  360 us (46%)
  waiting for transfers between devices  176 us (22%)
  starting transfers between devices  73.7 us (9%)
  matrix products  66.9 us (9%)
  local copies, waits for them, and re-layouts  52.8 us (7%)
  other arithmetic  41.4 us (5%)
    ppermute x49, waiting for transfers between devices, permute(): return lax.ppermute(value, axis_name, pairs)  176 us
    pallas_call x2, Pallas kernels, attention_backward(): pl.pallas_call(functools.partial(attention_backward_body, heads, width, b...  104 us
    ppermute x49, starting transfers between devices, permute(): return lax.ppermute(value, axis_name, pairs)  73.7 us
    pallas_call x2, Pallas kernels, attention_forward(): pl.pallas_call(functools.partial(attention_forward_body, heads, width, bq...  70 us
    dot_general x8, matrix products, dot_columns(): lax.dot_general(left, right, (((0,), (0,)), ((), ())), preferred_element_...  66.9 us
    pallas_call x2, Pallas kernels, feed_forward(): pl.pallas_call(functools.partial(feed_forward_body, len(filled)), out_sha...  64 us
    unnamed x177, local copies, waits for them, and re-layouts  30 us
    pallas_call x2, Pallas kernels, split_product(): pl.pallas_call(functools.partial(split_product_body, steps, turned, len(l...  19.9 us
  transfers between devices with their start and end apart: 49, of which 21 were waited for; matrix products, arithmetic and copies ran while one was open for 15% of the time, Pallas kernels for 38%

profile of v10, /device:TPU:0, one launch (start us, length us, event | category | flops | bytes accessed | tf_op | source)
XLA Modules:
  0.0 778.3 jit_solution(8881050617091509437)
XLA Ops:
  5.3 2.9 collective-permute-start
  9.1 2.8 reshape.194
  11.9 5.4 collective-permute-start.1
  17.9 16.6 %collective-permute-done = bf16[512,1152]{1,0:T(8,128)(2,1)} collective-permute-done((bf16[512,1152]{1,0:T(8,128)(2,1)}, bf16[512,1152]{1,0:T(8,128)(2,1)}, u32[]{:S(2)}, u32[]{:S(2)}) %collective-permute-start) | collective-permute-done | bytes 1179680 | tf_op jit(solution)/shard_map/ppermute | solution.py:959
  42.1 5.9 collective-permute-start.2
  56.2 13.3 %collective-permute-done.2 = bf16[560,840]{1,0:T(8,128)(2,1)} collective-permute-done((bf16[560,840]{1,0:T(8,128)(2,1)}, bf16[560,840]{1,0:T(8,128)(2,1)}, u32[]{:S(2)}, u32[]{:S(2)}) %collective-permute-start.2) | collective-permute-done | bytes 940832 | tf_op jit(solution)/shard_map/ppermute | solution.py:959
  78.8 16.0 %collective-permute-done.6.a1 = bf16[560,840]{1,0:T(8,128)(2,1)} collective-permute-done((bf16[560,840]{1,0:T(8,128)(2,1)S(1)}, bf16[560,840]{1,0:T(8,128)(2,1)}, u32[]{:S(2)}, u32[]{:S(2)}) %collective-permute-start.6) | collective-permute-done | bytes 940832 | tf_op jit(solution)/shard_map/ppermute | solution.py:959
  101.4 4.7 square_sums.1
  106.1 20.4 %collective-permute-done.10.refs_4_ = bf16[420,1120]{1,0:T(8,128)(2,1)} collective-permute-done((bf16[420,1120]{1,0:T(8,128)(2,1)}, bf16[420,1120]{1,0:T(8,128)(2,1)}, u32[]{:S(2)}, u32[]{:S(2)}) %collective-permute-start.10) | collective-permute-done | bytes 940832 | tf_op jit(solution)/shard_map/ppermute | solution.py:959
  129.8 3.4 collective-permute-start.14
  133.2 2.4 collective-permute-start.13
  135.6 2.4 collective-permute-start.15
  138.1 3.4 collective-permute-start.16
  141.5 16.6 %project.1 = (bf16[2048,840]{1,0:T(8,128)(2,1)}, bf16[2048,840]{1,0:T(8,128)(2,1)}, bf16[2048,1120]{1,0:T(8,128)(2,1)}, bf16[1120,840]{1,0:T(8,128)(2,1)S(1)}, bf16[1120,840]{1,0:T(8,128)(2,1)}) custom-call(s32[1]{0:T(128)} %bitcast.place_ref, bf16[1024,1152]{1,0:T(8,128)(2,1)} %pad.16.own_ref, bf16[1024,1152]{1,0:T(8,128)(2,1)} %collective-permute-done.5.other_ref, ...), custom_call_target="tpu_custom_call" | custom-call | flops 16000000000 | bytes 4096 | tf_op jit(solution)/shard_map/project/pallas_call | solution.py:628
  158.1 35.3 %attention_forward.2 = (bf16[2048,280]{1,0:T(8,128)(2,1)S(1)}, f32[4,280,512]{2,1,0:T(8,128)S(1)}, f32[4,8,512]{2,1,0:T(8,128)S(1)}) custom-call(s32[4]{0:T(128)S(1)} %and_select_fusion.low_ref, s32[1]{0:T(128)} %bitcast.8.core_ref, s32[4,1,512]{2,1,0:T(1,128)S(1)} %compare_select_fusion.start_ref, bf16[2048,840]{1,0:T(8,128)(2,1)} %get-tuple-element.174.qkv_ref), custom_call_target="tpu_custom_call" | custom-call | flops 35000000512 | bytes 4096 | tf_op jit(solution)/shard_map/attention_forward/pallas_call | solution.py:274
  197.4 3.9 collective-permute-start.20
  201.3 4.1 collective-permute-start.21
  205.5 34.7 %attention_forward.3 = (bf16[2048,280]{1,0:T(8,128)(2,1)S(1)}, f32[4,280,512]{2,1,0:T(8,128)S(1)}, f32[4,8,512]{2,1,0:T(8,128)S(1)}) custom-call(s32[4]{0:T(128)S(1)} %and_select_fusion.low_ref, s32[1]{0:T(128)} %bitcast.8.core_ref, s32[4,1,512]{2,1,0:T(1,128)S(1)} %compare_select_fusion.start_ref, bf16[2048,840]{1,0:T(8,128)(2,1)} %get-tuple-element.180.qkv_ref), custom_call_target="tpu_custom_call" | custom-call | flops 35000000512 | bytes 4096 | tf_op jit(solution)/shard_map/attention_forward/pallas_call | solution.py:274
  245.4 2.5 collective-permute-start.22
  247.9 5.7 unpack_share.2
  253.6 11.2 %collective-permute-done.17 = bf16[512,1152]{1,0:T(8,128)(2,1)} collective-permute-done((bf16[512,1152]{1,0:T(8,128)(2,1)S(1)}, bf16[512,1152]{1,0:T(8,128)(2,1)}, u32[]{:S(2)}, u32[]{:S(2)}) %collective-permute-start.17) | collective-permute-done | bytes 1179680 | tf_op jit(solution)/shard_map/ppermute | solution.py:959
  268.4 5.5 unpack_share.3
  274.0 8.4 %split_product.2 = (bf16[1024,1152]{1,0:T(8,128)(2,1)}, f32[1024,1120]{1,0:T(8,128)}) custom-call(bf16[2048,280]{1,0:T(8,128)(2,1)S(1)} %get-tuple-element.181.refs_0_, bf16[2048,280]{1,0:T(8,128)(2,1)S(1)} %copy-done.28, bf16[280,1120]{1,0:T(8,128)(2,1)S(1)} %get-tuple-element.199.refs_2_.w_a, bf16[280,1120]{1,0:T(8,128)(2,1)S(1)} %get-tuple-element.209.refs_3_.w_b), custom_call_target="tpu_custom_call" | custom-call | flops 8999999488 | bytes 4096 | tf_op jit(solution)/shard_map/split_product/pallas_call | solution.py:735
  283.2 4.3 collective-permute-done.23.got_ref
  287.5 2.4 middle_norm.1
  293.5 3.1 collective-permute-done.24.rows_ref
  298.0 31.8 %feed_forward.2 = (bf16[2048,1120]{1,0:T(8,128)(2,1)}, bf16[2048,1120]{1,0:T(8,128)(2,1)}, bf16[2048,1120]{1,0:T(8,128)(2,1)}, bf16[2048,1120]{1,0:T(8,128)(2,1)...) custom-call(bf16[1024,1152]{1,0:T(8,128)(2,1)} %copy-done.72, ...), custom_call_target="tpu_custom_call" | custom-call | flops 33999998976 | bytes 4096 | tf_op jit(solution)/shard_map/feed_forward/pallas_call | solution.py:936
  330.0 32.3 %feed_forward.3 = (bf16[2048,1120]{1,0:T(8,128)(2,1)}, bf16[2048,1120]{1,0:T(8,128)(2,1)}, bf16[2048,1120]{1,0:T(8,128)(2,1)}, bf16[2048,1120]{1,0:T(8,128)(2,1)...) custom-call(bf16[1024,1152]{1,0:T(8,128)(2,1)} %copy-done.14, ...), custom_call_target="tpu_custom_call", output_to_operand_aliasing={{0}: (5, {}), {1}: (6, {}), {2}: (7, {}), {3}: (8, {}), {4}... | custom-call | flops 33999998976 | bytes 4096 | tf_op jit(solution)/shard_map/feed_forward/pallas_call | solution.py:936
  362.3 2.3 copy-done.1
  364.6 7.8 %norm_back.2 = (f32[1024,1120]{1,0:T(8,128)S(1)}, bf16[1024,1152]{1,0:T(8,128)(2,1)}, f32[8,1120]{1,0:T(8,128)S(1)}) custom-call(f32[1024,1120]{1,0:T(8,128)S(1)} %copy-done.1, f32[1024,1152]{1,0:T(8,128)} %get-tuple-element.226.kept_ref, f32[1024,1152]{1,0:T(8,128)} %collective-permute-done.26.got_ref, bf16[1024,1152]{1,0:T(8,128)(2,1)S(1)} %copy-done.6, ...), custom_call_target="tpu_custom_call" | custom-call | flops 7000000000 | bytes 4096 | tf_op jit(solution)/shard_map/norm_back/pallas_call | solution.py:877
  372.4 13.2 %convolution_convert_fusion.1 = bf16[1120,1120]{1,0:T(8,128)(2,1)} fusion(bf16[2048,1120]{1,0:T(8,128)(2,1)} %get-tuple-element.224, bf16[2048,1120]{1,0:T(8,128)(2,1)} %get-tuple-element.238), kind=kOutput, calls=%fused_computation.1 | convolution fusion | flops 5139276800 | bytes 11683840 | tf_op jit(solution)/shard_map/dot_general | solution.py:39
  388.0 3.0 fusion.23
  392.4 11.5 %convolution_convert_fusion = bf16[1120,1120]{1,0:T(8,128)(2,1)} fusion(bf16[2048,1120]{1,0:T(8,128)(2,1)} %get-tuple-element.239, bf16[2048,1120]{1,0:T(8,128)(2,1)} %get-tuple-element.234), kind=kOutput, calls=%fused_computation | convolution fusion | flops 5139276800 | bytes 11683840 | tf_op jit(solution)/shard_map/dot_general | solution.py:39
  403.9 8.2 %out_grads.1 = (bf16[2048,280]{1,0:T(8,128)(2,1)S(1)}, bf16[2048,280]{1,0:T(8,128)(2,1)S(1)}, bf16[2048,1120]{1,0:T(8,128)(2,1)}) custom-call(bf16[1024,1152]{1,0:T(8,128)(2,1)} %get-tuple-element.235.own_ref, bf16[1024,1152]{1,0:T(8,128)(2,1)} %collective-permute-done.27.other_ref, bf16[280,1120]{1,0:T(8,128)(2,1)S(1)} %copy-done.41, ...), custom_call_target="tpu_custom_call" | custom-call | flops 8000000000 | bytes 4096 | tf_op jit(solution)/shard_map/out_grads/pallas_call | solution.py:661
  412.2 6.0 convolution_convert_fusion.3
  420.1 8.4 %fusion.42.in_ref = f32[1120,1120]{1,0:T(8,128)} fusion(bf16[2048,1120]{1,0:T(8,128)(2,1)S(1)} %bitcast.74, bf16[2048,1120]{1,0:T(8,128)(2,1)S(1)} %bitcast.72), kind=kOutput, calls=%fused_computation.127 | convolution fusion | flops 5138022400 | bytes 14192640 | tf_op jit(solution)/shard_map/dot_general | solution.py:39
  428.5 8.7 %fusion.41.back_ref = f32[1120,1120]{1,0:T(8,128)} fusion(bf16[2048,1120]{1,0:T(8,128)(2,1)S(1)} %bitcast.70, bf16[2048,1120]{1,0:T(8,128)(2,1)S(1)} %bitcast.76), kind=kOutput, calls=%fused_computation.126 | convolution fusion | flops 5138022400 | bytes 14192640 | tf_op jit(solution)/shard_map/dot_general | solution.py:39
  439.3 51.9 %attention_backward.2.left = bf16[2048,896]{1,0:T(8,128)(2,1)} custom-call(s32[4]{0:T(128)} %copy-done.26, s32[1]{0:T(128)} %bitcast.8.core_ref, s32[4,1,512]{2,1,0:T(1,128)} %copy-done.13, bf16[2048,840]{1,0:T(8,128)(2,1)} %get-tuple-element.180.qkv_ref, bf16[2048,280]{1,0:T(8,128)(2,1)} %copy-done.43, f32[4,280,512]{2,1,0:T(8,128)} %copy-done.45, ...), custom_call_target="tpu_custom_call" | custom-call | flops 56000000000 | bytes 4096 | tf_op jit(solution)/shard_map/attention_backward/pallas_call | solution.py:317
  491.2 9.9 %convolution_convert_fusion.2 = bf16[1120,896]{1,0:T(8,128)(2,1)} fusion(bf16[2048,1120]{1,0:T(8,128)(2,1)} %get-tuple-element.173, bf16[2048,896]{1,0:T(8,128)(2,1)} %attention_backward.2.left), kind=kOutput, calls=%fused_computation.17 | convolution fusion | flops 4111421440 | bytes 10264576 | tf_op jit(solution)/shard_map/dot_general | solution.py:39
  501.1 8.1 %partial_product.1.refs_2_ = f32[2048,1120]{1,0:T(8,128)} custom-call(bf16[2048,896]{1,0:T(8,128)(2,1)S(1)} %copy-done.2, bf16[1120,840]{1,0:T(8,128)(2,1)S(1)} %copy-done.37), custom_call_target="tpu_custom_call" | custom-call | flops 8999999488 | bytes 4096 | tf_op jit(solution)/shard_map/partial_product/pallas_call | solution.py:715
  509.2 4.9 fusion.8
  515.0 5.0 collective-permute-done.30.in_got
  520.0 10.3 %pack_rest.1 = (f32[3,420,1120]{2,1,0:T(8,128)}, bf16[3,420,1120]{2,1,0:T(8,128)(2,1)}) custom-call(s32[1]{0:T(128)} %bitcast.place_ref, f32[280,1120]{1,0:T(8,128)S(1)} %fusion.43.out_ref, f32[1120,1120]{1,0:T(8,128)} %fusion.42.in_ref, f32[1120,1120]{1,0:T(8,128)} %fusion.41.back_ref, bf16[280,1120]{1,0:T(8,128)(2,1)S(1)} %copy-done.25, ...), custom_call_target="tpu_custom_call" | custom-call | flops 10000000000 | bytes 4096 | tf_op jit(solution)/shard_map/pack_rest/pallas_call | solution.py:567
  532.7 51.9 %attention_backward.3.refs_0_ = bf16[2048,896]{1,0:T(8,128)(2,1)} custom-call(s32[4]{0:T(128)} %copy-done.26, s32[1]{0:T(128)} %bitcast.8.core_ref, s32[4,1,512]{2,1,0:T(1,128)} %copy-done.13, bf16[2048,840]{1,0:T(8,128)(2,1)} %get-tuple-element.174.qkv_ref, bf16[2048,280]{1,0:T(8,128)(2,1)} %copy-done.42, f32[4,280,512]{2,1,0:T(8,128)} %copy-done.44, ...), custom_call_target="tpu_custom_call" | custom-call | flops 56000000000 | bytes 4096 | tf_op jit(solution)/shard_map/attention_backward/pallas_call | solution.py:317
  584.6 3.0 collective-permute-done.32.received_ref
  589.2 11.5 %split_product.3 = (bf16[1024,1152]{1,0:T(8,128)(2,1)}, f32[1024,1120]{1,0:T(8,128)}) custom-call(bf16[2048,896]{1,0:T(8,128)(2,1)} %attention_backward.3.refs_0_, bf16[1120,840]{1,0:T(8,128)(2,1)S(1)} %copy-done.36, f32[2048,1120]{1,0:T(8,128)} %partial_product.1.refs_2_), custom_call_target="tpu_custom_call" | custom-call | flops 8999999488 | bytes 4096 | tf_op jit(solution)/shard_map/split_product/pallas_call | solution.py:735
  600.7 7.5 fusion.44
  612.1 3.3 fusion.32
  618.6 16.1 %collective-permute-done.35 = bf16[560,896]{1,0:T(8,128)(2,1)S(1)} collective-permute-done((bf16[560,896]{1,0:T(8,128)(2,1)S(1)}, bf16[560,896]{1,0:T(8,128)(2,1)S(1)}, u32[]{:S(2)}, u32[]{:S(2)}) %collective-permute-start.35) | collective-permute-done | bytes 1003552 | tf_op jit(solution)/shard_map/ppermute | solution.py:959
  639.0 20.6 %collective-permute-done.37 = bf16[420,1120]{1,0:T(8,128)(2,1)S(1)} collective-permute-done((bf16[420,1120]{1,0:T(8,128)(2,1)S(1)}, bf16[420,1120]{1,0:T(8,128)(2,1)S(1)}, u32[]{:S(2)}, u32[]{:S(2)}) %collective-permute-start.37) | collective-permute-done | bytes 940832 | tf_op jit(solution)/shard_map/ppermute | solution.py:959
  666.6 7.4 collective-permute-start.43
  674.0 2.3 copy-done.34
  676.3 7.1 norm_back.3
  686.5 27.7 %collective-permute-done.39 = bf16[560,896]{1,0:T(8,128)(2,1)} collective-permute-done((bf16[560,896]{1,0:T(8,128)(2,1)}, bf16[560,896]{1,0:T(8,128)(2,1)}, u32[]{:S(2)}, u32[]{:S(2)}) %collective-permute-start.39) | collective-permute-done | bytes 1003552 | tf_op jit(solution)/shard_map/ppermute | solution.py:959
  714.2 2.7 slice_add_fusion.1
  716.8 6.0 reshape.200.lead_ref
  724.8 4.0 reshape.203.rest_ref
  731.9 10.5 %new_moments.1 = (f32[1,1,470400]{2,1,0:T(1,128)}, f32[2,1,1,470400]{3,2,1,0:T(1,128)}, f32[1,1,470400]{2,1,0:T(1,128)S(1)}, f32[2]{0:T(128)S(1)}) custom-call(s32[2]{0:T(128)S(1)} %pad_add_fusion.ints_ref, f32[2]{0:T(128)S(1)} %pad_maximum_fusion.8.floats_ref, f32[1,1,470400]{2,1,0:T(1,128)S(1)} %copy-done.10, f32[1,1,470400]{2,1,0:T(1,128)S(1)} %copy-done.9, ...), custom_call_target="tpu_custom_call" | custom-call | flops 10000000000 | bytes 4096 | tf_op jit(solution)/shard_map/new_moments/pallas_call | solution.py:433
  744.2 2.5 fusion.24
  748.4 4.1 collective-permute-done.45
  757.0 4.3 collective-permute-done.47
  761.5 3.2 place_rows.3
  764.7 2.6 collective-permute-done.48
  771.4 6.7 new_weights.1
  (339 shorter events, 105.4 us)
Async XLA Ops:
  1.5 384.4 %copy-start.11 = (f32[12,1120]{1,0:T(8,128)}, f32[12,1120]{1,0:T(8,128)S(1)}, u32[]{:S(2)}) copy-start(f32[12,1120]{1,0:T(8,128)S(1)} %copy.52.small_ref) | copy-start | bytes 161284
  5.3 29.2 %collective-permute-start = (bf16[512,1152]{1,0:T(8,128)(2,1)}, bf16[512,1152]{1,0:T(8,128)(2,1)}, u32[]{:S(2)}, u32[]{:S(2)}) collective-permute-start(bf16[512,1152]{1,0:T(8,128)(2,1)} %get-tuple-element.163), channel_id=1, source_target_pairs={{0,2},{1,3},{2,0},{3,1},{4,6},{5,7},{6,4},{7,5},{8,10},{9,11},{10,... | collective-permute-start | bytes 3538952 | tf_op jit(solution)/shard_map/ppermute | solution.py:959
  11.9 29.1 %collective-permute-start.1 = (bf16[560,840]{1,0:T(8,128)(2,1)}, bf16[560,840]{1,0:T(8,128)(2,1)}, u32[]{:S(2)}, u32[]{:S(2)}) collective-permute-start(bf16[560,840]{1,0:T(8,128)(2,1)} %reshape.194), channel_id=1, source_target_pairs={{0,16},{4,20},{1,17},{5,21},{2,18},{6,22},{3,19},{7,23}} | collective-permute-start | bytes 2822408 | tf_op jit(solution)/shard_map/ppermute | solution.py:959
  40.9 29.8 %collective-permute-start.5 = (bf16[1024,1152]{1,0:T(8,128)(2,1)}, bf16[1024,1152]{1,0:T(8,128)(2,1)}, u32[]{:S(2)}, u32[]{:S(2)}) collective-permute-start(bf16[1024,1152]{1,0:T(8,128)(2,1)} %pad.16.own_ref), channel_id=1, source_target_pairs={{0,1},{1,0},{2,3},{3,2},{4,5},{5,4},{6,7},{7,6},{8,9},{9,8},{10,11... | collective-permute-start | bytes 7077896 | tf_op jit(solution)/shard_map/ppermute | solution.py:959
  42.1 27.3 %collective-permute-start.2 = (bf16[560,840]{1,0:T(8,128)(2,1)}, bf16[560,840]{1,0:T(8,128)(2,1)}, u32[]{:S(2)}, u32[]{:S(2)}) collective-permute-start(bf16[560,840]{1,0:T(8,128)(2,1)} %broadcast_select_fusion.4), channel_id=1, source_target_pairs={{0,8},{4,12},{16,24},{20,28},{1,9},{5,13},{17,25},{21,29},{2,10},{... | collective-permute-start | bytes 2822408 | tf_op jit(solution)/shard_map/ppermute | solution.py:959
  50.2 20.6 %collective-permute-start.3 = (bf16[420,1120]{1,0:T(8,128)(2,1)}, bf16[420,1120]{1,0:T(8,128)(2,1)}, u32[]{:S(2)}, u32[]{:S(2)}) collective-permute-start(bf16[420,1120]{1,0:T(8,128)(2,1)} %reshape.195.refs_0_), channel_id=1, source_target_pairs={{8,12},{9,13},{10,14},{11,15},{12,8},{13,9},{14,10},{15,11},{16,20... | collective-permute-start | bytes 2822408 | tf_op jit(solution)/shard_map/ppermute | solution.py:959
  51.8 19.0 %collective-permute-start.4 = (bf16[420,1120]{1,0:T(8,128)(2,1)}, bf16[420,1120]{1,0:T(8,128)(2,1)}, u32[]{:S(2)}, u32[]{:S(2)}) collective-permute-start(bf16[420,1120]{1,0:T(8,128)(2,1)} %reshape.195.refs_0_), channel_id=1, source_target_pairs={{8,10},{9,11},{10,8},{11,9},{12,14},{13,15},{14,12},{15,13},{16,18... | collective-permute-start | bytes 2822408 | tf_op jit(solution)/shard_map/ppermute | solution.py:959
  56.1 40.1 %copy-start.68 = (s32[4]{0:T(128)S(1)}, s32[4]{0:T(128)}, u32[]{:S(2)}) copy-start(s32[4]{0:T(128)} %constant.164.clone) | copy-start | bytes 52
  70.8 24.0 %collective-permute-start.6 = (bf16[560,840]{1,0:T(8,128)(2,1)S(1)}, bf16[560,840]{1,0:T(8,128)(2,1)}, u32[]{:S(2)}, u32[]{:S(2)}) collective-permute-start(bf16[560,840]{1,0:T(8,128)(2,1)S(1)} %broadcast_select_fusion.5.a0), channel_id=1, source_target_pairs={{0,4},{4,0},{8,12},{12,8},{16,20},{20,16},{24,28},{28,24},{1,5},{5... | collective-permute-start | bytes 2822408 | tf_op jit(solution)/shard_map/ppermute | solution.py:959
  72.9 132.7 %copy-start.26 = (s32[4]{0:T(128)}, s32[4]{0:T(128)S(1)}, u32[]{:S(2)}) copy-start(s32[4]{0:T(128)S(1)} %and_select_fusion.low_ref) | copy-start | bytes 52
  72.9 33.3 %collective-permute-start.7 = (bf16[560,840]{1,0:T(8,128)(2,1)S(1)}, bf16[560,840]{1,0:T(8,128)(2,1)}, u32[]{:S(2)}, u32[]{:S(2)}) collective-permute-start(bf16[560,840]{1,0:T(8,128)(2,1)S(1)} %broadcast_select_fusion.5.a0), channel_id=1, source_target_pairs={{0,2},{1,3},{2,0},{3,1},{4,6},{5,7},{6,4},{7,5},{8,10},{9,11},{10,... | collective-permute-start | bytes 2822408 | tf_op jit(solution)/shard_map/ppermute | solution.py:959
  74.4 52.1 %collective-permute-start.10 = (bf16[420,1120]{1,0:T(8,128)(2,1)}, bf16[420,1120]{1,0:T(8,128)(2,1)}, u32[]{:S(2)}, u32[]{:S(2)}) collective-permute-start(bf16[420,1120]{1,0:T(8,128)(2,1)} %reshape.195.refs_0_), channel_id=1, source_target_pairs={{8,24},{9,25},{10,26},{11,27},{12,28},{13,29},{14,30},{15,31},{16,... | collective-permute-start | bytes 2822408 | tf_op jit(solution)/shard_map/ppermute | solution.py:959
  75.7 52.1 %collective-permute-start.9 = (bf16[420,1120]{1,0:T(8,128)(2,1)}, bf16[420,1120]{1,0:T(8,128)(2,1)}, u32[]{:S(2)}, u32[]{:S(2)}) collective-permute-start(bf16[420,1120]{1,0:T(8,128)(2,1)} %reshape.195.refs_0_), channel_id=1, source_target_pairs={{8,0},{9,1},{10,2},{11,3},{12,4},{13,5},{14,6},{15,7},{16,24},{17,... | collective-permute-start | bytes 2822408 | tf_op jit(solution)/shard_map/ppermute | solution.py:959
  77.0 49.5 %collective-permute-start.11 = (bf16[420,1120]{1,0:T(8,128)(2,1)}, bf16[420,1120]{1,0:T(8,128)(2,1)}, u32[]{:S(2)}, u32[]{:S(2)}) collective-permute-start(bf16[420,1120]{1,0:T(8,128)(2,1)} %collective-permute-done.4.refs_0_), channel_id=1, source_target_pairs={{8,12},{9,13},{10,14},{11,15},{12,8},{13,9},{14,10},{15,11},{16,20... | collective-permute-start | bytes 2822408 | tf_op jit(solution)/shard_map/ppermute | solution.py:959
  94.8 33.1 %collective-permute-start.8 = (bf16[560,840]{1,0:T(8,128)(2,1)}, bf16[560,840]{1,0:T(8,128)(2,1)}, u32[]{:S(2)}, u32[]{:S(2)}) collective-permute-start(bf16[560,840]{1,0:T(8,128)(2,1)} %collective-permute-done.6.a1), channel_id=1, source_target_pairs={{0,2},{1,3},{2,0},{3,1},{4,6},{5,7},{6,4},{7,5},{8,10},{9,11},{10,... | collective-permute-start | bytes 2822408 | tf_op jit(solution)/shard_map/ppermute | solution.py:959
  99.9 105.6 %copy-start.13 = (s32[4,1,512]{2,1,0:T(1,128)}, s32[4,1,512]{2,1,0:T(1,128)S(1)}, u32[]{:S(2)}) copy-start(s32[4,1,512]{2,1,0:T(1,128)S(1)} %compare_select_fusion.start_ref) | copy-start | bytes 24580
  127.9 65.6 %collective-permute-start.12 = (bf16[420,1120]{1,0:T(8,128)(2,1)}, bf16[420,1120]{1,0:T(8,128)(2,1)}, u32[]{:S(2)}, u32[]{:S(2)}) collective-permute-start(bf16[420,1120]{1,0:T(8,128)(2,1)} %collective-permute-done.10.refs_4_), channel_id=1, source_target_pairs={{0,8},{1,9},{2,10},{3,11},{4,12},{5,13},{6,14},{7,15},{8,0},{9,1},... | collective-permute-start | bytes 2822408 | tf_op jit(solution)/shard_map/ppermute | solution.py:959
  129.8 63.7 %collective-permute-start.14 = (bf16[420,1120]{1,0:T(8,128)(2,1)}, bf16[420,1120]{1,0:T(8,128)(2,1)}, u32[]{:S(2)}, u32[]{:S(2)}) collective-permute-start(bf16[420,1120]{1,0:T(8,128)(2,1)} %collective-permute-done.10.refs_4_), channel_id=1, source_target_pairs={{0,4},{1,5},{2,6},{3,7},{4,0},{5,1},{6,2},{7,3},{8,12},{9,13},{10,... | collective-permute-start | bytes 2822408 | tf_op jit(solution)/shard_map/ppermute | solution.py:959
  133.2 60.2 %collective-permute-start.13 = (bf16[420,1120]{1,0:T(8,128)(2,1)}, bf16[420,1120]{1,0:T(8,128)(2,1)S(1)}, u32[]{:S(2)}, u32[]{:S(2)}) collective-permute-start(bf16[420,1120]{1,0:T(8,128)(2,1)} %collective-permute-done.9.refs_2_), channel_id=1, source_target_pairs={{0,4},{1,5},{2,6},{3,7},{4,0},{5,1},{6,2},{7,3},{16,20},{17,21},{1... | collective-permute-start | bytes 2822408 | tf_op jit(solution)/shard_map/ppermute | solution.py:959
  135.6 57.8 %collective-permute-start.15 = (bf16[420,1120]{1,0:T(8,128)(2,1)}, bf16[420,1120]{1,0:T(8,128)(2,1)S(1)}, u32[]{:S(2)}, u32[]{:S(2)}) collective-permute-start(bf16[420,1120]{1,0:T(8,128)(2,1)} %collective-permute-done.9.refs_2_), channel_id=1, source_target_pairs={{0,2},{1,3},{2,0},{3,1},{4,6},{5,7},{6,4},{7,5},{16,18},{17,19},{1... | collective-permute-start | bytes 2822408 | tf_op jit(solution)/shard_map/ppermute | solution.py:959
  138.1 55.4 %collective-permute-start.16 = (bf16[420,1120]{1,0:T(8,128)(2,1)}, bf16[420,1120]{1,0:T(8,128)(2,1)S(1)}, u32[]{:S(2)}, u32[]{:S(2)}) collective-permute-start(bf16[420,1120]{1,0:T(8,128)(2,1)} %collective-permute-done.10.refs_4_), channel_id=1, source_target_pairs={{0,2},{1,3},{2,0},{3,1},{4,6},{5,7},{6,4},{7,5},{8,10},{9,11},{10,... | collective-permute-start | bytes 2822408 | tf_op jit(solution)/shard_map/ppermute | solution.py:959
  158.1 35.3 %copy-start.35 = (bf16[1120,840]{1,0:T(8,128)(2,1)}, bf16[1120,840]{1,0:T(8,128)(2,1)S(1)}, u32[]{:S(2)}) copy-start(bf16[1120,840]{1,0:T(8,128)(2,1)S(1)} %get-tuple-element.265.refs_1_) | copy-start | bytes 5644804
  158.1 47.3 %copy-start.21 = (bf16[512,1152]{1,0:T(8,128)(2,1)S(1)}, bf16[512,1152]{1,0:T(8,128)(2,1)}, u32[]{:S(2)}) copy-start(bf16[512,1152]{1,0:T(8,128)(2,1)} %copy-done.20) | copy-start | bytes 3538948
  193.4 46.9 %copy-start.44 = (f32[4,280,512]{2,1,0:T(8,128)}, f32[4,280,512]{2,1,0:T(8,128)S(1)}, u32[]{:S(2)}) copy-start(f32[4,280,512]{2,1,0:T(8,128)S(1)} %get-tuple-element.262.outt_ref) | copy-start | bytes 6881284
  193.4 46.8 %copy-start.46 = (f32[4,8,512]{2,1,0:T(8,128)}, f32[4,8,512]{2,1,0:T(8,128)S(1)}, u32[]{:S(2)}) copy-start(f32[4,8,512]{2,1,0:T(8,128)S(1)} %get-tuple-element.179.lse_ref) | copy-start | bytes 196612
  193.5 49.9 %collective-permute-start.18 = (bf16[420,1120]{1,0:T(8,128)(2,1)}, bf16[420,1120]{1,0:T(8,128)(2,1)}, u32[]{:S(2)}, u32[]{:S(2)}) collective-permute-start(bf16[420,1120]{1,0:T(8,128)(2,1)} %collective-permute-done.12.refs_6_), channel_id=1, source_target_pairs={{0,4},{1,5},{2,6},{3,7},{4,0},{5,1},{6,2},{7,3},{8,12},{9,13},{10,... | collective-permute-start | bytes 2822408 | tf_op jit(solution)/shard_map/ppermute | solution.py:959
  195.4 48.0 %collective-permute-start.19 = (bf16[420,1120]{1,0:T(8,128)(2,1)}, bf16[420,1120]{1,0:T(8,128)(2,1)}, u32[]{:S(2)}, u32[]{:S(2)}) collective-permute-start(bf16[420,1120]{1,0:T(8,128)(2,1)} %collective-permute-done.12.refs_6_), channel_id=1, source_target_pairs={{0,2},{1,3},{2,0},{3,1},{4,6},{5,7},{6,4},{7,5},{8,10},{9,11},{10,... | collective-permute-start | bytes 2822408 | tf_op jit(solution)/shard_map/ppermute | solution.py:959
  197.4 46.1 %collective-permute-start.20 = (bf16[420,1120]{1,0:T(8,128)(2,1)S(1)}, bf16[420,1120]{1,0:T(8,128)(2,1)S(1)}, u32[]{:S(2)}, u32[]{:S(2)}) collective-permute-start(bf16[420,1120]{1,0:T(8,128)(2,1)S(1)} %collective-permute-done.15.refs_2_), channel_id=1, source_target_pairs={{0,4},{1,5},{2,6},{3,7},{4,0},{5,1},{6,2},{7,3},{16,20},{17,21},{1... | collective-permute-start | bytes 2822408 | tf_op jit(solution)/shard_map/ppermute | solution.py:959
  201.3 43.2 %collective-permute-start.21 = (bf16[420,1120]{1,0:T(8,128)(2,1)}, bf16[420,1120]{1,0:T(8,128)(2,1)S(1)}, u32[]{:S(2)}, u32[]{:S(2)}) collective-permute-start(bf16[420,1120]{1,0:T(8,128)(2,1)} %collective-permute-done.14.refs_5_), channel_id=1, source_target_pairs={{0,2},{1,3},{2,0},{3,1},{4,6},{5,7},{6,4},{7,5},{8,10},{9,11},{10,... | collective-permute-start | bytes 2822408 | tf_op jit(solution)/shard_map/ppermute | solution.py:959
  205.4 59.4 %collective-permute-start.17 = (bf16[512,1152]{1,0:T(8,128)(2,1)S(1)}, bf16[512,1152]{1,0:T(8,128)(2,1)}, u32[]{:S(2)}, u32[]{:S(2)}) collective-permute-start(bf16[512,1152]{1,0:T(8,128)(2,1)S(1)} %copy-done.21), channel_id=1, source_target_pairs={{0,2},{1,3},{2,0},{3,1},{4,6},{5,7},{6,4},{7,5},{8,10},{9,11},{10,... | collective-permute-start | bytes 3538952 | tf_op jit(solution)/shard_map/ppermute | solution.py:959
  245.4 22.0 %collective-permute-start.22 = (bf16[420,1120]{1,0:T(8,128)(2,1)}, bf16[420,1120]{1,0:T(8,128)(2,1)S(1)}, u32[]{:S(2)}, u32[]{:S(2)}) collective-permute-start(bf16[420,1120]{1,0:T(8,128)(2,1)} %collective-permute-done.19.refs_6_), channel_id=1, source_target_pairs={{0,4},{1,5},{2,6},{3,7},{4,0},{5,1},{6,2},{7,3},{8,12},{9,13},{10,... | collective-permute-start | bytes 2822408 | tf_op jit(solution)/shard_map/ppermute | solution.py:959
  253.6 20.3 %copy-start.40 = (bf16[280,1120]{1,0:T(8,128)(2,1)}, bf16[280,1120]{1,0:T(8,128)(2,1)S(1)}, u32[]{:S(2)}) copy-start(bf16[280,1120]{1,0:T(8,128)(2,1)S(1)} %get-tuple-element.199.refs_2_.w_a) | copy-start | bytes 1881604
  282.4 5.1 collective-permute-start.23
  282.6 10.4 %collective-permute-start.25 = (bf16[1024,1152]{1,0:T(8,128)(2,1)S(1)}, bf16[1024,1152]{1,0:T(8,128)(2,1)S(1)}, u32[]{:S(2)}, u32[]{:S(2)}) collective-permute-start(bf16[1024,1152]{1,0:T(8,128)(2,1)S(1)} %pad_maximum_fusion.1.cot_ref.base_ref), channel_id=1, source_target_pairs={{0,1},{1,0},{2,3},{3,2},{4,5},{5,4},{6,7},{7,6},{8,9},{9,8},{10,11... | collective-permute-start | bytes 7077896 | tf_op jit(solution)/shard_map/ppermute | solution.py:959
  292.0 4.5 collective-permute-start.24
  329.8 32.5 %collective-permute-start.26 = (f32[1024,1152]{1,0:T(8,128)}, f32[1024,1152]{1,0:T(8,128)}, u32[]{:S(2)}, u32[]{:S(2)}) collective-permute-start(f32[1024,1152]{1,0:T(8,128)} %get-tuple-element.227), channel_id=1, source_target_pairs={{0,1},{1,0},{2,3},{3,2},{4,5},{5,4},{6,7},{7,6},{8,9},{9,8},{10,11... | collective-permute-start | bytes 14155784 | tf_op jit(solution)/shard_map/ppermute | solution.py:959
  330.0 32.3 %copy-start.6 = (bf16[1024,1152]{1,0:T(8,128)(2,1)S(1)}, bf16[1024,1152]{1,0:T(8,128)(2,1)}, u32[]{:S(2)}) copy-start(bf16[1024,1152]{1,0:T(8,128)(2,1)} %copy-done.5) | copy-start | bytes 7077892
  372.4 18.8 %copy-start.59 = (f32[8,2304]{1,0:T(8,128)S(1)}, f32[8,2304]{1,0:T(8,128)}, u32[]{:S(2)}) copy-start(f32[8,2304]{1,0:T(8,128)} %get-tuple-element.298) | copy-start | bytes 221188
  372.4 18.8 %copy-start.60 = (f32[8,2304]{1,0:T(8,128)S(1)}, f32[8,2304]{1,0:T(8,128)}, u32[]{:S(2)}) copy-start(f32[8,2304]{1,0:T(8,128)} %get-tuple-element.299) | copy-start | bytes 221188
  385.6 6.8 collective-permute-start.27
  391.1 118.1 %collective-permute-start.29 = (f32[1024,1152]{1,0:T(8,128)}, f32[1024,1152]{1,0:T(8,128)}, u32[]{:S(2)}, u32[]{:S(2)}) collective-permute-start(f32[1024,1152]{1,0:T(8,128)} %get-tuple-element.249), channel_id=1, source_target_pairs={{0,1},{1,0},{2,3},{3,2},{4,5},{5,4},{6,7},{7,6},{8,9},{9,8},{10,11... | collective-permute-start | bytes 14155784 | tf_op jit(solution)/shard_map/ppermute | solution.py:959
  391.7 123.3 %collective-permute-start.31 = (bf16[1120,1120]{1,0:T(8,128)(2,1)}, bf16[1120,1120]{1,0:T(8,128)(2,1)}, u32[]{:S(2)}, u32[]{:S(2)}) collective-permute-start(bf16[1120,1120]{1,0:T(8,128)(2,1)} %convolution_convert_fusion.1), channel_id=1, source_target_pairs={{0,2},{1,3},{2,0},{3,1},{4,6},{5,7},{6,4},{7,5},{8,10},{9,11},{10,... | collective-permute-start | bytes 7526408 | tf_op jit(solution)/shard_map/ppermute | solution.py:959
  437.3 63.8 %collective-permute-start.28 = (bf16[280,1120]{1,0:T(8,128)(2,1)}, bf16[280,1120]{1,0:T(8,128)(2,1)S(1)}, u32[]{:S(2)}, u32[]{:S(2)}) collective-permute-start(bf16[280,1120]{1,0:T(8,128)(2,1)} %convolution_convert_fusion.3), channel_id=1, source_target_pairs={{0,2},{1,3},{2,0},{3,1},{4,6},{5,7},{6,4},{7,5},{8,10},{9,11},{10,... | collective-permute-start | bytes 1881608 | tf_op jit(solution)/shard_map/ppermute | solution.py:959
  439.3 80.7 %collective-permute-start.30 = (bf16[1120,1120]{1,0:T(8,128)(2,1)}, bf16[1120,1120]{1,0:T(8,128)(2,1)}, u32[]{:S(2)}, u32[]{:S(2)}) collective-permute-start(bf16[1120,1120]{1,0:T(8,128)(2,1)} %convolution_convert_fusion), channel_id=1, source_target_pairs={{0,2},{1,3},{2,0},{3,1},{4,6},{5,7},{6,4},{7,5},{8,10},{9,11},{10,... | collective-permute-start | bytes 7526408 | tf_op jit(solution)/shard_map/ppermute | solution.py:959
  515.0 93.3 %collective-permute-start.33 = (bf16[1120,896]{1,0:T(8,128)(2,1)}, bf16[1120,896]{1,0:T(8,128)(2,1)}, u32[]{:S(2)}, u32[]{:S(2)}) collective-permute-start(bf16[1120,896]{1,0:T(8,128)(2,1)} %convolution_convert_fusion.2), channel_id=1, source_target_pairs={{0,2},{1,3},{2,0},{3,1},{4,6},{5,7},{6,4},{7,5},{8,10},{9,11},{10,... | collective-permute-start | bytes 6021128 | tf_op jit(solution)/shard_map/ppermute | solution.py:959
  531.5 56.2 %collective-permute-start.32 = (bf16[512,1152]{1,0:T(8,128)(2,1)}, bf16[512,1152]{1,0:T(8,128)(2,1)S(1)}, u32[]{:S(2)}, u32[]{:S(2)}) collective-permute-start(bf16[512,1152]{1,0:T(8,128)(2,1)} %slice_select_fusion.2), channel_id=1, source_target_pairs={{0,2},{1,3},{2,0},{3,1},{4,6},{5,7},{6,4},{7,5},{8,10},{9,11},{10,... | collective-permute-start | bytes 3538952 | tf_op jit(solution)/shard_map/ppermute | solution.py:959
  531.5 80.5 %collective-permute-start.34 = (bf16[3,420,1120]{2,1,0:T(8,128)(2,1)}, bf16[3,420,1120]{2,1,0:T(8,128)(2,1)}, u32[]{:S(2)}, u32[]{:S(2)}) collective-permute-start(bf16[3,420,1120]{2,1,0:T(8,128)(2,1)} %get-tuple-element.272), channel_id=1, source_target_pairs={{0,4},{4,0},{8,12},{12,8},{16,20},{20,16},{24,28},{28,24},{1,5},{5... | collective-permute-start | bytes 8467208 | tf_op jit(solution)/shard_map/ppermute | solution.py:959
  610.9 23.8 %collective-permute-start.35 = (bf16[560,896]{1,0:T(8,128)(2,1)S(1)}, bf16[560,896]{1,0:T(8,128)(2,1)S(1)}, u32[]{:S(2)}, u32[]{:S(2)}) collective-permute-start(bf16[560,896]{1,0:T(8,128)(2,1)S(1)} %select_convert_fusion), channel_id=1, source_target_pairs={{0,4},{4,0},{8,12},{12,8},{16,20},{20,16},{24,28},{28,24},{1,5},{5... | collective-permute-start | bytes 3010568 | tf_op jit(solution)/shard_map/ppermute | solution.py:959
  612.0 62.0 %collective-permute-start.41 = (bf16[1024,1152]{1,0:T(8,128)(2,1)}, bf16[1024,1152]{1,0:T(8,128)(2,1)}, u32[]{:S(2)}, u32[]{:S(2)}) collective-permute-start(bf16[1024,1152]{1,0:T(8,128)(2,1)} %get-tuple-element.294), channel_id=1, source_target_pairs={{0,1},{1,0},{2,3},{3,2},{4,5},{5,4},{6,7},{7,6},{8,9},{9,8},{10,11... | collective-permute-start | bytes 7077896 | tf_op jit(solution)/shard_map/ppermute | solution.py:959
  615.4 23.6 %collective-permute-start.36 = (bf16[420,1120]{1,0:T(8,128)(2,1)}, bf16[420,1120]{1,0:T(8,128)(2,1)S(1)}, u32[]{:S(2)}, u32[]{:S(2)}) collective-permute-start(bf16[420,1120]{1,0:T(8,128)(2,1)} %get-tuple-element.277), channel_id=1, source_target_pairs={{0,8},{4,12},{16,24},{20,28},{1,9},{5,13},{17,25},{21,29},{2,10},{... | collective-permute-start | bytes 2822408 | tf_op jit(solution)/shard_map/ppermute | solution.py:959
  616.7 42.9 %collective-permute-start.37 = (bf16[420,1120]{1,0:T(8,128)(2,1)S(1)}, bf16[420,1120]{1,0:T(8,128)(2,1)S(1)}, u32[]{:S(2)}, u32[]{:S(2)}) collective-permute-start(bf16[420,1120]{1,0:T(8,128)(2,1)S(1)} %get-tuple-element.279), channel_id=1, source_target_pairs={{0,8},{4,12},{8,0},{12,4},{16,24},{20,28},{24,16},{28,20},{1,9},{5... | collective-permute-start | bytes 2822408 | tf_op jit(solution)/shard_map/ppermute | solution.py:959
  634.9 27.4 %collective-permute-start.38 = (bf16[560,896]{1,0:T(8,128)(2,1)S(1)}, bf16[560,896]{1,0:T(8,128)(2,1)S(1)}, u32[]{:S(2)}, u32[]{:S(2)}) collective-permute-start(bf16[560,896]{1,0:T(8,128)(2,1)S(1)} %get-tuple-element.283), channel_id=1, source_target_pairs={{8,0},{12,4},{24,16},{28,20},{9,1},{13,5},{25,17},{29,21},{10,2},{... | collective-permute-start | bytes 3010568 | tf_op jit(solution)/shard_map/ppermute | solution.py:959
  664.2 2.4 collective-permute-start.40
  665.3 48.9 %collective-permute-start.39 = (bf16[560,896]{1,0:T(8,128)(2,1)}, bf16[560,896]{1,0:T(8,128)(2,1)}, u32[]{:S(2)}, u32[]{:S(2)}) collective-permute-start(bf16[560,896]{1,0:T(8,128)(2,1)} %get-tuple-element.288), channel_id=1, source_target_pairs={{16,0},{20,4},{17,1},{21,5},{18,2},{22,6},{19,3},{23,7}} | collective-permute-start | bytes 3010568 | tf_op jit(solution)/shard_map/ppermute | solution.py:959
  666.6 56.3 %collective-permute-start.43 = (bf16[420,1120]{1,0:T(8,128)(2,1)}, bf16[420,1120]{1,0:T(8,128)(2,1)}, u32[]{:S(2)}, u32[]{:S(2)}) collective-permute-start(bf16[420,1120]{1,0:T(8,128)(2,1)} %get-tuple-element.304), channel_id=1, source_target_pairs={{24,8},{28,12},{0,16},{4,20},{8,24},{12,28},{25,9},{29,13},{1,17},... | collective-permute-start | bytes 2822408 | tf_op jit(solution)/shard_map/ppermute | solution.py:959
  683.4 30.7 %copy-start.53 = (f32[560,896]{1,0:T(8,128)S(1)}, f32[560,896]{1,0:T(8,128)}, u32[]{:S(2)}) copy-start(f32[560,896]{1,0:T(8,128)} %get-tuple-element.286) | copy-start | bytes 6021124
  686.1 75.3 %collective-permute-start.42 = (bf16[512,1152]{1,0:T(8,128)(2,1)}, bf16[512,1152]{1,0:T(8,128)(2,1)}, u32[]{:S(2)}, u32[]{:S(2)}) collective-permute-start(bf16[512,1152]{1,0:T(8,128)(2,1)} %slice_select_fusion.1), channel_id=1, source_target_pairs={{0,2},{1,3},{2,0},{3,1},{4,6},{5,7},{6,4},{7,5},{8,10},{9,11},{10,... | collective-permute-start | bytes 3538952 | tf_op jit(solution)/shard_map/ppermute | solution.py:959
  731.9 25.1 %copy-start.12 = (f32[12,1120]{1,0:T(8,128)S(1)}, f32[12,1120]{1,0:T(8,128)}, u32[]{:S(2)}) copy-start(f32[12,1120]{1,0:T(8,128)} %copy-done.11) | copy-start | bytes 161284
  731.9 29.6 %copy-start.8 = (bf16[1024,1152]{1,0:T(8,128)(2,1)S(1)}, bf16[1024,1152]{1,0:T(8,128)(2,1)}, u32[]{:S(2)}) copy-start(bf16[1024,1152]{1,0:T(8,128)(2,1)} %copy-done.7) | copy-start | bytes 7077892
  746.7 1.3 collective-permute-start.44
  748.1 4.4 collective-permute-start.45
  752.5 4.4 collective-permute-start.46
  756.9 4.4 collective-permute-start.47
  761.4 5.9 collective-permute-start.48
  (72 other events, 445.0 us)
